TPU v7x, 32 devices: a whole 2x2x4 slice. The times are simulated.
32 devices in a mesh: shard: 8 (over y, x, core), context: 2 (over z_hi), tensor: 2 (over z_lo).
Axes of the slice: x: 2, y: 2, z: 4 (z_hi: 2, z_lo: 2; z = z_hi * 2 + z_lo), core: 2. Of those that a mesh axis runs over, the one named last changes fastest.
Arguments:
- inputs: bfloat16 [8, 1024, 2048], P('shard', 'context'), may hold values from -6 to 6
- cotangent: bfloat16 [8, 1024, 2048], P('shard', 'context'), may hold values from -6 to 6
- qkv_weight: bfloat16 [2048, 8, 768], P(('shard', 'context'), 'tensor'), may hold values from -0.125 to 0.125
- dense_weight: bfloat16 [2048, 2048], P(('shard', 'context'), 'tensor'), may hold values from -0.25 to 0.25
- up_weight: bfloat16 [2048, 8192], P(('shard', 'context'), 'tensor'), may hold values from -0.125 to 0.125
- down_weight: bfloat16 [2048, 8192], P(('shard', 'context'), 'tensor'), may hold values from -0.0625 to 0.0625
- unit_biases: bfloat16 [8, 1792], P('tensor'), may hold values from -3 to 3
- vectors: bfloat16 [6, 2048], replicated, as said below
- qkv_moments: float32 [2, 2048, 8, 768], P(None, ('shard', 'context'), 'tensor'), as said below
- dense_moments: float32 [2, 2048, 2048], P(None, ('shard', 'context'), 'tensor'), as said below
- up_moments: float32 [2, 2048, 8192], P(None, ('shard', 'context'), 'tensor'), as said below
- down_moments: float32 [2, 2048, 8192], P(None, ('shard', 'context'), 'tensor'), as said below
- unit_moments: float32 [2, 8, 1792], P(None, 'tensor'), as said below
- vector_moments: float32 [2, 6, 2048], replicated, as said below
- step_count: int32 [], replicated, may hold values from 1 to 20
Outputs:
- outputs: bfloat16 [8, 1024, 2048], P('shard', 'context')
- input_grad: float32 [8, 1024, 2048], P('shard', 'context')
- qkv_grad: float32 [2048, 8, 768], P(('shard', 'context'), 'tensor')
- dense_grad: float32 [2048, 2048], P(('shard', 'context'), 'tensor')
- up_grad: float32 [2048, 8192], P(('shard', 'context'), 'tensor')
- down_grad: float32 [2048, 8192], P(('shard', 'context'), 'tensor')
- unit_grad: float32 [8, 1792], P('tensor')
- vector_grad: float32 [6, 2048], replicated
- qkv_moments_new: float32 [2, 2048, 8, 768], P(None, ('shard', 'context'), 'tensor')
- dense_moments_new: float32 [2, 2048, 2048], P(None, ('shard', 'context'), 'tensor')
- up_moments_new: float32 [2, 2048, 8192], P(None, ('shard', 'context'), 'tensor')
- down_moments_new: float32 [2, 2048, 8192], P(None, ('shard', 'context'), 'tensor')
- unit_moments_new: float32 [2, 8, 1792], P(None, 'tensor')
- vector_moments_new: float32 [2, 6, 2048], replicated
- qkv_update: float32 [2048, 8, 768], P(('shard', 'context'), 'tensor')
- dense_update: float32 [2048, 2048], P(('shard', 'context'), 'tensor')
- up_update: float32 [2048, 8192], P(('shard', 'context'), 'tensor')
- down_update: float32 [2048, 8192], P(('shard', 'context'), 'tensor')
- unit_update: float32 [8, 1792], P('tensor')
- vector_update: float32 [6, 2048], replicated
Inputs may be any that keep to these rules, and one draw needn't show every extreme that they name: `vectors`: rows 0 and 2 lie between 0.5 and 1.5; the other rows are of order one half. `qkv_moments`: the root mean square states are positive. `dense_moments`: the root mean square states are positive. `up_moments`: the root mean square states are positive. `down_moments`: the root mean square states are positive. `unit_moments`: the root mean square states are positive. `vector_moments`: the root mean square states are positive.
All inputs are finite; a program needn't handle non-finite values.
Results may differ from a plain program's by a relative error of at most 0.009.
Values may be sent and summed in bfloat16 or wider, within the bound.
No kernel may reach another device: no remote copies, remote signals or barrier semaphores. Data moves between devices by JAX's collectives and lax.ppermute only.
A program may use at most 256 MiB of HBM per device.

v0:
```python
import math

import jax
import jax.numpy as jnp
from jax import lax
from jax.sharding import PartitionSpec as P

HEAD_DIM = 256
ROTARY = 64


EPSILON = 1e-05
BETA_ONE = 0.9
BETA_TWO = 0.95
LEARN_RATE = 0.02
WEIGHT_DECAY = 0.01
ROOT_HALF = 0.7071067811865476
ROOT_TWO_PI = 2.5066282746310002
MASKED = -1000000000.0


def normalize(token_rows):
    center = token_rows - jnp.mean(token_rows, -1, keepdims=True)
    inv_std = lax.rsqrt(jnp.mean(center * center, -1, keepdims=True) + EPSILON)
    return (center * inv_std, inv_std)


def norm_back(grad_norm, gain, normed, inv_std):
    scaled = grad_norm * gain
    return inv_std * (
        scaled
        - jnp.mean(scaled, -1, keepdims=True)
        - normed * jnp.mean(scaled * normed, -1, keepdims=True)
    )


def gelu_value(hidden):
    return 0.5 * hidden * (1.0 + lax.erf(hidden * ROOT_HALF))


def gelu_slope(hidden):
    return (
        0.5 * (1.0 + lax.erf(hidden * ROOT_HALF))
        + hidden * jnp.exp(-0.5 * hidden * hidden) / ROOT_TWO_PI
    )


def angle_table(positions):
    half_index = jnp.arange(ROTARY // 2, dtype=jnp.float32)
    inverse = jnp.exp(half_index * (-2.0 / ROTARY) * math.log(10000.0))
    angles = positions.astype(jnp.float32)[:, None] * inverse[None, :]
    return (jnp.cos(angles), jnp.sin(angles))


def turn(block_data, cosine, sine_table, sign_flip):
    half_width = ROTARY // 2
    first_half = block_data[..., :half_width]
    second_half = block_data[..., half_width:ROTARY]
    cos_part = cosine[None, :, None, :]
    sin_part = sign_flip * sine_table[None, :, None, :]
    return jnp.concatenate(
        [
            first_half * cos_part - second_half * sin_part,
            second_half * cos_part + first_half * sin_part,
            block_data[..., ROTARY:],
        ],
        -1,
    )


def block_scores(query_part, key_rows, row_start, block_rows, length):
    scores = jnp.einsum(
        "sqge,skge->sgqk", query_part, key_rows, preferred_element_type=jnp.float32
    ) * HEAD_DIM ** (-0.5)
    row_ids = row_start + jnp.arange(block_rows)
    column_ids = jnp.arange(length)
    return jnp.where(row_ids[:, None] >= column_ids[None, :], scores, MASKED)


def attend_forward(packed):
    seq_count, length, group_count, packed_width = packed.shape
    queries = packed[..., :HEAD_DIM]
    key_rows = packed[..., HEAD_DIM : 2 * HEAD_DIM]
    value_rows = packed[..., 2 * HEAD_DIM :]
    block_rows = min(512, length)
    block_count = length // block_rows

    def one_block(block_index):
        row_start = block_index * block_rows
        query_part = lax.dynamic_slice_in_dim(queries, row_start, block_rows, 1)
        scores = block_scores(query_part, key_rows, row_start, block_rows, length)
        maximum = jnp.max(scores, -1, keepdims=True)
        exponent = jnp.exp(scores - maximum)
        row_total = jnp.sum(exponent, -1, keepdims=True)
        weights_low = (exponent / row_total).astype(jnp.bfloat16)
        mixed = jnp.einsum(
            "sgqk,skge->sqge", weights_low, value_rows, preferred_element_type=jnp.float32
        )
        return (mixed.astype(jnp.bfloat16), (maximum + jnp.log(row_total))[..., 0])

    mixed_blocks, log_blocks = lax.map(one_block, jnp.arange(block_count))
    mixed = mixed_blocks.transpose(1, 0, 2, 3, 4).reshape(seq_count, length, group_count, HEAD_DIM)
    log_totals = log_blocks.transpose(1, 2, 0, 3).reshape(seq_count, group_count, length)
    return (mixed, log_totals)


def attend_backward(packed, grad_mixed, log_totals):
    seq_count, length, group_count, packed_width = packed.shape
    queries = packed[..., :HEAD_DIM]
    key_rows = packed[..., HEAD_DIM : 2 * HEAD_DIM]
    value_rows = packed[..., 2 * HEAD_DIM :]
    block_rows = min(512, length)
    block_count = length // block_rows

    def one_block(running, block_index):
        key_grad, value_grad = running
        row_start = block_index * block_rows
        query_part = lax.dynamic_slice_in_dim(queries, row_start, block_rows, 1)
        grad_part = lax.dynamic_slice_in_dim(grad_mixed, row_start, block_rows, 1)
        scores = block_scores(query_part, key_rows, row_start, block_rows, length)
        log_part = lax.dynamic_slice_in_dim(log_totals, row_start, block_rows, 2)
        probs = jnp.exp(scores - log_part[..., None])
        weight_grad = jnp.einsum(
            "sqge,skge->sgqk", grad_part, value_rows, preferred_element_type=jnp.float32
        )
        score_grad = (
            probs * (weight_grad - jnp.sum(probs * weight_grad, -1, keepdims=True))
        ).astype(jnp.bfloat16)
        query_grad = jnp.einsum(
            "sgqk,skge->sqge", score_grad, key_rows, preferred_element_type=jnp.float32
        ) * HEAD_DIM ** (-0.5)
        key_grad = key_grad + jnp.einsum(
            "sgqk,sqge->skge", score_grad, query_part, preferred_element_type=jnp.float32
        ) * HEAD_DIM ** (-0.5)
        value_grad = value_grad + jnp.einsum(
            "sgqk,sqge->skge",
            probs.astype(jnp.bfloat16),
            grad_part,
            preferred_element_type=jnp.float32,
        )
        return ((key_grad, value_grad), query_grad)

    zero_rows = jnp.zeros((seq_count, length, group_count, HEAD_DIM), jnp.float32)
    (key_grad, value_grad), query_blocks = lax.scan(
        one_block, (zero_rows, zero_rows), jnp.arange(block_count)
    )
    query_grad = query_blocks.transpose(1, 0, 2, 3, 4).reshape(
        seq_count, length, group_count, HEAD_DIM
    )
    return jnp.concatenate([query_grad, key_grad, value_grad], -1).astype(jnp.bfloat16)


def adam_step(weight, moments, gradient, count_value, decay_rate):
    first_new = BETA_ONE * moments[0] + (1.0 - BETA_ONE) * gradient
    root_new = jnp.sqrt(BETA_TWO * moments[1] * moments[1] + (1.0 - BETA_TWO) * gradient * gradient)
    fix_one = 1.0 - jnp.power(BETA_ONE, count_value)
    fix_two = 1.0 - jnp.power(BETA_TWO, count_value)
    change = -LEARN_RATE * (
        first_new / fix_one / (root_new / jnp.sqrt(fix_two) + 1e-08) + decay_rate * weight
    )
    return (jnp.stack([first_new, root_new]), change)


def vector_sums(attn_norm_grad, mlp_norm_grad, normed, grad_float):
    return jnp.stack(
        [
            jnp.sum(attn_norm_grad * normed, 0),
            jnp.sum(attn_norm_grad, 0),
            jnp.sum(mlp_norm_grad * normed, 0),
            jnp.sum(mlp_norm_grad, 0),
            jnp.sum(grad_float, 0),
            jnp.sum(grad_float, 0),
        ]
    )


def on_device(
    inputs,
    cotangent,
    qkv_weight,
    dense_weight,
    up_weight,
    down_weight,
    unit_biases,
    vectors,
    qkv_moments,
    dense_moments,
    up_moments,
    down_moments,
    unit_moments,
    vector_moments,
    step_count,
):
    seq_count, local_len, feature_width = inputs.shape
    token_rows = seq_count * local_len
    w_qkv, w_dense, w_up, w_down = (
        lax.all_gather(qkv_weight, ("shard", "context"), axis=0, tiled=True),
        lax.all_gather(dense_weight, ("shard", "context"), axis=0, tiled=True),
        lax.all_gather(up_weight, ("shard", "context"), axis=0, tiled=True),
        lax.all_gather(down_weight, ("shard", "context"), axis=0, tiled=True),
    )
    heads_local = w_qkv.shape[1]
    units_local = w_up.shape[1]
    vector_vals = vectors.astype(jnp.float32)
    unit_vals = unit_biases.astype(jnp.float32)
    inputs_flat = inputs.reshape(token_rows, feature_width).astype(jnp.float32)
    normed, inv_std = normalize(inputs_flat)
    a_attn = (normed * vector_vals[0] + vector_vals[1]).astype(jnp.bfloat16)
    a_mlp = (normed * vector_vals[2] + vector_vals[3]).astype(jnp.bfloat16)
    linear = (
        jnp.einsum("td,dhe->the", a_attn, w_qkv, preferred_element_type=jnp.float32)
        + unit_vals[:, : 3 * HEAD_DIM]
    )
    linear = linear.reshape(seq_count, local_len, heads_local, 3 * HEAD_DIM)
    positions = lax.axis_index("context") * local_len + jnp.arange(local_len)
    cosine, sine_table = angle_table(positions)
    packed = jnp.concatenate(
        [
            turn(linear[..., :HEAD_DIM], cosine, sine_table, 1.0),
            turn(linear[..., HEAD_DIM : 2 * HEAD_DIM], cosine, sine_table, 1.0),
            linear[..., 2 * HEAD_DIM :],
        ],
        -1,
    ).astype(jnp.bfloat16)
    grouped = lax.all_to_all(packed, "context", split_axis=2, concat_axis=1, tiled=True)
    mixed_grouped, log_totals = attend_forward(grouped)
    context_out = lax.all_to_all(mixed_grouped, "context", split_axis=1, concat_axis=2, tiled=True)
    context_flat = context_out.reshape(token_rows, heads_local * HEAD_DIM)
    hidden = jnp.dot(a_mlp, w_up, preferred_element_type=jnp.float32) + unit_vals[
        :, 3 * HEAD_DIM :
    ].reshape(units_local)
    active = gelu_value(hidden).astype(jnp.bfloat16)
    out_bias = vector_vals[4] + vector_vals[5]
    branch = jnp.einsum("tc,dc->td", context_flat, w_dense, preferred_element_type=jnp.float32)
    branch = branch + jnp.einsum("tf,df->td", active, w_down, preferred_element_type=jnp.float32)
    branch = lax.psum(branch.astype(jnp.bfloat16), "tensor").astype(jnp.float32)
    outputs = (inputs_flat + branch + out_bias).astype(jnp.bfloat16)
    outputs = outputs.reshape(seq_count, local_len, feature_width)
    grad_rows = cotangent.reshape(token_rows, feature_width)
    grad_float = grad_rows.astype(jnp.float32)
    down_partial = jnp.einsum("td,tf->df", grad_rows, active, preferred_element_type=jnp.float32)
    dense_partial = jnp.einsum(
        "td,tc->dc", grad_rows, context_flat, preferred_element_type=jnp.float32
    )
    d_hidden = jnp.dot(grad_rows, w_down, preferred_element_type=jnp.float32) * gelu_slope(hidden)
    d_hidden_low = d_hidden.astype(jnp.bfloat16)
    up_partial = jnp.einsum("td,tf->df", a_mlp, d_hidden_low, preferred_element_type=jnp.float32)
    d_context = jnp.dot(grad_rows, w_dense, preferred_element_type=jnp.float32).astype(jnp.bfloat16)
    d_context = d_context.reshape(seq_count, local_len, heads_local, HEAD_DIM)
    d_grouped = lax.all_to_all(d_context, "context", split_axis=2, concat_axis=1, tiled=True)
    d_packed_grouped = attend_backward(grouped, d_grouped, log_totals)
    d_packed = lax.all_to_all(
        d_packed_grouped, "context", split_axis=1, concat_axis=2, tiled=True
    ).astype(jnp.float32)
    d_qkv = jnp.concatenate(
        [
            turn(d_packed[..., :HEAD_DIM], cosine, sine_table, -1.0),
            turn(d_packed[..., HEAD_DIM : 2 * HEAD_DIM], cosine, sine_table, -1.0),
            d_packed[..., 2 * HEAD_DIM :],
        ],
        -1,
    )
    d_qkv = d_qkv.reshape(token_rows, heads_local, 3 * HEAD_DIM)
    d_qkv_low = d_qkv.astype(jnp.bfloat16)
    qkv_partial = jnp.einsum("td,the->dhe", a_attn, d_qkv_low, preferred_element_type=jnp.float32)
    attn_part = jnp.einsum("the,dhe->td", d_qkv_low, w_qkv, preferred_element_type=jnp.float32)
    mlp_part = jnp.einsum("tf,df->td", d_hidden_low, w_up, preferred_element_type=jnp.float32)
    unit_partial = jnp.concatenate(
        [jnp.sum(d_qkv, 0), jnp.sum(d_hidden, 0).reshape(heads_local, units_local // heads_local)],
        1,
    )
    attn_norm_grad, mlp_norm_grad = (
        lax.psum(attn_part.astype(jnp.bfloat16), "tensor").astype(jnp.float32),
        lax.psum(mlp_part.astype(jnp.bfloat16), "tensor").astype(jnp.float32),
    )
    input_grad = (
        grad_float
        + norm_back(attn_norm_grad, vector_vals[0], normed, inv_std)
        + norm_back(mlp_norm_grad, vector_vals[2], normed, inv_std)
    )
    vector_partial = vector_sums(attn_norm_grad, mlp_norm_grad, normed, grad_float)
    input_grad = input_grad.reshape(seq_count, local_len, feature_width)
    vector_grad, unit_grad = lax.psum((vector_partial, unit_partial), ("shard", "context"))
    qkv_grad, dense_grad, up_grad, down_grad = (
        lax.psum_scatter(qkv_partial, ("shard", "context"), scatter_dimension=0, tiled=True),
        lax.psum_scatter(dense_partial, ("shard", "context"), scatter_dimension=0, tiled=True),
        lax.psum_scatter(up_partial, ("shard", "context"), scatter_dimension=0, tiled=True),
        lax.psum_scatter(down_partial, ("shard", "context"), scatter_dimension=0, tiled=True),
    )
    count_value = step_count.astype(jnp.float32)
    qkv_new, qkv_change = adam_step(
        qkv_weight.astype(jnp.float32), qkv_moments, qkv_grad, count_value, WEIGHT_DECAY
    )
    dense_new, dense_change = adam_step(
        dense_weight.astype(jnp.float32), dense_moments, dense_grad, count_value, WEIGHT_DECAY
    )
    up_new, up_change = adam_step(
        up_weight.astype(jnp.float32), up_moments, up_grad, count_value, WEIGHT_DECAY
    )
    down_new, down_change = adam_step(
        down_weight.astype(jnp.float32), down_moments, down_grad, count_value, WEIGHT_DECAY
    )
    unit_new, unit_change = adam_step(unit_vals, unit_moments, unit_grad, count_value, 0.0)
    vector_new, vector_change = adam_step(
        vector_vals, vector_moments, vector_grad, count_value, 0.0
    )
    return (
        outputs,
        input_grad,
        qkv_grad,
        dense_grad,
        up_grad,
        down_grad,
        unit_grad,
        vector_grad,
        qkv_new,
        dense_new,
        up_new,
        down_new,
        unit_new,
        vector_new,
        qkv_change,
        dense_change,
        up_change,
        down_change,
        unit_change,
        vector_change,
    )


def solution(mesh):
    placed = (
        P("shard", "context", None),
        P("shard", "context", None),
        P(("shard", "context"), "tensor", None),
        P(("shard", "context"), "tensor"),
        P(("shard", "context"), "tensor"),
        P(("shard", "context"), "tensor"),
        P("tensor", None),
        P(),
        P(None, ("shard", "context"), "tensor", None),
        P(None, ("shard", "context"), "tensor"),
        P(None, ("shard", "context"), "tensor"),
        P(None, ("shard", "context"), "tensor"),
        P(None, "tensor", None),
        P(),
        P(),
    )
    return jax.shard_map(
        on_device,
        mesh=mesh,
        in_specs=placed,
        out_specs=(
            P("shard", "context", None),
            P("shard", "context", None),
            P(("shard", "context"), "tensor", None),
            P(("shard", "context"), "tensor"),
            P(("shard", "context"), "tensor"),
            P(("shard", "context"), "tensor"),
            P("tensor", None),
            P(),
            P(None, ("shard", "context"), "tensor", None),
            P(None, ("shard", "context"), "tensor"),
            P(None, ("shard", "context"), "tensor"),
            P(None, ("shard", "context"), "tensor"),
            P(None, "tensor", None),
            P(),
            P(("shard", "context"), "tensor", None),
            P(("shard", "context"), "tensor"),
            P(("shard", "context"), "tensor"),
            P(("shard", "context"), "tensor"),
            P("tensor", None),
            P(),
        ),
        check_vma=False,
    )
```

profile of v0, /device:TPU:0, one launch (start us, length us, event | category | flops | bytes accessed | tf_op | source)
XLA Modules:
  0.0 4285.5 jit_solution(6937927172047186091)
XLA Ops:
  15.0 53.1 %all-gather.7.cloned.1.call-done = bf16[2048,1024]{1,0:T(8,128)(2,1)} async-done(((bf16[128,1024]{1,0:T(8,128)(2,1)}), bf16[2048,1024]{1,0:T(8,128)(2,1)}) %all-gather.7.cloned.1.call-update) | async-done | bytes 4194320 | tf_op jit(solution)/shard_map/all_gather | solution.py:198
  68.2 6.1 fusion.116
  80.9 114.6 %all-gather.5.cloned.1.call-done = bf16[2048,4,768]{2,0,1:T(8,128)(2,1)} async-done(((bf16[128,4,768]{2,0,1:T(8,128)(2,1)}), bf16[2048,4,768]{2,0,1:T(8,128)(2,1)}) %all-gather.5.cloned.1.call-update) | async-done | bytes 12582928 | tf_op jit(solution)/shard_map/all_gather | solution.py:197
  195.5 9.7 fusion.147
  209.7 7.0 concatenate.52
  216.8 15.7 all-to-all-start
  232.6 137.9 %all-to-all-done = bf16[1,512,4,768]{3,1,0,2:T(8,128)(2,1)} async-done(((bf16[1,512,4,768]{3,1,0,2:T(8,128)(2,1)}), bf16[1,512,4,768]{3,1,0,2:T(8,128)(2,1)}, u32[]{:S(2)}, u32[]{:S(2)}) %all-to-all-start) | async-done | bytes 3145760 | tf_op jit(solution)/shard_map/all_to_all | solution.py:225
  374.2 13.6 while.27
  394.3 36.2 while.28
  448.4 6.9 fusion.149
  455.3 122.2 %all-to-all-done.3 = bf16[1,1024,2,768]{3,2,0,1:T(2,128)(2,1)S(1)} async-done(((bf16[1,1024,2,768]{3,2,0,1:T(2,128)(2,1)}), bf16[1,1024,2,768]{3,2,0,1:T(2,128)(2,1)S(1)}, u32[]{:S(2)}, u32[]{:S(2)}) %all-to-all-start.3) | async-done | bytes 3145760 | tf_op jit(solution)/shard_map/all_to_all | solution.py:252
  586.0 9.3 concatenate.55
  595.3 13.8 bitcast_convert_fusion
  609.2 14.6 fusion.140
  623.8 18.3 fusion.148
  642.1 30.1 add_convert_fusion
  672.2 14.8 convolution_convert_fusion
  691.5 149.1 %all-reduce.7.cloned.1.call-done = (bf16[512,2048]{1,0:T(8,128)(2,1)}, bf16[512,2048]{1,0:T(8,128)(2,1)}, bf16[512,2048]{1,0:T(8,128)(2,1)}) async-done(((bf16[512,2048]{1,0:T(8,128)(2,1)}, bf16[512,2048]{1,0:T(8,128)(2,1)}, bf16[512,2048]{1,0:T(8,128)(2,1)}), (bf16[512,2048]{1,0:T(8,128)(2,1)}, bf16[512,2048]{1,0:T(8,128)(2,1)}, bf16[512,2048]{1,0:T(8,128)(2,1)})) %all-reduce.7.cloned.1.call-update) | async-done | bytes 6291472 | tf_op jit(solution)/shard_map/psum | solution.py:236
  840.6 5.6 fusion.83
  846.2 6.8 convert_reduce_fusion.3
  853.9 7.2 convolution_bitcast_fusion.1
  867.8 7.7 concatenate.62
  875.4 13.9 fusion.91
  889.4 17.8 fusion.105
  908.7 17.8 convolution_bitcast_fusion
  934.0 36.7 all-reduce.5.cloned.1.call-done
  975.2 343.5 %reduce-scatter.7.cloned.1.call-done = f32[128,1024]{0,1:T(8,128)} async-done(((f32[2048,1024]{0,1:T(8,128)}), f32[128,1024]{0,1:T(8,128)}) %reduce-scatter.7.cloned.1.call-update) | async-done | bytes 524304 | tf_op jit(solution)/shard_map/reduce_scatter | solution.py:286
  1329.0 219.4 %reduce-scatter.5.cloned.1.call-done = f32[128,4,768]{2,0,1:T(8,128)} async-done(((f32[2048,4,768]{2,0,1:T(8,128)}), f32[128,4,768]{2,0,1:T(8,128)}) %reduce-scatter.5.cloned.1.call-update) | async-done | bytes 1572880 | tf_op jit(solution)/shard_map/reduce_scatter | solution.py:285
  1559.6 1349.3 %reduce-scatter.9.cloned.1.call-done = f32[128,4096]{1,0:T(8,128)} async-done(((f32[2048,4096]{1,0:T(8,128)}), f32[128,4096]{1,0:T(8,128)}) %reduce-scatter.9.cloned.1.call-update) | async-done | bytes 2097168 | tf_op jit(solution)/shard_map/reduce_scatter | solution.py:287
  2908.8 5.8 add_multiply_fusion.1
  2917.0 1352.1 %reduce-scatter.11.cloned.1.call-done = f32[128,4096]{1,0:T(8,128)} async-done(((f32[2048,4096]{1,0:T(8,128)}), f32[128,4096]{1,0:T(8,128)}) %reduce-scatter.11.cloned.1.call-update) | async-done | bytes 2097168 | tf_op jit(solution)/shard_map/reduce_scatter | solution.py:288
  4269.1 5.8 add_multiply_fusion
  (235 shorter events, 154.1 us)
Async XLA Ops:
  7.2 61.0 %all-gather.7.cloned.1.call-start = ((), (), s32[]{:S(2)}) async-start(), calls=%async_computation.9 | async-start | bytes 4456448 | tf_op jit(solution)/shard_map/all_gather | solution.py:198
  7.9 187.6 %all-gather.5.cloned.1.call-start = ((), (), s32[]{:S(2)}) async-start(), calls=%async_computation.8 | async-start | bytes 13369344 | tf_op jit(solution)/shard_map/all_gather | solution.py:197
  10.1 599.0 %all-gather.9.cloned.1.call-start = ((), (), s32[]{:S(2)}) async-start(), calls=%async_computation.10 | async-start | bytes 17825792 | tf_op jit(solution)/shard_map/all_gather | solution.py:199
  10.9 612.9 %all-gather.11.cloned.1.call-start = ((), (), s32[]{:S(2)}) async-start(), calls=%async_computation.11 | async-start | bytes 17825792 | tf_op jit(solution)/shard_map/all_gather | solution.py:200
  11.9 183.7 %copy-start.35 = (f32[512]{0:T(512)}, f32[512]{0:T(512)S(1)}, u32[]{:S(2)}) copy-start(f32[512]{0:T(512)S(1)} %broadcast_multiply_fusion.5) | copy-start | bytes 6148
  12.6 183.0 %copy-start.37 = (f32[512]{0:T(512)}, f32[512]{0:T(512)S(1)}, u32[]{:S(2)}) copy-start(f32[512]{0:T(512)S(1)} %add_rsqrt_fusion) | copy-start | bytes 6148
  15.0 180.5 %copy-start.33 = (f32[1,2048]{1,0:T(1,128)}, f32[1,2048]{1,0:T(1,128)S(1)}, u32[]{:S(2)}) copy-start(f32[1,2048]{1,0:T(1,128)S(1)} %get-tuple-element.334) | copy-start | bytes 24580
  15.0 180.5 %copy-start.40 = (f32[1,2048]{1,0:T(1,128)}, f32[1,2048]{1,0:T(1,128)S(1)}, u32[]{:S(2)}) copy-start(f32[1,2048]{1,0:T(1,128)S(1)} %get-tuple-element.335) | copy-start | bytes 24580
  77.3 139.5 %all-to-all-start.2 = ((bf16[1,512,4,256]{3,1,0,2:T(8,128)(2,1)}), bf16[1,512,4,256]{3,1,0,2:T(8,128)(2,1)S(1)}, u32[]{:S(2)}, u32[]{:S(2)}) async-start(bf16[1,512,4,256]{3,1,0,2:T(8,128)(2,1)} %copy.126), calls=%async_computation.2 | async-start | bytes 2097152 | tf_op jit(solution)/shard_map/all_to_all | solution.py:250
  216.8 153.7 %all-to-all-start = ((bf16[1,512,4,768]{3,1,0,2:T(8,128)(2,1)}), bf16[1,512,4,768]{3,1,0,2:T(8,128)(2,1)}, u32[]{:S(2)}, u32[]{:S(2)}) async-start(bf16[1,512,4,768]{3,1,0,2:T(8,128)(2,1)} %bitcast.14), calls=%async_computation | async-start | bytes 6291456 | tf_op jit(solution)/shard_map/all_to_all | solution.py:225
  389.8 49.4 %all-to-all-start.1 = ((bf16[1,1024,2,256]{3,2,0,1:T(2,128)(2,1)}), bf16[1,1024,2,256]{3,2,0,1:T(2,128)(2,1)}, u32[]{:S(2)}, u32[]{:S(2)}) async-start(bf16[1,1024,2,256]{3,2,0,1:T(2,128)(2,1)} %copy.123), calls=%async_computation.1 | async-start | bytes 2097152 | tf_op jit(solution)/shard_map/all_to_all | solution.py:227
  401.3 6.3 copy-start.1
  418.7 7.0 copy-start.1
  439.3 138.3 %all-to-all-start.3 = ((bf16[1,1024,2,768]{3,2,0,1:T(2,128)(2,1)}), bf16[1,1024,2,768]{3,2,0,1:T(2,128)(2,1)S(1)}, u32[]{:S(2)}, u32[]{:S(2)}) async-start(bf16[1,1024,2,768]{3,2,0,1:T(2,128)(2,1)} %copy.131), calls=%async_computation.3 | async-start | bytes 6291456 | tf_op jit(solution)/shard_map/all_to_all | solution.py:252
  443.6 397.1 %all-reduce.7.cloned.1.call-start = ((), (), s32[]{:S(2)}) async-start(), calls=%async_computation.17 | async-start | bytes 12582912 | tf_op jit(solution)/shard_map/psum | solution.py:236
  595.3 13.9 copy-start.8
  595.3 13.9 copy-start.32
  595.3 13.9 copy-start.36
  595.3 13.9 copy-start.38
  595.3 13.9 copy-start.39
  687.0 153.7 %copy-start.34 = (f32[1,2048]{1,0:T(1,128)S(1)}, f32[1,2048]{1,0:T(1,128)}, u32[]{:S(2)}) copy-start(f32[1,2048]{1,0:T(1,128)} %copy-done.33) | copy-start | bytes 24580
  687.0 283.8 %all-reduce.5.cloned.1.call-start = ((), (), s32[]{:S(2)}) async-start(), calls=%async_computation.16 | async-start | bytes 188416 | tf_op jit(solution)/shard_map/psum | solution.py:283
  846.2 7.6 copy-start.17
  853.8 464.8 %reduce-scatter.7.cloned.1.call-start = ((), (), s32[]{:S(2)}) async-start(), calls=%async_computation.13 | async-start | bytes 8912896 | tf_op jit(solution)/shard_map/reduce_scatter | solution.py:286
  861.1 687.2 %reduce-scatter.5.cloned.1.call-start = ((), (), s32[]{:S(2)}) async-start(), calls=%async_computation.12 | async-start | bytes 26738688 | tf_op jit(solution)/shard_map/reduce_scatter | solution.py:285
  867.8 7.7 copy-start.41
  889.3 2019.5 %reduce-scatter.9.cloned.1.call-start = ((), (), s32[]{:S(2)}) async-start(), calls=%async_computation.14 | async-start | bytes 35651584 | tf_op jit(solution)/shard_map/reduce_scatter | solution.py:287
  907.2 3362.0 %reduce-scatter.11.cloned.1.call-start = ((), (), s32[]{:S(2)}) async-start(), calls=%async_computation.15 | async-start | bytes 35651584 | tf_op jit(solution)/shard_map/reduce_scatter | solution.py:288
  929.5 43.5 %copy-start.30 = (bf16[4,1792]{1,0:T(4,128)(2,1)S(1)}, bf16[4,1792]{1,0:T(4,128)(2,1)}, u32[]{:S(2)}) copy-start(bf16[4,1792]{1,0:T(4,128)(2,1)} %param.25) | copy-start | bytes 43012
  1551.5 5.9 copy-start.11
  1555.2 1353.6 %copy-start.12 = (bf16[128,4096]{1,0:T(8,128)(2,1)S(1)}, bf16[128,4096]{1,0:T(8,128)(2,1)}, u32[]{:S(2)}) copy-start(bf16[128,4096]{1,0:T(8,128)(2,1)} %param.23) | copy-start | bytes 3145732
  2914.6 1354.5 %copy-start.13 = (bf16[128,4096]{1,0:T(8,128)(2,1)S(1)}, bf16[128,4096]{1,0:T(8,128)(2,1)}, u32[]{:S(2)}) copy-start(bf16[128,4096]{1,0:T(8,128)(2,1)} %param.24) | copy-start | bytes 3145732
  (32 other events, 111.6 us)
Sparse Core Ops, SparseCore 0:
  10.4 57.7 all-gather.6
  71.1 124.4 all-gather.4
  197.9 194.2 all-gather.8
  394.3 204.9 all-gather.10
  687.1 153.4 all-reduce.6
  853.9 116.8 all-reduce.4
  973.1 345.5 reduce-scatter.6
  1323.5 224.8 reduce-scatter.4
  1551.3 1357.4 reduce-scatter.8
  2911.6 1357.4 reduce-scatter.10
where the time goes:
time: 4290 us
  waiting for transfers between devices  3880 us (90%)
  matrix products  207 us (5%)
  local copies, waits for them, and re-layouts  93.6 us (2%)
  other arithmetic  57.7 us (1%)
    reduce_scatter x1, waiting for transfers between devices, on_device(): lax.psum_scatter(down_partial, ('shard', 'context'), scatter_dimension=0,...  1350 us
    reduce_scatter x1, waiting for transfers between devices, on_device(): lax.psum_scatter(up_partial, ('shard', 'context'), scatter_dimension=0, t...  1350 us
    reduce_scatter x1, waiting for transfers between devices, on_device(): lax.psum_scatter(dense_partial, ('shard', 'context'), scatter_dimension=0...  343 us
    reduce_scatter x1, waiting for transfers between devices, on_device(): lax.psum_scatter(qkv_partial, ('shard', 'context'), scatter_dimension=0,...  219 us
    psum x1, waiting for transfers between devices, on_device(): branch = lax.psum(branch.astype(jnp.bfloat16), 'tensor').astype(jnp.float32)  149 us
    all_to_all x1, waiting for transfers between devices, on_device(): lax.all_to_all(packed, 'context', split_axis=2, concat_axis=1, tiled=True)  138 us
    all_to_all x1, waiting for transfers between devices, on_device(): lax.all_to_all(d_packed_grouped, 'context', split_axis=1, concat_axis=2,...  122 us
    all_gather x1, waiting for transfers between devices, on_device(): lax.all_gather(qkv_weight, ('shard', 'context'), axis=0, tiled=True)  115 us
  transfers between devices with their start and end apart: 14, of which 10 were waited for; matrix products, arithmetic and copies ran while one was open for 6% of the time, Pallas kernels for 0%

commit v1 on v0

v1 whole, which is shorter than its diff:
```python
import functools
import math

import jax
import jax.numpy as jnp
from jax import lax
from jax.experimental import pallas as pl
from jax.experimental.pallas import tpu as pltpu
from jax.sharding import PartitionSpec as P

HEAD_DIM = 256
ROTARY = 64
EPSILON = 1e-05
BETA_ONE = 0.9
BETA_TWO = 0.95
LEARN_RATE = 0.02
WEIGHT_DECAY = 0.01
ROOT_HALF = 0.7071067811865476
ROOT_TWO_PI = 2.5066282746310002
MASKED = -1000000000.0
BF = jnp.bfloat16
F32 = jnp.float32


def dot(a, b, ca, cb):
    return lax.dot_general(a, b, (((ca,), (cb,)), ((), ())), preferred_element_type=F32)


def gelu_value(hidden):
    return 0.5 * hidden * (1.0 + lax.erf(hidden * ROOT_HALF))


def gelu_slope(hidden):
    return (
        0.5 * (1.0 + lax.erf(hidden * ROOT_HALF))
        + hidden * jnp.exp(-0.5 * hidden * hidden) / ROOT_TWO_PI
    )


BLOCK = 128
MIB = 1024 * 1024


def whole(shape):
    return pl.BlockSpec(shape, lambda *_: (0,) * len(shape))


def call(kernel, grid, in_specs, out_specs, out_shape, name, flops, nbytes, prefetch=0, scratch=(), limit=56):
    return pl.pallas_call(
        kernel,
        grid_spec=pltpu.PrefetchScalarGridSpec(
            num_scalar_prefetch=prefetch, grid=grid, in_specs=in_specs, out_specs=out_specs, scratch_shapes=list(scratch)
        ),
        out_shape=out_shape,
        compiler_params=pltpu.CompilerParams(vmem_limit_bytes=limit * MIB),
        cost_estimate=pl.CostEstimate(flops=flops, bytes_accessed=nbytes, transcendentals=0),
        name=name,
    )


def like(shape, dtype):
    return jax.ShapeDtypeStruct(shape, dtype)


def arrange_kernel(place_ref, x_ref, d_ref, v_ref, up_ref, down_ref, xo_ref, do_ref, xs_ref, ds_ref, vo_ref, *quarter_refs):
    width = x_ref.shape[1]
    count = width // BLOCK
    rows = x_ref.shape[0] // 2
    n = quarter_refs[0].shape[1]
    for k in range(2):
        cols = pl.ds(pl.multiple_of((place_ref[2 * count + 1] ^ k) * n, n), n)
        quarter_refs[k][...] = up_ref[:, cols]
        quarter_refs[2 + k][...] = down_ref[:, cols]
    for j in range(count):
        out = slice(j * BLOCK, (j + 1) * BLOCK)
        col = pl.ds(pl.multiple_of(place_ref[j] * BLOCK, BLOCK), BLOCK)
        sent = pl.ds(pl.multiple_of(place_ref[count + j] * BLOCK, BLOCK), BLOCK)
        for b in range(2):
            row = pl.ds(pl.multiple_of((place_ref[2 * count] ^ b) * rows, rows), rows)
            xo_ref[b * rows : (b + 1) * rows, out] = x_ref[row, col]
            do_ref[b * rows : (b + 1) * rows, out] = d_ref[row, col]
            if b == 0:
                xs_ref[:, out] = x_ref[row, sent]
                ds_ref[:, out] = d_ref[row, sent]
        vo_ref[:, out] = v_ref[:, col].astype(F32)


def arrange(place, x, d, v, up, down):
    sent = (x.shape[0] // 2, x.shape[1])
    part = (up.shape[0], up.shape[1] // 2)
    operands = (x, d, v, up, down)
    outs = [(x.shape, BF), (d.shape, BF), (sent, BF), (sent, BF), (v.shape, F32)] + [(part, BF)] * 4
    return call(
        arrange_kernel,
        (1,),
        [whole(a.shape) for a in operands],
        [whole(a) for a, _ in outs],
        [like(*a) for a in outs],
        "arrange",
        0,
        5 * x.size * 2,
        prefetch=1,
    )(place, *operands)


def unorder_kernel(place_ref, v_ref, o_ref):
    for j in range(v_ref.shape[1] // BLOCK):
        col = pl.ds(pl.multiple_of(place_ref[j] * BLOCK, BLOCK), BLOCK)
        o_ref[:, col] = v_ref[:, j * BLOCK : (j + 1) * BLOCK]


def unorder(place, v):
    return call(
        unorder_kernel, (1,), [whole(v.shape)], whole(v.shape), like(v.shape, v.dtype), "unorder", 0, v.size * 8, prefetch=1
    )(place, v)


def pack_kernel(*refs):
    *pieces, out_ref = refs
    row = 0
    for piece in pieces:
        out_ref[row : row + piece.shape[0], :] = piece[...]
        row += piece.shape[0]


def pack(*pieces):
    rows, n = sum(p.shape[0] for p in pieces), pieces[0].shape[1]
    return call(
        pack_kernel, (1,), [whole(p.shape) for p in pieces], whole((rows, n)), like((rows, n), BF), "pack", 0, rows * n * 4
    )(*pieces)


def norm_kernel(x_ref, v_ref, attn_ref, mlp_ref, mean_ref, inv_ref):
    x = x_ref[...].astype(F32)
    mean = jnp.mean(x, -1, keepdims=True)
    center = x - mean
    inv_std = lax.rsqrt(jnp.mean(center * center, -1, keepdims=True) + EPSILON)
    normed = center * inv_std
    attn_ref[...] = (normed * v_ref[0:1, :] + v_ref[1:2, :]).astype(BF)
    mlp_ref[...] = (normed * v_ref[2:3, :] + v_ref[3:4, :]).astype(BF)
    mean_ref[...] = jnp.broadcast_to(mean, mean_ref.shape)
    inv_ref[...] = jnp.broadcast_to(inv_std, inv_ref.shape)


def norm(x, vec):
    rows, width = x.shape
    tile = rows // 4
    block = pl.BlockSpec((tile, width), lambda i: (i, 0))
    stat = pl.BlockSpec((tile, 128), lambda i: (i, 0))
    return call(
        norm_kernel,
        (4,),
        [block, whole(vec.shape)],
        [block, block, stat, stat],
        [like(x.shape, BF), like(x.shape, BF), like((rows, 128), F32), like((rows, 128), F32)],
        "norm",
        x.size * 12,
        x.size * 6,
    )(x, vec)


def both(a_ref, near_ref, far_ref):
    half = a_ref.shape[1] // 2
    return dot(a_ref[:, :half], near_ref[...], 1, 0) + dot(a_ref[:, half:], far_ref[...], 1, 0)


def hidden_kernel(a_ref, near_ref, far_ref, b_ref, act_ref, slope_ref):
    hidden = both(a_ref, near_ref, far_ref) + b_ref[...]
    cdf = 0.5 * (1.0 + lax.erf(hidden * ROOT_HALF))
    act_ref[...] = (hidden * cdf).astype(BF)
    slope_ref[...] = cdf + hidden * jnp.exp(-0.5 * hidden * hidden) * (1.0 / ROOT_TWO_PI)


def hidden_of(a, weight, bias, tile=256):
    near, far = weight
    (rows, width), n = a.shape, near.shape[1]
    wide = pl.BlockSpec((width // 2, tile), lambda j: (0, j))
    out = pl.BlockSpec((rows, tile), lambda j: (0, j))
    return call(
        hidden_kernel,
        (n // tile,),
        [whole(a.shape), wide, wide, pl.BlockSpec((1, tile), lambda j: (0, j))],
        [out, out],
        [like((rows, n), BF), like((rows, n), F32)],
        "hidden",
        2 * rows * width * n,
        (a.size + near.size * 2 + rows * n * 3) * 2,
    )(a, near, far, bias)


def d_hidden_kernel(d_ref, near_ref, far_ref, slope_ref, low_ref, sum_ref):
    grad = both(d_ref, near_ref, far_ref) * slope_ref[...]
    low_ref[...] = grad.astype(BF)
    sum_ref[...] = jnp.broadcast_to(jnp.sum(grad, 0, keepdims=True), sum_ref.shape)


def d_hidden_of(d, weight, slope, tile=256):
    near, far = weight
    (rows, width), n = d.shape, near.shape[1]
    wide = pl.BlockSpec((width // 2, tile), lambda j: (0, j))
    out = pl.BlockSpec((rows, tile), lambda j: (0, j))
    return call(
        d_hidden_kernel,
        (n // tile,),
        [whole(d.shape), wide, wide, out],
        [out, pl.BlockSpec((8, tile), lambda j: (0, j))],
        [like((rows, n), BF), like((8, n), F32)],
        "d_hidden",
        2 * rows * width * n,
        (d.size + near.size * 2 + rows * n * 3) * 2,
    )(d, near, far, slope)


def turn(block, cosine, sine):
    head = block[:, :128]
    lane = lax.broadcasted_iota(jnp.int32, head.shape, 1)
    half = ROTARY // 2
    partner = jnp.where(lane < half, -pltpu.roll(head, 128 - half, 1), pltpu.roll(head, half, 1))
    return jnp.concatenate([head * cosine + partner * sine, block[:, 128:]], 1)


def attend_kernel(
    z_ref, a0_ref, a1_ref, near_ref, far_ref, b_ref, cos_ref, sin_ref, ctx_ref, pack_ref, log_ref
):
    z = z_ref[0]
    size = a0_ref.shape[0] // 2
    hd = HEAD_DIM
    scale = hd**-0.5

    def row_of(p):
        return pl.ds(pl.multiple_of((z ^ p) * size, size), size)

    for b in range(4):
        a = (a0_ref, a1_ref)[b // 2][b % 2 * size : (b % 2 + 1) * size, :]
        half = a.shape[1] // 2
        lin = dot(a[:, :half], near_ref[...], 1, 0) + dot(a[:, half:], far_ref[...], 1, 0) + b_ref[...]
        mine = slice(b * size, (b + 1) * size)
        cosine, sine = cos_ref[mine, :], sin_ref[mine, :]
        rows = row_of(b)
        pack_ref[rows, :hd] = turn(lin[:, :hd], cosine, sine).astype(BF)
        pack_ref[rows, hd : 2 * hd] = turn(lin[:, hd : 2 * hd], cosine, sine).astype(BF)
        pack_ref[rows, 2 * hd :] = lin[:, 2 * hd :].astype(BF)
    for p in range(4):
        here, seen = slice(p * size, (p + 1) * size), slice(0, (p + 1) * size)
        scores = dot(pack_ref[here, :hd], pack_ref[seen, hd : 2 * hd], 1, 1) * scale
        row_ids = p * size + lax.broadcasted_iota(jnp.int32, scores.shape, 0)
        col_ids = lax.broadcasted_iota(jnp.int32, scores.shape, 1)
        scores = jnp.where(row_ids >= col_ids, scores, MASKED)
        top = jnp.max(scores, -1, keepdims=True)
        exponent = jnp.exp(scores - top)
        total = jnp.sum(exponent, -1, keepdims=True)
        low = (exponent * (1.0 / total)).astype(BF)
        ctx_ref[row_of(p), :] = dot(low, pack_ref[seen, 2 * hd :], 1, 0).astype(BF)
        log_ref[here, :] = jnp.broadcast_to(top + jnp.log(total), (size, log_ref.shape[1]))


def attend(z, a0, a1, weight, bias, cosine, sine):
    near, far = weight
    length, width = 2 * a0.shape[0], a0.shape[1]
    hd = HEAD_DIM
    heads = bias.shape[1] // (3 * hd)
    column = lambda rows, cols: pl.BlockSpec((rows, cols), lambda h, p: (0, h))
    return call(
        attend_kernel,
        (heads,),
        [
            whole(a0.shape),
            whole(a1.shape),
            column(near.shape[0], 3 * hd),
            column(far.shape[0], 3 * hd),
            column(1, 3 * hd),
            whole(cosine.shape),
            whole(sine.shape),
        ],
        [column(length, hd), column(length, 3 * hd), column(length, 128)],
        [like((length, heads * hd), BF), like((length, heads * 3 * hd), BF), like((length, heads * 128), F32)],
        "attend",
        (3 * length * length * hd + 6 * length * width * hd) * heads,
        length * width * 8,
        prefetch=1,
    )(z, a0, a1, near, far, bias, cosine, sine)


def attend_back_kernel(
    z_ref, pack_ref, log_ref, d0_ref, d1_ref, near_ref, far_ref, cos_ref, sin_ref, dl_ref, us_ref, g_s, dk_s, dv_s
):
    z = z_ref[0]
    size = d0_ref.shape[0] // 2
    hd = HEAD_DIM
    scale = hd**-0.5

    def row_of(p):
        return pl.ds(pl.multiple_of((z ^ p) * size, size), size)

    for half, d_ref in enumerate((d0_ref, d1_ref)):
        grad = both(d_ref, near_ref, far_ref).astype(BF)
        g_s[row_of(2 * half), :] = grad[:size]
        g_s[row_of(2 * half + 1), :] = grad[size:]
    dk_s[...] = jnp.zeros_like(dk_s)
    dv_s[...] = jnp.zeros_like(dv_s)
    q_sum = jnp.zeros((1, hd), F32)
    for p in range(4):
        here, seen = slice(p * size, (p + 1) * size), slice(0, (p + 1) * size)
        rows = row_of(p)
        queries, grads = pack_ref[here, :hd], g_s[here, :]
        keys, values = pack_ref[seen, hd : 2 * hd], pack_ref[seen, 2 * hd :]
        scores = dot(queries, keys, 1, 1) * scale
        row_ids = p * size + lax.broadcasted_iota(jnp.int32, scores.shape, 0)
        col_ids = lax.broadcasted_iota(jnp.int32, scores.shape, 1)
        scores = jnp.where(row_ids >= col_ids, scores, MASKED)
        probs = jnp.exp(scores - log_ref[here, 0:1])
        low = probs.astype(BF)
        weight_grad = dot(grads, values, 1, 1)
        score_grad = (
            probs * (weight_grad - jnp.sum(probs * weight_grad, -1, keepdims=True))
        ).astype(BF)
        query_grad = (dot(score_grad, keys, 1, 0) * scale).astype(BF).astype(F32)
        dk_s[seen, :] += dot(score_grad, queries, 0, 0)
        dv_s[seen, :] += dot(low, grads, 0, 0)
        query_grad = turn(query_grad, cos_ref[rows, :], -sin_ref[rows, :])
        q_sum = q_sum + jnp.sum(query_grad, 0, keepdims=True)
        dl_ref[rows, :hd] = query_grad.astype(BF)
    k_sum = jnp.zeros((1, hd), F32)
    v_sum = jnp.zeros((1, hd), F32)
    for p in range(4):
        here = slice(p * size, (p + 1) * size)
        rows = row_of(p)
        key_grad = (dk_s[here, :] * scale).astype(BF).astype(F32)
        key_grad = turn(key_grad, cos_ref[rows, :], -sin_ref[rows, :])
        k_sum = k_sum + jnp.sum(key_grad, 0, keepdims=True)
        dl_ref[rows, hd : 2 * hd] = key_grad.astype(BF)
        value_grad = dv_s[here, :].astype(BF)
        v_sum = v_sum + jnp.sum(value_grad.astype(F32), 0, keepdims=True)
        dl_ref[rows, 2 * hd :] = value_grad
    us_ref[...] = jnp.broadcast_to(jnp.concatenate([q_sum, k_sum, v_sum], 1), us_ref.shape)


def attend_back(z, packed, logs, d0, d1, weight, cosine, sine):
    near, far = weight
    length, wide = packed.shape
    hd = HEAD_DIM
    heads = wide // (3 * hd)
    first = wide // hd
    column = lambda rows, cols: pl.BlockSpec((rows, cols), lambda h, p: (0, h))
    dense = pl.BlockSpec((near.shape[0], hd), lambda h, p: (0, first + h))
    return call(
        attend_back_kernel,
        (heads,),
        [
            column(length, 3 * hd),
            column(length, 128),
            whole(d0.shape),
            whole(d1.shape),
            dense,
            dense,
            whole(cosine.shape),
            whole(sine.shape),
        ],
        [column(length, 3 * hd), column(8, 3 * hd)],
        [like((length, wide), BF), like((8, wide), F32)],
        "attend_back",
        (9 * length * length * hd + 2 * length * d0.shape[1] * hd) * heads,
        length * wide * 8,
        prefetch=1,
        scratch=[pltpu.VMEM((length, hd), BF)] + [pltpu.VMEM((length, hd), F32)] * 2,
    )(z, packed, logs, d0, d1, near, far, cosine, sine)


def near_or_far(near_ref, far_ref, body):
    j = pl.program_id(0)
    count = pl.num_programs(0) // 2

    @pl.when(j < count)
    def _():
        body(*near_ref)

    @pl.when(j >= count)
    def _():
        body(*far_ref)


def row_specs(shape, count, col=0):
    half = count // 2
    return [
        pl.BlockSpec(shape, lambda j: (jnp.minimum(j, half - 1), col)),
        pl.BlockSpec(shape, lambda j: (jnp.maximum(j - half, 0), col)),
    ]


def branch_kernel(a0_ref, a1_ref, ctx_ref, dn_ref, df_ref, sn_ref, sf_ref, *outs):
    size = outs[0].shape[0]

    def body(down_ref, dense_ref):
        for k, act_ref in enumerate((a0_ref, a1_ref)):
            ctx = ctx_ref[2 * k * size : 2 * (k + 1) * size, :]
            part = dot(act_ref[...], down_ref[...], 1, 1) + dot(ctx, dense_ref[...], 1, 1)
            outs[2 * k][...] = part[:size]
            outs[2 * k + 1][...] = part[size:].astype(BF)

    near_or_far((dn_ref, sn_ref), (df_ref, sf_ref), body)


def token_outs(size, width, tile):
    spec = pl.BlockSpec((size, tile), lambda j: (0, j))
    return [spec] * 4, [like((size, width), F32), like((size, width), BF)] * 2


def branch_of(a0, a1, context_out, down, attn, tile=256):
    rows, n = a0.shape
    width = 2 * down[0].shape[0]
    cols = context_out.shape[1]
    count = width // tile
    specs, shapes = token_outs(rows // 2, width, tile)
    return call(
        branch_kernel,
        (count,),
        [
            whole(a0.shape),
            whole(a1.shape),
            whole(context_out.shape),
            *row_specs((tile, n), count),
            *row_specs((tile, cols), count, attn[0].shape[1] // cols - 1),
        ],
        specs,
        shapes,
        "branch",
        4 * rows * width * (n + cols),
        (2 * rows * (n + cols) + width * (n + cols) + 2 * rows * width * 2) * 2,
    )(a0, a1, context_out, *down, *attn)


def input_grad_kernel(
    dl_ref, h0_ref, h1_ref, an_ref, af_ref, un_ref, uf_ref, x0_ref, x1_ref, m0_ref, m1_ref, i0_ref, i1_ref, v_ref, *outs
):
    size = outs[0].shape[0]
    wide = dl_ref.shape[1]
    halves = ((h0_ref, x0_ref, m0_ref, i0_ref), (h1_ref, x1_ref, m1_ref, i1_ref))

    def body(attn_ref, up_ref):
        total = [0.0] * 4
        for k, (dh_ref, x_ref, mean_ref, inv_ref) in enumerate(halves):
            attn = dot(dl_ref[2 * k * size : 2 * (k + 1) * size, :], attn_ref[:, :wide], 1, 1)
            mlp = dot(dh_ref[...], up_ref[...], 1, 1)
            part = attn * v_ref[0:1, :] + mlp * v_ref[2:3, :]
            outs[2 * k][...] = part[:size]
            outs[2 * k + 1][...] = part[size:].astype(BF)
            normed = (x_ref[...].astype(F32) - mean_ref[:, 0:1]) * inv_ref[:, 0:1]
            sums = [jnp.sum(v, 0, keepdims=True) for v in (attn * normed, attn, mlp * normed, mlp)]
            total = [u + v for u, v in zip(total, sums)]
        outs[4][...] = jnp.concatenate(total + [jnp.zeros((4, attn.shape[1]), F32)], 0)

    near_or_far((an_ref, un_ref), (af_ref, uf_ref), body)


def input_grad_of(d_linear, h0, h1, attn, up, xs, means, invs, vec, tile=256):
    rows, n = h0.shape
    width = xs[0].shape[1]
    wide = d_linear.shape[1]
    count = width // tile
    specs, shapes = token_outs(rows // 2, width, tile)
    column = pl.BlockSpec((rows, tile), lambda j: (0, j))
    return call(
        input_grad_kernel,
        (count,),
        [
            whole(d_linear.shape),
            whole(h0.shape),
            whole(h1.shape),
            *row_specs((tile, attn[0].shape[1]), count),
            *row_specs((tile, n), count),
            column,
            column,
            *[whole(a.shape) for a in (*means, *invs)],
            pl.BlockSpec((vec.shape[0], tile), lambda j: (0, j)),
        ],
        [*specs, pl.BlockSpec((8, tile), lambda j: (0, j))],
        [*shapes, like((8, width), F32)],
        "input_grad",
        4 * rows * width * (n + wide),
        (2 * rows * (n + wide) + width * (n + wide) + 2 * rows * width * 3) * 2,
    )(d_linear, h0, h1, *attn, *up, *xs, *means, *invs, vec)


def grad_kernel(pairs, near, *refs):
    operands = refs[: 4 * pairs]
    outs = refs[4 * pairs + near :]
    j = pl.program_id(0)
    col = 0
    for k in range(pairs):
        l0, l1, r0, r1 = (r[...] for r in operands[4 * k : 4 * k + 4])
        part = dot(l0, r0, 0, 0) + dot(l1, r1, 0, 0)
        cols = slice(col, col + part.shape[1])
        col += part.shape[1]
        if near:
            part = (part + refs[4 * pairs][:, cols].astype(F32)).astype(BF)
            for i, out_ref in enumerate(outs):

                @pl.when(j == i)
                def _(out_ref=out_ref, part=part, cols=cols):
                    out_ref[:, cols] = part

        else:
            outs[0][:, cols] = part.astype(BF)


def grad_of(factors, add=None):
    width = factors[0][0].shape[1]
    near = add is not None
    tile = width // 8
    first = 0 if near else 4
    in_specs, operands, n, flops, nbytes = [], [], 0, 0, 0
    for l0, l1, r0, r1 in factors:
        rows = l0.shape[0]
        for left in (l0, l1):
            in_specs.append(pl.BlockSpec((rows, tile), lambda j: (0, first + j)))
            operands.append(left)
        cols = r0[0].shape[1]
        for right, k in (r0, r1):
            in_specs.append(pl.BlockSpec((rows, cols), lambda j, k=k: (k, 0)))
            operands.append(right)
        n += cols
        flops += 2 * rows * width * cols
        nbytes += 2 * rows * (width + 2 * cols)
    block = pl.BlockSpec((tile, n), lambda j: (j, 0))
    if near:
        in_specs.append(block)
        operands.append(add)
        nbytes += width * n
    return call(
        functools.partial(grad_kernel, len(factors), near),
        (4,),
        in_specs,
        [whole((tile, n))] * 4 if near else block,
        [like((tile, n), BF)] * 4 if near else like((width // 2, n), BF),
        "grad_near" if near else "grad_far",
        flops,
        nbytes + width * n,
    )(*operands)


def fold_kernel(cross, keep_ref, got_ref, o_ref):
    for j, k in enumerate(cross):
        here = slice(j * BLOCK, (j + 1) * BLOCK)
        o_ref[:, k * BLOCK : (k + 1) * BLOCK] = (keep_ref[:, here] + got_ref[:, here].astype(F32)).astype(BF)


def fold(cross, keep, got):
    rows, width = keep.shape
    tile = rows // 4
    block = pl.BlockSpec((tile, width), lambda i: (i, 0))
    return call(
        functools.partial(fold_kernel, cross), (4,), [block, block], block, like(keep.shape, BF), "fold", keep.size, keep.size * 8
    )(keep, got)


def finish_kernel(place_ref, o0_ref, o1_ref, g0_ref, g1_ref, x_ref, d_ref, out_ref, grad_ref):
    width = x_ref.shape[1]
    count = width // BLOCK
    x = x_ref[...].astype(F32)
    center = x - jnp.mean(x, -1, keepdims=True)
    inv_std = lax.rsqrt(jnp.mean(center * center, -1, keepdims=True) + EPSILON)
    normed = center * inv_std

    def body(o_ref, g_ref):
        g = g_ref[...].astype(F32)
        grad = d_ref[...].astype(F32) + inv_std * (
            g - jnp.mean(g, -1, keepdims=True) - normed * jnp.mean(g * normed, -1, keepdims=True)
        )
        for j in range(count):
            col = pl.ds(pl.multiple_of(place_ref[j] * BLOCK, BLOCK), BLOCK)
            part = slice(j * BLOCK, (j + 1) * BLOCK)
            out_ref[:, col] = o_ref[:, part]
            grad_ref[:, col] = grad[:, part]

    near_or_far((o0_ref, g0_ref), (o1_ref, g1_ref), body)


def finish(place, o0, o1, g0, g1, x, d):
    rows, width = o0.shape
    per = 4
    tile = rows // per
    at = 2 * width // BLOCK
    first = pl.BlockSpec((tile, width), lambda i, p: (jnp.minimum(i, per - 1), 0))
    second = pl.BlockSpec((tile, width), lambda i, p: (jnp.maximum(i - per, 0), 0))
    local = pl.BlockSpec((tile, width), lambda i, p: (i, 0))
    out = pl.BlockSpec((tile, width), lambda i, p: ((p[at] ^ (i // per)) * per + i % per, 0))
    return call(
        finish_kernel,
        (2 * per,),
        [first, second, first, second, local, local],
        [out, out],
        [like(x.shape, BF), like(x.shape, F32)],
        "finish",
        x.size * 20,
        x.size * 14,
        prefetch=1,
    )(place, o0, o1, g0, g1, x, d)


def step_values(weight, first, root, gradient, fix_one, fix_two, decay_rate):
    first_new = BETA_ONE * first + (1.0 - BETA_ONE) * gradient
    root_new = jnp.sqrt(BETA_TWO * root * root + (1.0 - BETA_TWO) * gradient * gradient)
    change = -LEARN_RATE * (
        first_new / fix_one / (root_new / fix_two + 1e-08) + decay_rate * weight
    )
    return first_new, root_new, change


def adam_kernel(c_ref, fix_ref, w_ref, m_ref, a_ref, b_ref, e_ref, t_ref, g_ref, n_ref, u_ref):
    def body(gradient):
        first, root, change = step_values(
            w_ref[...].astype(F32), m_ref[0], m_ref[1], gradient, fix_ref[0], fix_ref[1], WEIGHT_DECAY
        )
        g_ref[...] = gradient
        n_ref[0] = first
        n_ref[1] = root
        u_ref[...] = change

    @pl.when(pl.program_id(0) == 0)
    def _():
        body(a_ref[...].astype(F32) + b_ref[...].astype(F32) + e_ref[...].astype(F32))

    @pl.when(pl.program_id(0) == 1)
    def _():
        body(t_ref[...].astype(F32))


def adam(ctx, fixes, weight, moments, terms, theirs, tile=1024, first=0):
    rows, cols = weight.shape
    n = cols // 2
    per = n // tile
    at = lambda k, i, c: (0, (c[0] ^ k) * per + i)
    mine = pl.BlockSpec((rows, tile), lambda k, i, c: (0, first + i + k * (per - 1 - i)))
    other = pl.BlockSpec((rows, tile), lambda k, i, c: (0, first + i * k))
    matrix = pl.BlockSpec((rows, tile), at)
    pair = pl.BlockSpec((2, rows, tile), lambda k, i, c: (0, *at(k, i, c)))
    return call(
        adam_kernel,
        (2, per),
        [pl.BlockSpec(memory_space=pltpu.SMEM), matrix, pair, mine, mine, mine, other],
        [matrix, pair, matrix],
        [like(weight.shape, F32), like(moments.shape, F32), like(weight.shape, F32)],
        "adam",
        weight.size * 20,
        weight.size * 30,
        prefetch=1,
    )(ctx, fixes, weight, moments, *terms, theirs)


def adam_heads_kernel(c_ref, fix_ref, w_ref, m_ref, a_ref, b_ref, e_ref, t_ref, g_ref, n_ref, u_ref):
    mine = a_ref[...].astype(F32) + b_ref[...].astype(F32) + e_ref[...].astype(F32)
    theirs = t_ref[...].astype(F32)
    heads, wide = w_ref.shape[1] // 2, w_ref.shape[2]
    for h in range(2 * heads):
        cols = slice(h % heads * wide, (h % heads + 1) * wide)
        gradient = jnp.where(c_ref[0] == h // heads, mine[:, cols], theirs[:, cols])
        first, root, change = step_values(
            w_ref[:, h, :].astype(F32), m_ref[0, :, h, :], m_ref[1, :, h, :], gradient, fix_ref[0], fix_ref[1], WEIGHT_DECAY
        )
        g_ref[:, h, :] = gradient
        n_ref[0, :, h, :] = first
        n_ref[1, :, h, :] = root
        u_ref[:, h, :] = change


def adam_heads(ctx, fixes, weight, moments, terms, theirs):
    rows, heads, wide = weight.shape
    tile = rows // 4
    part = pl.BlockSpec((tile, heads // 2 * wide), lambda i, c: (i, 0))
    cube = pl.BlockSpec((tile, heads, wide), lambda i, c: (i, 0, 0))
    pair = pl.BlockSpec((2, tile, heads, wide), lambda i, c: (0, i, 0, 0))
    return call(
        adam_heads_kernel,
        (4,),
        [pl.BlockSpec(memory_space=pltpu.SMEM), cube, pair, part, part, part, part],
        [cube, pair, cube],
        [like(weight.shape, F32), like(moments.shape, F32), like(weight.shape, F32)],
        "adam_heads",
        weight.size * 20,
        weight.size * 30,
        prefetch=1,
    )(ctx, fixes, weight, moments, *terms, theirs)


def rotary_tables(positions):
    lane = jnp.arange(128)
    inverse = jnp.exp((lane % (ROTARY // 2)).astype(F32) * (-2.0 / ROTARY) * math.log(10000.0))
    angles = positions.astype(F32)[:, None] * inverse[None, :]
    turned = lane[None, :] < ROTARY
    return (jnp.where(turned, jnp.cos(angles), 1.0), jnp.where(turned, jnp.sin(angles), 0.0))


def adam_step(weight, moments, gradient, count_value, decay_rate):
    first_new = BETA_ONE * moments[0] + (1.0 - BETA_ONE) * gradient
    root_new = jnp.sqrt(BETA_TWO * moments[1] * moments[1] + (1.0 - BETA_TWO) * gradient * gradient)
    fix_one = 1.0 - jnp.power(BETA_ONE, count_value)
    fix_two = 1.0 - jnp.power(BETA_TWO, count_value)
    change = -LEARN_RATE * (
        first_new / fix_one / (root_new / jnp.sqrt(fix_two) + 1e-08) + decay_rate * weight
    )
    return (jnp.stack([first_new, root_new]), change)


def on_device(
    shard_count,
    inputs,
    cotangent,
    qkv_weight,
    dense_weight,
    up_weight,
    down_weight,
    unit_biases,
    vectors,
    qkv_moments,
    dense_moments,
    up_moments,
    down_moments,
    unit_moments,
    vector_moments,
    step_count,
):
    shard, ctx, ten = (lax.axis_index(a) for a in ("shard", "context", "tensor"))
    fast = shard_count == 8
    _, local_len, width = inputs.shape
    quarter = local_len // 2
    row_count, heads_local, head_wide = qkv_weight.shape
    heads = heads_local // 2
    units = up_weight.shape[1] // 2
    head_cols = heads * HEAD_DIM
    n_qkv = heads * head_wide
    count = width // BLOCK

    def along(axis, size, bit):
        return lambda v: lax.ppermute(v, axis, [(i, i ^ bit) for i in range(size)])

    to_core, to_x, to_y = (along("shard", shard_count, bit) for bit in (1, 2, 4))
    to_ctx, to_ten = along("context", 2, 1), along("tensor", 2, 1)

    if fast:
        chips = ((0, 4, 2, 6), (0, 2, 4, 6))
        relative = [(core + chips[ab][k], ab) for core in range(2) for ab in range(2) for k in range(4)]
        places = [[(shard ^ s) * 2 + (ctx ^ f ^ ab) for s, ab in relative] for f in range(2)]
        cross = [core * 8 + (1 - ab) * 4 + (0, 2, 1, 3)[k] for core in range(2) for ab in range(2) for k in range(4)]
    else:
        places = [[jnp.int32(j) for j in range(count)]] * 2
        cross = list(range(count))
    place = jnp.stack([*places[0], *places[1], ten, ctx]).astype(jnp.int32)
    z = ctx * 2 + ten
    ctx_scalar, z_scalar = (v.reshape(1).astype(jnp.int32) for v in (ctx, z))

    def after(value, *others):
        return lax.optimization_barrier((value, *others))[0]

    def gather_rows(mine, other):
        if not fast:
            block = jnp.where(ctx == 0, jnp.concatenate([mine, other], 0), jnp.concatenate([other, mine], 0))
            full = lax.all_gather(block, "shard", axis=0, tiled=True)
            return full[: width // 2], full[width // 2 :]
        a1 = to_y(mine)
        a2 = to_x(pack(mine, a1))
        b1 = to_x(other)
        b2 = to_y(pack(other, b1))
        near = pack(mine, a1, a2, other, b1, b2)
        return near, to_core(near)

    def scatter_rows(factors):
        far_part = grad_of(factors)
        r = row_count
        if not fast:
            part = jnp.concatenate([*grad_of(factors, jnp.zeros_like(far_part)), far_part], 0)
            total = lax.psum_scatter(part, "shard", scatter_dimension=0, tiled=True)
            mine = lax.dynamic_slice_in_dim(total, ctx * r, r, 0)
            away = lax.dynamic_slice_in_dim(total, (1 - ctx) * r, r, 0)
            zero = jnp.zeros_like(mine)
            return (mine, zero, zero), to_ctx(away)
        a_own, a_x, b_own, b_y = grad_of(factors, to_core(far_part))
        add = lambda u, v: (u.astype(F32) + v.astype(F32)).astype(BF)
        b_got = to_y(b_y)
        a_got = to_x(a_x)
        b_last = to_x(add(b_own[r:], b_got[r:]))
        a_last = to_y(add(a_own[r:], a_got[r:]))
        away = (b_own[:r].astype(F32) + b_got[:r].astype(F32) + b_last.astype(F32)).astype(BF)
        return (a_own, a_got, a_last), to_ctx(away)

    def reduce_tokens(own, other):
        far = to_ctx(fold(cross, other[0], to_ten(other[1])))
        return own[0] + to_ten(own[1]).astype(F32) + far.astype(F32)

    def attn_quarter(q):
        qkv = lax.dynamic_slice_in_dim(qkv_weight, q * heads, heads, 1).reshape(row_count, n_qkv)
        dense = lax.dynamic_slice_in_dim(dense_weight, q * head_cols, head_cols, 1)
        return jnp.concatenate([qkv, dense], 1)

    x_own, d_own, x_sent, d_sent, vec, up_mine, up_theirs, down_mine, down_theirs = arrange(
        place, inputs.reshape(local_len, width), cotangent.reshape(local_len, width), vectors, up_weight, down_weight
    )
    up_other = to_ctx(up_theirs)
    attn_other = to_ctx(attn_quarter(1 - ctx))
    down_other = to_ctx(down_theirs)
    x_first = to_ctx(after(x_sent, up_other, attn_other, down_other))
    d_first = to_ctx(after(d_sent, x_first))
    w_up = gather_rows(up_mine, up_other)
    w_attn = gather_rows(attn_quarter(ctx), attn_other)
    w_down = gather_rows(down_mine, down_other)
    x_oth = pack(x_first, to_ten(x_first))
    d_oth = pack(d_first, to_ten(d_first))

    unit_vals = unit_biases.astype(F32)
    my_units = lax.dynamic_slice_in_dim(unit_vals, ctx * heads, heads, 0)
    qkv_bias, unit_bias = my_units[:, :head_wide].reshape(1, n_qkv), my_units[:, head_wide:].reshape(1, units)
    attn_own, mlp_own, mean_own, inv_own = norm(x_own, vec)
    attn_oth, mlp_oth, mean_oth, inv_oth = norm(x_oth, vec)

    positions = ((jnp.arange(4) ^ z)[:, None] * quarter + jnp.arange(quarter)[None, :]).reshape(-1)
    cosine, sine = rotary_tables(positions)
    active_own, slope_own = hidden_of(mlp_own, w_up, unit_bias)
    low_own, sum_own = d_hidden_of(d_own, w_down, slope_own)
    active_oth, slope_oth = hidden_of(mlp_oth, w_up, unit_bias)
    context_out, packed, logs = attend(z_scalar, attn_own, attn_oth, w_attn, qkv_bias, cosine, sine)
    *branch_own, branch_keep, branch_send = branch_of(active_own, active_oth, context_out, w_down, w_attn)
    branch_sum = reduce_tokens(branch_own, (branch_keep, branch_send))

    low_oth, sum_oth = d_hidden_of(d_oth, w_down, slope_oth)
    d_linear, unit_sums = attend_back(z_scalar, packed, logs, d_own, d_oth, w_attn, cosine, sine)
    *g_own, g_keep, g_send, sums = input_grad_of(
        d_linear, low_own, low_oth, w_attn, w_up, (x_own, x_oth), (mean_own, mean_oth), (inv_own, inv_oth), vec
    )
    g_sum = reduce_tokens(g_own, (g_keep, g_send)).astype(BF)

    down_terms, down_theirs = scatter_rows([(d_own, d_oth, (active_own, 0), (active_oth, 0))])
    up_terms, up_theirs = scatter_rows([(mlp_own, mlp_oth, (low_own, 0), (low_oth, 0))])
    attn_terms, attn_theirs = scatter_rows(
        [
            (attn_own, attn_oth, (d_linear, 0), (d_linear, 1)),
            (d_own, d_oth, (context_out, 0), (context_out, 1)),
        ]
    )

    out_own = (x_own[:quarter].astype(F32) + branch_sum + (vec[4] + vec[5])).astype(BF)
    outputs, input_grad = finish(place, out_own, to_ten(out_own), g_sum, to_ten(g_sum), x_own, d_own)

    d_sum = jnp.sum(d_own[:quarter].astype(F32), 0, keepdims=True)
    sums = unorder(place, jnp.concatenate([sums[:4], d_sum, jnp.zeros((3, width), F32)], 0))
    unit_part = jnp.concatenate(
        [unit_sums[0].reshape(heads, head_wide), (sum_own + sum_oth)[0].reshape(heads, units // heads)], 1
    )
    unit_rows = jnp.where(jnp.arange(4)[:, None, None] == ten * 2 + ctx, unit_part[None], 0.0)
    total = jnp.concatenate([sums.reshape(-1), unit_rows.reshape(-1)]).reshape(-1, BLOCK)
    for move in [to_ten, to_ctx] + [along("shard", shard_count, 1 << k) for k in range(shard_count.bit_length() - 1)]:
        total = total + move(total)
    total = total.reshape(-1)
    vector_grad = total[: 5 * width].reshape(5, width)
    vector_grad = jnp.concatenate([vector_grad, vector_grad[4:]], 0)
    unit_all = total[8 * width :].reshape(4 * heads, unit_part.shape[1])
    unit_grad = lax.dynamic_slice_in_dim(unit_all, ten * 2 * heads, 2 * heads, 0)

    count_value = step_count.astype(F32)
    fixes = jnp.stack([1.0 - jnp.power(BETA_ONE, count_value), jnp.sqrt(1.0 - jnp.power(BETA_TWO, count_value))])
    qkv_grad, qkv_new, qkv_change = adam_heads(ctx_scalar, fixes, qkv_weight, qkv_moments, attn_terms, attn_theirs)
    dense_grad, dense_new, dense_change = adam(
        ctx_scalar, fixes, dense_weight, dense_moments, attn_terms, attn_theirs, head_cols, n_qkv // head_cols
    )
    up_grad, up_new, up_change = adam(ctx_scalar, fixes, up_weight, up_moments, up_terms, up_theirs)
    down_grad, down_new, down_change = adam(ctx_scalar, fixes, down_weight, down_moments, down_terms, down_theirs)
    unit_new, unit_change = adam_step(unit_vals, unit_moments, unit_grad, count_value, 0.0)
    vector_new, vector_change = adam_step(vectors.astype(F32), vector_moments, vector_grad, count_value, 0.0)
    return (
        outputs.reshape(inputs.shape),
        input_grad.reshape(inputs.shape),
        qkv_grad,
        dense_grad,
        up_grad,
        down_grad,
        unit_grad,
        vector_grad,
        qkv_new,
        dense_new,
        up_new,
        down_new,
        unit_new,
        vector_new,
        qkv_change,
        dense_change,
        up_change,
        down_change,
        unit_change,
        vector_change,
    )


def solution(mesh):
    rows = ("shard", "context")
    tokens = P("shard", "context", None)
    qkv, matrix, units = P(rows, "tensor", None), P(rows, "tensor"), P("tensor", None)
    qkv_pair, matrix_pair, units_pair = P(None, rows, "tensor", None), P(None, rows, "tensor"), P(None, "tensor", None)
    params = (qkv, matrix, matrix, matrix, units, P())
    states = (qkv_pair, matrix_pair, matrix_pair, matrix_pair, units_pair, P())
    return jax.shard_map(
        functools.partial(on_device, mesh.shape["shard"]),
        mesh=mesh,
        in_specs=(tokens, tokens, *params, *states, P()),
        out_specs=(tokens, tokens, *params, *states, *params),
        check_vma=False,
    )
```

time: 4290 us -> 729 us (0.17)
  waiting for transfers between devices: 3880 us -> 357 us
  Pallas kernels: 0 us -> 276 us
  matrix products: 207 us -> 0 us
  local copies, waits for them, and re-layouts: 93.6 us -> 23.5 us
    reduce_scatter x4 -> x0, waiting for transfers between devices: 3260 us -> none  [the longest x1 1350 us: on_device(): lax.psum_scatter(down_partial, ('shard', 'context'), scatter_dimension=0,...]
    ppermute x0 -> x53, waiting for transfers between devices: none -> 357 us  [along(): return lambda v: lax.ppermute(v, axis, [(i, i ^ bit) for i in range(size)])]
    pallas_call x0 -> x36, Pallas kernels: none -> 276 us  [the longest x6 59.6 us: grad_of(): call(functools.partial(grad_kernel, len(factors), near), (4,), in_specs,...]
    all_to_all x4 -> x0, waiting for transfers between devices: 260 us -> none  [the longest x1 138 us: on_device(): lax.all_to_all(packed, 'context', split_axis=2, concat_axis=1, tiled=True)]
    dot_general x26 -> x0, matrix products: 207 us -> none  [the longest x1 30.1 us: on_device(): jnp.einsum('tf,df->td', active, w_down, preferred_element_type=jnp.float32)]
    psum x2 -> x0, waiting for transfers between devices: 186 us -> none  [the longest x1 149 us: on_device(): branch = lax.psum(branch.astype(jnp.bfloat16), 'tensor').astype(jnp.float32)]
    all_gather x4 -> x0, waiting for transfers between devices: 168 us -> none  [the longest x1 115 us: on_device(): lax.all_gather(qkv_weight, ('shard', 'context'), axis=0, tiled=True)]
  transfers between devices with their start and end apart: 14 -> 53, of which waited for: 10 -> 23; matrix products, arithmetic and copies ran while one was open for 6% -> 3% of each run, Pallas kernels for 0% -> 30%
where the time goes in v1:
time: 729 us; the launch traced here: 720 us
  waiting for transfers between devices  357 us (49%)
  Pallas kernels  276 us (38%)
  starting transfers between devices  41.7 us (6%)
  local copies, waits for them, and re-layouts  23.5 us (3%)
  other arithmetic  18.9 us (3%)
    ppermute x53, waiting for transfers between devices, along(): return lambda v: lax.ppermute(v, axis, [(i, i ^ bit) for i in range(size)])  357 us
    pallas_call x6, Pallas kernels, grad_of(): call(functools.partial(grad_kernel, len(factors), near), (4,), in_specs,...  59.6 us
    ppermute x53, starting transfers between devices, along(): return lambda v: lax.ppermute(v, axis, [(i, i ^ bit) for i in range(size)])  41.7 us
    pallas_call x11, Pallas kernels, pack(): call(pack_kernel, (1,), [whole(p.shape) for p in pieces], whole((rows, n)...  33 us
    pallas_call x2, Pallas kernels, hidden_of(): call(hidden_kernel, (n // tile,), [whole(a.shape), wide, wide, pl.BlockSp...  24.3 us
    pallas_call x1, Pallas kernels, input_grad_of(): call(input_grad_kernel, (count,), [whole(d_linear.shape), whole(h0.shape)...  24.2 us
    pallas_call x2, Pallas kernels, d_hidden_of(): call(d_hidden_kernel, (n // tile,), [whole(d.shape), wide, wide, out], [o...  23.3 us
    unnamed x115, local copies, waits for them, and re-layouts  18.3 us
  transfers between devices with their start and end apart: 53, of which 23 were waited for; matrix products, arithmetic and copies ran while one was open for 3% of the time, Pallas kernels for 30%

profile of v1, /device:TPU:0, one launch (start us, length us, event | category | flops | bytes accessed | tf_op | source)
XLA Modules:
  0.0 720.1 jit_solution(1887333307892606345)
XLA Ops:
  10.1 20.8 %collective-permute-done.6.refs_0_.refs_3_ = bf16[128,2048]{1,0:T(8,128)(2,1)S(1)} collective-permute-done((bf16[128,2048]{1,0:T(8,128)(2,1)S(1)}, bf16[128,2048]{1,0:T(8,128)(2,1)S(1)}, u32[]{:S(2)}, u32[]{:S(2)}) %collective-permute-start.6) | collective-permute-done | bytes 524320 | tf_op jit(solution)/shard_map/ppermute | solution.py:734
  36.0 9.8 %collective-permute-done.12.refs_1_.refs_4_ = bf16[128,2048]{1,0:T(8,128)(2,1)S(1)} collective-permute-done((bf16[128,2048]{1,0:T(8,128)(2,1)S(1)}, bf16[128,2048]{1,0:T(8,128)(2,1)S(1)}, u32[]{:S(2)}, u32[]{:S(2)}) %collective-permute-start.12) | collective-permute-done | bytes 524320 | tf_op jit(solution)/shard_map/ppermute | solution.py:734
  51.1 8.7 %arrange.1 = (bf16[512,2048]{1,0:T(8,128)(2,1)}, bf16[512,2048]{1,0:T(8,128)(2,1)}, bf16[256,2048]{1,0:T(8,128)(2,1)}, bf16[256,2048]{1,0:T(8,128)(2,1)}, f32[6,...) custom-call(s32[34]{0:T(128)} %stack.138.place_ref, ...), custom_call_target="tpu_custom_call" | custom-call | bytes 10485760 | tf_op jit(solution)/shard_map/arrange/pallas_call | solution.py:93
  60.2 21.4 %collective-permute-done.2.refs_0_.refs_3_ = bf16[128,2048]{1,0:T(8,128)(2,1)S(1)} collective-permute-done((bf16[128,2048]{1,0:T(8,128)(2,1)}, bf16[128,2048]{1,0:T(8,128)(2,1)S(1)}, u32[]{:S(2)}, u32[]{:S(2)}) %collective-permute-start.2) | collective-permute-done | bytes 524320 | tf_op jit(solution)/shard_map/ppermute | solution.py:734
  98.2 16.3 %collective-permute-done.7.refs_0_.refs_3_ = bf16[128,2048]{1,0:T(8,128)(2,1)S(1)} collective-permute-done((bf16[128,2048]{1,0:T(8,128)(2,1)S(1)}, bf16[128,2048]{1,0:T(8,128)(2,1)S(1)}, u32[]{:S(2)}, u32[]{:S(2)}) %collective-permute-start.7) | collective-permute-done | bytes 524320 | tf_op jit(solution)/shard_map/ppermute | solution.py:734
  118.1 11.5 %collective-permute-done.17.refs_1_.refs_4_ = bf16[128,2048]{1,0:T(8,128)(2,1)S(1)} collective-permute-done((bf16[128,2048]{1,0:T(8,128)(2,1)S(1)}, bf16[128,2048]{1,0:T(8,128)(2,1)S(1)}, u32[]{:S(2)}, u32[]{:S(2)}) %collective-permute-start.17) | collective-permute-done | bytes 524320 | tf_op jit(solution)/shard_map/ppermute | solution.py:734
  139.0 24.4 %collective-permute-done.8.refs_0_ = bf16[256,2048]{1,0:T(8,128)(2,1)S(1)} collective-permute-done((bf16[256,2048]{1,0:T(8,128)(2,1)}, bf16[256,2048]{1,0:T(8,128)(2,1)S(1)}, u32[]{:S(2)}, u32[]{:S(2)}) %collective-permute-start.8) | collective-permute-done | bytes 1048608 | tf_op jit(solution)/shard_map/ppermute | solution.py:734
  171.8 39.1 %collective-permute-done.24.refs_0_ = bf16[256,2048]{1,0:T(8,128)(2,1)} collective-permute-done((bf16[256,2048]{1,0:T(8,128)(2,1)}, bf16[256,2048]{1,0:T(8,128)(2,1)}, u32[]{:S(2)}, u32[]{:S(2)}) %collective-permute-start.24) | collective-permute-done | bytes 1048608 | tf_op jit(solution)/shard_map/ppermute | solution.py:734
  229.0 11.4 %collective-permute-done.25.refs_1_ = bf16[256,2048]{1,0:T(8,128)(2,1)} collective-permute-done((bf16[256,2048]{1,0:T(8,128)(2,1)}, bf16[256,2048]{1,0:T(8,128)(2,1)}, u32[]{:S(2)}, u32[]{:S(2)}) %collective-permute-start.25) | collective-permute-done | bytes 1048608 | tf_op jit(solution)/shard_map/ppermute | solution.py:734
  243.6 16.3 %attend.1 = (bf16[1024,512]{1,0:T(8,128)(2,1)}, bf16[1024,1536]{1,0:T(8,128)(2,1)}, f32[1024,256]{1,0:T(8,128)}) custom-call(s32[1]{0:T(128)} %bitcast.29.z_ref, bf16[512,2048]{1,0:T(8,128)(2,1)} %get-tuple-element.98.a0_ref.refs_0_, bf16[512,2048]{1,0:T(8,128)(2,1)} %get-tuple-element.99.a1_ref.refs_1_, bf16[1024,2048]{1,0:T(8,128)(2,1)} %pack.17.near_ref.sn_ref.an_ref, ...), custom_call_target="tpu_custom_call" | custom-call | flops 8053063680 | bytes 16777216 | tf_op jit(solution)/shard_map/attend/pallas_call | solution.py:263
  259.9 14.0 %attend_back.1 = (bf16[1024,1536]{1,0:T(8,128)(2,1)}, f32[8,1536]{1,0:T(8,128)}) custom-call(s32[1]{0:T(128)} %bitcast.29.z_ref, bf16[1024,1536]{1,0:T(8,128)(2,1)} %get-tuple-element.106.pack_ref, f32[1024,256]{1,0:T(8,128)} %get-tuple-element.107.log_ref, bf16[512,2048]{1,0:T(8,128)(2,1)} %get-tuple-element.108.d0_ref.d_ref.refs_4_.refs_0_, ...), custom_call_target="tpu_custom_call" | custom-call | flops 6979321856 | bytes 12582912 | tf_op jit(solution)/shard_map/attend_back/pallas_call | solution.py:346
  274.7 12.1 %hidden.2 = (bf16[512,2048]{1,0:T(8,128)(2,1)}, f32[512,2048]{1,0:T(8,128)}) custom-call(bf16[512,2048]{1,0:T(8,128)(2,1)} %get-tuple-element.89.a_ref.refs_0_, bf16[1024,2048]{1,0:T(8,128)(2,1)} %pack.13.near_ref.un_ref, bf16[1024,2048]{1,0:T(8,128)(2,1)} %collective-permute-done.5.far_ref.uf_ref, f32[1,2048]{1,0:T(1,128)} %bitcast.113), custom_call_target="tpu_custom_call" | custom-call | flops 4294967296 | bytes 16777216 | tf_op jit(solution)/shard_map/hidden/pallas_call | solution.py:179
  286.9 12.1 %hidden.3 = (bf16[512,2048]{1,0:T(8,128)(2,1)}, f32[512,2048]{1,0:T(8,128)}) custom-call(bf16[512,2048]{1,0:T(8,128)(2,1)} %get-tuple-element.96.a_ref.refs_1_, bf16[1024,2048]{1,0:T(8,128)(2,1)} %pack.13.near_ref.un_ref, bf16[1024,2048]{1,0:T(8,128)(2,1)} %collective-permute-done.5.far_ref.uf_ref, f32[1,2048]{1,0:T(1,128)} %bitcast.114), custom_call_target="tpu_custom_call" | custom-call | flops 4294967296 | bytes 16777216 | tf_op jit(solution)/shard_map/hidden/pallas_call | solution.py:179
  299.0 11.6 %d_hidden.2 = (bf16[512,2048]{1,0:T(8,128)(2,1)}, f32[8,2048]{1,0:T(8,128)}) custom-call(bf16[512,2048]{1,0:T(8,128)(2,1)} %get-tuple-element.108.d0_ref.d_ref.refs_4_.refs_0_, bf16[1024,2048]{1,0:T(8,128)(2,1)} %pack.20.dn_ref.near_ref, bf16[1024,2048]{1,0:T(8,128)(2,1)} %collective-permute-done.19.df_ref.far_ref, f32[512,2048]{1,0:T(8,128)} %get-tuple-element.112.slope_ref), custom_call_target="tpu_custom_call" | custom-call | flops 4294967296 | bytes 16777216 | tf_op jit(solution)/shard_map/d_hidden/pallas_call | solution.py:202
  310.6 11.6 %d_hidden.3 = (bf16[512,2048]{1,0:T(8,128)(2,1)}, f32[8,2048]{1,0:T(8,128)}) custom-call(bf16[512,2048]{1,0:T(8,128)(2,1)} %pack.21.d1_ref.d_ref.refs_5_.refs_1_, bf16[1024,2048]{1,0:T(8,128)(2,1)} %pack.20.dn_ref.near_ref, bf16[1024,2048]{1,0:T(8,128)(2,1)} %collective-permute-done.19.df_ref.far_ref, f32[512,2048]{1,0:T(8,128)} %get-tuple-element.114.slope_ref), custom_call_target="tpu_custom_call" | custom-call | flops 4294967296 | bytes 16777216 | tf_op jit(solution)/shard_map/d_hidden/pallas_call | solution.py:202
  323.2 24.2 %input_grad.1 = (f32[256,2048]{1,0:T(8,128)}, bf16[256,2048]{1,0:T(8,128)(2,1)}, f32[256,2048]{1,0:T(8,128)}, bf16[256,2048]{1,0:T(8,128)(2,1)}, f32[8,2048]{1,0:T(8,128)}) custom-call(bf16[1024,1536]{1,0:T(8,128)(2,1)} %get-tuple-element.111.dl_ref.refs_2_.refs_3_, bf16[512,2048]{1,0:T(8,128)(2,1)} %get-tuple-element.113.h0_ref.refs_2_, ...), custom_call_target="tpu_custom_call" | custom-call | flops 15032385536 | bytes 34603008 | tf_op jit(solution)/shard_map/input_grad/pallas_call | solution.py:462
  358.7 9.1 %grad_far.3 = bf16[1024,2048]{1,0:T(8,128)(2,1)} custom-call(bf16[512,2048]{1,0:T(8,128)(2,1)} %get-tuple-element.98.a0_ref.refs_0_, bf16[512,2048]{1,0:T(8,128)(2,1)} %get-tuple-element.99.a1_ref.refs_1_, bf16[1024,1536]{1,0:T(8,128)(2,1)} %get-tuple-element.111.dl_ref.refs_2_.refs_3_, bf16[1024,1536]{1,0:T(8,128)(2,1)} %get-tuple-element.111.dl_ref.refs_2_.refs_3_, ...), custom_call_target="tpu_custom_call" | custom-call | flops 4294967296 | bytes 12582912 | tf_op jit(solution)/shard_map/grad_far/pallas_call | solution.py:529
  368.4 17.0 %branch.1 = (f32[256,2048]{1,0:T(8,128)}, bf16[256,2048]{1,0:T(8,128)(2,1)}, f32[256,2048]{1,0:T(8,128)}, bf16[256,2048]{1,0:T(8,128)(2,1)}) custom-call(bf16[512,2048]{1,0:T(8,128)(2,1)} %get-tuple-element.92.a0_ref.refs_2_, bf16[512,2048]{1,0:T(8,128)(2,1)} %get-tuple-element.97.a1_ref.refs_3_, ...), custom_call_target="tpu_custom_call" | custom-call | flops 10737418240 | bytes 24117248 | tf_op jit(solution)/shard_map/branch/pallas_call | solution.py:414
  387.0 8.7 %grad_far.5 = bf16[1024,2048]{1,0:T(8,128)(2,1)} custom-call(bf16[512,2048]{1,0:T(8,128)(2,1)} %get-tuple-element.108.d0_ref.d_ref.refs_4_.refs_0_, bf16[512,2048]{1,0:T(8,128)(2,1)} %pack.21.d1_ref.d_ref.refs_5_.refs_1_, bf16[512,2048]{1,0:T(8,128)(2,1)} %get-tuple-element.92.a0_ref.refs_2_, bf16[512,2048]{1,0:T(8,128)(2,1)} %get-tuple-element.97.a1_ref.refs_3_), custom_call_target="tpu_custom_call" | custom-call | flops 4294967296 | bytes 10485760 | tf_op jit(solution)/shard_map/grad_far/pallas_call | solution.py:529
  410.3 11.7 %collective-permute-done.21.got_ref = bf16[256,2048]{1,0:T(8,128)(2,1)S(1)} collective-permute-done((bf16[256,2048]{1,0:T(8,128)(2,1)}, bf16[256,2048]{1,0:T(8,128)(2,1)S(1)}, u32[]{:S(2)}, u32[]{:S(2)}) %collective-permute-start.21) | collective-permute-done | bytes 1048608 | tf_op jit(solution)/shard_map/ppermute | solution.py:734
  427.5 16.9 %collective-permute-done.27.got_ref = bf16[256,2048]{1,0:T(8,128)(2,1)S(1)} collective-permute-done((bf16[256,2048]{1,0:T(8,128)(2,1)}, bf16[256,2048]{1,0:T(8,128)(2,1)S(1)}, u32[]{:S(2)}, u32[]{:S(2)}) %collective-permute-start.27) | collective-permute-done | bytes 1048608 | tf_op jit(solution)/shard_map/ppermute | solution.py:734
  450.6 35.7 %collective-permute-done.20 = bf16[256,2048]{1,0:T(8,128)(2,1)S(1)} collective-permute-done((bf16[256,2048]{1,0:T(8,128)(2,1)}, bf16[256,2048]{1,0:T(8,128)(2,1)S(1)}, u32[]{:S(2)}, u32[]{:S(2)}) %collective-permute-start.20) | collective-permute-done | bytes 1048608 | tf_op jit(solution)/shard_map/ppermute | solution.py:734
  494.5 12.3 %grad_near.3 = (bf16[256,2048]{1,0:T(8,128)(2,1)}, bf16[256,2048]{1,0:T(8,128)(2,1)}, bf16[256,2048]{1,0:T(8,128)(2,1)}, bf16[256,2048]{1,0:T(8,128)(2,1)}) custom-call(bf16[512,2048]{1,0:T(8,128)(2,1)} %get-tuple-element.98.a0_ref.refs_0_, bf16[512,2048]{1,0:T(8,128)(2,1)} %get-tuple-element.99.a1_ref.refs_1_, ...), custom_call_target="tpu_custom_call" | custom-call | flops 4294967296 | bytes 16777216 | tf_op jit(solution)/shard_map/grad_near/pallas_call | solution.py:529
  506.8 29.0 %collective-permute-done.26 = bf16[256,2048]{1,0:T(8,128)(2,1)S(1)} collective-permute-done((bf16[256,2048]{1,0:T(8,128)(2,1)}, bf16[256,2048]{1,0:T(8,128)(2,1)S(1)}, u32[]{:S(2)}, u32[]{:S(2)}) %collective-permute-start.26) | collective-permute-done | bytes 1048608 | tf_op jit(solution)/shard_map/ppermute | solution.py:734
  538.1 10.5 %grad_near.5 = (bf16[256,2048]{1,0:T(8,128)(2,1)}, bf16[256,2048]{1,0:T(8,128)(2,1)}, bf16[256,2048]{1,0:T(8,128)(2,1)}, bf16[256,2048]{1,0:T(8,128)(2,1)}) custom-call(bf16[512,2048]{1,0:T(8,128)(2,1)} %get-tuple-element.108.d0_ref.d_ref.refs_4_.refs_0_, bf16[512,2048]{1,0:T(8,128)(2,1)} %pack.21.d1_ref.d_ref.refs_5_.refs_1_, ...), custom_call_target="tpu_custom_call" | custom-call | flops 4294967296 | bytes 14680064 | tf_op jit(solution)/shard_map/grad_near/pallas_call | solution.py:529
  549.5 10.5 %grad_near.4 = (bf16[256,2048]{1,0:T(8,128)(2,1)}, bf16[256,2048]{1,0:T(8,128)(2,1)}, bf16[256,2048]{1,0:T(8,128)(2,1)}, bf16[256,2048]{1,0:T(8,128)(2,1)}) custom-call(bf16[512,2048]{1,0:T(8,128)(2,1)} %get-tuple-element.89.a_ref.refs_0_, bf16[512,2048]{1,0:T(8,128)(2,1)} %get-tuple-element.96.a_ref.refs_1_, ...), custom_call_target="tpu_custom_call" | custom-call | flops 4294967296 | bytes 14680064 | tf_op jit(solution)/shard_map/grad_near/pallas_call | solution.py:529
  566.3 18.2 %collective-permute-done.43.b_ref = bf16[256,2048]{1,0:T(8,128)(2,1)S(1)} collective-permute-done((bf16[256,2048]{1,0:T(8,128)(2,1)}, bf16[256,2048]{1,0:T(8,128)(2,1)S(1)}, u32[]{:S(2)}, u32[]{:S(2)}) %collective-permute-start.43) | collective-permute-done | bytes 1048608 | tf_op jit(solution)/shard_map/ppermute | solution.py:734
  587.7 16.6 %collective-permute-done.37.b_ref = bf16[256,2048]{1,0:T(8,128)(2,1)S(1)} collective-permute-done((bf16[256,2048]{1,0:T(8,128)(2,1)}, bf16[256,2048]{1,0:T(8,128)(2,1)S(1)}, u32[]{:S(2)}, u32[]{:S(2)}) %collective-permute-start.37) | collective-permute-done | bytes 1048608 | tf_op jit(solution)/shard_map/ppermute | solution.py:734
  620.7 9.7 %collective-permute-done.46 = bf16[128,2048]{1,0:T(8,128)(2,1)S(1)} collective-permute-done((bf16[128,2048]{1,0:T(8,128)(2,1)S(1)}, bf16[128,2048]{1,0:T(8,128)(2,1)S(1)}, u32[]{:S(2)}, u32[]{:S(2)}) %collective-permute-start.46) | collective-permute-done | bytes 524320 | tf_op jit(solution)/shard_map/ppermute | solution.py:734
  642.8 10.6 %finish.1 = (bf16[512,2048]{1,0:T(8,128)(2,1)}, f32[512,2048]{1,0:T(8,128)}) custom-call(s32[34]{0:T(128)} %stack.138.place_ref, bf16[256,2048]{1,0:T(8,128)(2,1)} %copy-done.6, bf16[256,2048]{1,0:T(8,128)(2,1)} %collective-permute-done.23.o1_ref, bf16[256,2048]{1,0:T(8,128)(2,1)} %copy-done.5, bf16[256,2048]{1,0:T(8,128)(2,1)} %collective-permute-done.29.g1_ref, ...), custom_call_target="tpu_custom_call" | custom-call | flops 20971520 | bytes 14680064 | tf_op jit(solution)/shard_map/finish/pallas_call | solution.py:587
  653.4 26.8 %collective-permute-done.35.t_ref = bf16[128,2048]{1,0:T(8,128)(2,1)S(1)} collective-permute-done((bf16[128,2048]{1,0:T(8,128)(2,1)}, bf16[128,2048]{1,0:T(8,128)(2,1)S(1)}, u32[]{:S(2)}, u32[]{:S(2)}) %collective-permute-start.35) | collective-permute-done | bytes 524320 | tf_op jit(solution)/shard_map/ppermute | solution.py:734
  691.5 11.2 %collective-permute-done.41.t_ref = bf16[128,2048]{1,0:T(8,128)(2,1)S(1)} collective-permute-done((bf16[128,2048]{1,0:T(8,128)(2,1)}, bf16[128,2048]{1,0:T(8,128)(2,1)S(1)}, u32[]{:S(2)}, u32[]{:S(2)}) %collective-permute-start.41) | collective-permute-done | bytes 524320 | tf_op jit(solution)/shard_map/ppermute | solution.py:734
  (283 shorter events, 197.8 us)
Async XLA Ops:
  35.5 47.6 %collective-permute-start.11 = (bf16[256,2048]{1,0:T(8,128)(2,1)}, bf16[256,2048]{1,0:T(8,128)(2,1)S(1)}, u32[]{:S(2)}, u32[]{:S(2)}) collective-permute-start(bf16[256,2048]{1,0:T(8,128)(2,1)} %pack.15), channel_id=1, source_target_pairs={{0,8},{4,12},{8,0},{12,4},{16,24},{20,28},{24,16},{28,20},{1,9},{5... | collective-permute-start | bytes 3145736 | tf_op jit(solution)/shard_map/ppermute | solution.py:734
  48.9 34.2 %collective-permute-start.13 = (bf16[256,2048]{1,0:T(8,128)(2,1)}, bf16[256,2048]{1,0:T(8,128)(2,1)S(1)}, u32[]{:S(2)}, u32[]{:S(2)}) collective-permute-start(bf16[256,2048]{1,0:T(8,128)(2,1)} %pack.16), channel_id=1, source_target_pairs={{0,16},{4,20},{8,24},{12,28},{16,0},{20,4},{24,8},{28,12},{1,17},{... | collective-permute-start | bytes 3145736 | tf_op jit(solution)/shard_map/ppermute | solution.py:734
  59.8 29.8 %collective-permute-start = (bf16[128,2048]{1,0:T(8,128)(2,1)}, bf16[128,2048]{1,0:T(8,128)(2,1)S(1)}, u32[]{:S(2)}, u32[]{:S(2)}) collective-permute-start(bf16[128,2048]{1,0:T(8,128)(2,1)} %get-tuple-element.90.refs_0_), channel_id=1, source_target_pairs={{0,16},{4,20},{8,24},{12,28},{16,0},{20,4},{24,8},{28,12},{1,17},{... | collective-permute-start | bytes 1572872 | tf_op jit(solution)/shard_map/ppermute | solution.py:734
  89.5 154.1 %collective-permute-start.14 = (bf16[1024,2048]{1,0:T(8,128)(2,1)}, bf16[1024,2048]{1,0:T(8,128)(2,1)}, u32[]{:S(2)}, u32[]{:S(2)}) collective-permute-start(bf16[1024,2048]{1,0:T(8,128)(2,1)} %pack.17.near_ref.sn_ref.an_ref), channel_id=1, source_target_pairs={{0,4},{4,0},{8,12},{12,8},{16,20},{20,16},{24,28},{28,24},{1,5},{5... | collective-permute-start | bytes 12582920 | tf_op jit(solution)/shard_map/ppermute | solution.py:734
  92.7 40.0 %collective-permute-start.1 = (bf16[256,2048]{1,0:T(8,128)(2,1)}, bf16[256,2048]{1,0:T(8,128)(2,1)S(1)}, u32[]{:S(2)}, u32[]{:S(2)}) collective-permute-start(bf16[256,2048]{1,0:T(8,128)(2,1)} %pack.11), channel_id=1, source_target_pairs={{0,8},{4,12},{8,0},{12,4},{16,24},{20,28},{24,16},{28,20},{1,9},{5... | collective-permute-start | bytes 3145736 | tf_op jit(solution)/shard_map/ppermute | solution.py:734
  97.4 36.2 %collective-permute-start.4 = (bf16[256,2048]{1,0:T(8,128)(2,1)}, bf16[256,2048]{1,0:T(8,128)(2,1)S(1)}, u32[]{:S(2)}, u32[]{:S(2)}) collective-permute-start(bf16[256,2048]{1,0:T(8,128)(2,1)} %pack.12), channel_id=1, source_target_pairs={{0,16},{4,20},{8,24},{12,28},{16,0},{20,4},{24,8},{28,12},{1,17},{... | collective-permute-start | bytes 3145736 | tf_op jit(solution)/shard_map/ppermute | solution.py:734
  115.0 48.4 %collective-permute-start.8 = (bf16[256,2048]{1,0:T(8,128)(2,1)}, bf16[256,2048]{1,0:T(8,128)(2,1)S(1)}, u32[]{:S(2)}, u32[]{:S(2)}) collective-permute-start(bf16[256,2048]{1,0:T(8,128)(2,1)} %get-tuple-element.95), channel_id=1, source_target_pairs={{0,2},{2,0},{1,3},{3,1},{4,6},{6,4},{5,7},{7,5},{8,10},{10,8},{9,1... | collective-permute-start | bytes 3145736 | tf_op jit(solution)/shard_map/ppermute | solution.py:734
  129.6 33.9 %collective-permute-start.16 = (bf16[256,2048]{1,0:T(8,128)(2,1)}, bf16[256,2048]{1,0:T(8,128)(2,1)S(1)}, u32[]{:S(2)}, u32[]{:S(2)}) collective-permute-start(bf16[256,2048]{1,0:T(8,128)(2,1)} %pack.18), channel_id=1, source_target_pairs={{0,8},{4,12},{8,0},{12,4},{16,24},{20,28},{24,16},{28,20},{1,9},{5... | collective-permute-start | bytes 3145736 | tf_op jit(solution)/shard_map/ppermute | solution.py:734
  132.6 30.9 %collective-permute-start.18 = (bf16[256,2048]{1,0:T(8,128)(2,1)}, bf16[256,2048]{1,0:T(8,128)(2,1)S(1)}, u32[]{:S(2)}, u32[]{:S(2)}) collective-permute-start(bf16[256,2048]{1,0:T(8,128)(2,1)} %pack.19), channel_id=1, source_target_pairs={{0,16},{4,20},{8,24},{12,28},{16,0},{20,4},{24,8},{28,12},{1,17},{... | collective-permute-start | bytes 3145736 | tf_op jit(solution)/shard_map/ppermute | solution.py:734
  139.0 135.7 %collective-permute-start.5 = (bf16[1024,2048]{1,0:T(8,128)(2,1)}, bf16[1024,2048]{1,0:T(8,128)(2,1)}, u32[]{:S(2)}, u32[]{:S(2)}) collective-permute-start(bf16[1024,2048]{1,0:T(8,128)(2,1)} %pack.13.near_ref.un_ref), channel_id=1, source_target_pairs={{0,4},{4,0},{8,12},{12,8},{16,20},{20,16},{24,28},{28,24},{1,5},{5... | collective-permute-start | bytes 12582920 | tf_op jit(solution)/shard_map/ppermute | solution.py:734
  163.5 47.4 %collective-permute-start.24 = (bf16[256,2048]{1,0:T(8,128)(2,1)}, bf16[256,2048]{1,0:T(8,128)(2,1)}, u32[]{:S(2)}, u32[]{:S(2)}) collective-permute-start(bf16[256,2048]{1,0:T(8,128)(2,1)} %get-tuple-element.110), channel_id=1, source_target_pairs={{0,2},{2,0},{1,3},{3,1},{4,6},{6,4},{5,7},{7,5},{8,10},{10,8},{9,1... | collective-permute-start | bytes 3145736 | tf_op jit(solution)/shard_map/ppermute | solution.py:734
  169.9 129.1 %collective-permute-start.19 = (bf16[1024,2048]{1,0:T(8,128)(2,1)}, bf16[1024,2048]{1,0:T(8,128)(2,1)}, u32[]{:S(2)}, u32[]{:S(2)}) collective-permute-start(bf16[1024,2048]{1,0:T(8,128)(2,1)} %pack.20.dn_ref.near_ref), channel_id=1, source_target_pairs={{0,4},{4,0},{8,12},{12,8},{16,20},{20,16},{24,28},{28,24},{1,5},{5... | collective-permute-start | bytes 12582920 | tf_op jit(solution)/shard_map/ppermute | solution.py:734
  170.0 50.8 %collective-permute-start.9 = (bf16[256,2048]{1,0:T(8,128)(2,1)S(1)}, bf16[256,2048]{1,0:T(8,128)(2,1)}, u32[]{:S(2)}, u32[]{:S(2)}) collective-permute-start(bf16[256,2048]{1,0:T(8,128)(2,1)S(1)} %collective-permute-done.8.refs_0_), channel_id=1, source_target_pairs={{0,1},{1,0},{2,3},{3,2},{4,5},{5,4},{6,7},{7,6},{8,9},{9,8},{10,11... | collective-permute-start | bytes 3145736 | tf_op jit(solution)/shard_map/ppermute | solution.py:734
  210.9 29.6 %collective-permute-start.25 = (bf16[256,2048]{1,0:T(8,128)(2,1)}, bf16[256,2048]{1,0:T(8,128)(2,1)}, u32[]{:S(2)}, u32[]{:S(2)}) collective-permute-start(bf16[256,2048]{1,0:T(8,128)(2,1)} %collective-permute-done.24.refs_0_), channel_id=1, source_target_pairs={{0,1},{1,0},{2,3},{3,2},{4,5},{5,4},{6,7},{7,6},{8,9},{9,8},{10,11... | collective-permute-start | bytes 3145736 | tf_op jit(solution)/shard_map/ppermute | solution.py:734
  367.8 126.6 %collective-permute-start.30 = (bf16[1024,2048]{1,0:T(8,128)(2,1)}, bf16[1024,2048]{1,0:T(8,128)(2,1)}, u32[]{:S(2)}, u32[]{:S(2)}) collective-permute-start(bf16[1024,2048]{1,0:T(8,128)(2,1)} %grad_far.3), channel_id=1, source_target_pairs={{0,4},{4,0},{8,12},{12,8},{16,20},{20,16},{24,28},{28,24},{1,5},{5... | collective-permute-start | bytes 12582920 | tf_op jit(solution)/shard_map/ppermute | solution.py:734
  397.4 47.0 %collective-permute-start.27 = (bf16[256,2048]{1,0:T(8,128)(2,1)}, bf16[256,2048]{1,0:T(8,128)(2,1)S(1)}, u32[]{:S(2)}, u32[]{:S(2)}) collective-permute-start(bf16[256,2048]{1,0:T(8,128)(2,1)} %get-tuple-element.123), channel_id=1, source_target_pairs={{0,1},{1,0},{2,3},{3,2},{4,5},{5,4},{6,7},{7,6},{8,9},{9,8},{10,11... | collective-permute-start | bytes 3145736 | tf_op jit(solution)/shard_map/ppermute | solution.py:734
  397.7 139.2 %collective-permute-start.42 = (bf16[1024,2048]{1,0:T(8,128)(2,1)}, bf16[1024,2048]{1,0:T(8,128)(2,1)}, u32[]{:S(2)}, u32[]{:S(2)}) collective-permute-start(bf16[1024,2048]{1,0:T(8,128)(2,1)} %grad_far.5), channel_id=1, source_target_pairs={{0,4},{4,0},{8,12},{12,8},{16,20},{20,16},{24,28},{28,24},{1,5},{5... | collective-permute-start | bytes 12582920 | tf_op jit(solution)/shard_map/ppermute | solution.py:734
  407.0 141.5 %collective-permute-start.36 = (bf16[1024,2048]{1,0:T(8,128)(2,1)}, bf16[1024,2048]{1,0:T(8,128)(2,1)}, u32[]{:S(2)}, u32[]{:S(2)}) collective-permute-start(bf16[1024,2048]{1,0:T(8,128)(2,1)} %grad_far.4), channel_id=1, source_target_pairs={{0,4},{4,0},{8,12},{12,8},{16,20},{20,16},{24,28},{28,24},{1,5},{5... | collective-permute-start | bytes 12582920 | tf_op jit(solution)/shard_map/ppermute | solution.py:734
  422.0 64.4 %collective-permute-start.20 = (bf16[256,2048]{1,0:T(8,128)(2,1)}, bf16[256,2048]{1,0:T(8,128)(2,1)S(1)}, u32[]{:S(2)}, u32[]{:S(2)}) collective-permute-start(bf16[256,2048]{1,0:T(8,128)(2,1)} %get-tuple-element.103), channel_id=1, source_target_pairs={{0,1},{1,0},{2,3},{3,2},{4,5},{5,4},{6,7},{7,6},{8,9},{9,8},{10,11... | collective-permute-start | bytes 3145736 | tf_op jit(solution)/shard_map/ppermute | solution.py:734
  444.4 46.6 %collective-permute-start.22 = (bf16[256,2048]{1,0:T(8,128)(2,1)}, bf16[256,2048]{1,0:T(8,128)(2,1)}, u32[]{:S(2)}, u32[]{:S(2)}) collective-permute-start(bf16[256,2048]{1,0:T(8,128)(2,1)} %fold.2), channel_id=1, source_target_pairs={{0,2},{2,0},{1,3},{3,1},{4,6},{6,4},{5,7},{7,5},{8,10},{10,8},{9,1... | collective-permute-start | bytes 3145736 | tf_op jit(solution)/shard_map/ppermute | solution.py:734
  486.3 49.5 %collective-permute-start.26 = (bf16[256,2048]{1,0:T(8,128)(2,1)}, bf16[256,2048]{1,0:T(8,128)(2,1)S(1)}, u32[]{:S(2)}, u32[]{:S(2)}) collective-permute-start(bf16[256,2048]{1,0:T(8,128)(2,1)} %get-tuple-element.121), channel_id=1, source_target_pairs={{0,1},{1,0},{2,3},{3,2},{4,5},{5,4},{6,7},{7,6},{8,9},{9,8},{10,11... | collective-permute-start | bytes 3145736 | tf_op jit(solution)/shard_map/ppermute | solution.py:734
  491.0 45.3 %collective-permute-start.28 = (bf16[256,2048]{1,0:T(8,128)(2,1)}, bf16[256,2048]{1,0:T(8,128)(2,1)S(1)}, u32[]{:S(2)}, u32[]{:S(2)}) collective-permute-start(bf16[256,2048]{1,0:T(8,128)(2,1)} %fold.3), channel_id=1, source_target_pairs={{0,2},{2,0},{1,3},{3,1},{4,6},{6,4},{5,7},{7,5},{8,10},{10,8},{9,1... | collective-permute-start | bytes 3145736 | tf_op jit(solution)/shard_map/ppermute | solution.py:734
  494.4 143.3 %collective-permute-start.23 = (bf16[256,2048]{1,0:T(8,128)(2,1)S(1)}, bf16[256,2048]{1,0:T(8,128)(2,1)}, u32[]{:S(2)}, u32[]{:S(2)}) collective-permute-start(bf16[256,2048]{1,0:T(8,128)(2,1)S(1)} %add_convert_fusion.1.o0_ref), channel_id=1, source_target_pairs={{0,1},{1,0},{2,3},{3,2},{4,5},{5,4},{6,7},{7,6},{8,9},{9,8},{10,11... | collective-permute-start | bytes 3145736 | tf_op jit(solution)/shard_map/ppermute | solution.py:734
  536.8 100.9 %collective-permute-start.29 = (bf16[256,2048]{1,0:T(8,128)(2,1)S(1)}, bf16[256,2048]{1,0:T(8,128)(2,1)}, u32[]{:S(2)}, u32[]{:S(2)}) collective-permute-start(bf16[256,2048]{1,0:T(8,128)(2,1)S(1)} %add_convert_fusion.g0_ref), channel_id=1, source_target_pairs={{0,1},{1,0},{2,3},{3,2},{4,5},{5,4},{6,7},{7,6},{8,9},{9,8},{10,11... | collective-permute-start | bytes 3145736 | tf_op jit(solution)/shard_map/ppermute | solution.py:734
  548.6 36.0 %collective-permute-start.43 = (bf16[256,2048]{1,0:T(8,128)(2,1)}, bf16[256,2048]{1,0:T(8,128)(2,1)S(1)}, u32[]{:S(2)}, u32[]{:S(2)}) collective-permute-start(bf16[256,2048]{1,0:T(8,128)(2,1)} %get-tuple-element.138), channel_id=1, source_target_pairs={{0,8},{4,12},{8,0},{12,4},{16,24},{20,28},{24,16},{28,20},{1,9},{5... | collective-permute-start | bytes 3145736 | tf_op jit(solution)/shard_map/ppermute | solution.py:734
  563.8 40.5 %collective-permute-start.37 = (bf16[256,2048]{1,0:T(8,128)(2,1)}, bf16[256,2048]{1,0:T(8,128)(2,1)S(1)}, u32[]{:S(2)}, u32[]{:S(2)}) collective-permute-start(bf16[256,2048]{1,0:T(8,128)(2,1)} %get-tuple-element.133), channel_id=1, source_target_pairs={{0,8},{4,12},{8,0},{12,4},{16,24},{20,28},{24,16},{28,20},{1,9},{5... | collective-permute-start | bytes 3145736 | tf_op jit(solution)/shard_map/ppermute | solution.py:734
  586.1 54.5 %collective-permute-start.32 = (bf16[128,2048]{1,0:T(8,128)(2,1)S(1)}, bf16[128,2048]{1,0:T(8,128)(2,1)S(1)}, u32[]{:S(2)}, u32[]{:S(2)}) collective-permute-start(bf16[128,2048]{1,0:T(8,128)(2,1)S(1)} %add_convert_fusion.10), channel_id=1, source_target_pairs={{0,16},{4,20},{8,24},{12,28},{16,0},{20,4},{24,8},{28,12},{1,17},{... | collective-permute-start | bytes 1572872 | tf_op jit(solution)/shard_map/ppermute | solution.py:734
  630.4 80.4 %collective-permute-start.44 = (bf16[128,2048]{1,0:T(8,128)(2,1)}, bf16[128,2048]{1,0:T(8,128)(2,1)S(1)}, u32[]{:S(2)}, u32[]{:S(2)}) collective-permute-start(bf16[128,2048]{1,0:T(8,128)(2,1)} %add_convert_fusion.4), channel_id=1, source_target_pairs={{0,16},{4,20},{8,24},{12,28},{16,0},{20,4},{24,8},{28,12},{1,17},{... | collective-permute-start | bytes 1572872 | tf_op jit(solution)/shard_map/ppermute | solution.py:734
  636.1 55.4 %collective-permute-start.38 = (bf16[128,2048]{1,0:T(8,128)(2,1)}, bf16[128,2048]{1,0:T(8,128)(2,1)S(1)}, u32[]{:S(2)}, u32[]{:S(2)}) collective-permute-start(bf16[128,2048]{1,0:T(8,128)(2,1)} %add_convert_fusion.7), channel_id=1, source_target_pairs={{0,16},{4,20},{8,24},{12,28},{16,0},{20,4},{24,8},{28,12},{1,17},{... | collective-permute-start | bytes 1572872 | tf_op jit(solution)/shard_map/ppermute | solution.py:734
  637.7 42.6 %collective-permute-start.35 = (bf16[128,2048]{1,0:T(8,128)(2,1)}, bf16[128,2048]{1,0:T(8,128)(2,1)S(1)}, u32[]{:S(2)}, u32[]{:S(2)}) collective-permute-start(bf16[128,2048]{1,0:T(8,128)(2,1)} %add_convert_fusion.8), channel_id=1, source_target_pairs={{0,2},{2,0},{1,3},{3,1},{4,6},{6,4},{5,7},{7,5},{8,10},{10,8},{9,1... | collective-permute-start | bytes 1572872 | tf_op jit(solution)/shard_map/ppermute | solution.py:734
  637.7 73.1 %collective-permute-start.47 = (bf16[128,2048]{1,0:T(8,128)(2,1)}, bf16[128,2048]{1,0:T(8,128)(2,1)S(1)}, u32[]{:S(2)}, u32[]{:S(2)}) collective-permute-start(bf16[128,2048]{1,0:T(8,128)(2,1)} %add_convert_fusion.2), channel_id=1, source_target_pairs={{0,2},{2,0},{1,3},{3,1},{4,6},{6,4},{5,7},{7,5},{8,10},{10,8},{9,1... | collective-permute-start | bytes 1572872 | tf_op jit(solution)/shard_map/ppermute | solution.py:734
  640.6 62.0 %collective-permute-start.41 = (bf16[128,2048]{1,0:T(8,128)(2,1)}, bf16[128,2048]{1,0:T(8,128)(2,1)S(1)}, u32[]{:S(2)}, u32[]{:S(2)}) collective-permute-start(bf16[128,2048]{1,0:T(8,128)(2,1)} %add_convert_fusion.5), channel_id=1, source_target_pairs={{0,2},{2,0},{1,3},{3,1},{4,6},{6,4},{5,7},{7,5},{8,10},{10,8},{9,1... | collective-permute-start | bytes 1572872 | tf_op jit(solution)/shard_map/ppermute | solution.py:734
  (74 other events, 1184.1 us)

commit v2 on v1

--- a/solution.py
+++ b/solution.py
@@ -39,57 +39,110 @@
 
 BLOCK = 128
 MIB = 1024 * 1024
+COSTS = [50, 50, 50, 50, 50, 50, 50, 5, 5, 50, 50, 5, 0.5, 50, 50, 2, 50, 50, 50, 50, 50, 50, 50, 0.5, 20, 10, 10, 50, 0.5, 50, 2, 50, 10, 0, 50, 50, 0.5, 50, 50, 50, 50, 0.5, 50, 50, 5, 5, 5, 50, 50, 10, 50, 20, 10, 50, 50, 50, 50, 50, 50, 50, 50, 50, 50, 10]
 
 
 def whole(shape):
-    return pl.BlockSpec(shape, lambda *_: (0,) * len(shape))
+    return pl.BlockSpec(shape, lambda *_: (0,) * len(shape), pipeline_mode=pl.Buffered(1))
+
+
+ORDER = []
+CALLS = []
 
 
 def call(kernel, grid, in_specs, out_specs, out_shape, name, flops, nbytes, prefetch=0, scratch=(), limit=56):
-    return pl.pallas_call(
-        kernel,
+    single = not isinstance(out_shape, (list, tuple))
+    specs, shapes = ([out_specs], [out_shape]) if single else (list(out_specs), list(out_shape))
+    waits = tuple(ORDER)
+    cost = COSTS[len(CALLS)] if len(CALLS) < len(COSTS) else 10
+    CALLS.append(name)
+    first, outs = prefetch + len(in_specs), len(shapes)
+    anywhere = pl.BlockSpec(memory_space=pl.ANY)
+
+    def ordered(*refs):
+        rest = refs[first + len(waits) :]
+        kernel(*refs[:first], *rest[:outs], *rest[outs + 1 :])
+
+    run = pl.pallas_call(
+        ordered,
         grid_spec=pltpu.PrefetchScalarGridSpec(
-            num_scalar_prefetch=prefetch, grid=grid, in_specs=in_specs, out_specs=out_specs, scratch_shapes=list(scratch)
+            num_scalar_prefetch=prefetch,
+            grid=grid,
+            in_specs=[*in_specs, *[anywhere] * len(waits)],
+            out_specs=[*specs, anywhere],
+            scratch_shapes=list(scratch),
         ),
-        out_shape=out_shape,
+        out_shape=[*shapes, like((8, 128), F32)],
         compiler_params=pltpu.CompilerParams(vmem_limit_bytes=limit * MIB),
-        cost_estimate=pl.CostEstimate(flops=flops, bytes_accessed=nbytes, transcendentals=0),
+        cost_estimate=pl.CostEstimate(flops=int(cost * 1e9), bytes_accessed=1, transcendentals=0),
         name=name,
     )
 
+    def ordered_call(*operands):
+        *results, token = run(*operands, *waits)
+        ORDER[:] = [token]
+        return results[0] if single else results
+
+    return ordered_call
+
 
 def like(shape, dtype):
     return jax.ShapeDtypeStruct(shape, dtype)
 
 
-def arrange_kernel(place_ref, x_ref, d_ref, v_ref, up_ref, down_ref, xo_ref, do_ref, xs_ref, ds_ref, vo_ref, *quarter_refs):
+def cut_kernel(flip, c_ref, *refs):
+    *operands, out_ref = refs
+    col = 0
+    for ref in operands:
+        if len(ref.shape) == 3:
+            heads, wide = ref.shape[1] // 2, ref.shape[2]
+            for c in range(2):
+
+                @pl.when(c_ref[0] == c)
+                def _(c=c, ref=ref, col=col):
+                    for h in range(heads):
+                        out_ref[:, col + h * wide : col + (h + 1) * wide] = ref[:, (c ^ flip) * heads + h, :]
+
+            col += heads * wide
+        else:
+            n = ref.shape[1] // 2
+            out_ref[:, col : col + n] = ref[:, pl.ds(pl.multiple_of((c_ref[0] ^ flip) * n, n), n)]
+            col += n
+
+
+def cut_quarter(ctx, flip, *operands):
+    rows = operands[0].shape[0]
+    n = sum(a.size for a in operands) // rows // 2
+    return call(
+        functools.partial(cut_kernel, flip),
+        (1,),
+        [whole(a.shape) for a in operands],
+        whole((rows, n)),
+        like((rows, n), BF),
+        "cut",
+        0,
+        6 * rows * n,
+        prefetch=1,
+    )(ctx, *operands)
+
+
+def arrange_kernel(place_ref, x_ref, d_ref, v_ref, xo_ref, do_ref, vo_ref):
     width = x_ref.shape[1]
     count = width // BLOCK
     rows = x_ref.shape[0] // 2
-    n = quarter_refs[0].shape[1]
-    for k in range(2):
-        cols = pl.ds(pl.multiple_of((place_ref[2 * count + 1] ^ k) * n, n), n)
-        quarter_refs[k][...] = up_ref[:, cols]
-        quarter_refs[2 + k][...] = down_ref[:, cols]
     for j in range(count):
         out = slice(j * BLOCK, (j + 1) * BLOCK)
         col = pl.ds(pl.multiple_of(place_ref[j] * BLOCK, BLOCK), BLOCK)
-        sent = pl.ds(pl.multiple_of(place_ref[count + j] * BLOCK, BLOCK), BLOCK)
         for b in range(2):
             row = pl.ds(pl.multiple_of((place_ref[2 * count] ^ b) * rows, rows), rows)
             xo_ref[b * rows : (b + 1) * rows, out] = x_ref[row, col]
             do_ref[b * rows : (b + 1) * rows, out] = d_ref[row, col]
-            if b == 0:
-                xs_ref[:, out] = x_ref[row, sent]
-                ds_ref[:, out] = d_ref[row, sent]
         vo_ref[:, out] = v_ref[:, col].astype(F32)
 
 
-def arrange(place, x, d, v, up, down):
-    sent = (x.shape[0] // 2, x.shape[1])
-    part = (up.shape[0], up.shape[1] // 2)
-    operands = (x, d, v, up, down)
-    outs = [(x.shape, BF), (d.shape, BF), (sent, BF), (sent, BF), (v.shape, F32)] + [(part, BF)] * 4
+def arrange(place, x, d, v):
+    operands = (x, d, v)
+    outs = [(x.shape, BF), (d.shape, BF), (v.shape, F32)]
     return call(
         arrange_kernel,
         (1,),
@@ -98,9 +151,31 @@
         [like(*a) for a in outs],
         "arrange",
         0,
-        5 * x.size * 2,
+        4 * x.size * 2,
         prefetch=1,
     )(place, *operands)
+
+
+def outgoing_kernel(place_ref, x_ref, o_ref):
+    count = x_ref.shape[1] // BLOCK
+    for j in range(count):
+        col = pl.ds(pl.multiple_of(place_ref[count + j] * BLOCK, BLOCK), BLOCK)
+        o_ref[:, j * BLOCK : (j + 1) * BLOCK] = x_ref[:, col]
+
+
+def outgoing(place, x):
+    rows, width = x.shape[0] // 2, x.shape[1]
+    return call(
+        outgoing_kernel,
+        (1,),
+        [pl.BlockSpec((rows, width), lambda i, p: (p[2 * width // BLOCK], 0))],
+        whole((rows, width)),
+        like((rows, width), BF),
+        "outgoing",
+        0,
+        x.size * 2,
+        prefetch=1,
+    )(place, x)
 
 
 def unorder_kernel(place_ref, v_ref, o_ref):
@@ -123,11 +198,72 @@
         row += piece.shape[0]
 
 
-def pack(*pieces):
-    rows, n = sum(p.shape[0] for p in pieces), pieces[0].shape[1]
-    return call(
-        pack_kernel, (1,), [whole(p.shape) for p in pieces], whole((rows, n)), like((rows, n), BF), "pack", 0, rows * n * 4
-    )(*pieces)
+def pack(n, *pieces):
+    pieces = [p if isinstance(p, tuple) else (p, 0) for p in pieces]
+    rows = sum(p.shape[0] for p, _ in pieces)
+    return call(
+        pack_kernel,
+        (1,),
+        [pl.BlockSpec((p.shape[0], n), lambda i, k=k: (0, k)) for p, k in pieces],
+        whole((rows, n)),
+        like((rows, n), BF),
+        "pack",
+        0,
+        rows * n * 4,
+    )(*[p for p, _ in pieces])
+
+
+def halves_kernel(u_ref, v_ref, top_ref, low_ref):
+    top_ref[...] = u_ref[...]
+    low_ref[...] = v_ref[...]
+
+
+def halves(u, v):
+    rows, n = u.shape[0] // 2, u.shape[1]
+    return call(
+        halves_kernel,
+        (1,),
+        [pl.BlockSpec((rows, n), lambda i: (0, 0)), pl.BlockSpec((rows, n), lambda i: (1, 0))],
+        [whole((rows, n))] * 2,
+        [like((rows, n), BF)] * 2,
+        "halves",
+        0,
+        8 * rows * n,
+    )(u, v)
+
+
+def total_kernel(counts, *refs):
+    at = 0
+    for k, count in enumerate(counts):
+        total = refs[at][...].astype(F32)
+        for ref in refs[at + 1 : at + count]:
+            total = total + ref[...].astype(F32)
+        out_ref = refs[sum(counts) + k]
+        out_ref[...] = total.astype(out_ref.dtype)
+        at += count
+
+
+def totals(rows, *groups, dtype=BF, steps=1):
+    tile = rows // steps
+    in_specs, operands = [], []
+    for group in groups:
+        for a, k in group:
+            if a.shape[0] == 1:
+                in_specs.append(whole(a.shape))
+            else:
+                in_specs.append(pl.BlockSpec((tile, a.shape[1]), lambda i, k=k: (k * steps + i, 0)))
+            operands.append(a)
+    width = operands[0].shape[1]
+    return call(
+        functools.partial(total_kernel, [len(g) for g in groups]),
+        (steps,),
+        in_specs,
+        [pl.BlockSpec((tile, width), lambda i: (i, 0))] * len(groups),
+        [like((rows, width), dtype)] * len(groups),
+        "totals",
+        0,
+        8 * rows * width,
+    )(*operands)
 
 
 def norm_kernel(x_ref, v_ref, attn_ref, mlp_ref, mean_ref, inv_ref):
@@ -159,56 +295,60 @@
     )(x, vec)
 
 
-def both(a_ref, near_ref, far_ref):
-    half = a_ref.shape[1] // 2
-    return dot(a_ref[:, :half], near_ref[...], 1, 0) + dot(a_ref[:, half:], far_ref[...], 1, 0)
-
-
-def hidden_kernel(a_ref, near_ref, far_ref, b_ref, act_ref, slope_ref):
-    hidden = both(a_ref, near_ref, far_ref) + b_ref[...]
+def over_rows(a, weight):
+    rows = weight[0].shape[0]
+    return sum(dot(a[:, k * rows : (k + 1) * rows], part[...], 1, 0) for k, part in enumerate(weight))
+
+
+def hidden_kernel(a_ref, b_ref, *refs):
+    *weight, act_ref, slope_ref = refs
+    hidden = over_rows(a_ref[...], weight) + b_ref[...]
     cdf = 0.5 * (1.0 + lax.erf(hidden * ROOT_HALF))
     act_ref[...] = (hidden * cdf).astype(BF)
     slope_ref[...] = cdf + hidden * jnp.exp(-0.5 * hidden * hidden) * (1.0 / ROOT_TWO_PI)
 
 
-def hidden_of(a, weight, bias, tile=256):
-    near, far = weight
-    (rows, width), n = a.shape, near.shape[1]
-    wide = pl.BlockSpec((width // 2, tile), lambda j: (0, j))
+def column_specs(weight, tile, at):
+    return [pl.BlockSpec((part.shape[0], tile), at) for part in weight]
+
+
+def hidden_of(a, weight, bias, tile=512):
+    (rows, width), n = a.shape, weight[0].shape[1]
+    tile = min(tile, n)
     out = pl.BlockSpec((rows, tile), lambda j: (0, j))
     return call(
         hidden_kernel,
         (n // tile,),
-        [whole(a.shape), wide, wide, pl.BlockSpec((1, tile), lambda j: (0, j))],
+        [whole(a.shape), pl.BlockSpec((1, tile), lambda j: (0, j)), *column_specs(weight, tile, lambda j: (0, j))],
         [out, out],
         [like((rows, n), BF), like((rows, n), F32)],
         "hidden",
         2 * rows * width * n,
-        (a.size + near.size * 2 + rows * n * 3) * 2,
-    )(a, near, far, bias)
-
-
-def d_hidden_kernel(d_ref, near_ref, far_ref, slope_ref, low_ref, sum_ref):
-    grad = both(d_ref, near_ref, far_ref) * slope_ref[...]
+        (a.size + width * n + rows * n * 3) * 2,
+    )(a, bias, *weight)
+
+
+def d_hidden_kernel(d_ref, slope_ref, *refs):
+    *weight, low_ref, sum_ref = refs
+    grad = over_rows(d_ref[...], weight) * slope_ref[...]
     low_ref[...] = grad.astype(BF)
     sum_ref[...] = jnp.broadcast_to(jnp.sum(grad, 0, keepdims=True), sum_ref.shape)
 
 
-def d_hidden_of(d, weight, slope, tile=256):
-    near, far = weight
-    (rows, width), n = d.shape, near.shape[1]
-    wide = pl.BlockSpec((width // 2, tile), lambda j: (0, j))
+def d_hidden_of(d, weight, slope, tile=512):
+    (rows, width), n = d.shape, weight[0].shape[1]
+    tile = min(tile, n)
     out = pl.BlockSpec((rows, tile), lambda j: (0, j))
     return call(
         d_hidden_kernel,
         (n // tile,),
-        [whole(d.shape), wide, wide, out],
+        [whole(d.shape), out, *column_specs(weight, tile, lambda j: (0, j))],
         [out, pl.BlockSpec((8, tile), lambda j: (0, j))],
         [like((rows, n), BF), like((8, n), F32)],
         "d_hidden",
         2 * rows * width * n,
-        (d.size + near.size * 2 + rows * n * 3) * 2,
-    )(d, near, far, slope)
+        (d.size + width * n + rows * n * 3) * 2,
+    )(d, slope, *weight)
 
 
 def turn(block, cosine, sine):
@@ -220,8 +360,9 @@
 
 
 def attend_kernel(
-    z_ref, a0_ref, a1_ref, near_ref, far_ref, b_ref, cos_ref, sin_ref, ctx_ref, pack_ref, log_ref
+    z_ref, a0_ref, a1_ref, b_ref, cos_ref, sin_ref, *refs
 ):
+    *weight, ctx_ref, pack_ref, log_ref = refs
     z = z_ref[0]
     size = a0_ref.shape[0] // 2
     hd = HEAD_DIM
@@ -232,8 +373,7 @@
 
     for b in range(4):
         a = (a0_ref, a1_ref)[b // 2][b % 2 * size : (b % 2 + 1) * size, :]
-        half = a.shape[1] // 2
-        lin = dot(a[:, :half], near_ref[...], 1, 0) + dot(a[:, half:], far_ref[...], 1, 0) + b_ref[...]
+        lin = over_rows(a, weight) + b_ref[...]
         mine = slice(b * size, (b + 1) * size)
         cosine, sine = cos_ref[mine, :], sin_ref[mine, :]
         rows = row_of(b)
@@ -255,7 +395,6 @@
 
 
 def attend(z, a0, a1, weight, bias, cosine, sine):
-    near, far = weight
     length, width = 2 * a0.shape[0], a0.shape[1]
     hd = HEAD_DIM
     heads = bias.shape[1] // (3 * hd)
@@ -266,11 +405,10 @@
         [
             whole(a0.shape),
             whole(a1.shape),
-            column(near.shape[0], 3 * hd),
-            column(far.shape[0], 3 * hd),
             column(1, 3 * hd),
             whole(cosine.shape),
             whole(sine.shape),
+            *column_specs(weight, 3 * hd, lambda h, p: (0, h)),
         ],
         [column(length, hd), column(length, 3 * hd), column(length, 128)],
         [like((length, heads * hd), BF), like((length, heads * 3 * hd), BF), like((length, heads * 128), F32)],
@@ -278,12 +416,13 @@
         (3 * length * length * hd + 6 * length * width * hd) * heads,
         length * width * 8,
         prefetch=1,
-    )(z, a0, a1, near, far, bias, cosine, sine)
+    )(z, a0, a1, bias, cosine, sine, *weight)
 
 
 def attend_back_kernel(
-    z_ref, pack_ref, log_ref, d0_ref, d1_ref, near_ref, far_ref, cos_ref, sin_ref, dl_ref, us_ref, g_s, dk_s, dv_s
+    z_ref, pack_ref, log_ref, d0_ref, d1_ref, cos_ref, sin_ref, *refs
 ):
+    *weight, dl_ref, us_ref, g_s, dk_s, dv_s = refs
     z = z_ref[0]
     size = d0_ref.shape[0] // 2
     hd = HEAD_DIM
@@ -293,7 +432,7 @@
         return pl.ds(pl.multiple_of((z ^ p) * size, size), size)
 
     for half, d_ref in enumerate((d0_ref, d1_ref)):
-        grad = both(d_ref, near_ref, far_ref).astype(BF)
+        grad = over_rows(d_ref[...], weight).astype(BF)
         g_s[row_of(2 * half), :] = grad[:size]
         g_s[row_of(2 * half + 1), :] = grad[size:]
     dk_s[...] = jnp.zeros_like(dk_s)
@@ -336,13 +475,11 @@
 
 
 def attend_back(z, packed, logs, d0, d1, weight, cosine, sine):
-    near, far = weight
     length, wide = packed.shape
     hd = HEAD_DIM
     heads = wide // (3 * hd)
     first = wide // hd
     column = lambda rows, cols: pl.BlockSpec((rows, cols), lambda h, p: (0, h))
-    dense = pl.BlockSpec((near.shape[0], hd), lambda h, p: (0, first + h))
     return call(
         attend_back_kernel,
         (heads,),
@@ -351,10 +488,9 @@
             column(length, 128),
             whole(d0.shape),
             whole(d1.shape),
-            dense,
-            dense,
             whole(cosine.shape),
             whole(sine.shape),
+            *column_specs(weight, hd, lambda h, p: (0, first + h)),
         ],
         [column(length, 3 * hd), column(8, 3 * hd)],
         [like((length, wide), BF), like((8, wide), F32)],
@@ -363,31 +499,26 @@
         length * wide * 8,
         prefetch=1,
         scratch=[pltpu.VMEM((length, hd), BF)] + [pltpu.VMEM((length, hd), F32)] * 2,
-    )(z, packed, logs, d0, d1, near, far, cosine, sine)
-
-
-def near_or_far(near_ref, far_ref, body):
+    )(z, packed, logs, d0, d1, cosine, sine, *weight)
+
+
+def in_turn(parts, body):
     j = pl.program_id(0)
-    count = pl.num_programs(0) // 2
-
-    @pl.when(j < count)
-    def _():
-        body(*near_ref)
-
-    @pl.when(j >= count)
-    def _():
-        body(*far_ref)
-
-
-def row_specs(shape, count, col=0):
-    half = count // 2
-    return [
-        pl.BlockSpec(shape, lambda j: (jnp.minimum(j, half - 1), col)),
-        pl.BlockSpec(shape, lambda j: (jnp.maximum(j - half, 0), col)),
-    ]
-
-
-def branch_kernel(a0_ref, a1_ref, ctx_ref, dn_ref, df_ref, sn_ref, sf_ref, *outs):
+    each = pl.num_programs(0) // len(parts)
+    for k, part in enumerate(parts):
+
+        @pl.when(j // each == k)
+        def _(part=part):
+            body(*part)
+
+
+def row_specs(shape, count, parts, col=0):
+    each = count // parts
+    return [pl.BlockSpec(shape, lambda j, k=k: (jnp.clip(j - k * each, 0, each - 1), col)) for k in range(parts)]
+
+
+def branch_kernel(parts, a0_ref, a1_ref, ctx_ref, *refs):
+    weights, outs = refs[: 2 * parts], refs[2 * parts :]
     size = outs[0].shape[0]
 
     def body(down_ref, dense_ref):
@@ -397,7 +528,7 @@
             outs[2 * k][...] = part[:size]
             outs[2 * k + 1][...] = part[size:].astype(BF)
 
-    near_or_far((dn_ref, sn_ref), (df_ref, sf_ref), body)
+    in_turn(list(zip(weights[:parts], weights[parts:])), body)
 
 
 def token_outs(size, width, tile):
@@ -407,19 +538,20 @@
 
 def branch_of(a0, a1, context_out, down, attn, tile=256):
     rows, n = a0.shape
-    width = 2 * down[0].shape[0]
+    parts = len(down)
+    width = parts * down[0].shape[0]
     cols = context_out.shape[1]
     count = width // tile
     specs, shapes = token_outs(rows // 2, width, tile)
     return call(
-        branch_kernel,
+        functools.partial(branch_kernel, parts),
         (count,),
         [
             whole(a0.shape),
             whole(a1.shape),
             whole(context_out.shape),
-            *row_specs((tile, n), count),
-            *row_specs((tile, cols), count, attn[0].shape[1] // cols - 1),
+            *row_specs((tile, n), count, parts),
+            *row_specs((tile, cols), count, parts, attn[0].shape[1] // cols - 1),
         ],
         specs,
         shapes,
@@ -430,8 +562,9 @@
 
 
 def input_grad_kernel(
-    dl_ref, h0_ref, h1_ref, an_ref, af_ref, un_ref, uf_ref, x0_ref, x1_ref, m0_ref, m1_ref, i0_ref, i1_ref, v_ref, *outs
+    parts, dl_ref, h0_ref, h1_ref, x0_ref, x1_ref, m0_ref, m1_ref, i0_ref, i1_ref, v_ref, *refs
 ):
+    weights, outs = refs[: 2 * parts], refs[2 * parts :]
     size = outs[0].shape[0]
     wide = dl_ref.shape[1]
     halves = ((h0_ref, x0_ref, m0_ref, i0_ref), (h1_ref, x1_ref, m1_ref, i1_ref))
@@ -449,41 +582,42 @@
             total = [u + v for u, v in zip(total, sums)]
         outs[4][...] = jnp.concatenate(total + [jnp.zeros((4, attn.shape[1]), F32)], 0)
 
-    near_or_far((an_ref, un_ref), (af_ref, uf_ref), body)
+    in_turn(list(zip(weights[:parts], weights[parts:])), body)
 
 
 def input_grad_of(d_linear, h0, h1, attn, up, xs, means, invs, vec, tile=256):
     rows, n = h0.shape
     width = xs[0].shape[1]
     wide = d_linear.shape[1]
+    parts = len(attn)
     count = width // tile
     specs, shapes = token_outs(rows // 2, width, tile)
     column = pl.BlockSpec((rows, tile), lambda j: (0, j))
     return call(
-        input_grad_kernel,
+        functools.partial(input_grad_kernel, parts),
         (count,),
         [
             whole(d_linear.shape),
             whole(h0.shape),
             whole(h1.shape),
-            *row_specs((tile, attn[0].shape[1]), count),
-            *row_specs((tile, n), count),
             column,
             column,
             *[whole(a.shape) for a in (*means, *invs)],
             pl.BlockSpec((vec.shape[0], tile), lambda j: (0, j)),
+            *row_specs((tile, attn[0].shape[1]), count, parts),
+            *row_specs((tile, n), count, parts),
         ],
         [*specs, pl.BlockSpec((8, tile), lambda j: (0, j))],
         [*shapes, like((8, width), F32)],
         "input_grad",
         4 * rows * width * (n + wide),
         (2 * rows * (n + wide) + width * (n + wide) + 2 * rows * width * 3) * 2,
-    )(d_linear, h0, h1, *attn, *up, *xs, *means, *invs, vec)
+    )(d_linear, h0, h1, *xs, *means, *invs, vec, *attn, *up)
 
 
 def grad_kernel(pairs, near, *refs):
-    operands = refs[: 4 * pairs]
-    outs = refs[4 * pairs + near :]
+    operands, refs = refs[: 4 * pairs], refs[4 * pairs :]
+    adds, outs = (refs[:4], refs[4:]) if near else (None, refs)
     j = pl.program_id(0)
     col = 0
     for k in range(pairs):
@@ -491,23 +625,20 @@
         part = dot(l0, r0, 0, 0) + dot(l1, r1, 0, 0)
         cols = slice(col, col + part.shape[1])
         col += part.shape[1]
-        if near:
-            part = (part + refs[4 * pairs][:, cols].astype(F32)).astype(BF)
-            for i, out_ref in enumerate(outs):
-
-                @pl.when(j == i)
-                def _(out_ref=out_ref, part=part, cols=cols):
-                    out_ref[:, cols] = part
-
-        else:
-            outs[0][:, cols] = part.astype(BF)
-
-
-def grad_of(factors, add=None):
+        for i, out_ref in enumerate(outs):
+
+            @pl.when(j == i)
+            def _(i=i, out_ref=out_ref, part=part, cols=cols):
+                if near:
+                    out_ref[:, cols] = (part + adds[i][:, cols].astype(F32)).astype(BF)
+                else:
+                    out_ref[:, cols] = part.astype(BF)
+
+
+def grad_of(factors, adds=()):
     width = factors[0][0].shape[1]
-    near = add is not None
     tile = width // 8
-    first = 0 if near else 4
+    first = 0 if adds else 4
     in_specs, operands, n, flops, nbytes = [], [], 0, 0, 0
     for l0, l1, r0, r1 in factors:
         rows = l0.shape[0]
@@ -516,26 +647,22 @@
             operands.append(left)
         cols = r0[0].shape[1]
         for right, k in (r0, r1):
-            in_specs.append(pl.BlockSpec((rows, cols), lambda j, k=k: (k, 0)))
+            in_specs.append(pl.BlockSpec((rows, cols), lambda j, k=k: (k, 0), pipeline_mode=pl.Buffered(1)))
             operands.append(right)
         n += cols
         flops += 2 * rows * width * cols
         nbytes += 2 * rows * (width + 2 * cols)
-    block = pl.BlockSpec((tile, n), lambda j: (j, 0))
-    if near:
-        in_specs.append(block)
-        operands.append(add)
-        nbytes += width * n
-    return call(
-        functools.partial(grad_kernel, len(factors), near),
+    in_specs += [whole((tile, n)) for _ in adds]
+    return call(
+        functools.partial(grad_kernel, len(factors), bool(adds)),
         (4,),
         in_specs,
-        [whole((tile, n))] * 4 if near else block,
-        [like((tile, n), BF)] * 4 if near else like((width // 2, n), BF),
-        "grad_near" if near else "grad_far",
+        [whole((tile, n))] * 4,
+        [like((tile, n), BF)] * 4,
+        "grad_near" if adds else "grad_far",
         flops,
         nbytes + width * n,
-    )(*operands)
+    )(*operands, *adds)
 
 
 def fold_kernel(cross, keep_ref, got_ref, o_ref):
@@ -572,7 +699,7 @@
             out_ref[:, col] = o_ref[:, part]
             grad_ref[:, col] = grad[:, part]
 
-    near_or_far((o0_ref, g0_ref), (o1_ref, g1_ref), body)
+    in_turn(((o0_ref, g0_ref), (o1_ref, g1_ref)), body)
 
 
 def finish(place, o0, o1, g0, g1, x, d):
@@ -628,6 +755,8 @@
 def adam(ctx, fixes, weight, moments, terms, theirs, tile=1024, first=0):
     rows, cols = weight.shape
     n = cols // 2
+    tile = min(tile, n)
+    first //= tile
     per = n // tile
     at = lambda k, i, c: (0, (c[0] ^ k) * per + i)
     mine = pl.BlockSpec((rows, tile), lambda k, i, c: (0, first + i + k * (per - 1 - i)))
@@ -719,6 +848,8 @@
     vector_moments,
     step_count,
 ):
+    ORDER.clear()
+    CALLS.clear()
     shard, ctx, ten = (lax.axis_index(a) for a in ("shard", "context", "tensor"))
     fast = shard_count == 8
     _, local_len, width = inputs.shape
@@ -744,100 +875,132 @@
     else:
         places = [[jnp.int32(j) for j in range(count)]] * 2
         cross = list(range(count))
-    place = jnp.stack([*places[0], *places[1], ten, ctx]).astype(jnp.int32)
+    place = jnp.stack([*places[0], *places[1], ten]).astype(jnp.int32)
     z = ctx * 2 + ten
     ctx_scalar, z_scalar = (v.reshape(1).astype(jnp.int32) for v in (ctx, z))
 
-    def after(value, *others):
-        return lax.optimization_barrier((value, *others))[0]
-
-    def gather_rows(mine, other):
-        if not fast:
-            block = jnp.where(ctx == 0, jnp.concatenate([mine, other], 0), jnp.concatenate([other, mine], 0))
-            full = lax.all_gather(block, "shard", axis=0, tiled=True)
-            return full[: width // 2], full[width // 2 :]
-        a1 = to_y(mine)
-        a2 = to_x(pack(mine, a1))
-        b1 = to_x(other)
-        b2 = to_y(pack(other, b1))
-        near = pack(mine, a1, a2, other, b1, b2)
-        return near, to_core(near)
-
-    def scatter_rows(factors):
-        far_part = grad_of(factors)
-        r = row_count
-        if not fast:
-            part = jnp.concatenate([*grad_of(factors, jnp.zeros_like(far_part)), far_part], 0)
-            total = lax.psum_scatter(part, "shard", scatter_dimension=0, tiled=True)
-            mine = lax.dynamic_slice_in_dim(total, ctx * r, r, 0)
-            away = lax.dynamic_slice_in_dim(total, (1 - ctx) * r, r, 0)
-            zero = jnp.zeros_like(mine)
-            return (mine, zero, zero), to_ctx(away)
-        a_own, a_x, b_own, b_y = grad_of(factors, to_core(far_part))
-        add = lambda u, v: (u.astype(F32) + v.astype(F32)).astype(BF)
-        b_got = to_y(b_y)
-        a_got = to_x(a_x)
-        b_last = to_x(add(b_own[r:], b_got[r:]))
-        a_last = to_y(add(a_own[r:], a_got[r:]))
-        away = (b_own[:r].astype(F32) + b_got[:r].astype(F32) + b_last.astype(F32)).astype(BF)
-        return (a_own, a_got, a_last), to_ctx(away)
-
-    def reduce_tokens(own, other):
-        far = to_ctx(fold(cross, other[0], to_ten(other[1])))
-        return own[0] + to_ten(own[1]).astype(F32) + far.astype(F32)
-
-    def attn_quarter(q):
-        qkv = lax.dynamic_slice_in_dim(qkv_weight, q * heads, heads, 1).reshape(row_count, n_qkv)
-        dense = lax.dynamic_slice_in_dim(dense_weight, q * head_cols, head_cols, 1)
-        return jnp.concatenate([qkv, dense], 1)
-
-    x_own, d_own, x_sent, d_sent, vec, up_mine, up_theirs, down_mine, down_theirs = arrange(
-        place, inputs.reshape(local_len, width), cotangent.reshape(local_len, width), vectors, up_weight, down_weight
-    )
-    up_other = to_ctx(up_theirs)
-    attn_other = to_ctx(attn_quarter(1 - ctx))
-    down_other = to_ctx(down_theirs)
-    x_first = to_ctx(after(x_sent, up_other, attn_other, down_other))
-    d_first = to_ctx(after(d_sent, x_first))
-    w_up = gather_rows(up_mine, up_other)
-    w_attn = gather_rows(attn_quarter(ctx), attn_other)
-    w_down = gather_rows(down_mine, down_other)
-    x_oth = pack(x_first, to_ten(x_first))
-    d_oth = pack(d_first, to_ten(d_first))
-
+    def wait(*values):
+        ORDER.extend(values)
+
+    def full_rows(mine, other):
+        block = jnp.where(ctx == 0, jnp.concatenate([mine, other], 0), jnp.concatenate([other, mine], 0))
+        full = lax.all_gather(block, "shard", axis=0, tiled=True)
+        return tuple(full[k * width // 4 : (k + 1) * width // 4] for k in range(4))
+
+    r = row_count
+    x_in, d_in = inputs.reshape(local_len, width), cotangent.reshape(local_len, width)
     unit_vals = unit_biases.astype(F32)
     my_units = lax.dynamic_slice_in_dim(unit_vals, ctx * heads, heads, 0)
     qkv_bias, unit_bias = my_units[:, :head_wide].reshape(1, n_qkv), my_units[:, head_wide:].reshape(1, units)
-    attn_own, mlp_own, mean_own, inv_own = norm(x_own, vec)
-    attn_oth, mlp_oth, mean_oth, inv_oth = norm(x_oth, vec)
-
     positions = ((jnp.arange(4) ^ z)[:, None] * quarter + jnp.arange(quarter)[None, :]).reshape(-1)
     cosine, sine = rotary_tables(positions)
+
+    n = up_weight.shape[1] // 2
+    units_other = to_ctx(cut_quarter(ctx_scalar, 1, up_weight, down_weight))
+    mine = cut_quarter(ctx_scalar, 0, up_weight, down_weight, qkv_weight, dense_weight)
+    if fast:
+        a_x, a_y = to_x(mine), to_y(mine)
+    x_own, d_own, vec = arrange(place, x_in, d_in, vectors)
+    attn_own, mlp_own, mean_own, inv_own = norm(x_own, vec)
+    if fast:
+        top, low = halves(a_y, a_x)
+        a_top, a_low = to_x(top), to_y(low)
+    wait(units_other)
+    attn_other = to_ctx(cut_quarter(ctx_scalar, 1, qkv_weight, dense_weight))
+    if fast:
+        units_x, units_y = to_x(units_other), to_y(units_other)
+    wait(attn_other)
+    x_first = to_ctx(outgoing(place, x_in))
+
+    def packed(pieces, k):
+        near = pack(n, *[(a, k) for a in pieces])
+        return near, to_core(near)
+
+    if fast:
+        mine_parts = (mine, a_y, a_x, a_top, a_low)
+        up_a, up_far_a = packed(mine_parts, 0)
+        down_a, down_far_a = packed(mine_parts, 1)
+        top, low = halves(units_y, units_x)
+        units_parts = (units_other, units_x, units_y, to_x(top), to_y(low))
+        attn_x, attn_y = to_x(attn_other), to_y(attn_other)
+        attn_a, attn_far_a = packed(mine_parts, 2)
+        up_b, up_far_b = packed(units_parts, 0)
+        top, low = halves(attn_y, attn_x)
+        attn_parts = (attn_other, attn_x, attn_y, to_x(top), to_y(low))
+        down_b, down_far_b = packed(units_parts, 1)
+        w_up, w_down = (up_a, up_b, up_far_a, up_far_b), (down_a, down_b, down_far_a, down_far_b)
+    else:
+        w_up = full_rows(mine[:, :n], units_other[:, :n])
+        w_down = full_rows(mine[:, n : 2 * n], units_other[:, n:])
+        w_attn = full_rows(mine[:, 2 * n :], attn_other)
     active_own, slope_own = hidden_of(mlp_own, w_up, unit_bias)
+    if fast:
+        attn_b, attn_far_b = packed(attn_parts, 0)
+        w_attn = (attn_a, attn_b, attn_far_a, attn_far_b)
+    wait(x_first)
+    d_first = to_ctx(outgoing(place, d_in))
+    x_second = to_ten(x_first)
     low_own, sum_own = d_hidden_of(d_own, w_down, slope_own)
+    x_oth = pack(width, x_first, x_second)
+    attn_oth, mlp_oth, mean_oth, inv_oth = norm(x_oth, vec)
     active_oth, slope_oth = hidden_of(mlp_oth, w_up, unit_bias)
-    context_out, packed, logs = attend(z_scalar, attn_own, attn_oth, w_attn, qkv_bias, cosine, sine)
+    wait(d_first)
+    d_second = to_ten(d_first)
+    context_out, packed_qkv, logs = attend(z_scalar, attn_own, attn_oth, w_attn, qkv_bias, cosine, sine)
     *branch_own, branch_keep, branch_send = branch_of(active_own, active_oth, context_out, w_down, w_attn)
-    branch_sum = reduce_tokens(branch_own, (branch_keep, branch_send))
+    branch_got = to_ten(branch_send)
+    branch_near = to_ten(branch_own[1])
+    d_oth = pack(width, d_first, d_second)
+
+    def far_parts(factors):
+        parts = grad_of(factors)
+        return [to_core(part) for part in parts] if fast else parts
+
+    def near_parts(factors, far):
+        if fast:
+            a_own, a_x, b_own, b_y = grad_of(factors, far)
+            return a_own, b_own, to_y(b_y), to_x(a_x)
+        near = grad_of(factors, [jnp.zeros_like(part) for part in far])
+        return lax.psum_scatter(jnp.concatenate([*near, *far], 0), "shard", scatter_dimension=0, tiled=True)
+
+    def second(parts):
+        if not fast:
+            return parts
+        a_own, b_own, b_got, a_got = parts
+        b_sum, a_sum = totals(r, ((b_own, 1), (b_got, 1)), ((a_own, 1), (a_got, 1)))
+        return (*parts, to_x(b_sum), to_y(a_sum))
+
+    def third(parts):
+        if not fast:
+            kept = lax.dynamic_slice_in_dim(parts, ctx * r, r, 0)
+            zero = jnp.zeros_like(kept)
+            return (kept, zero, zero), to_ctx(lax.dynamic_slice_in_dim(parts, (1 - ctx) * r, r, 0))
+        a_own, b_own, b_got, a_got, b_last, a_last = parts
+        (away,) = totals(r, ((b_own, 0), (b_got, 0), (b_last, 0)))
+        return (a_own, a_got, a_last), to_ctx(away)
 
     low_oth, sum_oth = d_hidden_of(d_oth, w_down, slope_oth)
-    d_linear, unit_sums = attend_back(z_scalar, packed, logs, d_own, d_oth, w_attn, cosine, sine)
+    unit_factors = [(mlp_own, mlp_oth, (low_own, 0), (low_oth, 0)), (d_own, d_oth, (active_own, 0), (active_oth, 0))]
+    unit_far = far_parts(unit_factors)
+    branch_far = to_ctx(fold(cross, branch_keep, branch_got))
+    d_linear, unit_sums = attend_back(z_scalar, packed_qkv, logs, d_own, d_oth, w_attn, cosine, sine)
+    unit_pieces = near_parts(unit_factors, unit_far)
     *g_own, g_keep, g_send, sums = input_grad_of(
         d_linear, low_own, low_oth, w_attn, w_up, (x_own, x_oth), (mean_own, mean_oth), (inv_own, inv_oth), vec
     )
-    g_sum = reduce_tokens(g_own, (g_keep, g_send)).astype(BF)
-
-    down_terms, down_theirs = scatter_rows([(d_own, d_oth, (active_own, 0), (active_oth, 0))])
-    up_terms, up_theirs = scatter_rows([(mlp_own, mlp_oth, (low_own, 0), (low_oth, 0))])
-    attn_terms, attn_theirs = scatter_rows(
-        [
-            (attn_own, attn_oth, (d_linear, 0), (d_linear, 1)),
-            (d_own, d_oth, (context_out, 0), (context_out, 1)),
-        ]
-    )
-
-    out_own = (x_own[:quarter].astype(F32) + branch_sum + (vec[4] + vec[5])).astype(BF)
-    outputs, input_grad = finish(place, out_own, to_ten(out_own), g_sum, to_ten(g_sum), x_own, d_own)
+    g_got = to_ten(g_send)
+    g_near = to_ten(g_own[1])
+    attn_factors = [
+        (attn_own, attn_oth, (d_linear, 0), (d_linear, 1)),
+        (d_own, d_oth, (context_out, 0), (context_out, 1)),
+    ]
+    attn_far = far_parts(attn_factors)
+    unit_pieces = second(unit_pieces)
+    out_bias = (vec[4] + vec[5]).reshape(1, width)
+    (out_own,) = totals(quarter, ((branch_own[0], 0), (branch_near, 0), (branch_far, 0), (x_own, 0), (out_bias, 0)), steps=2)
+    out_other = to_ten(out_own)
+    g_far = to_ctx(fold(cross, g_keep, g_got))
+    attn_pieces = near_parts(attn_factors, attn_far)
 
     d_sum = jnp.sum(d_own[:quarter].astype(F32), 0, keepdims=True)
     sums = unorder(place, jnp.concatenate([sums[:4], d_sum, jnp.zeros((3, width), F32)], 0))
@@ -846,22 +1009,35 @@
     )
     unit_rows = jnp.where(jnp.arange(4)[:, None, None] == ten * 2 + ctx, unit_part[None], 0.0)
     total = jnp.concatenate([sums.reshape(-1), unit_rows.reshape(-1)]).reshape(-1, BLOCK)
-    for move in [to_ten, to_ctx] + [along("shard", shard_count, 1 << k) for k in range(shard_count.bit_length() - 1)]:
-        total = total + move(total)
-    total = total.reshape(-1)
+    moves = [to_ten, to_ctx] + [along("shard", shard_count, 1 << k) for k in range(shard_count.bit_length() - 1)]
+
+    def shared(total, moves):
+        for move in moves:
+            (total,) = totals(total.shape[0], ((total, 0), (move(total), 0)), dtype=F32)
+        return total
+
+    count_value = step_count.astype(F32)
+    fixes = jnp.stack([1.0 - jnp.power(BETA_ONE, count_value), jnp.sqrt(1.0 - jnp.power(BETA_TWO, count_value))])
+    total = shared(total, moves[:1])
+    unit_terms, unit_theirs = third(unit_pieces)
+    attn_pieces = second(attn_pieces)
+    total = shared(total, moves[1:2])
+    (g_sum,) = totals(quarter, ((g_own[0], 0), (g_near, 0), (g_far, 0)), steps=2)
+    g_other = to_ten(g_sum)
+    total = shared(total, moves[2:3])
+    attn_terms, attn_theirs = third(attn_pieces)
+    total = shared(total, moves[3:]).reshape(-1)
     vector_grad = total[: 5 * width].reshape(5, width)
     vector_grad = jnp.concatenate([vector_grad, vector_grad[4:]], 0)
     unit_all = total[8 * width :].reshape(4 * heads, unit_part.shape[1])
     unit_grad = lax.dynamic_slice_in_dim(unit_all, ten * 2 * heads, 2 * heads, 0)
-
-    count_value = step_count.astype(F32)
-    fixes = jnp.stack([1.0 - jnp.power(BETA_ONE, count_value), jnp.sqrt(1.0 - jnp.power(BETA_TWO, count_value))])
+    up_grad, up_new, up_change = adam(ctx_scalar, fixes, up_weight, up_moments, unit_terms, unit_theirs)
+    down_grad, down_new, down_change = adam(ctx_scalar, fixes, down_weight, down_moments, unit_terms, unit_theirs, first=n)
+    outputs, input_grad = finish(place, out_own, out_other, g_sum, g_other, x_own, d_own)
     qkv_grad, qkv_new, qkv_change = adam_heads(ctx_scalar, fixes, qkv_weight, qkv_moments, attn_terms, attn_theirs)
     dense_grad, dense_new, dense_change = adam(
-        ctx_scalar, fixes, dense_weight, dense_moments, attn_terms, attn_theirs, head_cols, n_qkv // head_cols
+        ctx_scalar, fixes, dense_weight, dense_moments, attn_terms, attn_theirs, tile=head_cols, first=n_qkv
     )
-    up_grad, up_new, up_change = adam(ctx_scalar, fixes, up_weight, up_moments, up_terms, up_theirs)
-    down_grad, down_new, down_change = adam(ctx_scalar, fixes, down_weight, down_moments, down_terms, down_theirs)
     unit_new, unit_change = adam_step(unit_vals, unit_moments, unit_grad, count_value, 0.0)
     vector_new, vector_change = adam_step(vectors.astype(F32), vector_moments, vector_grad, count_value, 0.0)
     return (

time: 729 us -> 611 us (0.84)
  waiting for transfers between devices: 357 us -> 195 us
  Pallas kernels: 276 us -> 317 us
  starting transfers between devices: 41.7 us -> 53.6 us
  other arithmetic: 18.9 us -> 10.6 us
    ppermute x53 -> x55, waiting for transfers between devices: 357 us -> 195 us  [along(): return lambda v: lax.ppermute(v, axis, [(i, i ^ bit) for i in range(size)])]
    pallas_call x36 -> x50, Pallas kernels: 276 us -> 317 us  [ordered_call(): *results, token = run(*operands, *waits)]
    ppermute x53 -> x55, starting transfers between devices: 41.7 us -> 53.6 us  [along(): return lambda v: lax.ppermute(v, axis, [(i, i ^ bit) for i in range(size)])]
    convert_element_type x11 -> x0, other arithmetic: 9.36 us -> none  [the longest x6 3.65 us: scatter_rows(): add = lambda u, v: (u.astype(F32) + v.astype(F32)).astype(BF)]
    unnamed x115 -> x123, local copies, waits for them, and re-layouts: 18.3 us -> 17.4 us
  transfers between devices with their start and end apart: 53 -> 55, of which waited for: 23 -> 19; matrix products, arithmetic and copies ran while one was open for 3% -> 3% of each run, Pallas kernels for 30% -> 49%
where the time goes in v2:
time: 611 us; the launch traced here: 602 us
  Pallas kernels  317 us (52%)
  waiting for transfers between devices  195 us (32%)
  starting transfers between devices  53.6 us (9%)
  local copies, waits for them, and re-layouts  23.4 us (4%)
  other arithmetic  10.6 us (2%)
    pallas_call x50, Pallas kernels, ordered_call(): *results, token = run(*operands, *waits)  317 us
    ppermute x55, waiting for transfers between devices, along(): return lambda v: lax.ppermute(v, axis, [(i, i ^ bit) for i in range(size)])  195 us
    ppermute x55, starting transfers between devices, along(): return lambda v: lax.ppermute(v, axis, [(i, i ^ bit) for i in range(size)])  53.6 us
    unnamed x123, local copies, waits for them, and re-layouts  17.4 us
  transfers between devices with their start and end apart: 55, of which 19 were waited for; matrix products, arithmetic and copies ran while one was open for 3% of the time, Pallas kernels for 49%

profile of v2, /device:TPU:0, one launch (start us, length us, event | category | flops | bytes accessed | tf_op | source)
XLA Modules:
  0.0 602.5 jit_solution(4643050273278021927)
XLA Ops:
  14.7 6.1 %arrange.1 = (bf16[512,2048]{1,0:T(8,128)(2,1)}, bf16[512,2048]{1,0:T(8,128)(2,1)}, f32[6,2048]{1,0:T(8,128)}, f32[8,128]{1,0:T(8,128)}) custom-call(s32[33]{0:T(128)} %stack.134.refs_0_, bf16[512,2048]{1,0:T(8,128)(2,1)} %bitcast.102, bf16[512,2048]{1,0:T(8,128)(2,1)} %bitcast.104, bf16[6,2048]{1,0:T(8,128)(2,1)} %refs_3_.7, ...), custom_call_target="tpu_custom_call" | custom-call | flops 49999998976 | bytes 1 | tf_op jit(solution)/shard_map/arrange/pallas_call | solution.py:82
  32.0 12.6 %collective-permute-done.refs_0_.refs_1_ = bf16[128,6144]{1,0:T(8,128)(2,1)} collective-permute-done((bf16[128,6144]{1,0:T(8,128)(2,1)}, bf16[128,6144]{1,0:T(8,128)(2,1)}, u32[]{:S(2)}, u32[]{:S(2)}) %collective-permute-start) | collective-permute-done | bytes 1572896 | tf_op jit(solution)/shard_map/ppermute | solution.py:865
  48.7 10.8 %collective-permute-done.4.refs_4_.refs_0_ = bf16[128,4096]{1,0:T(8,128)(2,1)} collective-permute-done((bf16[128,4096]{1,0:T(8,128)(2,1)}, bf16[128,4096]{1,0:T(8,128)(2,1)}, u32[]{:S(2)}, u32[]{:S(2)}) %collective-permute-start.4) | collective-permute-done | bytes 1048608 | tf_op jit(solution)/shard_map/ppermute | solution.py:865
  68.4 19.0 %collective-permute-done.5.refs_3_.refs_0_ = bf16[128,2048]{1,0:T(8,128)(2,1)S(1)} collective-permute-done((bf16[128,2048]{1,0:T(8,128)(2,1)}, bf16[128,2048]{1,0:T(8,128)(2,1)S(1)}, u32[]{:S(2)}, u32[]{:S(2)}) %collective-permute-start.5) | collective-permute-done | bytes 524320 | tf_op jit(solution)/shard_map/ppermute | solution.py:865
  91.3 14.1 %collective-permute-done.2.refs_3_ = bf16[64,6144]{1,0:T(8,128)(2,1)S(1)} collective-permute-done((bf16[64,6144]{1,0:T(8,128)(2,1)S(1)}, bf16[64,6144]{1,0:T(8,128)(2,1)S(1)}, u32[]{:S(2)}, u32[]{:S(2)}) %collective-permute-start.2) | collective-permute-done | bytes 786464 | tf_op jit(solution)/shard_map/ppermute | solution.py:865
  122.1 6.9 %collective-permute-done.8.refs_3_ = bf16[64,4096]{1,0:T(8,128)(2,1)S(1)} collective-permute-done((bf16[64,4096]{1,0:T(8,128)(2,1)}, bf16[64,4096]{1,0:T(8,128)(2,1)S(1)}, u32[]{:S(2)}, u32[]{:S(2)}) %collective-permute-start.8) | collective-permute-done | bytes 524320 | tf_op jit(solution)/shard_map/ppermute | solution.py:865
  143.5 11.0 %hidden.2 = (bf16[512,2048]{1,0:T(8,128)(2,1)}, f32[512,2048]{1,0:T(8,128)}, f32[8,128]{1,0:T(8,128)}) custom-call(bf16[512,2048]{1,0:T(8,128)(2,1)} %get-tuple-element.172.refs_0_, f32[1,2048]{1,0:T(1,128)} %bitcast.99, bf16[512,2048]{1,0:T(8,128)(2,1)} %get-tuple-element.182.refs_2_.refs_14_, bf16[512,2048]{1,0:T(8,128)(2,1)} %get-tuple-element.189.refs_3_.refs_15_, ...), custom_call_target="tpu_custom_call" | custom-call | flops 49999998976 | bytes 1 | tf_op jit(solution)/shard_map/hidden/pallas_call | solution.py:82
  154.8 5.8 collective-permute-start.15
  169.4 9.8 %d_hidden.2 = (bf16[512,2048]{1,0:T(8,128)(2,1)}, f32[8,2048]{1,0:T(8,128)}, f32[8,128]{1,0:T(8,128)}) custom-call(bf16[512,2048]{1,0:T(8,128)(2,1)} %get-tuple-element.195.refs_0_.refs_4_.refs_3_.refs_6_, f32[512,2048]{1,0:T(8,128)} %get-tuple-element.196.refs_1_, bf16[512,2048]{1,0:T(8,128)(2,1)} %get-tuple-element.197.refs_2_.refs_3_, ...), custom_call_target="tpu_custom_call" | custom-call | flops 49999998976 | bytes 1 | tf_op jit(solution)/shard_map/d_hidden/pallas_call | solution.py:82
  179.2 18.7 %collective-permute-done.15.refs_1_ = bf16[256,2048]{1,0:T(8,128)(2,1)S(1)} collective-permute-done((bf16[256,2048]{1,0:T(8,128)(2,1)}, bf16[256,2048]{1,0:T(8,128)(2,1)S(1)}, u32[]{:S(2)}, u32[]{:S(2)}) %collective-permute-start.15) | collective-permute-done | bytes 1048608 | tf_op jit(solution)/shard_map/ppermute | solution.py:865
  207.1 10.8 %hidden.3 = (bf16[512,2048]{1,0:T(8,128)(2,1)}, f32[512,2048]{1,0:T(8,128)}, f32[8,128]{1,0:T(8,128)}) custom-call(bf16[512,2048]{1,0:T(8,128)(2,1)} %get-tuple-element.207.refs_0_.refs_1_, f32[1,2048]{1,0:T(1,128)} %bitcast.100, bf16[512,2048]{1,0:T(8,128)(2,1)} %get-tuple-element.182.refs_2_.refs_14_, ...), custom_call_target="tpu_custom_call" | custom-call | flops 49999998976 | bytes 1 | tf_op jit(solution)/shard_map/hidden/pallas_call | solution.py:82
  218.0 17.9 %attend.1 = (bf16[1024,512]{1,0:T(8,128)(2,1)}, bf16[1024,1536]{1,0:T(8,128)(2,1)}, f32[1024,256]{1,0:T(8,128)}, f32[8,128]{1,0:T(8,128)}) custom-call(s32[1]{0:T(128)} %bitcast.28.refs_0_, bf16[512,2048]{1,0:T(8,128)(2,1)} %get-tuple-element.210.refs_1_.refs_0_, bf16[512,2048]{1,0:T(8,128)(2,1)} %get-tuple-element.211.refs_2_.refs_1_, f32[1,1536]{1,0:T(1,128)} %bitcast.101, ...), custom_call_target="tpu_custom_call" | custom-call | flops 49999998976 | bytes 1 | tf_op jit(solution)/shard_map/attend/pallas_call | solution.py:82
  235.8 18.6 %branch.1 = (f32[256,2048]{1,0:T(8,128)}, bf16[256,2048]{1,0:T(8,128)(2,1)}, f32[256,2048]{1,0:T(8,128)}, bf16[256,2048]{1,0:T(8,128)(2,1)}, f32[8,128]{1,0:T(8,128)}) custom-call(bf16[512,2048]{1,0:T(8,128)(2,1)} %get-tuple-element.193.refs_0_.refs_6_, bf16[512,2048]{1,0:T(8,128)(2,1)} %get-tuple-element.209.refs_1_.refs_7_, ...), custom_call_target="tpu_custom_call" | custom-call | flops 49999998976 | bytes 1 | tf_op jit(solution)/shard_map/branch/pallas_call | solution.py:82
  260.5 9.8 %d_hidden.3 = (bf16[512,2048]{1,0:T(8,128)(2,1)}, f32[8,2048]{1,0:T(8,128)}, f32[8,128]{1,0:T(8,128)}) custom-call(bf16[512,2048]{1,0:T(8,128)(2,1)} %get-tuple-element.224.refs_0_.refs_5_.refs_4_, f32[512,2048]{1,0:T(8,128)} %get-tuple-element.225.refs_1_, bf16[512,2048]{1,0:T(8,128)(2,1)} %get-tuple-element.197.refs_2_.refs_3_, ...), custom_call_target="tpu_custom_call" | custom-call | flops 20000000000 | bytes 1 | tf_op jit(solution)/shard_map/d_hidden/pallas_call | solution.py:82
  270.3 18.5 %grad_far.2 = (bf16[256,4096]{1,0:T(8,128)(2,1)}, bf16[256,4096]{1,0:T(8,128)(2,1)}, bf16[256,4096]{1,0:T(8,128)(2,1)}, bf16[256,4096]{1,0:T(8,128)(2,1)}, f32[8,128]{1,0:T(8,128)}) custom-call(bf16[512,2048]{1,0:T(8,128)(2,1)} %get-tuple-element.172.refs_0_, bf16[512,2048]{1,0:T(8,128)(2,1)} %get-tuple-element.207.refs_0_.refs_1_, ...), custom_call_target="tpu_custom_call" | custom-call | flops 10000000000 | bytes 1 | tf_op jit(solution)/shard_map/grad_far/pallas_call | solution.py:82
  294.6 14.6 %attend_back.1 = (bf16[1024,1536]{1,0:T(8,128)(2,1)}, f32[8,1536]{1,0:T(8,128)}, f32[8,128]{1,0:T(8,128)}) custom-call(s32[1]{0:T(128)} %bitcast.28.refs_0_, bf16[1024,1536]{1,0:T(8,128)(2,1)} %get-tuple-element.235.refs_1_, f32[1024,256]{1,0:T(8,128)} %get-tuple-element.236.refs_2_, bf16[512,2048]{1,0:T(8,128)(2,1)} %get-tuple-element.195.refs_0_.refs_4_.refs_3_.refs_6_, ...), custom_call_target="tpu_custom_call" | custom-call | flops 49999998976 | bytes 1 | tf_op jit(solution)/shard_map/attend_back/pallas_call | solution.py:82
  310.9 5.4 collective-permute-start.26
  316.3 21.4 %grad_near.2 = (bf16[256,4096]{1,0:T(8,128)(2,1)}, bf16[256,4096]{1,0:T(8,128)(2,1)}, bf16[256,4096]{1,0:T(8,128)(2,1)}, bf16[256,4096]{1,0:T(8,128)(2,1)}, f32[8,128]{1,0:T(8,128)}) custom-call(bf16[512,2048]{1,0:T(8,128)(2,1)} %get-tuple-element.172.refs_0_, bf16[512,2048]{1,0:T(8,128)(2,1)} %get-tuple-element.207.refs_0_.refs_1_, ...), custom_call_target="tpu_custom_call" | custom-call | flops 500000000 | bytes 1 | tf_op jit(solution)/shard_map/grad_near/pallas_call | solution.py:82
  339.9 26.2 %input_grad.1 = (f32[256,2048]{1,0:T(8,128)}, bf16[256,2048]{1,0:T(8,128)(2,1)}, f32[256,2048]{1,0:T(8,128)}, bf16[256,2048]{1,0:T(8,128)(2,1)}, f32[8,2048]{1,0:T(8,128)}, /*index=5*/f32[8,128]{1,0:T(8,128)}) custom-call(bf16[1024,1536]{1,0:T(8,128)(2,1)} %get-tuple-element.243.refs_0_.refs_2_.refs_3_, ...), custom_call_target="tpu_custom_call" | custom-call | flops 49999998976 | bytes 1 | tf_op jit(solution)/shard_map/input_grad/pallas_call | solution.py:82
  367.1 11.0 %grad_far.3 = (bf16[256,2048]{1,0:T(8,128)(2,1)}, bf16[256,2048]{1,0:T(8,128)(2,1)}, bf16[256,2048]{1,0:T(8,128)(2,1)}, bf16[256,2048]{1,0:T(8,128)(2,1)}, f32[8,128]{1,0:T(8,128)}) custom-call(bf16[512,2048]{1,0:T(8,128)(2,1)} %get-tuple-element.210.refs_1_.refs_0_, bf16[512,2048]{1,0:T(8,128)(2,1)} %get-tuple-element.211.refs_2_.refs_1_, ...), custom_call_target="tpu_custom_call" | custom-call | flops 2000000000 | bytes 1 | tf_op jit(solution)/shard_map/grad_far/pallas_call | solution.py:82
  379.3 5.6 collective-permute-done.31.refs_1_
  400.8 12.8 %grad_near.3 = (bf16[256,2048]{1,0:T(8,128)(2,1)}, bf16[256,2048]{1,0:T(8,128)(2,1)}, bf16[256,2048]{1,0:T(8,128)(2,1)}, bf16[256,2048]{1,0:T(8,128)(2,1)}, f32[8,128]{1,0:T(8,128)}) custom-call(bf16[512,2048]{1,0:T(8,128)(2,1)} %get-tuple-element.210.refs_1_.refs_0_, bf16[512,2048]{1,0:T(8,128)(2,1)} %get-tuple-element.211.refs_2_.refs_1_, ...), custom_call_target="tpu_custom_call" | custom-call | flops 49999998976 | bytes 1 | tf_op jit(solution)/shard_map/grad_near/pallas_call | solution.py:82
  430.9 12.0 %collective-permute-done.43.refs_1_ = bf16[256,2048]{1,0:T(8,128)(2,1)S(1)} collective-permute-done((bf16[256,2048]{1,0:T(8,128)(2,1)S(1)}, bf16[256,2048]{1,0:T(8,128)(2,1)S(1)}, u32[]{:S(2)}, u32[]{:S(2)}) %collective-permute-start.43) | collective-permute-done | bytes 1048608 | tf_op jit(solution)/shard_map/ppermute | solution.py:865
  447.4 26.6 %collective-permute-done.42.refs_1_ = f32[240,128]{1,0:T(8,128)S(1)} collective-permute-done((f32[240,128]{1,0:T(8,128)}, f32[240,128]{1,0:T(8,128)S(1)}, u32[]{:S(2)}, u32[]{:S(2)}) %collective-permute-start.42) | collective-permute-done | bytes 122912 | tf_op jit(solution)/shard_map/ppermute | solution.py:865
  483.8 7.3 %collective-permute-done.51.refs_2_ = bf16[128,2048]{1,0:T(8,128)(2,1)S(1)} collective-permute-done((bf16[128,2048]{1,0:T(8,128)(2,1)S(1)}, bf16[128,2048]{1,0:T(8,128)(2,1)S(1)}, u32[]{:S(2)}, u32[]{:S(2)}) %collective-permute-start.51) | collective-permute-done | bytes 524320 | tf_op jit(solution)/shard_map/ppermute | solution.py:865
  511.7 14.4 %collective-permute-done.47.refs_6_ = bf16[128,4096]{1,0:T(8,128)(2,1)} collective-permute-done((bf16[128,4096]{1,0:T(8,128)(2,1)S(1)}, bf16[128,4096]{1,0:T(8,128)(2,1)}, u32[]{:S(2)}, u32[]{:S(2)}) %collective-permute-start.47) | collective-permute-done | bytes 1048608 | tf_op jit(solution)/shard_map/ppermute | solution.py:865
  526.1 23.4 %collective-permute-done.48.refs_7_ = bf16[128,4096]{1,0:T(8,128)(2,1)} collective-permute-done((bf16[128,4096]{1,0:T(8,128)(2,1)}, bf16[128,4096]{1,0:T(8,128)(2,1)}, u32[]{:S(2)}, u32[]{:S(2)}) %collective-permute-start.48) | collective-permute-done | bytes 1048608 | tf_op jit(solution)/shard_map/ppermute | solution.py:865
  549.5 7.3 %adam.3 = (f32[128,4096]{1,0:T(8,128)}, f32[2,128,4096]{2,1,0:T(8,128)}, f32[128,4096]{1,0:T(8,128)}, f32[8,128]{1,0:T(8,128)}) custom-call(s32[1]{0:T(128)} %bitcast.27.refs_0_, f32[2]{0:T(128)} %pad_maximum_fusion.5.refs_1_, bf16[128,4096]{1,0:T(8,128)(2,1)} %refs_2_.10, f32[2,128,4096]{2,1,0:T(8,128)} %refs_3_.8, ...), custom_call_target="tpu_custom_call" | custom-call | flops 5000000000 | bytes 1 | tf_op jit(solution)/shard_map/adam/pallas_call | solution.py:82
  556.8 7.3 %adam.4 = (f32[128,4096]{1,0:T(8,128)}, f32[2,128,4096]{2,1,0:T(8,128)}, f32[128,4096]{1,0:T(8,128)}, f32[8,128]{1,0:T(8,128)}) custom-call(s32[1]{0:T(128)} %bitcast.27.refs_0_, f32[2]{0:T(128)} %pad_maximum_fusion.5.refs_1_, bf16[128,4096]{1,0:T(8,128)(2,1)} %refs_2_.11, f32[2,128,4096]{2,1,0:T(8,128)} %refs_3_.9, ...), custom_call_target="tpu_custom_call" | custom-call | flops 5000000000 | bytes 1 | tf_op jit(solution)/shard_map/adam/pallas_call | solution.py:82
  564.2 16.2 %collective-permute-done.46.refs_4_ = bf16[256,2048]{1,0:T(8,128)(2,1)} collective-permute-done((bf16[256,2048]{1,0:T(8,128)(2,1)}, bf16[256,2048]{1,0:T(8,128)(2,1)}, u32[]{:S(2)}, u32[]{:S(2)}) %collective-permute-start.46) | collective-permute-done | bytes 1048608 | tf_op jit(solution)/shard_map/ppermute | solution.py:865
  580.4 10.6 %finish.1 = (bf16[512,2048]{1,0:T(8,128)(2,1)}, f32[512,2048]{1,0:T(8,128)}, f32[8,128]{1,0:T(8,128)}) custom-call(s32[33]{0:T(128)} %stack.134.refs_0_, bf16[256,2048]{1,0:T(8,128)(2,1)} %get-tuple-element.252.refs_1_, bf16[256,2048]{1,0:T(8,128)(2,1)} %collective-permute-done.33.refs_2_, bf16[256,2048]{1,0:T(8,128)(2,1)} %get-tuple-element.281.refs_3_, ...), custom_call_target="tpu_custom_call" | custom-call | flops 49999998976 | bytes 1 | tf_op jit(solution)/shard_map/finish/pallas_call | solution.py:82
  591.8 7.6 %adam_heads.1 = (f32[128,4,768]{2,1,0:T(4,128)}, f32[2,128,4,768]{3,2,1,0:T(4,128)}, f32[128,4,768]{2,1,0:T(4,128)}, f32[8,128]{1,0:T(8,128)}) custom-call(s32[1]{0:T(128)} %bitcast.27.refs_0_, f32[2]{0:T(128)} %pad_maximum_fusion.5.refs_1_, bf16[128,4,768]{2,1,0:T(4,128)(2,1)} %refs_2_.12, f32[2,128,4,768]{3,2,1,0:T(4,128)} %refs_3_.10, ...), custom_call_target="tpu_custom_call" | custom-call | flops 49999998976 | bytes 1 | tf_op jit(solution)/shard_map/adam_heads/pallas_call | solution.py:82
  (287 shorter events, 180.1 us)
Async XLA Ops:
  7.0 37.7 %collective-permute-start = (bf16[128,6144]{1,0:T(8,128)(2,1)}, bf16[128,6144]{1,0:T(8,128)(2,1)}, u32[]{:S(2)}, u32[]{:S(2)}) collective-permute-start(bf16[128,6144]{1,0:T(8,128)(2,1)} %get-tuple-element.173.refs_0_), channel_id=1, source_target_pairs={{0,16},{4,20},{8,24},{12,28},{16,0},{20,4},{24,8},{28,12},{1,17},{... | collective-permute-start | bytes 4718600 | tf_op jit(solution)/shard_map/ppermute | solution.py:865
  10.0 36.2 %collective-permute-start.1 = (bf16[128,6144]{1,0:T(8,128)(2,1)}, bf16[128,6144]{1,0:T(8,128)(2,1)}, u32[]{:S(2)}, u32[]{:S(2)}) collective-permute-start(bf16[128,6144]{1,0:T(8,128)(2,1)} %get-tuple-element.173.refs_0_), channel_id=1, source_target_pairs={{0,8},{4,12},{8,0},{12,4},{16,24},{20,28},{24,16},{28,20},{1,9},{5... | collective-permute-start | bytes 4718600 | tf_op jit(solution)/shard_map/ppermute | solution.py:865
  11.4 48.0 %collective-permute-start.4 = (bf16[128,4096]{1,0:T(8,128)(2,1)}, bf16[128,4096]{1,0:T(8,128)(2,1)}, u32[]{:S(2)}, u32[]{:S(2)}) collective-permute-start(bf16[128,4096]{1,0:T(8,128)(2,1)} %get-tuple-element.178), channel_id=1, source_target_pairs={{0,2},{2,0},{1,3},{3,1},{4,6},{6,4},{5,7},{7,5},{8,10},{10,8},{9,1... | collective-permute-start | bytes 3145736 | tf_op jit(solution)/shard_map/ppermute | solution.py:865
  64.4 49.1 %collective-permute-start.6 = (bf16[128,4096]{1,0:T(8,128)(2,1)}, bf16[128,4096]{1,0:T(8,128)(2,1)S(1)}, u32[]{:S(2)}, u32[]{:S(2)}) collective-permute-start(bf16[128,4096]{1,0:T(8,128)(2,1)} %collective-permute-done.4.refs_4_.refs_0_), channel_id=1, source_target_pairs={{0,8},{4,12},{8,0},{12,4},{16,24},{20,28},{24,16},{28,20},{1,9},{5... | collective-permute-start | bytes 3145736 | tf_op jit(solution)/shard_map/ppermute | solution.py:865
  64.9 48.5 %collective-permute-start.7 = (bf16[128,4096]{1,0:T(8,128)(2,1)}, bf16[128,4096]{1,0:T(8,128)(2,1)S(1)}, u32[]{:S(2)}, u32[]{:S(2)}) collective-permute-start(bf16[128,4096]{1,0:T(8,128)(2,1)} %collective-permute-done.4.refs_4_.refs_0_), channel_id=1, source_target_pairs={{0,16},{4,20},{8,24},{12,28},{16,0},{20,4},{24,8},{28,12},{1,17},{... | collective-permute-start | bytes 3145736 | tf_op jit(solution)/shard_map/ppermute | solution.py:865
  65.4 40.1 %collective-permute-start.2 = (bf16[64,6144]{1,0:T(8,128)(2,1)S(1)}, bf16[64,6144]{1,0:T(8,128)(2,1)S(1)}, u32[]{:S(2)}, u32[]{:S(2)}) collective-permute-start(bf16[64,6144]{1,0:T(8,128)(2,1)S(1)} %copy-done.39), channel_id=1, source_target_pairs={{0,8},{4,12},{8,0},{12,4},{16,24},{20,28},{24,16},{28,20},{1,9},{5... | collective-permute-start | bytes 2359304 | tf_op jit(solution)/shard_map/ppermute | solution.py:865
  66.9 39.0 %collective-permute-start.3 = (bf16[64,6144]{1,0:T(8,128)(2,1)S(1)}, bf16[64,6144]{1,0:T(8,128)(2,1)S(1)}, u32[]{:S(2)}, u32[]{:S(2)}) collective-permute-start(bf16[64,6144]{1,0:T(8,128)(2,1)S(1)} %copy-done.38), channel_id=1, source_target_pairs={{0,16},{4,20},{8,24},{12,28},{16,0},{20,4},{24,8},{28,12},{1,17},{... | collective-permute-start | bytes 2359304 | tf_op jit(solution)/shard_map/ppermute | solution.py:865
  91.3 63.2 %collective-permute-start.14 = (bf16[256,2048]{1,0:T(8,128)(2,1)}, bf16[256,2048]{1,0:T(8,128)(2,1)}, u32[]{:S(2)}, u32[]{:S(2)}) collective-permute-start(bf16[256,2048]{1,0:T(8,128)(2,1)} %get-tuple-element.194), channel_id=1, source_target_pairs={{0,2},{2,0},{1,3},{3,1},{4,6},{6,4},{5,7},{7,5},{8,10},{10,8},{9,1... | collective-permute-start | bytes 3145736 | tf_op jit(solution)/shard_map/ppermute | solution.py:865
  105.5 27.4 %collective-permute-start.12 = (bf16[128,2048]{1,0:T(8,128)(2,1)}, bf16[128,2048]{1,0:T(8,128)(2,1)S(1)}, u32[]{:S(2)}, u32[]{:S(2)}) collective-permute-start(bf16[128,2048]{1,0:T(8,128)(2,1)} %copy-done.41), channel_id=1, source_target_pairs={{0,16},{4,20},{8,24},{12,28},{16,0},{20,4},{24,8},{28,12},{1,17},{... | collective-permute-start | bytes 1572872 | tf_op jit(solution)/shard_map/ppermute | solution.py:865
  106.0 27.3 %collective-permute-start.13 = (bf16[128,2048]{1,0:T(8,128)(2,1)}, bf16[128,2048]{1,0:T(8,128)(2,1)S(1)}, u32[]{:S(2)}, u32[]{:S(2)}) collective-permute-start(bf16[128,2048]{1,0:T(8,128)(2,1)} %copy-done.41), channel_id=1, source_target_pairs={{0,8},{4,12},{8,0},{12,4},{16,24},{20,28},{24,16},{28,20},{1,9},{5... | collective-permute-start | bytes 1572872 | tf_op jit(solution)/shard_map/ppermute | solution.py:865
  129.0 39.0 %collective-permute-start.16 = (bf16[512,2048]{1,0:T(8,128)(2,1)}, bf16[512,2048]{1,0:T(8,128)(2,1)}, u32[]{:S(2)}, u32[]{:S(2)}) collective-permute-start(bf16[512,2048]{1,0:T(8,128)(2,1)} %get-tuple-element.197.refs_2_.refs_3_), channel_id=1, source_target_pairs={{0,4},{4,0},{8,12},{12,8},{16,20},{20,16},{24,28},{28,24},{1,5},{5... | collective-permute-start | bytes 6291464 | tf_op jit(solution)/shard_map/ppermute | solution.py:865
  132.9 85.0 %collective-permute-start.20 = (bf16[512,2048]{1,0:T(8,128)(2,1)}, bf16[512,2048]{1,0:T(8,128)(2,1)}, u32[]{:S(2)}, u32[]{:S(2)}) collective-permute-start(bf16[512,2048]{1,0:T(8,128)(2,1)} %get-tuple-element.212.refs_6_.refs_7_.refs_10_), channel_id=1, source_target_pairs={{0,4},{4,0},{8,12},{12,8},{16,20},{20,16},{24,28},{28,24},{1,5},{5... | collective-permute-start | bytes 6291464 | tf_op jit(solution)/shard_map/ppermute | solution.py:865
  154.8 43.1 %collective-permute-start.15 = (bf16[256,2048]{1,0:T(8,128)(2,1)}, bf16[256,2048]{1,0:T(8,128)(2,1)S(1)}, u32[]{:S(2)}, u32[]{:S(2)}) collective-permute-start(bf16[256,2048]{1,0:T(8,128)(2,1)} %collective-permute-done.14.refs_3_.refs_0_), channel_id=1, source_target_pairs={{0,1},{1,0},{2,3},{3,2},{4,5},{5,4},{6,7},{7,6},{8,9},{9,8},{10,11... | collective-permute-start | bytes 3145736 | tf_op jit(solution)/shard_map/ppermute | solution.py:865
  167.4 50.5 %collective-permute-start.22 = (bf16[256,2048]{1,0:T(8,128)(2,1)}, bf16[256,2048]{1,0:T(8,128)(2,1)}, u32[]{:S(2)}, u32[]{:S(2)}) collective-permute-start(bf16[256,2048]{1,0:T(8,128)(2,1)} %get-tuple-element.215), channel_id=1, source_target_pairs={{0,2},{2,0},{1,3},{3,1},{4,6},{6,4},{5,7},{7,5},{8,10},{10,8},{9,1... | collective-permute-start | bytes 3145736 | tf_op jit(solution)/shard_map/ppermute | solution.py:865
  168.0 49.9 %collective-permute-start.21 = (bf16[512,2048]{1,0:T(8,128)(2,1)}, bf16[512,2048]{1,0:T(8,128)(2,1)}, u32[]{:S(2)}, u32[]{:S(2)}) collective-permute-start(bf16[512,2048]{1,0:T(8,128)(2,1)} %get-tuple-element.213.refs_7_.refs_8_.refs_11_), channel_id=1, source_target_pairs={{0,4},{4,0},{8,12},{12,8},{16,20},{20,16},{24,28},{28,24},{1,5},{5... | collective-permute-start | bytes 6291464 | tf_op jit(solution)/shard_map/ppermute | solution.py:865
  217.9 38.6 %collective-permute-start.25 = (bf16[256,2048]{1,0:T(8,128)(2,1)}, bf16[256,2048]{1,0:T(8,128)(2,1)S(1)}, u32[]{:S(2)}, u32[]{:S(2)}) collective-permute-start(bf16[256,2048]{1,0:T(8,128)(2,1)} %collective-permute-done.22.refs_11_.refs_0_), channel_id=1, source_target_pairs={{0,1},{1,0},{2,3},{3,2},{4,5},{5,4},{6,7},{7,6},{8,9},{9,8},{10,11... | collective-permute-start | bytes 3145736 | tf_op jit(solution)/shard_map/ppermute | solution.py:865
  254.4 36.3 %collective-permute-start.24 = (bf16[256,2048]{1,0:T(8,128)(2,1)}, bf16[256,2048]{1,0:T(8,128)(2,1)}, u32[]{:S(2)}, u32[]{:S(2)}) collective-permute-start(bf16[256,2048]{1,0:T(8,128)(2,1)} %get-tuple-element.221), channel_id=1, source_target_pairs={{0,1},{1,0},{2,3},{3,2},{4,5},{5,4},{6,7},{7,6},{8,9},{9,8},{10,11... | collective-permute-start | bytes 3145736 | tf_op jit(solution)/shard_map/ppermute | solution.py:865
  288.8 27.5 %collective-permute-start.28 = (bf16[256,4096]{1,0:T(8,128)(2,1)}, bf16[256,4096]{1,0:T(8,128)(2,1)}, u32[]{:S(2)}, u32[]{:S(2)}) collective-permute-start(bf16[256,4096]{1,0:T(8,128)(2,1)} %get-tuple-element.232), channel_id=1, source_target_pairs={{0,4},{4,0},{8,12},{12,8},{16,20},{20,16},{24,28},{28,24},{1,5},{5... | collective-permute-start | bytes 6291464 | tf_op jit(solution)/shard_map/ppermute | solution.py:865
  290.7 88.1 %collective-permute-start.23 = (bf16[256,2048]{1,0:T(8,128)(2,1)S(1)}, bf16[256,2048]{1,0:T(8,128)(2,1)}, u32[]{:S(2)}, u32[]{:S(2)}) collective-permute-start(bf16[256,2048]{1,0:T(8,128)(2,1)S(1)} %copy-done.25), channel_id=1, source_target_pairs={{0,1},{1,0},{2,3},{3,2},{4,5},{5,4},{6,7},{7,6},{8,9},{9,8},{10,11... | collective-permute-start | bytes 3145736 | tf_op jit(solution)/shard_map/ppermute | solution.py:865
  310.9 67.9 %collective-permute-start.26 = (bf16[256,2048]{1,0:T(8,128)(2,1)}, bf16[256,2048]{1,0:T(8,128)(2,1)}, u32[]{:S(2)}, u32[]{:S(2)}) collective-permute-start(bf16[256,2048]{1,0:T(8,128)(2,1)} %get-tuple-element.230), channel_id=1, source_target_pairs={{0,2},{2,0},{1,3},{3,1},{4,6},{6,4},{5,7},{7,5},{8,10},{10,8},{9,1... | collective-permute-start | bytes 3145736 | tf_op jit(solution)/shard_map/ppermute | solution.py:865
  337.7 47.3 %collective-permute-start.31 = (bf16[256,4096]{1,0:T(8,128)(2,1)}, bf16[256,4096]{1,0:T(8,128)(2,1)S(1)}, u32[]{:S(2)}, u32[]{:S(2)}) collective-permute-start(bf16[256,4096]{1,0:T(8,128)(2,1)} %get-tuple-element.240), channel_id=1, source_target_pairs={{0,16},{4,20},{8,24},{12,28},{16,0},{20,4},{24,8},{28,12},{1,17},{... | collective-permute-start | bytes 6291464 | tf_op jit(solution)/shard_map/ppermute | solution.py:865
  338.9 47.0 %collective-permute-start.32 = (bf16[256,4096]{1,0:T(8,128)(2,1)}, bf16[256,4096]{1,0:T(8,128)(2,1)S(1)}, u32[]{:S(2)}, u32[]{:S(2)}) collective-permute-start(bf16[256,4096]{1,0:T(8,128)(2,1)} %get-tuple-element.242), channel_id=1, source_target_pairs={{0,8},{4,12},{8,0},{12,4},{16,24},{20,28},{24,16},{28,20},{1,9},{5... | collective-permute-start | bytes 6291464 | tf_op jit(solution)/shard_map/ppermute | solution.py:865
  366.1 28.6 %collective-permute-start.35 = (bf16[256,2048]{1,0:T(8,128)(2,1)}, bf16[256,2048]{1,0:T(8,128)(2,1)S(1)}, u32[]{:S(2)}, u32[]{:S(2)}) collective-permute-start(bf16[256,2048]{1,0:T(8,128)(2,1)} %get-tuple-element.256), channel_id=1, source_target_pairs={{0,1},{1,0},{2,3},{3,2},{4,5},{5,4},{6,7},{7,6},{8,9},{9,8},{10,11... | collective-permute-start | bytes 3145736 | tf_op jit(solution)/shard_map/ppermute | solution.py:865
  394.7 31.6 %collective-permute-start.45 = (bf16[128,4096]{1,0:T(8,128)(2,1)S(1)}, bf16[128,4096]{1,0:T(8,128)(2,1)S(1)}, u32[]{:S(2)}, u32[]{:S(2)}) collective-permute-start(bf16[128,4096]{1,0:T(8,128)(2,1)S(1)} %copy-done.29), channel_id=1, source_target_pairs={{0,8},{4,12},{8,0},{12,4},{16,24},{20,28},{24,16},{28,20},{1,9},{5... | collective-permute-start | bytes 3145736 | tf_op jit(solution)/shard_map/ppermute | solution.py:865
  417.2 60.2 %collective-permute-start.34 = (bf16[256,2048]{1,0:T(8,128)(2,1)}, bf16[256,2048]{1,0:T(8,128)(2,1)}, u32[]{:S(2)}, u32[]{:S(2)}) collective-permute-start(bf16[256,2048]{1,0:T(8,128)(2,1)} %get-tuple-element.254), channel_id=1, source_target_pairs={{0,1},{1,0},{2,3},{3,2},{4,5},{5,4},{6,7},{7,6},{8,9},{9,8},{10,11... | collective-permute-start | bytes 3145736 | tf_op jit(solution)/shard_map/ppermute | solution.py:865
  423.1 54.3 %collective-permute-start.36 = (bf16[256,2048]{1,0:T(8,128)(2,1)}, bf16[256,2048]{1,0:T(8,128)(2,1)}, u32[]{:S(2)}, u32[]{:S(2)}) collective-permute-start(bf16[256,2048]{1,0:T(8,128)(2,1)} %get-tuple-element.258), channel_id=1, source_target_pairs={{0,2},{2,0},{1,3},{3,1},{4,6},{6,4},{5,7},{7,5},{8,10},{10,8},{9,1... | collective-permute-start | bytes 3145736 | tf_op jit(solution)/shard_map/ppermute | solution.py:865
  426.3 47.8 %collective-permute-start.42 = (f32[240,128]{1,0:T(8,128)}, f32[240,128]{1,0:T(8,128)S(1)}, u32[]{:S(2)}, u32[]{:S(2)}) collective-permute-start(f32[240,128]{1,0:T(8,128)} %get-tuple-element.271.refs_0_), channel_id=1, source_target_pairs={{0,2},{2,0},{1,3},{3,1},{4,6},{6,4},{5,7},{7,5},{8,10},{10,8},{9,1... | collective-permute-start | bytes 368648 | tf_op jit(solution)/shard_map/ppermute | solution.py:865
  500.2 63.9 %collective-permute-start.33 = (bf16[256,2048]{1,0:T(8,128)(2,1)S(1)}, bf16[256,2048]{1,0:T(8,128)(2,1)}, u32[]{:S(2)}, u32[]{:S(2)}) collective-permute-start(bf16[256,2048]{1,0:T(8,128)(2,1)S(1)} %copy-done.22), channel_id=1, source_target_pairs={{0,1},{1,0},{2,3},{3,2},{4,5},{5,4},{6,7},{7,6},{8,9},{9,8},{10,11... | collective-permute-start | bytes 3145736 | tf_op jit(solution)/shard_map/ppermute | solution.py:865
  500.2 49.3 %collective-permute-start.48 = (bf16[128,4096]{1,0:T(8,128)(2,1)}, bf16[128,4096]{1,0:T(8,128)(2,1)}, u32[]{:S(2)}, u32[]{:S(2)}) collective-permute-start(bf16[128,4096]{1,0:T(8,128)(2,1)} %get-tuple-element.283), channel_id=1, source_target_pairs={{0,2},{2,0},{1,3},{3,1},{4,6},{6,4},{5,7},{7,5},{8,10},{10,8},{9,1... | collective-permute-start | bytes 3145736 | tf_op jit(solution)/shard_map/ppermute | solution.py:865
  502.1 78.3 %collective-permute-start.46 = (bf16[256,2048]{1,0:T(8,128)(2,1)}, bf16[256,2048]{1,0:T(8,128)(2,1)}, u32[]{:S(2)}, u32[]{:S(2)}) collective-permute-start(bf16[256,2048]{1,0:T(8,128)(2,1)} %get-tuple-element.281.refs_3_), channel_id=1, source_target_pairs={{0,1},{1,0},{2,3},{3,2},{4,5},{5,4},{6,7},{7,6},{8,9},{9,8},{10,11... | collective-permute-start | bytes 3145736 | tf_op jit(solution)/shard_map/ppermute | solution.py:865
  502.4 88.6 %collective-permute-start.53 = (bf16[128,2048]{1,0:T(8,128)(2,1)S(1)}, bf16[128,2048]{1,0:T(8,128)(2,1)}, u32[]{:S(2)}, u32[]{:S(2)}) collective-permute-start(bf16[128,2048]{1,0:T(8,128)(2,1)S(1)} %copy-done.40), channel_id=1, source_target_pairs={{0,16},{4,20},{8,24},{12,28},{16,0},{20,4},{24,8},{28,12},{1,17},{... | collective-permute-start | bytes 1572872 | tf_op jit(solution)/shard_map/ppermute | solution.py:865
  526.1 64.9 %collective-permute-start.54 = (bf16[128,2048]{1,0:T(8,128)(2,1)}, bf16[128,2048]{1,0:T(8,128)(2,1)S(1)}, u32[]{:S(2)}, u32[]{:S(2)}) collective-permute-start(bf16[128,2048]{1,0:T(8,128)(2,1)} %get-tuple-element.298), channel_id=1, source_target_pairs={{0,2},{2,0},{1,3},{3,1},{4,6},{6,4},{5,7},{7,5},{8,10},{10,8},{9,1... | collective-permute-start | bytes 1572872 | tf_op jit(solution)/shard_map/ppermute | solution.py:865
  (81 other events, 649.0 us)

commit v3 on v2

--- a/solution.py
+++ b/solution.py
@@ -39,7 +39,7 @@
 
 BLOCK = 128
 MIB = 1024 * 1024
-COSTS = [50, 50, 50, 50, 50, 50, 50, 5, 5, 50, 50, 5, 0.5, 50, 50, 2, 50, 50, 50, 50, 50, 50, 50, 0.5, 20, 10, 10, 50, 0.5, 50, 2, 50, 10, 0, 50, 50, 0.5, 50, 50, 50, 50, 0.5, 50, 50, 5, 5, 5, 50, 50, 10, 50, 20, 10, 50, 50, 50, 50, 50, 50, 50, 50, 50, 50, 10]
+COSTS = [50, 50, 50, 50, 50, 10, 0.5, 5, 5, 50, 50, 5, 0.5, 50, 50, 2, 0, 50, 50, 50, 50, 0.5, 50, 0.5, 20, 10, 10, 50, 0.5, 50, 2, 50, 10, 0, 50, 50, 0.5, 50, 50, 50, 50, 0.5, 0, 50, 5, 5, 5, 0, 20, 0.5, 50, 20, 10, 50, 20, 50, 50, 0.5, 0, 50, 50, 50, 50, 10, 50]
 
 
 def whole(shape):
@@ -280,12 +280,12 @@
 
 def norm(x, vec):
     rows, width = x.shape
-    tile = rows // 4
+    tile = rows // 2
     block = pl.BlockSpec((tile, width), lambda i: (i, 0))
     stat = pl.BlockSpec((tile, 128), lambda i: (i, 0))
     return call(
         norm_kernel,
-        (4,),
+        (2,),
         [block, whole(vec.shape)],
         [block, block, stat, stat],
         [like(x.shape, BF), like(x.shape, BF), like((rows, 128), F32), like((rows, 128), F32)],
@@ -306,6 +306,33 @@
     cdf = 0.5 * (1.0 + lax.erf(hidden * ROOT_HALF))
     act_ref[...] = (hidden * cdf).astype(BF)
     slope_ref[...] = cdf + hidden * jnp.exp(-0.5 * hidden * hidden) * (1.0 / ROOT_TWO_PI)
+
+
+def units_kernel(parts, a_ref, d_ref, b_ref, *refs):
+    weights, (act_ref, low_ref, sum_ref) = refs[: 2 * parts], refs[2 * parts :]
+    hidden = over_rows(a_ref[...], weights[:parts]) + b_ref[...]
+    cdf = 0.5 * (1.0 + lax.erf(hidden * ROOT_HALF))
+    act_ref[...] = (hidden * cdf).astype(BF)
+    slope = cdf + hidden * jnp.exp(-0.5 * hidden * hidden) * (1.0 / ROOT_TWO_PI)
+    grad = over_rows(d_ref[...], weights[parts:]) * slope
+    low_ref[...] = grad.astype(BF)
+    sum_ref[...] = jnp.broadcast_to(jnp.sum(grad, 0, keepdims=True), sum_ref.shape)
+
+
+def units_of(a, d, up, down, bias, tile=256):
+    (rows, width), n = a.shape, up[0].shape[1]
+    out = pl.BlockSpec((rows, tile), lambda j: (0, j))
+    at = lambda j: (0, j)
+    return call(
+        functools.partial(units_kernel, len(up)),
+        (n // tile,),
+        [whole(a.shape), whole(d.shape), pl.BlockSpec((1, tile), at), *column_specs((*up, *down), tile, at)],
+        [out, out, pl.BlockSpec((8, tile), at)],
+        [like((rows, n), BF), like((rows, n), BF), like((8, n), F32)],
+        "units",
+        4 * rows * width * n,
+        (a.size * 2 + width * n * 2 + rows * n * 2) * 2,
+    )(a, d, bias, *up, *down)
 
 
 def column_specs(weight, tile, at):
@@ -673,10 +700,10 @@
 
 def fold(cross, keep, got):
     rows, width = keep.shape
-    tile = rows // 4
+    tile = rows // 2
     block = pl.BlockSpec((tile, width), lambda i: (i, 0))
     return call(
-        functools.partial(fold_kernel, cross), (4,), [block, block], block, like(keep.shape, BF), "fold", keep.size, keep.size * 8
+        functools.partial(fold_kernel, cross), (2,), [block, block], block, like(keep.shape, BF), "fold", keep.size, keep.size * 8
     )(keep, got)
 
 
@@ -704,7 +731,7 @@
 
 def finish(place, o0, o1, g0, g1, x, d):
     rows, width = o0.shape
-    per = 4
+    per = 2
     tile = rows // per
     at = 2 * width // BLOCK
     first = pl.BlockSpec((tile, width), lambda i, p: (jnp.minimum(i, per - 1), 0))
@@ -752,7 +779,7 @@
         body(t_ref[...].astype(F32))
 
 
-def adam(ctx, fixes, weight, moments, terms, theirs, tile=1024, first=0):
+def adam(ctx, fixes, weight, moments, terms, theirs, tile=2048, first=0):
     rows, cols = weight.shape
     n = cols // 2
     tile = min(tile, n)
@@ -1002,6 +1029,8 @@
     g_far = to_ctx(fold(cross, g_keep, g_got))
     attn_pieces = near_parts(attn_factors, attn_far)
 
+    unit_terms, unit_theirs = third(unit_pieces)
+
     d_sum = jnp.sum(d_own[:quarter].astype(F32), 0, keepdims=True)
     sums = unorder(place, jnp.concatenate([sums[:4], d_sum, jnp.zeros((3, width), F32)], 0))
     unit_part = jnp.concatenate(
@@ -1018,21 +1047,21 @@
 
     count_value = step_count.astype(F32)
     fixes = jnp.stack([1.0 - jnp.power(BETA_ONE, count_value), jnp.sqrt(1.0 - jnp.power(BETA_TWO, count_value))])
-    total = shared(total, moves[:1])
-    unit_terms, unit_theirs = third(unit_pieces)
     attn_pieces = second(attn_pieces)
-    total = shared(total, moves[1:2])
+    wait(out_other)
     (g_sum,) = totals(quarter, ((g_own[0], 0), (g_near, 0), (g_far, 0)), steps=2)
     g_other = to_ten(g_sum)
-    total = shared(total, moves[2:3])
+    total = shared(total, moves[:1])
     attn_terms, attn_theirs = third(attn_pieces)
-    total = shared(total, moves[3:]).reshape(-1)
+    total = shared(total, moves[1:2])
+    up_grad, up_new, up_change = adam(ctx_scalar, fixes, up_weight, up_moments, unit_terms, unit_theirs)
+    total = shared(total, moves[2:4])
+    down_grad, down_new, down_change = adam(ctx_scalar, fixes, down_weight, down_moments, unit_terms, unit_theirs, first=n)
+    total = shared(total, moves[4:]).reshape(-1)
     vector_grad = total[: 5 * width].reshape(5, width)
     vector_grad = jnp.concatenate([vector_grad, vector_grad[4:]], 0)
     unit_all = total[8 * width :].reshape(4 * heads, unit_part.shape[1])
     unit_grad = lax.dynamic_slice_in_dim(unit_all, ten * 2 * heads, 2 * heads, 0)
-    up_grad, up_new, up_change = adam(ctx_scalar, fixes, up_weight, up_moments, unit_terms, unit_theirs)
-    down_grad, down_new, down_change = adam(ctx_scalar, fixes, down_weight, down_moments, unit_terms, unit_theirs, first=n)
     outputs, input_grad = finish(place, out_own, out_other, g_sum, g_other, x_own, d_own)
     qkv_grad, qkv_new, qkv_change = adam_heads(ctx_scalar, fixes, qkv_weight, qkv_moments, attn_terms, attn_theirs)
     dense_grad, dense_new, dense_change = adam(

time: 611 us -> 576 us (0.943)
  waiting for transfers between devices: 195 us -> 166 us
    ppermute x55, waiting for transfers between devices: 195 us -> 166 us  [along(): return lambda v: lax.ppermute(v, axis, [(i, i ^ bit) for i in range(size)])]
    pallas_call x50, Pallas kernels: 317 us -> 311 us  [ordered_call(): *results, token = run(*operands, *waits)]
    unnamed x123 -> x115, local copies, waits for them, and re-layouts: 17.4 us -> 22.8 us
  transfers between devices with their start and end apart: 55 -> 55, of which waited for: 19 -> 16; matrix products, arithmetic and copies ran while one was open for 3% -> 3% of each run, Pallas kernels for 49% -> 52%
where the time goes in v3:
time: 576 us; the launch traced here: 568 us
  Pallas kernels  311 us (54%)
  waiting for transfers between devices  166 us (29%)
  starting transfers between devices  48.6 us (8%)
  local copies, waits for them, and re-layouts  28.8 us (5%)
  other arithmetic  10.4 us (2%)
    pallas_call x50, Pallas kernels, ordered_call(): *results, token = run(*operands, *waits)  311 us
    ppermute x55, waiting for transfers between devices, along(): return lambda v: lax.ppermute(v, axis, [(i, i ^ bit) for i in range(size)])  166 us
    ppermute x55, starting transfers between devices, along(): return lambda v: lax.ppermute(v, axis, [(i, i ^ bit) for i in range(size)])  48.6 us
    unnamed x115, local copies, waits for them, and re-layouts  22.8 us
  transfers between devices with their start and end apart: 55, of which 16 were waited for; matrix products, arithmetic and copies ran while one was open for 3% of the time, Pallas kernels for 52%

profile of v3, /device:TPU:0, one launch (start us, length us, event | category | flops | bytes accessed | tf_op | source)
XLA Modules:
  0.0 567.5 jit_solution(714140238992905529)
XLA Ops:
  14.7 6.1 %arrange.1 = (bf16[512,2048]{1,0:T(8,128)(2,1)}, bf16[512,2048]{1,0:T(8,128)(2,1)}, f32[6,2048]{1,0:T(8,128)}, f32[8,128]{1,0:T(8,128)}) custom-call(s32[33]{0:T(128)} %stack.134.refs_0_, bf16[512,2048]{1,0:T(8,128)(2,1)} %bitcast.93, bf16[512,2048]{1,0:T(8,128)(2,1)} %bitcast.95, bf16[6,2048]{1,0:T(8,128)(2,1)} %refs_3_.7, f32[8,128]{1,0:T(8,128)} %get-tuple-element.168.refs_4_), custom_call_target="tpu_custom_call" | custom-call | flops 49999998976 | bytes 1 | tf_op jit(solution)/shard_map/arrange/pallas_call | solution.py:82
  20.8 4.8 norm.2
  31.5 13.2 %collective-permute-done.refs_0_.refs_1_ = bf16[128,6144]{1,0:T(8,128)(2,1)} collective-permute-done((bf16[128,6144]{1,0:T(8,128)(2,1)}, bf16[128,6144]{1,0:T(8,128)(2,1)}, u32[]{:S(2)}, u32[]{:S(2)}) %collective-permute-start) | collective-permute-done | bytes 1572896 | tf_op jit(solution)/shard_map/ppermute | solution.py:892
  50.7 8.8 %collective-permute-done.4.refs_4_.refs_0_ = bf16[128,4096]{1,0:T(8,128)(2,1)} collective-permute-done((bf16[128,4096]{1,0:T(8,128)(2,1)}, bf16[128,4096]{1,0:T(8,128)(2,1)}, u32[]{:S(2)}, u32[]{:S(2)}) %collective-permute-start.4) | collective-permute-done | bytes 1048608 | tf_op jit(solution)/shard_map/ppermute | solution.py:892
  65.2 22.1 %collective-permute-done.5.refs_3_.refs_0_ = bf16[128,2048]{1,0:T(8,128)(2,1)S(1)} collective-permute-done((bf16[128,2048]{1,0:T(8,128)(2,1)}, bf16[128,2048]{1,0:T(8,128)(2,1)S(1)}, u32[]{:S(2)}, u32[]{:S(2)}) %collective-permute-start.5) | collective-permute-done | bytes 524320 | tf_op jit(solution)/shard_map/ppermute | solution.py:892
  107.9 6.9 %collective-permute-done.8.refs_3_ = bf16[64,4096]{1,0:T(8,128)(2,1)S(1)} collective-permute-done((bf16[64,4096]{1,0:T(8,128)(2,1)}, bf16[64,4096]{1,0:T(8,128)(2,1)S(1)}, u32[]{:S(2)}, u32[]{:S(2)}) %collective-permute-start.8) | collective-permute-done | bytes 524320 | tf_op jit(solution)/shard_map/ppermute | solution.py:892
  128.3 10.9 %hidden.2 = (bf16[512,2048]{1,0:T(8,128)(2,1)}, f32[512,2048]{1,0:T(8,128)}, f32[8,128]{1,0:T(8,128)}) custom-call(bf16[512,2048]{1,0:T(8,128)(2,1)} %get-tuple-element.172.refs_0_, f32[1,2048]{1,0:T(1,128)} %bitcast.104, bf16[512,2048]{1,0:T(8,128)(2,1)} %get-tuple-element.182.refs_2_.refs_14_, bf16[512,2048]{1,0:T(8,128)(2,1)} %get-tuple-element.189.refs_3_.refs_15_, ...), custom_call_target="tpu_custom_call" | custom-call | flops 49999998976 | bytes 1 | tf_op jit(solution)/shard_map/hidden/pallas_call | solution.py:82
  151.3 9.8 %d_hidden.2 = (bf16[512,2048]{1,0:T(8,128)(2,1)}, f32[8,2048]{1,0:T(8,128)}, f32[8,128]{1,0:T(8,128)}) custom-call(bf16[512,2048]{1,0:T(8,128)(2,1)} %get-tuple-element.195.refs_0_.refs_4_.refs_3_.refs_6_, f32[512,2048]{1,0:T(8,128)} %get-tuple-element.196.refs_1_, bf16[512,2048]{1,0:T(8,128)(2,1)} %get-tuple-element.197.refs_2_.refs_3_, ...), custom_call_target="tpu_custom_call" | custom-call | flops 49999998976 | bytes 1 | tf_op jit(solution)/shard_map/d_hidden/pallas_call | solution.py:82
  161.1 19.3 %collective-permute-done.15.refs_1_ = bf16[256,2048]{1,0:T(8,128)(2,1)S(1)} collective-permute-done((bf16[256,2048]{1,0:T(8,128)(2,1)}, bf16[256,2048]{1,0:T(8,128)(2,1)S(1)}, u32[]{:S(2)}, u32[]{:S(2)}) %collective-permute-start.15) | collective-permute-done | bytes 1048608 | tf_op jit(solution)/shard_map/ppermute | solution.py:892
  184.5 4.6 norm.3
  189.1 10.8 %hidden.3 = (bf16[512,2048]{1,0:T(8,128)(2,1)}, f32[512,2048]{1,0:T(8,128)}, f32[8,128]{1,0:T(8,128)}) custom-call(bf16[512,2048]{1,0:T(8,128)(2,1)} %get-tuple-element.207.refs_0_.refs_1_, f32[1,2048]{1,0:T(1,128)} %bitcast.105, bf16[512,2048]{1,0:T(8,128)(2,1)} %get-tuple-element.182.refs_2_.refs_14_, ...), custom_call_target="tpu_custom_call" | custom-call | flops 49999998976 | bytes 1 | tf_op jit(solution)/shard_map/hidden/pallas_call | solution.py:82
  200.0 17.9 %attend.1 = (bf16[1024,512]{1,0:T(8,128)(2,1)}, bf16[1024,1536]{1,0:T(8,128)(2,1)}, f32[1024,256]{1,0:T(8,128)}, f32[8,128]{1,0:T(8,128)}) custom-call(s32[1]{0:T(128)} %bitcast.28.refs_0_, bf16[512,2048]{1,0:T(8,128)(2,1)} %get-tuple-element.210.refs_1_.refs_0_, bf16[512,2048]{1,0:T(8,128)(2,1)} %get-tuple-element.211.refs_2_.refs_1_, f32[1,1536]{1,0:T(1,128)} %bitcast.102, ...), custom_call_target="tpu_custom_call" | custom-call | flops 500000000 | bytes 1 | tf_op jit(solution)/shard_map/attend/pallas_call | solution.py:82
  217.9 18.6 %branch.1 = (f32[256,2048]{1,0:T(8,128)}, bf16[256,2048]{1,0:T(8,128)(2,1)}, f32[256,2048]{1,0:T(8,128)}, bf16[256,2048]{1,0:T(8,128)(2,1)}, f32[8,128]{1,0:T(8,128)}) custom-call(bf16[512,2048]{1,0:T(8,128)(2,1)} %get-tuple-element.193.refs_0_.refs_6_, bf16[512,2048]{1,0:T(8,128)(2,1)} %get-tuple-element.209.refs_1_.refs_7_, ...), custom_call_target="tpu_custom_call" | custom-call | flops 49999998976 | bytes 1 | tf_op jit(solution)/shard_map/branch/pallas_call | solution.py:82
  242.6 9.8 %d_hidden.3 = (bf16[512,2048]{1,0:T(8,128)(2,1)}, f32[8,2048]{1,0:T(8,128)}, f32[8,128]{1,0:T(8,128)}) custom-call(bf16[512,2048]{1,0:T(8,128)(2,1)} %get-tuple-element.224.refs_0_.refs_5_.refs_4_, f32[512,2048]{1,0:T(8,128)} %get-tuple-element.225.refs_1_, bf16[512,2048]{1,0:T(8,128)(2,1)} %get-tuple-element.197.refs_2_.refs_3_, ...), custom_call_target="tpu_custom_call" | custom-call | flops 20000000000 | bytes 1 | tf_op jit(solution)/shard_map/d_hidden/pallas_call | solution.py:82
  253.3 18.5 %grad_far.2 = (bf16[256,4096]{1,0:T(8,128)(2,1)}, bf16[256,4096]{1,0:T(8,128)(2,1)}, bf16[256,4096]{1,0:T(8,128)(2,1)}, bf16[256,4096]{1,0:T(8,128)(2,1)}, f32[8,128]{1,0:T(8,128)}) custom-call(bf16[512,2048]{1,0:T(8,128)(2,1)} %get-tuple-element.172.refs_0_, bf16[512,2048]{1,0:T(8,128)(2,1)} %get-tuple-element.207.refs_0_.refs_1_, ...), custom_call_target="tpu_custom_call" | custom-call | flops 10000000000 | bytes 1 | tf_op jit(solution)/shard_map/grad_far/pallas_call | solution.py:82
  275.6 14.6 %attend_back.1 = (bf16[1024,1536]{1,0:T(8,128)(2,1)}, f32[8,1536]{1,0:T(8,128)}, f32[8,128]{1,0:T(8,128)}) custom-call(s32[1]{0:T(128)} %bitcast.28.refs_0_, bf16[1024,1536]{1,0:T(8,128)(2,1)} %get-tuple-element.235.refs_1_, f32[1024,256]{1,0:T(8,128)} %get-tuple-element.236.refs_2_, bf16[512,2048]{1,0:T(8,128)(2,1)} %get-tuple-element.195.refs_0_.refs_4_.refs_3_.refs_6_, ...), custom_call_target="tpu_custom_call" | custom-call | flops 49999998976 | bytes 1 | tf_op jit(solution)/shard_map/attend_back/pallas_call | solution.py:82
  296.5 21.4 %grad_near.2 = (bf16[256,4096]{1,0:T(8,128)(2,1)}, bf16[256,4096]{1,0:T(8,128)(2,1)}, bf16[256,4096]{1,0:T(8,128)(2,1)}, bf16[256,4096]{1,0:T(8,128)(2,1)}, f32[8,128]{1,0:T(8,128)}) custom-call(bf16[512,2048]{1,0:T(8,128)(2,1)} %get-tuple-element.172.refs_0_, bf16[512,2048]{1,0:T(8,128)(2,1)} %get-tuple-element.207.refs_0_.refs_1_, ...), custom_call_target="tpu_custom_call" | custom-call | flops 500000000 | bytes 1 | tf_op jit(solution)/shard_map/grad_near/pallas_call | solution.py:82
  319.9 26.3 %input_grad.1 = (f32[256,2048]{1,0:T(8,128)}, bf16[256,2048]{1,0:T(8,128)(2,1)}, f32[256,2048]{1,0:T(8,128)}, bf16[256,2048]{1,0:T(8,128)(2,1)}, f32[8,2048]{1,0:T(8,128)}, /*index=5*/f32[8,128]{1,0:T(8,128)}) custom-call(bf16[1024,1536]{1,0:T(8,128)(2,1)} %get-tuple-element.243.refs_0_.refs_2_.refs_3_, ...), custom_call_target="tpu_custom_call" | custom-call | flops 49999998976 | bytes 1 | tf_op jit(solution)/shard_map/input_grad/pallas_call | solution.py:82
  347.1 11.0 %grad_far.3 = (bf16[256,2048]{1,0:T(8,128)(2,1)}, bf16[256,2048]{1,0:T(8,128)(2,1)}, bf16[256,2048]{1,0:T(8,128)(2,1)}, bf16[256,2048]{1,0:T(8,128)(2,1)}, f32[8,128]{1,0:T(8,128)}) custom-call(bf16[512,2048]{1,0:T(8,128)(2,1)} %get-tuple-element.210.refs_1_.refs_0_, bf16[512,2048]{1,0:T(8,128)(2,1)} %get-tuple-element.211.refs_2_.refs_1_, ...), custom_call_target="tpu_custom_call" | custom-call | flops 2000000000 | bytes 1 | tf_op jit(solution)/shard_map/grad_far/pallas_call | solution.py:82
  359.4 5.7 %collective-permute-done.31.refs_1_ = bf16[256,4096]{1,0:T(8,128)(2,1)S(1)} collective-permute-done((bf16[256,4096]{1,0:T(8,128)(2,1)}, bf16[256,4096]{1,0:T(8,128)(2,1)S(1)}, u32[]{:S(2)}, u32[]{:S(2)}) %collective-permute-start.31) | collective-permute-done | bytes 2097184 | tf_op jit(solution)/shard_map/ppermute | solution.py:892
  380.7 12.9 %grad_near.3 = (bf16[256,2048]{1,0:T(8,128)(2,1)}, bf16[256,2048]{1,0:T(8,128)(2,1)}, bf16[256,2048]{1,0:T(8,128)(2,1)}, bf16[256,2048]{1,0:T(8,128)(2,1)}, f32[8,128]{1,0:T(8,128)}) custom-call(bf16[512,2048]{1,0:T(8,128)(2,1)} %get-tuple-element.210.refs_1_.refs_0_, bf16[512,2048]{1,0:T(8,128)(2,1)} %get-tuple-element.211.refs_2_.refs_1_, ...), custom_call_target="tpu_custom_call" | custom-call | flops 49999998976 | bytes 1 | tf_op jit(solution)/shard_map/grad_near/pallas_call | solution.py:82
  396.9 7.6 %collective-permute-done.43.refs_2_ = bf16[128,4096]{1,0:T(8,128)(2,1)} collective-permute-done((bf16[128,4096]{1,0:T(8,128)(2,1)S(1)}, bf16[128,4096]{1,0:T(8,128)(2,1)}, u32[]{:S(2)}, u32[]{:S(2)}) %collective-permute-start.43) | collective-permute-done | bytes 1048608 | tf_op jit(solution)/shard_map/ppermute | solution.py:892
  411.8 6.7 %collective-permute-done.41.refs_1_ = bf16[256,2048]{1,0:T(8,128)(2,1)S(1)} collective-permute-done((bf16[256,2048]{1,0:T(8,128)(2,1)}, bf16[256,2048]{1,0:T(8,128)(2,1)S(1)}, u32[]{:S(2)}, u32[]{:S(2)}) %collective-permute-start.41) | collective-permute-done | bytes 1048608 | tf_op jit(solution)/shard_map/ppermute | solution.py:892
  419.1 6.5 %collective-permute-done.42.refs_3_.refs_5_ = bf16[256,2048]{1,0:T(8,128)(2,1)S(1)} collective-permute-done((bf16[256,2048]{1,0:T(8,128)(2,1)}, bf16[256,2048]{1,0:T(8,128)(2,1)S(1)}, u32[]{:S(2)}, u32[]{:S(2)}) %collective-permute-start.42) | collective-permute-done | bytes 1048608 | tf_op jit(solution)/shard_map/ppermute | solution.py:892
  430.7 11.7 %collective-permute-done.36.refs_2_ = bf16[256,2048]{1,0:T(8,128)(2,1)S(1)} collective-permute-done((bf16[256,2048]{1,0:T(8,128)(2,1)S(1)}, bf16[256,2048]{1,0:T(8,128)(2,1)S(1)}, u32[]{:S(2)}, u32[]{:S(2)}) %collective-permute-start.36) | collective-permute-done | bytes 1048608 | tf_op jit(solution)/shard_map/ppermute | solution.py:892
  442.5 9.7 %collective-permute-done.33.refs_4_.refs_2_ = bf16[256,2048]{1,0:T(8,128)(2,1)S(1)} collective-permute-done((bf16[256,2048]{1,0:T(8,128)(2,1)S(1)}, bf16[256,2048]{1,0:T(8,128)(2,1)S(1)}, u32[]{:S(2)}, u32[]{:S(2)}) %collective-permute-start.33) | collective-permute-done | bytes 1048608 | tf_op jit(solution)/shard_map/ppermute | solution.py:892
  461.6 32.5 %collective-permute-done.46.refs_1_ = f32[240,128]{1,0:T(8,128)S(1)} collective-permute-done((f32[240,128]{1,0:T(8,128)}, f32[240,128]{1,0:T(8,128)S(1)}, u32[]{:S(2)}, u32[]{:S(2)}) %collective-permute-start.46) | collective-permute-done | bytes 122912 | tf_op jit(solution)/shard_map/ppermute | solution.py:892
  497.8 6.7 %adam.3 = (f32[128,4096]{1,0:T(8,128)}, f32[2,128,4096]{2,1,0:T(8,128)}, f32[128,4096]{1,0:T(8,128)}, f32[8,128]{1,0:T(8,128)}) custom-call(s32[1]{0:T(128)} %bitcast.27.refs_0_, f32[2]{0:T(128)} %pad_maximum_fusion.5.refs_1_, bf16[128,4096]{1,0:T(8,128)(2,1)} %refs_2_.10, f32[2,128,4096]{2,1,0:T(8,128)} %refs_3_.8, ...), custom_call_target="tpu_custom_call" | custom-call | bytes 1 | tf_op jit(solution)/shard_map/adam/pallas_call | solution.py:82
  517.4 6.7 %adam.4 = (f32[128,4096]{1,0:T(8,128)}, f32[2,128,4096]{2,1,0:T(8,128)}, f32[128,4096]{1,0:T(8,128)}, f32[8,128]{1,0:T(8,128)}) custom-call(s32[1]{0:T(128)} %bitcast.27.refs_0_, f32[2]{0:T(128)} %pad_maximum_fusion.5.refs_1_, bf16[128,4096]{1,0:T(8,128)(2,1)} %refs_2_.11, f32[2,128,4096]{2,1,0:T(8,128)} %refs_3_.9, ...), custom_call_target="tpu_custom_call" | custom-call | flops 5000000000 | bytes 1 | tf_op jit(solution)/shard_map/adam/pallas_call | solution.py:82
  533.3 11.8 %collective-permute-done.44.refs_4_ = bf16[256,2048]{1,0:T(8,128)(2,1)S(1)} collective-permute-done((bf16[256,2048]{1,0:T(8,128)(2,1)S(1)}, bf16[256,2048]{1,0:T(8,128)(2,1)S(1)}, u32[]{:S(2)}, u32[]{:S(2)}) %collective-permute-start.44) | collective-permute-done | bytes 1048608 | tf_op jit(solution)/shard_map/ppermute | solution.py:892
  546.1 9.1 %finish.1 = (bf16[512,2048]{1,0:T(8,128)(2,1)}, f32[512,2048]{1,0:T(8,128)}, f32[8,128]{1,0:T(8,128)}) custom-call(s32[33]{0:T(128)} %stack.134.refs_0_, bf16[256,2048]{1,0:T(8,128)(2,1)} %get-tuple-element.252.refs_1_, bf16[256,2048]{1,0:T(8,128)(2,1)} %copy-done.7, bf16[256,2048]{1,0:T(8,128)(2,1)} %get-tuple-element.274.refs_3_, ...), custom_call_target="tpu_custom_call" | custom-call | bytes 1 | tf_op jit(solution)/shard_map/finish/pallas_call | solution.py:82
  556.9 7.6 %adam_heads.1 = (f32[128,4,768]{2,1,0:T(4,128)}, f32[2,128,4,768]{3,2,1,0:T(4,128)}, f32[128,4,768]{2,1,0:T(4,128)}, f32[8,128]{1,0:T(8,128)}) custom-call(s32[1]{0:T(128)} %bitcast.27.refs_0_, f32[2]{0:T(128)} %pad_maximum_fusion.5.refs_1_, bf16[128,4,768]{2,1,0:T(4,128)(2,1)} %refs_2_.12, f32[2,128,4,768]{3,2,1,0:T(4,128)} %refs_3_.10, ...), custom_call_target="tpu_custom_call" | custom-call | flops 20000000000 | bytes 1 | tf_op jit(solution)/shard_map/adam_heads/pallas_call | solution.py:82
  (279 shorter events, 175.0 us)
Async XLA Ops:
  7.0 37.7 %collective-permute-start = (bf16[128,6144]{1,0:T(8,128)(2,1)}, bf16[128,6144]{1,0:T(8,128)(2,1)}, u32[]{:S(2)}, u32[]{:S(2)}) collective-permute-start(bf16[128,6144]{1,0:T(8,128)(2,1)} %get-tuple-element.173.refs_0_), channel_id=1, source_target_pairs={{0,16},{4,20},{8,24},{12,28},{16,0},{20,4},{24,8},{28,12},{1,17},{... | collective-permute-start | bytes 4718600 | tf_op jit(solution)/shard_map/ppermute | solution.py:892
  10.0 36.2 %collective-permute-start.1 = (bf16[128,6144]{1,0:T(8,128)(2,1)}, bf16[128,6144]{1,0:T(8,128)(2,1)}, u32[]{:S(2)}, u32[]{:S(2)}) collective-permute-start(bf16[128,6144]{1,0:T(8,128)(2,1)} %get-tuple-element.173.refs_0_), channel_id=1, source_target_pairs={{0,8},{4,12},{8,0},{12,4},{16,24},{20,28},{24,16},{28,20},{1,9},{5... | collective-permute-start | bytes 4718600 | tf_op jit(solution)/shard_map/ppermute | solution.py:892
  11.4 48.0 %collective-permute-start.4 = (bf16[128,4096]{1,0:T(8,128)(2,1)}, bf16[128,4096]{1,0:T(8,128)(2,1)}, u32[]{:S(2)}, u32[]{:S(2)}) collective-permute-start(bf16[128,4096]{1,0:T(8,128)(2,1)} %get-tuple-element.178), channel_id=1, source_target_pairs={{0,2},{2,0},{1,3},{3,1},{4,6},{6,4},{5,7},{7,5},{8,10},{10,8},{9,1... | collective-permute-start | bytes 3145736 | tf_op jit(solution)/shard_map/ppermute | solution.py:892
  48.7 42.5 %collective-permute-start.2 = (bf16[64,6144]{1,0:T(8,128)(2,1)}, bf16[64,6144]{1,0:T(8,128)(2,1)S(1)}, u32[]{:S(2)}, u32[]{:S(2)}) collective-permute-start(bf16[64,6144]{1,0:T(8,128)(2,1)} %get-tuple-element.175), channel_id=1, source_target_pairs={{0,8},{4,12},{8,0},{12,4},{16,24},{20,28},{24,16},{28,20},{1,9},{5... | collective-permute-start | bytes 2359304 | tf_op jit(solution)/shard_map/ppermute | solution.py:892
  50.2 41.6 %collective-permute-start.3 = (bf16[64,6144]{1,0:T(8,128)(2,1)}, bf16[64,6144]{1,0:T(8,128)(2,1)S(1)}, u32[]{:S(2)}, u32[]{:S(2)}) collective-permute-start(bf16[64,6144]{1,0:T(8,128)(2,1)} %get-tuple-element.176), channel_id=1, source_target_pairs={{0,16},{4,20},{8,24},{12,28},{16,0},{20,4},{24,8},{28,12},{1,17},{... | collective-permute-start | bytes 2359304 | tf_op jit(solution)/shard_map/ppermute | solution.py:892
  63.7 34.9 %collective-permute-start.6 = (bf16[128,4096]{1,0:T(8,128)(2,1)}, bf16[128,4096]{1,0:T(8,128)(2,1)S(1)}, u32[]{:S(2)}, u32[]{:S(2)}) collective-permute-start(bf16[128,4096]{1,0:T(8,128)(2,1)} %collective-permute-done.4.refs_4_.refs_0_), channel_id=1, source_target_pairs={{0,8},{4,12},{8,0},{12,4},{16,24},{20,28},{24,16},{28,20},{1,9},{5... | collective-permute-start | bytes 3145736 | tf_op jit(solution)/shard_map/ppermute | solution.py:892
  64.2 34.4 %collective-permute-start.7 = (bf16[128,4096]{1,0:T(8,128)(2,1)}, bf16[128,4096]{1,0:T(8,128)(2,1)S(1)}, u32[]{:S(2)}, u32[]{:S(2)}) collective-permute-start(bf16[128,4096]{1,0:T(8,128)(2,1)} %collective-permute-done.4.refs_4_.refs_0_), channel_id=1, source_target_pairs={{0,16},{4,20},{8,24},{12,28},{16,0},{20,4},{24,8},{28,12},{1,17},{... | collective-permute-start | bytes 3145736 | tf_op jit(solution)/shard_map/ppermute | solution.py:892
  91.2 48.0 %collective-permute-start.14 = (bf16[256,2048]{1,0:T(8,128)(2,1)}, bf16[256,2048]{1,0:T(8,128)(2,1)}, u32[]{:S(2)}, u32[]{:S(2)}) collective-permute-start(bf16[256,2048]{1,0:T(8,128)(2,1)} %get-tuple-element.194), channel_id=1, source_target_pairs={{0,2},{2,0},{1,3},{3,1},{4,6},{6,4},{5,7},{7,5},{8,10},{10,8},{9,1... | collective-permute-start | bytes 3145736 | tf_op jit(solution)/shard_map/ppermute | solution.py:892
  114.8 35.1 %collective-permute-start.16 = (bf16[512,2048]{1,0:T(8,128)(2,1)}, bf16[512,2048]{1,0:T(8,128)(2,1)}, u32[]{:S(2)}, u32[]{:S(2)}) collective-permute-start(bf16[512,2048]{1,0:T(8,128)(2,1)} %get-tuple-element.197.refs_2_.refs_3_), channel_id=1, source_target_pairs={{0,4},{4,0},{8,12},{12,8},{16,20},{20,16},{24,28},{28,24},{1,5},{5... | collective-permute-start | bytes 6291464 | tf_op jit(solution)/shard_map/ppermute | solution.py:892
  139.2 60.8 %collective-permute-start.20 = (bf16[512,2048]{1,0:T(8,128)(2,1)}, bf16[512,2048]{1,0:T(8,128)(2,1)}, u32[]{:S(2)}, u32[]{:S(2)}) collective-permute-start(bf16[512,2048]{1,0:T(8,128)(2,1)} %get-tuple-element.212.refs_6_.refs_7_.refs_10_), channel_id=1, source_target_pairs={{0,4},{4,0},{8,12},{12,8},{16,20},{20,16},{24,28},{28,24},{1,5},{5... | collective-permute-start | bytes 6291464 | tf_op jit(solution)/shard_map/ppermute | solution.py:892
  139.3 41.1 %collective-permute-start.15 = (bf16[256,2048]{1,0:T(8,128)(2,1)}, bf16[256,2048]{1,0:T(8,128)(2,1)S(1)}, u32[]{:S(2)}, u32[]{:S(2)}) collective-permute-start(bf16[256,2048]{1,0:T(8,128)(2,1)} %collective-permute-done.14.refs_3_.refs_0_), channel_id=1, source_target_pairs={{0,1},{1,0},{2,3},{3,2},{4,5},{5,4},{6,7},{7,6},{8,9},{9,8},{10,11... | collective-permute-start | bytes 3145736 | tf_op jit(solution)/shard_map/ppermute | solution.py:892
  149.6 50.3 %collective-permute-start.22 = (bf16[256,2048]{1,0:T(8,128)(2,1)}, bf16[256,2048]{1,0:T(8,128)(2,1)}, u32[]{:S(2)}, u32[]{:S(2)}) collective-permute-start(bf16[256,2048]{1,0:T(8,128)(2,1)} %get-tuple-element.215), channel_id=1, source_target_pairs={{0,2},{2,0},{1,3},{3,1},{4,6},{6,4},{5,7},{7,5},{8,10},{10,8},{9,1... | collective-permute-start | bytes 3145736 | tf_op jit(solution)/shard_map/ppermute | solution.py:892
  149.9 50.0 %collective-permute-start.21 = (bf16[512,2048]{1,0:T(8,128)(2,1)}, bf16[512,2048]{1,0:T(8,128)(2,1)}, u32[]{:S(2)}, u32[]{:S(2)}) collective-permute-start(bf16[512,2048]{1,0:T(8,128)(2,1)} %get-tuple-element.213.refs_7_.refs_8_.refs_11_), channel_id=1, source_target_pairs={{0,4},{4,0},{8,12},{12,8},{16,20},{20,16},{24,28},{28,24},{1,5},{5... | collective-permute-start | bytes 6291464 | tf_op jit(solution)/shard_map/ppermute | solution.py:892
  199.9 38.7 %collective-permute-start.25 = (bf16[256,2048]{1,0:T(8,128)(2,1)}, bf16[256,2048]{1,0:T(8,128)(2,1)S(1)}, u32[]{:S(2)}, u32[]{:S(2)}) collective-permute-start(bf16[256,2048]{1,0:T(8,128)(2,1)} %collective-permute-done.22.refs_11_.refs_0_), channel_id=1, source_target_pairs={{0,1},{1,0},{2,3},{3,2},{4,5},{5,4},{6,7},{7,6},{8,9},{9,8},{10,11... | collective-permute-start | bytes 3145736 | tf_op jit(solution)/shard_map/ppermute | solution.py:892
  236.5 36.3 %collective-permute-start.24 = (bf16[256,2048]{1,0:T(8,128)(2,1)}, bf16[256,2048]{1,0:T(8,128)(2,1)}, u32[]{:S(2)}, u32[]{:S(2)}) collective-permute-start(bf16[256,2048]{1,0:T(8,128)(2,1)} %get-tuple-element.221), channel_id=1, source_target_pairs={{0,1},{1,0},{2,3},{3,2},{4,5},{5,4},{6,7},{7,6},{8,9},{9,8},{10,11... | collective-permute-start | bytes 3145736 | tf_op jit(solution)/shard_map/ppermute | solution.py:892
  272.8 86.1 %collective-permute-start.23 = (bf16[256,2048]{1,0:T(8,128)(2,1)S(1)}, bf16[256,2048]{1,0:T(8,128)(2,1)}, u32[]{:S(2)}, u32[]{:S(2)}) collective-permute-start(bf16[256,2048]{1,0:T(8,128)(2,1)S(1)} %copy-done.29), channel_id=1, source_target_pairs={{0,1},{1,0},{2,3},{3,2},{4,5},{5,4},{6,7},{7,6},{8,9},{9,8},{10,11... | collective-permute-start | bytes 3145736 | tf_op jit(solution)/shard_map/ppermute | solution.py:892
  291.8 67.0 %collective-permute-start.26 = (bf16[256,2048]{1,0:T(8,128)(2,1)}, bf16[256,2048]{1,0:T(8,128)(2,1)}, u32[]{:S(2)}, u32[]{:S(2)}) collective-permute-start(bf16[256,2048]{1,0:T(8,128)(2,1)} %get-tuple-element.230), channel_id=1, source_target_pairs={{0,2},{2,0},{1,3},{3,1},{4,6},{6,4},{5,7},{7,5},{8,10},{10,8},{9,1... | collective-permute-start | bytes 3145736 | tf_op jit(solution)/shard_map/ppermute | solution.py:892
  317.8 47.3 %collective-permute-start.31 = (bf16[256,4096]{1,0:T(8,128)(2,1)}, bf16[256,4096]{1,0:T(8,128)(2,1)S(1)}, u32[]{:S(2)}, u32[]{:S(2)}) collective-permute-start(bf16[256,4096]{1,0:T(8,128)(2,1)} %get-tuple-element.240), channel_id=1, source_target_pairs={{0,16},{4,20},{8,24},{12,28},{16,0},{20,4},{24,8},{28,12},{1,17},{... | collective-permute-start | bytes 6291464 | tf_op jit(solution)/shard_map/ppermute | solution.py:892
  318.4 47.0 %collective-permute-start.32 = (bf16[256,4096]{1,0:T(8,128)(2,1)}, bf16[256,4096]{1,0:T(8,128)(2,1)S(1)}, u32[]{:S(2)}, u32[]{:S(2)}) collective-permute-start(bf16[256,4096]{1,0:T(8,128)(2,1)} %get-tuple-element.242), channel_id=1, source_target_pairs={{0,8},{4,12},{8,0},{12,4},{16,24},{20,28},{24,16},{28,20},{1,9},{5... | collective-permute-start | bytes 6291464 | tf_op jit(solution)/shard_map/ppermute | solution.py:892
  346.2 28.3 %collective-permute-start.35 = (bf16[256,2048]{1,0:T(8,128)(2,1)}, bf16[256,2048]{1,0:T(8,128)(2,1)S(1)}, u32[]{:S(2)}, u32[]{:S(2)}) collective-permute-start(bf16[256,2048]{1,0:T(8,128)(2,1)} %get-tuple-element.256), channel_id=1, source_target_pairs={{0,1},{1,0},{2,3},{3,2},{4,5},{5,4},{6,7},{7,6},{8,9},{9,8},{10,11... | collective-permute-start | bytes 3145736 | tf_op jit(solution)/shard_map/ppermute | solution.py:892
  374.5 54.7 %collective-permute-start.34 = (bf16[256,2048]{1,0:T(8,128)(2,1)}, bf16[256,2048]{1,0:T(8,128)(2,1)}, u32[]{:S(2)}, u32[]{:S(2)}) collective-permute-start(bf16[256,2048]{1,0:T(8,128)(2,1)} %get-tuple-element.254), channel_id=1, source_target_pairs={{0,1},{1,0},{2,3},{3,2},{4,5},{5,4},{6,7},{7,6},{8,9},{9,8},{10,11... | collective-permute-start | bytes 3145736 | tf_op jit(solution)/shard_map/ppermute | solution.py:892
  394.8 30.9 %collective-permute-start.42 = (bf16[256,2048]{1,0:T(8,128)(2,1)}, bf16[256,2048]{1,0:T(8,128)(2,1)S(1)}, u32[]{:S(2)}, u32[]{:S(2)}) collective-permute-start(bf16[256,2048]{1,0:T(8,128)(2,1)} %get-tuple-element.267), channel_id=1, source_target_pairs={{0,8},{4,12},{8,0},{12,4},{16,24},{20,28},{24,16},{28,20},{1,9},{5... | collective-permute-start | bytes 3145736 | tf_op jit(solution)/shard_map/ppermute | solution.py:892
  395.3 47.1 %collective-permute-start.36 = (bf16[256,2048]{1,0:T(8,128)(2,1)S(1)}, bf16[256,2048]{1,0:T(8,128)(2,1)S(1)}, u32[]{:S(2)}, u32[]{:S(2)}) collective-permute-start(bf16[256,2048]{1,0:T(8,128)(2,1)S(1)} %copy-done.32), channel_id=1, source_target_pairs={{0,2},{2,0},{1,3},{3,1},{4,6},{6,4},{5,7},{7,5},{8,10},{10,8},{9,1... | collective-permute-start | bytes 3145736 | tf_op jit(solution)/shard_map/ppermute | solution.py:892
  404.4 47.7 %collective-permute-start.33 = (bf16[256,2048]{1,0:T(8,128)(2,1)S(1)}, bf16[256,2048]{1,0:T(8,128)(2,1)S(1)}, u32[]{:S(2)}, u32[]{:S(2)}) collective-permute-start(bf16[256,2048]{1,0:T(8,128)(2,1)S(1)} %copy-done.6), channel_id=1, source_target_pairs={{0,1},{1,0},{2,3},{3,2},{4,5},{5,4},{6,7},{7,6},{8,9},{9,8},{10,11... | collective-permute-start | bytes 3145736 | tf_op jit(solution)/shard_map/ppermute | solution.py:892
  418.5 79.3 %collective-permute-start.49 = (bf16[128,4096]{1,0:T(8,128)(2,1)}, bf16[128,4096]{1,0:T(8,128)(2,1)}, u32[]{:S(2)}, u32[]{:S(2)}) collective-permute-start(bf16[128,4096]{1,0:T(8,128)(2,1)} %get-tuple-element.285), channel_id=1, source_target_pairs={{0,16},{4,20},{8,24},{12,28},{16,0},{20,4},{24,8},{28,12},{1,17},{... | collective-permute-start | bytes 3145736 | tf_op jit(solution)/shard_map/ppermute | solution.py:892
  425.6 30.6 %collective-permute-start.45 = (f32[240,128]{1,0:T(8,128)S(1)}, f32[240,128]{1,0:T(8,128)S(1)}, u32[]{:S(2)}, u32[]{:S(2)}) collective-permute-start(f32[240,128]{1,0:T(8,128)S(1)} %maximum_bitcast_fusion.refs_0_), channel_id=1, source_target_pairs={{0,1},{1,0},{2,3},{3,2},{4,5},{5,4},{6,7},{7,6},{8,9},{9,8},{10,11... | collective-permute-start | bytes 368648 | tf_op jit(solution)/shard_map/ppermute | solution.py:892
  429.2 29.3 %collective-permute-start.47 = (bf16[128,2048]{1,0:T(8,128)(2,1)}, bf16[128,2048]{1,0:T(8,128)(2,1)S(1)}, u32[]{:S(2)}, u32[]{:S(2)}) collective-permute-start(bf16[128,2048]{1,0:T(8,128)(2,1)} %get-tuple-element.281), channel_id=1, source_target_pairs={{0,8},{4,12},{8,0},{12,4},{16,24},{20,28},{24,16},{28,20},{1,9},{5... | collective-permute-start | bytes 1572872 | tf_op jit(solution)/shard_map/ppermute | solution.py:892
  442.5 55.4 %collective-permute-start.50 = (bf16[128,4096]{1,0:T(8,128)(2,1)}, bf16[128,4096]{1,0:T(8,128)(2,1)}, u32[]{:S(2)}, u32[]{:S(2)}) collective-permute-start(bf16[128,4096]{1,0:T(8,128)(2,1)} %get-tuple-element.286), channel_id=1, source_target_pairs={{0,2},{2,0},{1,3},{3,1},{4,6},{6,4},{5,7},{7,5},{8,10},{10,8},{9,1... | collective-permute-start | bytes 3145736 | tf_op jit(solution)/shard_map/ppermute | solution.py:892
  458.5 35.7 %collective-permute-start.46 = (f32[240,128]{1,0:T(8,128)}, f32[240,128]{1,0:T(8,128)S(1)}, u32[]{:S(2)}, u32[]{:S(2)}) collective-permute-start(f32[240,128]{1,0:T(8,128)} %get-tuple-element.280.refs_0_), channel_id=1, source_target_pairs={{0,2},{2,0},{1,3},{3,1},{4,6},{6,4},{5,7},{7,5},{8,10},{10,8},{9,1... | collective-permute-start | bytes 368648 | tf_op jit(solution)/shard_map/ppermute | solution.py:892
  508.5 36.6 %collective-permute-start.44 = (bf16[256,2048]{1,0:T(8,128)(2,1)S(1)}, bf16[256,2048]{1,0:T(8,128)(2,1)S(1)}, u32[]{:S(2)}, u32[]{:S(2)}) collective-permute-start(bf16[256,2048]{1,0:T(8,128)(2,1)S(1)} %copy-done.8), channel_id=1, source_target_pairs={{0,1},{1,0},{2,3},{3,2},{4,5},{5,4},{6,7},{7,6},{8,9},{9,8},{10,11... | collective-permute-start | bytes 3145736 | tf_op jit(solution)/shard_map/ppermute | solution.py:892
  508.6 47.3 %collective-permute-start.53 = (bf16[128,2048]{1,0:T(8,128)(2,1)}, bf16[128,2048]{1,0:T(8,128)(2,1)S(1)}, u32[]{:S(2)}, u32[]{:S(2)}) collective-permute-start(bf16[128,2048]{1,0:T(8,128)(2,1)} %get-tuple-element.297), channel_id=1, source_target_pairs={{0,16},{4,20},{8,24},{12,28},{16,0},{20,4},{24,8},{28,12},{1,17},{... | collective-permute-start | bytes 1572872 | tf_op jit(solution)/shard_map/ppermute | solution.py:892
  510.8 45.1 %collective-permute-start.54 = (bf16[128,2048]{1,0:T(8,128)(2,1)}, bf16[128,2048]{1,0:T(8,128)(2,1)S(1)}, u32[]{:S(2)}, u32[]{:S(2)}) collective-permute-start(bf16[128,2048]{1,0:T(8,128)(2,1)} %get-tuple-element.298), channel_id=1, source_target_pairs={{0,2},{2,0},{1,3},{3,1},{4,6},{6,4},{5,7},{7,5},{8,10},{10,8},{9,1... | collective-permute-start | bytes 1572872 | tf_op jit(solution)/shard_map/ppermute | solution.py:892
  (77 other events, 647.2 us)

commit v4 on v3

--- a/solution.py
+++ b/solution.py
@@ -39,7 +39,7 @@
 
 BLOCK = 128
 MIB = 1024 * 1024
-COSTS = [50, 50, 50, 50, 50, 10, 0.5, 5, 5, 50, 50, 5, 0.5, 50, 50, 2, 0, 50, 50, 50, 50, 0.5, 50, 0.5, 20, 10, 10, 50, 0.5, 50, 2, 50, 10, 0, 50, 50, 0.5, 50, 50, 50, 50, 0.5, 0, 50, 5, 5, 5, 0, 20, 0.5, 50, 20, 10, 50, 20, 50, 50, 0.5, 0, 50, 50, 50, 50, 10, 50]
+COSTS = [50, 50, 20, 0.5, 10, 10, 0.5, 5, 5, 2, 50, 50, 50, 50, 50, 20, 0, 50, 50, 5, 20, 0.5, 20, 0, 0, 50, 2, 50, 0.5, 2, 10, 0, 0, 0, 10, 10, 0, 0.5, 5, 0, 2, 0, 0, 0, 0, 20, 0, 0, 50, 0, 20, 0, 0, 20, 0, 0, 0, 0, 20, 0, 10, 10, 10, 5, 20, 0]
 
 
 def whole(shape):
@@ -1003,6 +1003,7 @@
             zero = jnp.zeros_like(kept)
             return (kept, zero, zero), to_ctx(lax.dynamic_slice_in_dim(parts, (1 - ctx) * r, r, 0))
         a_own, b_own, b_got, a_got, b_last, a_last = parts
+        wait(a_last)
         (away,) = totals(r, ((b_own, 0), (b_got, 0), (b_last, 0)))
         return (a_own, a_got, a_last), to_ctx(away)
 
@@ -1011,6 +1012,7 @@
     unit_far = far_parts(unit_factors)
     branch_far = to_ctx(fold(cross, branch_keep, branch_got))
     d_linear, unit_sums = attend_back(z_scalar, packed_qkv, logs, d_own, d_oth, w_attn, cosine, sine)
+    wait(branch_near)
     unit_pieces = near_parts(unit_factors, unit_far)
     *g_own, g_keep, g_send, sums = input_grad_of(
         d_linear, low_own, low_oth, w_attn, w_up, (x_own, x_oth), (mean_own, mean_oth), (inv_own, inv_oth), vec
@@ -1021,16 +1023,6 @@
         (attn_own, attn_oth, (d_linear, 0), (d_linear, 1)),
         (d_own, d_oth, (context_out, 0), (context_out, 1)),
     ]
-    attn_far = far_parts(attn_factors)
-    unit_pieces = second(unit_pieces)
-    out_bias = (vec[4] + vec[5]).reshape(1, width)
-    (out_own,) = totals(quarter, ((branch_own[0], 0), (branch_near, 0), (branch_far, 0), (x_own, 0), (out_bias, 0)), steps=2)
-    out_other = to_ten(out_own)
-    g_far = to_ctx(fold(cross, g_keep, g_got))
-    attn_pieces = near_parts(attn_factors, attn_far)
-
-    unit_terms, unit_theirs = third(unit_pieces)
-
     d_sum = jnp.sum(d_own[:quarter].astype(F32), 0, keepdims=True)
     sums = unorder(place, jnp.concatenate([sums[:4], d_sum, jnp.zeros((3, width), F32)], 0))
     unit_part = jnp.concatenate(
@@ -1038,26 +1030,38 @@
     )
     unit_rows = jnp.where(jnp.arange(4)[:, None, None] == ten * 2 + ctx, unit_part[None], 0.0)
     total = jnp.concatenate([sums.reshape(-1), unit_rows.reshape(-1)]).reshape(-1, BLOCK)
-    moves = [to_ten, to_ctx] + [along("shard", shard_count, 1 << k) for k in range(shard_count.bit_length() - 1)]
-
-    def shared(total, moves):
-        for move in moves:
-            (total,) = totals(total.shape[0], ((total, 0), (move(total), 0)), dtype=F32)
-        return total
+    moves = [to_ctx] + [along("shard", shard_count, 1 << k) for k in range(shard_count.bit_length() - 1)] + [to_ten]
+    moved = moves[0](total)
+
+    def shared(total, moved, moves):
+        (total,) = totals(total.shape[0], ((total, 0), (moved, 0)), dtype=F32)
+        return total, moves[0](total) if moves else None
+
+    attn_far = far_parts(attn_factors)
+    out_bias = (vec[4] + vec[5]).reshape(1, width)
+    (out_own,) = totals(quarter, ((branch_own[0], 0), (branch_near, 0), (branch_far, 0), (x_own, 0), (out_bias, 0)), steps=2)
+    out_other = to_ten(out_own)
+    total, moved = shared(total, moved, moves[1:2])
+    unit_pieces = second(unit_pieces)
+    total, moved = shared(total, moved, moves[2:3])
+    g_far = to_ctx(fold(cross, g_keep, g_got))
+    attn_pieces = near_parts(attn_factors, attn_far)
+    unit_terms, unit_theirs = third(unit_pieces)
+    (g_sum,) = totals(quarter, ((g_own[0], 0), (g_near, 0), (g_far, 0)), steps=2)
+    g_other = to_ten(g_sum)
+    total, moved = shared(total, moved, moves[3:4])
+    wait(out_other)
+    attn_pieces = second(attn_pieces)
+    total, moved = shared(total, moved, moves[4:5])
+    attn_terms, attn_theirs = third(attn_pieces)
 
     count_value = step_count.astype(F32)
     fixes = jnp.stack([1.0 - jnp.power(BETA_ONE, count_value), jnp.sqrt(1.0 - jnp.power(BETA_TWO, count_value))])
-    attn_pieces = second(attn_pieces)
-    wait(out_other)
-    (g_sum,) = totals(quarter, ((g_own[0], 0), (g_near, 0), (g_far, 0)), steps=2)
-    g_other = to_ten(g_sum)
-    total = shared(total, moves[:1])
-    attn_terms, attn_theirs = third(attn_pieces)
-    total = shared(total, moves[1:2])
     up_grad, up_new, up_change = adam(ctx_scalar, fixes, up_weight, up_moments, unit_terms, unit_theirs)
-    total = shared(total, moves[2:4])
     down_grad, down_new, down_change = adam(ctx_scalar, fixes, down_weight, down_moments, unit_terms, unit_theirs, first=n)
-    total = shared(total, moves[4:]).reshape(-1)
+    for k in range(5, len(moves) + 1):
+        total, moved = shared(total, moved, moves[k : k + 1])
+    total = total.reshape(-1)
     vector_grad = total[: 5 * width].reshape(5, width)
     vector_grad = jnp.concatenate([vector_grad, vector_grad[4:]], 0)
     unit_all = total[8 * width :].reshape(4 * heads, unit_part.shape[1])

time: 576 us -> 562 us (0.976)
  waiting for transfers between devices: 166 us -> 152 us
    ppermute x55, waiting for transfers between devices: 166 us -> 152 us  [along(): return lambda v: lax.ppermute(v, axis, [(i, i ^ bit) for i in range(size)])]
    unnamed x115 -> x125, local copies, waits for them, and re-layouts: 22.8 us -> 24.6 us
  transfers between devices with their start and end apart: 55 -> 55, of which waited for: 16 -> 14; matrix products, arithmetic and copies ran while one was open for 3% -> 3% of each run, Pallas kernels for 52% -> 53%
where the time goes in v4:
time: 562 us; the launch traced here: 556 us
  Pallas kernels  311 us (55%)
  waiting for transfers between devices  152 us (27%)
  starting transfers between devices  50.8 us (9%)
  local copies, waits for them, and re-layouts  30 us (5%)
  other arithmetic  10.5 us (2%)
    pallas_call x50, Pallas kernels, ordered_call(): *results, token = run(*operands, *waits)  311 us
    ppermute x55, waiting for transfers between devices, along(): return lambda v: lax.ppermute(v, axis, [(i, i ^ bit) for i in range(size)])  152 us
    ppermute x55, starting transfers between devices, along(): return lambda v: lax.ppermute(v, axis, [(i, i ^ bit) for i in range(size)])  50.8 us
    unnamed x125, local copies, waits for them, and re-layouts  24.6 us
  transfers between devices with their start and end apart: 55, of which 14 were waited for; matrix products, arithmetic and copies ran while one was open for 3% of the time, Pallas kernels for 53%

profile of v4, /device:TPU:0, one launch (start us, length us, event | category | flops | bytes accessed | tf_op | source)
XLA Modules:
  0.0 555.8 jit_solution(18199864917673896830)
XLA Ops:
  3.2 3.8 cut.4
  16.8 6.1 %arrange.1 = (bf16[512,2048]{1,0:T(8,128)(2,1)}, bf16[512,2048]{1,0:T(8,128)(2,1)}, f32[6,2048]{1,0:T(8,128)}, f32[8,128]{1,0:T(8,128)}) custom-call(s32[33]{0:T(128)} %stack.134.refs_0_, bf16[512,2048]{1,0:T(8,128)(2,1)} %bitcast.93, bf16[512,2048]{1,0:T(8,128)(2,1)} %bitcast.95, bf16[6,2048]{1,0:T(8,128)(2,1)} %refs_3_.7, f32[8,128]{1,0:T(8,128)} %get-tuple-element.168.refs_4_), custom_call_target="tpu_custom_call" | custom-call | flops 20000000000 | bytes 1 | tf_op jit(solution)/shard_map/arrange/pallas_call | solution.py:82
  22.9 4.6 norm.2
  27.5 17.1 %collective-permute-done.refs_0_.refs_1_ = bf16[128,6144]{1,0:T(8,128)(2,1)S(1)} collective-permute-done((bf16[128,6144]{1,0:T(8,128)(2,1)}, bf16[128,6144]{1,0:T(8,128)(2,1)S(1)}, u32[]{:S(2)}, u32[]{:S(2)}) %collective-permute-start) | collective-permute-done | bytes 1572896 | tf_op jit(solution)/shard_map/ppermute | solution.py:892
  52.0 7.5 %collective-permute-done.4.refs_4_.refs_0_ = bf16[128,4096]{1,0:T(8,128)(2,1)} collective-permute-done((bf16[128,4096]{1,0:T(8,128)(2,1)}, bf16[128,4096]{1,0:T(8,128)(2,1)}, u32[]{:S(2)}, u32[]{:S(2)}) %collective-permute-start.4) | collective-permute-done | bytes 1048608 | tf_op jit(solution)/shard_map/ppermute | solution.py:892
  67.9 19.7 %collective-permute-done.5.refs_3_.refs_0_ = bf16[128,2048]{1,0:T(8,128)(2,1)S(1)} collective-permute-done((bf16[128,2048]{1,0:T(8,128)(2,1)}, bf16[128,2048]{1,0:T(8,128)(2,1)S(1)}, u32[]{:S(2)}, u32[]{:S(2)}) %collective-permute-start.5) | collective-permute-done | bytes 524320 | tf_op jit(solution)/shard_map/ppermute | solution.py:892
  108.1 7.1 %collective-permute-done.8.refs_3_ = bf16[64,4096]{1,0:T(8,128)(2,1)S(1)} collective-permute-done((bf16[64,4096]{1,0:T(8,128)(2,1)}, bf16[64,4096]{1,0:T(8,128)(2,1)S(1)}, u32[]{:S(2)}, u32[]{:S(2)}) %collective-permute-start.8) | collective-permute-done | bytes 524320 | tf_op jit(solution)/shard_map/ppermute | solution.py:892
  128.5 10.8 %hidden.2 = (bf16[512,2048]{1,0:T(8,128)(2,1)}, f32[512,2048]{1,0:T(8,128)}, f32[8,128]{1,0:T(8,128)}) custom-call(bf16[512,2048]{1,0:T(8,128)(2,1)} %get-tuple-element.172.refs_0_, f32[1,2048]{1,0:T(1,128)} %bitcast.104, bf16[512,2048]{1,0:T(8,128)(2,1)} %get-tuple-element.182.refs_2_.refs_14_, bf16[512,2048]{1,0:T(8,128)(2,1)} %get-tuple-element.189.refs_3_.refs_15_, ...), custom_call_target="tpu_custom_call" | custom-call | flops 49999998976 | bytes 1 | tf_op jit(solution)/shard_map/hidden/pallas_call | solution.py:82
  150.1 9.8 %d_hidden.2 = (bf16[512,2048]{1,0:T(8,128)(2,1)}, f32[8,2048]{1,0:T(8,128)}, f32[8,128]{1,0:T(8,128)}) custom-call(bf16[512,2048]{1,0:T(8,128)(2,1)} %get-tuple-element.195.refs_0_.refs_4_.refs_3_.refs_6_, f32[512,2048]{1,0:T(8,128)} %get-tuple-element.196.refs_1_, bf16[512,2048]{1,0:T(8,128)(2,1)} %get-tuple-element.197.refs_2_.refs_3_, ...), custom_call_target="tpu_custom_call" | custom-call | flops 49999998976 | bytes 1 | tf_op jit(solution)/shard_map/d_hidden/pallas_call | solution.py:82
  160.0 20.4 %collective-permute-done.15.refs_1_ = bf16[256,2048]{1,0:T(8,128)(2,1)S(1)} collective-permute-done((bf16[256,2048]{1,0:T(8,128)(2,1)}, bf16[256,2048]{1,0:T(8,128)(2,1)S(1)}, u32[]{:S(2)}, u32[]{:S(2)}) %collective-permute-start.15) | collective-permute-done | bytes 1048608 | tf_op jit(solution)/shard_map/ppermute | solution.py:892
  184.3 4.6 norm.3
  189.0 10.8 %hidden.3 = (bf16[512,2048]{1,0:T(8,128)(2,1)}, f32[512,2048]{1,0:T(8,128)}, f32[8,128]{1,0:T(8,128)}) custom-call(bf16[512,2048]{1,0:T(8,128)(2,1)} %get-tuple-element.207.refs_0_.refs_1_, f32[1,2048]{1,0:T(1,128)} %bitcast.105, bf16[512,2048]{1,0:T(8,128)(2,1)} %get-tuple-element.182.refs_2_.refs_14_, ...), custom_call_target="tpu_custom_call" | custom-call | flops 20000000000 | bytes 1 | tf_op jit(solution)/shard_map/hidden/pallas_call | solution.py:82
  201.5 18.0 %attend.1 = (bf16[1024,512]{1,0:T(8,128)(2,1)}, bf16[1024,1536]{1,0:T(8,128)(2,1)}, f32[1024,256]{1,0:T(8,128)}, f32[8,128]{1,0:T(8,128)}) custom-call(s32[1]{0:T(128)} %bitcast.28.refs_0_, bf16[512,2048]{1,0:T(8,128)(2,1)} %get-tuple-element.210.refs_1_.refs_0_, bf16[512,2048]{1,0:T(8,128)(2,1)} %get-tuple-element.211.refs_2_.refs_1_, f32[1,1536]{1,0:T(1,128)} %bitcast.102, ...), custom_call_target="tpu_custom_call" | custom-call | flops 500000000 | bytes 1 | tf_op jit(solution)/shard_map/attend/pallas_call | solution.py:82
  219.5 18.4 %branch.1 = (f32[256,2048]{1,0:T(8,128)}, bf16[256,2048]{1,0:T(8,128)(2,1)}, f32[256,2048]{1,0:T(8,128)}, bf16[256,2048]{1,0:T(8,128)(2,1)}, f32[8,128]{1,0:T(8,128)}) custom-call(bf16[512,2048]{1,0:T(8,128)(2,1)} %get-tuple-element.193.refs_0_.refs_6_, bf16[512,2048]{1,0:T(8,128)(2,1)} %get-tuple-element.209.refs_1_.refs_7_, ...), custom_call_target="tpu_custom_call" | custom-call | flops 20000000000 | bytes 1 | tf_op jit(solution)/shard_map/branch/pallas_call | solution.py:82
  243.8 9.8 %d_hidden.3 = (bf16[512,2048]{1,0:T(8,128)(2,1)}, f32[8,2048]{1,0:T(8,128)}, f32[8,128]{1,0:T(8,128)}) custom-call(bf16[512,2048]{1,0:T(8,128)(2,1)} %get-tuple-element.224.refs_0_.refs_5_.refs_4_, f32[512,2048]{1,0:T(8,128)} %get-tuple-element.225.refs_1_, bf16[512,2048]{1,0:T(8,128)(2,1)} %get-tuple-element.197.refs_2_.refs_3_, ...), custom_call_target="tpu_custom_call" | custom-call | bytes 1 | tf_op jit(solution)/shard_map/d_hidden/pallas_call | solution.py:82
  253.6 18.7 %grad_far.2 = (bf16[256,4096]{1,0:T(8,128)(2,1)}, bf16[256,4096]{1,0:T(8,128)(2,1)}, bf16[256,4096]{1,0:T(8,128)(2,1)}, bf16[256,4096]{1,0:T(8,128)(2,1)}, f32[8,128]{1,0:T(8,128)}) custom-call(bf16[512,2048]{1,0:T(8,128)(2,1)} %get-tuple-element.172.refs_0_, bf16[512,2048]{1,0:T(8,128)(2,1)} %get-tuple-element.207.refs_0_.refs_1_, ...), custom_call_target="tpu_custom_call" | custom-call | flops 49999998976 | bytes 1 | tf_op jit(solution)/shard_map/grad_far/pallas_call | solution.py:82
  278.4 14.0 %attend_back.1 = (bf16[1024,1536]{1,0:T(8,128)(2,1)}, f32[8,1536]{1,0:T(8,128)}, f32[8,128]{1,0:T(8,128)}) custom-call(s32[1]{0:T(128)} %bitcast.28.refs_0_, bf16[1024,1536]{1,0:T(8,128)(2,1)} %get-tuple-element.231.refs_1_, f32[1024,256]{1,0:T(8,128)} %get-tuple-element.232.refs_2_, bf16[512,2048]{1,0:T(8,128)(2,1)} %get-tuple-element.195.refs_0_.refs_4_.refs_3_.refs_6_, ...), custom_call_target="tpu_custom_call" | custom-call | flops 49999998976 | bytes 1 | tf_op jit(solution)/shard_map/attend_back/pallas_call | solution.py:82
  293.4 7.3 %collective-permute-done.23.refs_13_.refs_1_ = bf16[256,2048]{1,0:T(8,128)(2,1)S(1)} collective-permute-done((bf16[256,2048]{1,0:T(8,128)(2,1)}, bf16[256,2048]{1,0:T(8,128)(2,1)S(1)}, u32[]{:S(2)}, u32[]{:S(2)}) %collective-permute-start.23) | collective-permute-done | bytes 1048608 | tf_op jit(solution)/shard_map/ppermute | solution.py:892
  304.9 21.3 %grad_near.2 = (bf16[256,4096]{1,0:T(8,128)(2,1)}, bf16[256,4096]{1,0:T(8,128)(2,1)}, bf16[256,4096]{1,0:T(8,128)(2,1)}, bf16[256,4096]{1,0:T(8,128)(2,1)}, f32[8,128]{1,0:T(8,128)}) custom-call(bf16[512,2048]{1,0:T(8,128)(2,1)} %get-tuple-element.172.refs_0_, bf16[512,2048]{1,0:T(8,128)(2,1)} %get-tuple-element.207.refs_0_.refs_1_, ...), custom_call_target="tpu_custom_call" | custom-call | flops 500000000 | bytes 1 | tf_op jit(solution)/shard_map/grad_near/pallas_call | solution.py:82
  328.3 26.2 %input_grad.1 = (f32[256,2048]{1,0:T(8,128)}, bf16[256,2048]{1,0:T(8,128)(2,1)}, f32[256,2048]{1,0:T(8,128)}, bf16[256,2048]{1,0:T(8,128)(2,1)}, f32[8,2048]{1,0:T(8,128)}, /*index=5*/f32[8,128]{1,0:T(8,128)}) custom-call(bf16[1024,1536]{1,0:T(8,128)(2,1)} %get-tuple-element.234.refs_0_.refs_2_.refs_3_, ...), custom_call_target="tpu_custom_call" | custom-call | flops 2000000000 | bytes 1 | tf_op jit(solution)/shard_map/input_grad/pallas_call | solution.py:82
  359.5 11.0 %grad_far.3 = (bf16[256,2048]{1,0:T(8,128)(2,1)}, bf16[256,2048]{1,0:T(8,128)(2,1)}, bf16[256,2048]{1,0:T(8,128)(2,1)}, bf16[256,2048]{1,0:T(8,128)(2,1)}, f32[8,128]{1,0:T(8,128)}) custom-call(bf16[512,2048]{1,0:T(8,128)(2,1)} %get-tuple-element.210.refs_1_.refs_0_, bf16[512,2048]{1,0:T(8,128)(2,1)} %get-tuple-element.211.refs_2_.refs_1_, ...), custom_call_target="tpu_custom_call" | custom-call | bytes 1 | tf_op jit(solution)/shard_map/grad_far/pallas_call | solution.py:82
  386.1 8.2 %collective-permute-done.33.refs_1_ = bf16[256,2048]{1,0:T(8,128)(2,1)S(1)} collective-permute-done((bf16[256,2048]{1,0:T(8,128)(2,1)}, bf16[256,2048]{1,0:T(8,128)(2,1)S(1)}, u32[]{:S(2)}, u32[]{:S(2)}) %collective-permute-start.33) | collective-permute-done | bytes 1048608 | tf_op jit(solution)/shard_map/ppermute | solution.py:892
  405.8 12.8 %grad_near.3 = (bf16[256,2048]{1,0:T(8,128)(2,1)}, bf16[256,2048]{1,0:T(8,128)(2,1)}, bf16[256,2048]{1,0:T(8,128)(2,1)}, bf16[256,2048]{1,0:T(8,128)(2,1)}, f32[8,128]{1,0:T(8,128)}) custom-call(bf16[512,2048]{1,0:T(8,128)(2,1)} %get-tuple-element.210.refs_1_.refs_0_, bf16[512,2048]{1,0:T(8,128)(2,1)} %get-tuple-element.211.refs_2_.refs_1_, ...), custom_call_target="tpu_custom_call" | custom-call | flops 500000000 | bytes 1 | tf_op jit(solution)/shard_map/grad_near/pallas_call | solution.py:82
  424.7 11.5 %collective-permute-done.32.refs_1_ = bf16[256,2048]{1,0:T(8,128)(2,1)S(1)} collective-permute-done((bf16[256,2048]{1,0:T(8,128)(2,1)}, bf16[256,2048]{1,0:T(8,128)(2,1)S(1)}, u32[]{:S(2)}, u32[]{:S(2)}) %collective-permute-start.32) | collective-permute-done | bytes 1048608 | tf_op jit(solution)/shard_map/ppermute | solution.py:892
  438.0 14.3 %collective-permute-done.38.refs_2_ = bf16[256,2048]{1,0:T(8,128)(2,1)S(1)} collective-permute-done((bf16[256,2048]{1,0:T(8,128)(2,1)}, bf16[256,2048]{1,0:T(8,128)(2,1)S(1)}, u32[]{:S(2)}, u32[]{:S(2)}) %collective-permute-start.38) | collective-permute-done | bytes 1048608 | tf_op jit(solution)/shard_map/ppermute | solution.py:892
  459.5 18.1 %collective-permute-done.31.refs_5_.refs_2_ = bf16[256,2048]{1,0:T(8,128)(2,1)S(1)} collective-permute-done((bf16[256,2048]{1,0:T(8,128)(2,1)S(1)}, bf16[256,2048]{1,0:T(8,128)(2,1)S(1)}, u32[]{:S(2)}, u32[]{:S(2)}) %collective-permute-start.31) | collective-permute-done | bytes 1048608 | tf_op jit(solution)/shard_map/ppermute | solution.py:892
  485.6 9.9 %collective-permute-done.47.refs_1_ = f32[240,128]{1,0:T(8,128)S(1)} collective-permute-done((f32[240,128]{1,0:T(8,128)S(1)}, f32[240,128]{1,0:T(8,128)S(1)}, u32[]{:S(2)}, u32[]{:S(2)}) %collective-permute-start.47) | collective-permute-done | bytes 122912 | tf_op jit(solution)/shard_map/ppermute | solution.py:892
  505.6 6.7 %adam.3 = (f32[128,4096]{1,0:T(8,128)}, f32[2,128,4096]{2,1,0:T(8,128)}, f32[128,4096]{1,0:T(8,128)}, f32[8,128]{1,0:T(8,128)}) custom-call(s32[1]{0:T(128)} %bitcast.27.refs_0_, f32[2]{0:T(128)} %pad_maximum_fusion.5.refs_1_, bf16[128,4096]{1,0:T(8,128)(2,1)} %refs_2_.10, f32[2,128,4096]{2,1,0:T(8,128)} %refs_3_.8, ...), custom_call_target="tpu_custom_call" | custom-call | bytes 1 | tf_op jit(solution)/shard_map/adam/pallas_call | solution.py:82
  512.3 6.7 %adam.4 = (f32[128,4096]{1,0:T(8,128)}, f32[2,128,4096]{2,1,0:T(8,128)}, f32[128,4096]{1,0:T(8,128)}, f32[8,128]{1,0:T(8,128)}) custom-call(s32[1]{0:T(128)} %bitcast.27.refs_0_, f32[2]{0:T(128)} %pad_maximum_fusion.5.refs_1_, bf16[128,4096]{1,0:T(8,128)(2,1)} %refs_2_.11, f32[2,128,4096]{2,1,0:T(8,128)} %refs_3_.9, ...), custom_call_target="tpu_custom_call" | custom-call | flops 20000000000 | bytes 1 | tf_op jit(solution)/shard_map/adam/pallas_call | solution.py:82
  519.0 8.7 %collective-permute-done.50.refs_1_ = f32[240,128]{1,0:T(8,128)S(1)} collective-permute-done((f32[240,128]{1,0:T(8,128)}, f32[240,128]{1,0:T(8,128)S(1)}, u32[]{:S(2)}, u32[]{:S(2)}) %collective-permute-start.50) | collective-permute-done | bytes 122912 | tf_op jit(solution)/shard_map/ppermute | solution.py:892
  534.5 9.1 %finish.1 = (bf16[512,2048]{1,0:T(8,128)(2,1)}, f32[512,2048]{1,0:T(8,128)}, f32[8,128]{1,0:T(8,128)}) custom-call(s32[33]{0:T(128)} %stack.134.refs_0_, bf16[256,2048]{1,0:T(8,128)(2,1)} %get-tuple-element.249.refs_1_, bf16[256,2048]{1,0:T(8,128)(2,1)} %copy-done.7, bf16[256,2048]{1,0:T(8,128)(2,1)} %get-tuple-element.277.refs_3_, ...), custom_call_target="tpu_custom_call" | custom-call | bytes 1 | tf_op jit(solution)/shard_map/finish/pallas_call | solution.py:82
  545.2 7.6 %adam_heads.1 = (f32[128,4,768]{2,1,0:T(4,128)}, f32[2,128,4,768]{3,2,1,0:T(4,128)}, f32[128,4,768]{2,1,0:T(4,128)}, f32[8,128]{1,0:T(8,128)}) custom-call(s32[1]{0:T(128)} %bitcast.27.refs_0_, f32[2]{0:T(128)} %pad_maximum_fusion.5.refs_1_, bf16[128,4,768]{2,1,0:T(4,128)(2,1)} %refs_2_.12, f32[2,128,4,768]{3,2,1,0:T(4,128)} %refs_3_.10, ...), custom_call_target="tpu_custom_call" | custom-call | flops 49999998976 | bytes 1 | tf_op jit(solution)/shard_map/adam_heads/pallas_call | solution.py:82
  (289 shorter events, 173.1 us)
Async XLA Ops:
  7.0 37.6 %collective-permute-start = (bf16[128,6144]{1,0:T(8,128)(2,1)}, bf16[128,6144]{1,0:T(8,128)(2,1)S(1)}, u32[]{:S(2)}, u32[]{:S(2)}) collective-permute-start(bf16[128,6144]{1,0:T(8,128)(2,1)} %get-tuple-element.173.refs_0_), channel_id=1, source_target_pairs={{0,16},{4,20},{8,24},{12,28},{16,0},{20,4},{24,8},{28,12},{1,17},{... | collective-permute-start | bytes 4718600 | tf_op jit(solution)/shard_map/ppermute | solution.py:892
  10.0 36.1 %collective-permute-start.1 = (bf16[128,6144]{1,0:T(8,128)(2,1)}, bf16[128,6144]{1,0:T(8,128)(2,1)S(1)}, u32[]{:S(2)}, u32[]{:S(2)}) collective-permute-start(bf16[128,6144]{1,0:T(8,128)(2,1)} %get-tuple-element.173.refs_0_), channel_id=1, source_target_pairs={{0,8},{4,12},{8,0},{12,4},{16,24},{20,28},{24,16},{28,20},{1,9},{5... | collective-permute-start | bytes 4718600 | tf_op jit(solution)/shard_map/ppermute | solution.py:892
  11.5 48.0 %collective-permute-start.4 = (bf16[128,4096]{1,0:T(8,128)(2,1)}, bf16[128,4096]{1,0:T(8,128)(2,1)}, u32[]{:S(2)}, u32[]{:S(2)}) collective-permute-start(bf16[128,4096]{1,0:T(8,128)(2,1)} %get-tuple-element.178), channel_id=1, source_target_pairs={{0,2},{2,0},{1,3},{3,1},{4,6},{6,4},{5,7},{7,5},{8,10},{10,8},{9,1... | collective-permute-start | bytes 3145736 | tf_op jit(solution)/shard_map/ppermute | solution.py:892
  49.7 41.8 %collective-permute-start.2 = (bf16[64,6144]{1,0:T(8,128)(2,1)}, bf16[64,6144]{1,0:T(8,128)(2,1)S(1)}, u32[]{:S(2)}, u32[]{:S(2)}) collective-permute-start(bf16[64,6144]{1,0:T(8,128)(2,1)} %get-tuple-element.175), channel_id=1, source_target_pairs={{0,8},{4,12},{8,0},{12,4},{16,24},{20,28},{24,16},{28,20},{1,9},{5... | collective-permute-start | bytes 2359304 | tf_op jit(solution)/shard_map/ppermute | solution.py:892
  51.2 40.9 %collective-permute-start.3 = (bf16[64,6144]{1,0:T(8,128)(2,1)}, bf16[64,6144]{1,0:T(8,128)(2,1)S(1)}, u32[]{:S(2)}, u32[]{:S(2)}) collective-permute-start(bf16[64,6144]{1,0:T(8,128)(2,1)} %get-tuple-element.176), channel_id=1, source_target_pairs={{0,16},{4,20},{8,24},{12,28},{16,0},{20,4},{24,8},{28,12},{1,17},{... | collective-permute-start | bytes 2359304 | tf_op jit(solution)/shard_map/ppermute | solution.py:892
  66.3 32.7 %collective-permute-start.6 = (bf16[128,4096]{1,0:T(8,128)(2,1)}, bf16[128,4096]{1,0:T(8,128)(2,1)S(1)}, u32[]{:S(2)}, u32[]{:S(2)}) collective-permute-start(bf16[128,4096]{1,0:T(8,128)(2,1)} %collective-permute-done.4.refs_4_.refs_0_), channel_id=1, source_target_pairs={{0,8},{4,12},{8,0},{12,4},{16,24},{20,28},{24,16},{28,20},{1,9},{5... | collective-permute-start | bytes 3145736 | tf_op jit(solution)/shard_map/ppermute | solution.py:892
  66.8 32.1 %collective-permute-start.7 = (bf16[128,4096]{1,0:T(8,128)(2,1)}, bf16[128,4096]{1,0:T(8,128)(2,1)S(1)}, u32[]{:S(2)}, u32[]{:S(2)}) collective-permute-start(bf16[128,4096]{1,0:T(8,128)(2,1)} %collective-permute-done.4.refs_4_.refs_0_), channel_id=1, source_target_pairs={{0,16},{4,20},{8,24},{12,28},{16,0},{20,4},{24,8},{28,12},{1,17},{... | collective-permute-start | bytes 3145736 | tf_op jit(solution)/shard_map/ppermute | solution.py:892
  91.5 47.7 %collective-permute-start.14 = (bf16[256,2048]{1,0:T(8,128)(2,1)}, bf16[256,2048]{1,0:T(8,128)(2,1)}, u32[]{:S(2)}, u32[]{:S(2)}) collective-permute-start(bf16[256,2048]{1,0:T(8,128)(2,1)} %get-tuple-element.194), channel_id=1, source_target_pairs={{0,2},{2,0},{1,3},{3,1},{4,6},{6,4},{5,7},{7,5},{8,10},{10,8},{9,1... | collective-permute-start | bytes 3145736 | tf_op jit(solution)/shard_map/ppermute | solution.py:892
  91.5 27.5 %collective-permute-start.12 = (bf16[128,2048]{1,0:T(8,128)(2,1)}, bf16[128,2048]{1,0:T(8,128)(2,1)S(1)}, u32[]{:S(2)}, u32[]{:S(2)}) collective-permute-start(bf16[128,2048]{1,0:T(8,128)(2,1)} %copy-done.24), channel_id=1, source_target_pairs={{0,16},{4,20},{8,24},{12,28},{16,0},{20,4},{24,8},{28,12},{1,17},{... | collective-permute-start | bytes 1572872 | tf_op jit(solution)/shard_map/ppermute | solution.py:892
  115.2 35.0 %collective-permute-start.16 = (bf16[512,2048]{1,0:T(8,128)(2,1)}, bf16[512,2048]{1,0:T(8,128)(2,1)}, u32[]{:S(2)}, u32[]{:S(2)}) collective-permute-start(bf16[512,2048]{1,0:T(8,128)(2,1)} %get-tuple-element.197.refs_2_.refs_3_), channel_id=1, source_target_pairs={{0,4},{4,0},{8,12},{12,8},{16,20},{20,16},{24,28},{28,24},{1,5},{5... | collective-permute-start | bytes 6291464 | tf_op jit(solution)/shard_map/ppermute | solution.py:892
  139.3 60.6 %collective-permute-start.20 = (bf16[512,2048]{1,0:T(8,128)(2,1)}, bf16[512,2048]{1,0:T(8,128)(2,1)}, u32[]{:S(2)}, u32[]{:S(2)}) collective-permute-start(bf16[512,2048]{1,0:T(8,128)(2,1)} %get-tuple-element.212.refs_6_.refs_7_.refs_10_), channel_id=1, source_target_pairs={{0,4},{4,0},{8,12},{12,8},{16,20},{20,16},{24,28},{28,24},{1,5},{5... | collective-permute-start | bytes 6291464 | tf_op jit(solution)/shard_map/ppermute | solution.py:892
  139.4 41.0 %collective-permute-start.15 = (bf16[256,2048]{1,0:T(8,128)(2,1)}, bf16[256,2048]{1,0:T(8,128)(2,1)S(1)}, u32[]{:S(2)}, u32[]{:S(2)}) collective-permute-start(bf16[256,2048]{1,0:T(8,128)(2,1)} %collective-permute-done.14.refs_3_.refs_0_), channel_id=1, source_target_pairs={{0,1},{1,0},{2,3},{3,2},{4,5},{5,4},{6,7},{7,6},{8,9},{9,8},{10,11... | collective-permute-start | bytes 3145736 | tf_op jit(solution)/shard_map/ppermute | solution.py:892
  149.7 50.0 %collective-permute-start.22 = (bf16[256,2048]{1,0:T(8,128)(2,1)}, bf16[256,2048]{1,0:T(8,128)(2,1)S(1)}, u32[]{:S(2)}, u32[]{:S(2)}) collective-permute-start(bf16[256,2048]{1,0:T(8,128)(2,1)} %get-tuple-element.215), channel_id=1, source_target_pairs={{0,2},{2,0},{1,3},{3,1},{4,6},{6,4},{5,7},{7,5},{8,10},{10,8},{9,1... | collective-permute-start | bytes 3145736 | tf_op jit(solution)/shard_map/ppermute | solution.py:892
  150.1 49.7 %collective-permute-start.21 = (bf16[512,2048]{1,0:T(8,128)(2,1)S(1)}, bf16[512,2048]{1,0:T(8,128)(2,1)S(1)}, u32[]{:S(2)}, u32[]{:S(2)}) collective-permute-start(bf16[512,2048]{1,0:T(8,128)(2,1)S(1)} %copy-done.1), channel_id=1, source_target_pairs={{0,4},{4,0},{8,12},{12,8},{16,20},{20,16},{24,28},{28,24},{1,5},{5... | collective-permute-start | bytes 6291464 | tf_op jit(solution)/shard_map/ppermute | solution.py:892
  199.8 40.0 %collective-permute-start.25 = (bf16[256,2048]{1,0:T(8,128)(2,1)S(1)}, bf16[256,2048]{1,0:T(8,128)(2,1)S(1)}, u32[]{:S(2)}, u32[]{:S(2)}) collective-permute-start(bf16[256,2048]{1,0:T(8,128)(2,1)S(1)} %collective-permute-done.22.refs_11_.refs_0_), channel_id=1, source_target_pairs={{0,1},{1,0},{2,3},{3,2},{4,5},{5,4},{6,7},{7,6},{8,9},{9,8},{10,11... | collective-permute-start | bytes 3145736 | tf_op jit(solution)/shard_map/ppermute | solution.py:892
  237.9 36.4 %collective-permute-start.24 = (bf16[256,2048]{1,0:T(8,128)(2,1)}, bf16[256,2048]{1,0:T(8,128)(2,1)S(1)}, u32[]{:S(2)}, u32[]{:S(2)}) collective-permute-start(bf16[256,2048]{1,0:T(8,128)(2,1)} %get-tuple-element.221), channel_id=1, source_target_pairs={{0,1},{1,0},{2,3},{3,2},{4,5},{5,4},{6,7},{7,6},{8,9},{9,8},{10,11... | collective-permute-start | bytes 3145736 | tf_op jit(solution)/shard_map/ppermute | solution.py:892
  273.3 30.3 %collective-permute-start.27 = (bf16[256,4096]{1,0:T(8,128)(2,1)}, bf16[256,4096]{1,0:T(8,128)(2,1)S(1)}, u32[]{:S(2)}, u32[]{:S(2)}) collective-permute-start(bf16[256,4096]{1,0:T(8,128)(2,1)} %get-tuple-element.239), channel_id=1, source_target_pairs={{0,4},{4,0},{8,12},{12,8},{16,20},{20,16},{24,28},{28,24},{1,5},{5... | collective-permute-start | bytes 6291464 | tf_op jit(solution)/shard_map/ppermute | solution.py:892
  273.4 30.2 %collective-permute-start.28 = (bf16[256,4096]{1,0:T(8,128)(2,1)}, bf16[256,4096]{1,0:T(8,128)(2,1)}, u32[]{:S(2)}, u32[]{:S(2)}) collective-permute-start(bf16[256,4096]{1,0:T(8,128)(2,1)} %get-tuple-element.240), channel_id=1, source_target_pairs={{0,4},{4,0},{8,12},{12,8},{16,20},{20,16},{24,28},{28,24},{1,5},{5... | collective-permute-start | bytes 6291464 | tf_op jit(solution)/shard_map/ppermute | solution.py:892
  273.8 29.7 %collective-permute-start.29 = (bf16[256,4096]{1,0:T(8,128)(2,1)}, bf16[256,4096]{1,0:T(8,128)(2,1)}, u32[]{:S(2)}, u32[]{:S(2)}) collective-permute-start(bf16[256,4096]{1,0:T(8,128)(2,1)} %get-tuple-element.241), channel_id=1, source_target_pairs={{0,4},{4,0},{8,12},{12,8},{16,20},{20,16},{24,28},{28,24},{1,5},{5... | collective-permute-start | bytes 6291464 | tf_op jit(solution)/shard_map/ppermute | solution.py:892
  273.9 29.7 %collective-permute-start.30 = (bf16[256,4096]{1,0:T(8,128)(2,1)}, bf16[256,4096]{1,0:T(8,128)(2,1)}, u32[]{:S(2)}, u32[]{:S(2)}) collective-permute-start(bf16[256,4096]{1,0:T(8,128)(2,1)} %get-tuple-element.242), channel_id=1, source_target_pairs={{0,4},{4,0},{8,12},{12,8},{16,20},{20,16},{24,28},{28,24},{1,5},{5... | collective-permute-start | bytes 6291464 | tf_op jit(solution)/shard_map/ppermute | solution.py:892
  300.7 71.6 %collective-permute-start.26 = (bf16[256,2048]{1,0:T(8,128)(2,1)}, bf16[256,2048]{1,0:T(8,128)(2,1)S(1)}, u32[]{:S(2)}, u32[]{:S(2)}) collective-permute-start(bf16[256,2048]{1,0:T(8,128)(2,1)} %get-tuple-element.230), channel_id=1, source_target_pairs={{0,2},{2,0},{1,3},{3,1},{4,6},{6,4},{5,7},{7,5},{8,10},{10,8},{9,1... | collective-permute-start | bytes 3145736 | tf_op jit(solution)/shard_map/ppermute | solution.py:892
  326.2 54.2 %collective-permute-start.36 = (bf16[256,4096]{1,0:T(8,128)(2,1)}, bf16[256,4096]{1,0:T(8,128)(2,1)}, u32[]{:S(2)}, u32[]{:S(2)}) collective-permute-start(bf16[256,4096]{1,0:T(8,128)(2,1)} %get-tuple-element.261), channel_id=1, source_target_pairs={{0,16},{4,20},{8,24},{12,28},{16,0},{20,4},{24,8},{28,12},{1,17},{... | collective-permute-start | bytes 6291464 | tf_op jit(solution)/shard_map/ppermute | solution.py:892
  326.9 53.6 %collective-permute-start.37 = (bf16[256,4096]{1,0:T(8,128)(2,1)}, bf16[256,4096]{1,0:T(8,128)(2,1)S(1)}, u32[]{:S(2)}, u32[]{:S(2)}) collective-permute-start(bf16[256,4096]{1,0:T(8,128)(2,1)} %get-tuple-element.263), channel_id=1, source_target_pairs={{0,8},{4,12},{8,0},{12,4},{16,24},{20,28},{24,16},{28,20},{1,9},{5... | collective-permute-start | bytes 6291464 | tf_op jit(solution)/shard_map/ppermute | solution.py:892
  394.3 41.9 %collective-permute-start.32 = (bf16[256,2048]{1,0:T(8,128)(2,1)}, bf16[256,2048]{1,0:T(8,128)(2,1)S(1)}, u32[]{:S(2)}, u32[]{:S(2)}) collective-permute-start(bf16[256,2048]{1,0:T(8,128)(2,1)} %get-tuple-element.251), channel_id=1, source_target_pairs={{0,1},{1,0},{2,3},{3,2},{4,5},{5,4},{6,7},{7,6},{8,9},{9,8},{10,11... | collective-permute-start | bytes 3145736 | tf_op jit(solution)/shard_map/ppermute | solution.py:892
  402.5 49.8 %collective-permute-start.38 = (bf16[256,2048]{1,0:T(8,128)(2,1)}, bf16[256,2048]{1,0:T(8,128)(2,1)S(1)}, u32[]{:S(2)}, u32[]{:S(2)}) collective-permute-start(bf16[256,2048]{1,0:T(8,128)(2,1)} %get-tuple-element.267), channel_id=1, source_target_pairs={{0,2},{2,0},{1,3},{3,1},{4,6},{6,4},{5,7},{7,5},{8,10},{10,8},{9,1... | collective-permute-start | bytes 3145736 | tf_op jit(solution)/shard_map/ppermute | solution.py:892
  404.9 72.7 %collective-permute-start.31 = (bf16[256,2048]{1,0:T(8,128)(2,1)S(1)}, bf16[256,2048]{1,0:T(8,128)(2,1)S(1)}, u32[]{:S(2)}, u32[]{:S(2)}) collective-permute-start(bf16[256,2048]{1,0:T(8,128)(2,1)S(1)} %copy-done.21), channel_id=1, source_target_pairs={{0,1},{1,0},{2,3},{3,2},{4,5},{5,4},{6,7},{7,6},{8,9},{9,8},{10,11... | collective-permute-start | bytes 3145736 | tf_op jit(solution)/shard_map/ppermute | solution.py:892
  418.6 59.0 %collective-permute-start.48 = (bf16[256,2048]{1,0:T(8,128)(2,1)}, bf16[256,2048]{1,0:T(8,128)(2,1)S(1)}, u32[]{:S(2)}, u32[]{:S(2)}) collective-permute-start(bf16[256,2048]{1,0:T(8,128)(2,1)} %get-tuple-element.282), channel_id=1, source_target_pairs={{0,16},{4,20},{8,24},{12,28},{16,0},{20,4},{24,8},{28,12},{1,17},{... | collective-permute-start | bytes 3145736 | tf_op jit(solution)/shard_map/ppermute | solution.py:892
  420.5 57.1 %collective-permute-start.49 = (bf16[256,2048]{1,0:T(8,128)(2,1)}, bf16[256,2048]{1,0:T(8,128)(2,1)S(1)}, u32[]{:S(2)}, u32[]{:S(2)}) collective-permute-start(bf16[256,2048]{1,0:T(8,128)(2,1)} %get-tuple-element.284), channel_id=1, source_target_pairs={{0,8},{4,12},{8,0},{12,4},{16,24},{20,28},{24,16},{28,20},{1,9},{5... | collective-permute-start | bytes 3145736 | tf_op jit(solution)/shard_map/ppermute | solution.py:892
  436.2 68.5 %collective-permute-start.51 = (bf16[128,4096]{1,0:T(8,128)(2,1)}, bf16[128,4096]{1,0:T(8,128)(2,1)S(1)}, u32[]{:S(2)}, u32[]{:S(2)}) collective-permute-start(bf16[128,4096]{1,0:T(8,128)(2,1)} %get-tuple-element.288), channel_id=1, source_target_pairs={{0,2},{2,0},{1,3},{3,1},{4,6},{6,4},{5,7},{7,5},{8,10},{10,8},{9,1... | collective-permute-start | bytes 3145736 | tf_op jit(solution)/shard_map/ppermute | solution.py:892
  485.6 48.9 %collective-permute-start.45 = (bf16[256,2048]{1,0:T(8,128)(2,1)S(1)}, bf16[256,2048]{1,0:T(8,128)(2,1)}, u32[]{:S(2)}, u32[]{:S(2)}) collective-permute-start(bf16[256,2048]{1,0:T(8,128)(2,1)S(1)} %copy-done.22), channel_id=1, source_target_pairs={{0,1},{1,0},{2,3},{3,2},{4,5},{5,4},{6,7},{7,6},{8,9},{9,8},{10,11... | collective-permute-start | bytes 3145736 | tf_op jit(solution)/shard_map/ppermute | solution.py:892
  497.8 29.9 %collective-permute-start.50 = (f32[240,128]{1,0:T(8,128)}, f32[240,128]{1,0:T(8,128)S(1)}, u32[]{:S(2)}, u32[]{:S(2)}) collective-permute-start(f32[240,128]{1,0:T(8,128)} %get-tuple-element.287.refs_0_), channel_id=1, source_target_pairs={{0,1},{1,0},{2,3},{3,2},{4,5},{5,4},{6,7},{7,6},{8,9},{9,8},{10,11... | collective-permute-start | bytes 368648 | tf_op jit(solution)/shard_map/ppermute | solution.py:892
  501.1 43.2 %collective-permute-start.54 = (bf16[128,2048]{1,0:T(8,128)(2,1)}, bf16[128,2048]{1,0:T(8,128)(2,1)S(1)}, u32[]{:S(2)}, u32[]{:S(2)}) collective-permute-start(bf16[128,2048]{1,0:T(8,128)(2,1)} %get-tuple-element.298), channel_id=1, source_target_pairs={{0,2},{2,0},{1,3},{3,1},{4,6},{6,4},{5,7},{7,5},{8,10},{10,8},{9,1... | collective-permute-start | bytes 1572872 | tf_op jit(solution)/shard_map/ppermute | solution.py:892
  (82 other events, 706.7 us)

commit v5 on v4

--- a/solution.py
+++ b/solution.py
@@ -39,7 +39,7 @@
 
 BLOCK = 128
 MIB = 1024 * 1024
-COSTS = [50, 50, 20, 0.5, 10, 10, 0.5, 5, 5, 2, 50, 50, 50, 50, 50, 20, 0, 50, 50, 5, 20, 0.5, 20, 0, 0, 50, 2, 50, 0.5, 2, 10, 0, 0, 0, 10, 10, 0, 0.5, 5, 0, 2, 0, 0, 0, 0, 20, 0, 0, 50, 0, 20, 0, 0, 20, 0, 0, 0, 0, 20, 0, 10, 10, 10, 5, 20, 0]
+COSTS = [50, 50, 20, 0.5, 0.5, 0, 0.5, 5, 5, 0, 50, 0, 50, 2, 50, 20, 0, 2, 50, 5, 20, 50, 20, 0.5, 50, 0, 5, 50, 0, 2, 10, 0, 0, 0.5, 10, 0, 0, 0.5, 0, 0, 2, 0, 0, 0, 0, 2, 0.5, 0, 0, 0.5, 10, 0, 0, 0, 20, 0.5, 0, 10, 5, 2, 2, 10, 0, 50, 5, 2]
 
 
 def whole(shape):
@@ -1012,8 +1012,8 @@
     unit_far = far_parts(unit_factors)
     branch_far = to_ctx(fold(cross, branch_keep, branch_got))
     d_linear, unit_sums = attend_back(z_scalar, packed_qkv, logs, d_own, d_oth, w_attn, cosine, sine)
+    unit_pieces = near_parts(unit_factors, unit_far)
     wait(branch_near)
-    unit_pieces = near_parts(unit_factors, unit_far)
     *g_own, g_keep, g_send, sums = input_grad_of(
         d_linear, low_own, low_oth, w_attn, w_up, (x_own, x_oth), (mean_own, mean_oth), (inv_own, inv_oth), vec
     )
@@ -1041,24 +1041,25 @@
     out_bias = (vec[4] + vec[5]).reshape(1, width)
     (out_own,) = totals(quarter, ((branch_own[0], 0), (branch_near, 0), (branch_far, 0), (x_own, 0), (out_bias, 0)), steps=2)
     out_other = to_ten(out_own)
+    unit_pieces = second(unit_pieces)
+    g_far = to_ctx(fold(cross, g_keep, g_got))
     total, moved = shared(total, moved, moves[1:2])
-    unit_pieces = second(unit_pieces)
-    total, moved = shared(total, moved, moves[2:3])
-    g_far = to_ctx(fold(cross, g_keep, g_got))
     attn_pieces = near_parts(attn_factors, attn_far)
     unit_terms, unit_theirs = third(unit_pieces)
     (g_sum,) = totals(quarter, ((g_own[0], 0), (g_near, 0), (g_far, 0)), steps=2)
     g_other = to_ten(g_sum)
-    total, moved = shared(total, moved, moves[3:4])
+    total, moved = shared(total, moved, moves[2:3])
     wait(out_other)
     attn_pieces = second(attn_pieces)
+    total, moved = shared(total, moved, moves[3:4])
+    attn_terms, attn_theirs = third(attn_pieces)
     total, moved = shared(total, moved, moves[4:5])
-    attn_terms, attn_theirs = third(attn_pieces)
 
     count_value = step_count.astype(F32)
     fixes = jnp.stack([1.0 - jnp.power(BETA_ONE, count_value), jnp.sqrt(1.0 - jnp.power(BETA_TWO, count_value))])
     up_grad, up_new, up_change = adam(ctx_scalar, fixes, up_weight, up_moments, unit_terms, unit_theirs)
     down_grad, down_new, down_change = adam(ctx_scalar, fixes, down_weight, down_moments, unit_terms, unit_theirs, first=n)
+    outputs, input_grad = finish(place, out_own, out_other, g_sum, g_other, x_own, d_own)
     for k in range(5, len(moves) + 1):
         total, moved = shared(total, moved, moves[k : k + 1])
     total = total.reshape(-1)
@@ -1066,7 +1067,6 @@
     vector_grad = jnp.concatenate([vector_grad, vector_grad[4:]], 0)
     unit_all = total[8 * width :].reshape(4 * heads, unit_part.shape[1])
     unit_grad = lax.dynamic_slice_in_dim(unit_all, ten * 2 * heads, 2 * heads, 0)
-    outputs, input_grad = finish(place, out_own, out_other, g_sum, g_other, x_own, d_own)
     qkv_grad, qkv_new, qkv_change = adam_heads(ctx_scalar, fixes, qkv_weight, qkv_moments, attn_terms, attn_theirs)
     dense_grad, dense_new, dense_change = adam(
         ctx_scalar, fixes, dense_weight, dense_moments, attn_terms, attn_theirs, tile=head_cols, first=n_qkv

time: 562 us -> 554 us (0.986)
    unnamed x125 -> x121, local copies, waits for them, and re-layouts: 24.6 us -> 20.2 us
  transfers between devices with their start and end apart: 55 -> 55, of which waited for: 14 -> 15; matrix products, arithmetic and copies ran while one was open for 3% -> 3% of each run, Pallas kernels for 53% -> 54%
where the time goes in v5:
time: 554 us; the launch traced here: 548 us
  Pallas kernels  311 us (56%)
  waiting for transfers between devices  149 us (27%)
  starting transfers between devices  48.7 us (9%)
  local copies, waits for them, and re-layouts  25.6 us (5%)
  other arithmetic  10.7 us (2%)
    pallas_call x50, Pallas kernels, ordered_call(): *results, token = run(*operands, *waits)  311 us
    ppermute x55, waiting for transfers between devices, along(): return lambda v: lax.ppermute(v, axis, [(i, i ^ bit) for i in range(size)])  149 us
    ppermute x55, starting transfers between devices, along(): return lambda v: lax.ppermute(v, axis, [(i, i ^ bit) for i in range(size)])  48.7 us
    unnamed x121, local copies, waits for them, and re-layouts  20.2 us
  transfers between devices with their start and end apart: 55, of which 15 were waited for; matrix products, arithmetic and copies ran while one was open for 3% of the time, Pallas kernels for 54%

profile of v5, /device:TPU:0, one launch (start us, length us, event | category | flops | bytes accessed | tf_op | source)
XLA Modules:
  0.0 547.8 jit_solution(1358631592801553381)
XLA Ops:
  14.7 6.3 %arrange.1 = (bf16[512,2048]{1,0:T(8,128)(2,1)}, bf16[512,2048]{1,0:T(8,128)(2,1)}, f32[6,2048]{1,0:T(8,128)}, f32[8,128]{1,0:T(8,128)}) custom-call(s32[33]{0:T(128)} %stack.134.refs_0_, bf16[512,2048]{1,0:T(8,128)(2,1)} %bitcast.93, bf16[512,2048]{1,0:T(8,128)(2,1)} %bitcast.95, bf16[6,2048]{1,0:T(8,128)(2,1)} %refs_3_.7, f32[8,128]{1,0:T(8,128)} %get-tuple-element.168.refs_4_), custom_call_target="tpu_custom_call" | custom-call | flops 20000000000 | bytes 1 | tf_op jit(solution)/shard_map/arrange/pallas_call | solution.py:82
  22.9 4.6 norm.2
  27.5 17.0 %collective-permute-done.refs_0_.refs_1_ = bf16[128,6144]{1,0:T(8,128)(2,1)S(1)} collective-permute-done((bf16[128,6144]{1,0:T(8,128)(2,1)}, bf16[128,6144]{1,0:T(8,128)(2,1)S(1)}, u32[]{:S(2)}, u32[]{:S(2)}) %collective-permute-start) | collective-permute-done | bytes 1572896 | tf_op jit(solution)/shard_map/ppermute | solution.py:892
  51.7 7.7 %collective-permute-done.4.refs_4_.refs_0_ = bf16[128,4096]{1,0:T(8,128)(2,1)S(1)} collective-permute-done((bf16[128,4096]{1,0:T(8,128)(2,1)}, bf16[128,4096]{1,0:T(8,128)(2,1)S(1)}, u32[]{:S(2)}, u32[]{:S(2)}) %collective-permute-start.4) | collective-permute-done | bytes 1048608 | tf_op jit(solution)/shard_map/ppermute | solution.py:892
  68.6 19.7 %collective-permute-done.5.refs_3_.refs_0_ = bf16[128,2048]{1,0:T(8,128)(2,1)S(1)} collective-permute-done((bf16[128,2048]{1,0:T(8,128)(2,1)}, bf16[128,2048]{1,0:T(8,128)(2,1)S(1)}, u32[]{:S(2)}, u32[]{:S(2)}) %collective-permute-start.5) | collective-permute-done | bytes 524320 | tf_op jit(solution)/shard_map/ppermute | solution.py:892
  108.9 6.9 %collective-permute-done.8.refs_3_ = bf16[64,4096]{1,0:T(8,128)(2,1)S(1)} collective-permute-done((bf16[64,4096]{1,0:T(8,128)(2,1)}, bf16[64,4096]{1,0:T(8,128)(2,1)S(1)}, u32[]{:S(2)}, u32[]{:S(2)}) %collective-permute-start.8) | collective-permute-done | bytes 524320 | tf_op jit(solution)/shard_map/ppermute | solution.py:892
  129.1 10.9 %hidden.2 = (bf16[512,2048]{1,0:T(8,128)(2,1)}, f32[512,2048]{1,0:T(8,128)}, f32[8,128]{1,0:T(8,128)}) custom-call(bf16[512,2048]{1,0:T(8,128)(2,1)} %get-tuple-element.172.refs_0_, f32[1,2048]{1,0:T(1,128)} %bitcast.103, bf16[512,2048]{1,0:T(8,128)(2,1)} %get-tuple-element.182.refs_2_.refs_14_, bf16[512,2048]{1,0:T(8,128)(2,1)} %get-tuple-element.189.refs_3_.refs_15_, ...), custom_call_target="tpu_custom_call" | custom-call | flops 49999998976 | bytes 1 | tf_op jit(solution)/shard_map/hidden/pallas_call | solution.py:82
  150.8 9.8 %d_hidden.2 = (bf16[512,2048]{1,0:T(8,128)(2,1)}, f32[8,2048]{1,0:T(8,128)}, f32[8,128]{1,0:T(8,128)}) custom-call(bf16[512,2048]{1,0:T(8,128)(2,1)} %get-tuple-element.195.refs_0_.refs_4_.refs_3_.refs_6_, f32[512,2048]{1,0:T(8,128)} %get-tuple-element.196.refs_1_, bf16[512,2048]{1,0:T(8,128)(2,1)} %get-tuple-element.197.refs_2_.refs_3_, ...), custom_call_target="tpu_custom_call" | custom-call | flops 2000000000 | bytes 1 | tf_op jit(solution)/shard_map/d_hidden/pallas_call | solution.py:82
  160.7 20.5 %collective-permute-done.15.refs_1_ = bf16[256,2048]{1,0:T(8,128)(2,1)} collective-permute-done((bf16[256,2048]{1,0:T(8,128)(2,1)}, bf16[256,2048]{1,0:T(8,128)(2,1)}, u32[]{:S(2)}, u32[]{:S(2)}) %collective-permute-start.15) | collective-permute-done | bytes 1048608 | tf_op jit(solution)/shard_map/ppermute | solution.py:892
  184.2 4.6 norm.3
  188.8 10.8 %hidden.3 = (bf16[512,2048]{1,0:T(8,128)(2,1)}, f32[512,2048]{1,0:T(8,128)}, f32[8,128]{1,0:T(8,128)}) custom-call(bf16[512,2048]{1,0:T(8,128)(2,1)} %get-tuple-element.207.refs_0_.refs_1_, f32[1,2048]{1,0:T(1,128)} %bitcast.104, bf16[512,2048]{1,0:T(8,128)(2,1)} %get-tuple-element.182.refs_2_.refs_14_, ...), custom_call_target="tpu_custom_call" | custom-call | flops 20000000000 | bytes 1 | tf_op jit(solution)/shard_map/hidden/pallas_call | solution.py:82
  201.4 18.2 %attend.1 = (bf16[1024,512]{1,0:T(8,128)(2,1)}, bf16[1024,1536]{1,0:T(8,128)(2,1)}, f32[1024,256]{1,0:T(8,128)}, f32[8,128]{1,0:T(8,128)}) custom-call(s32[1]{0:T(128)} %bitcast.28.refs_0_, bf16[512,2048]{1,0:T(8,128)(2,1)} %get-tuple-element.210.refs_1_.refs_0_, bf16[512,2048]{1,0:T(8,128)(2,1)} %get-tuple-element.211.refs_2_.refs_1_, f32[1,1536]{1,0:T(1,128)} %bitcast.105, ...), custom_call_target="tpu_custom_call" | custom-call | flops 49999998976 | bytes 1 | tf_op jit(solution)/shard_map/attend/pallas_call | solution.py:82
  219.5 18.4 %branch.1 = (f32[256,2048]{1,0:T(8,128)}, bf16[256,2048]{1,0:T(8,128)(2,1)}, f32[256,2048]{1,0:T(8,128)}, bf16[256,2048]{1,0:T(8,128)(2,1)}, f32[8,128]{1,0:T(8,128)}) custom-call(bf16[512,2048]{1,0:T(8,128)(2,1)} %get-tuple-element.193.refs_0_.refs_6_, bf16[512,2048]{1,0:T(8,128)(2,1)} %get-tuple-element.209.refs_1_.refs_7_, ...), custom_call_target="tpu_custom_call" | custom-call | flops 20000000000 | bytes 1 | tf_op jit(solution)/shard_map/branch/pallas_call | solution.py:82
  242.8 9.8 %d_hidden.3 = (bf16[512,2048]{1,0:T(8,128)(2,1)}, f32[8,2048]{1,0:T(8,128)}, f32[8,128]{1,0:T(8,128)}) custom-call(bf16[512,2048]{1,0:T(8,128)(2,1)} %get-tuple-element.224.refs_0_.refs_5_.refs_4_, f32[512,2048]{1,0:T(8,128)} %get-tuple-element.225.refs_1_, bf16[512,2048]{1,0:T(8,128)(2,1)} %get-tuple-element.197.refs_2_.refs_3_, ...), custom_call_target="tpu_custom_call" | custom-call | flops 49999998976 | bytes 1 | tf_op jit(solution)/shard_map/d_hidden/pallas_call | solution.py:82
  253.5 18.8 %grad_far.2 = (bf16[256,4096]{1,0:T(8,128)(2,1)}, bf16[256,4096]{1,0:T(8,128)(2,1)}, bf16[256,4096]{1,0:T(8,128)(2,1)}, bf16[256,4096]{1,0:T(8,128)(2,1)}, f32[8,128]{1,0:T(8,128)}) custom-call(bf16[512,2048]{1,0:T(8,128)(2,1)} %get-tuple-element.172.refs_0_, bf16[512,2048]{1,0:T(8,128)(2,1)} %get-tuple-element.207.refs_0_.refs_1_, ...), custom_call_target="tpu_custom_call" | custom-call | bytes 1 | tf_op jit(solution)/shard_map/grad_far/pallas_call | solution.py:82
  277.3 14.2 %attend_back.1 = (bf16[1024,1536]{1,0:T(8,128)(2,1)}, f32[8,1536]{1,0:T(8,128)}, f32[8,128]{1,0:T(8,128)}) custom-call(s32[1]{0:T(128)} %bitcast.28.refs_0_, bf16[1024,1536]{1,0:T(8,128)(2,1)} %get-tuple-element.231.refs_1_, f32[1024,256]{1,0:T(8,128)} %get-tuple-element.232.refs_2_, bf16[512,2048]{1,0:T(8,128)(2,1)} %get-tuple-element.195.refs_0_.refs_4_.refs_3_.refs_6_, ...), custom_call_target="tpu_custom_call" | custom-call | flops 49999998976 | bytes 1 | tf_op jit(solution)/shard_map/attend_back/pallas_call | solution.py:82
  292.4 4.4 collective-permute-start.26
  296.8 21.4 %grad_near.2 = (bf16[256,4096]{1,0:T(8,128)(2,1)}, bf16[256,4096]{1,0:T(8,128)(2,1)}, bf16[256,4096]{1,0:T(8,128)(2,1)}, bf16[256,4096]{1,0:T(8,128)(2,1)}, f32[8,128]{1,0:T(8,128)}) custom-call(bf16[512,2048]{1,0:T(8,128)(2,1)} %get-tuple-element.172.refs_0_, bf16[512,2048]{1,0:T(8,128)(2,1)} %get-tuple-element.207.refs_0_.refs_1_, ...), custom_call_target="tpu_custom_call" | custom-call | bytes 1 | tf_op jit(solution)/shard_map/grad_near/pallas_call | solution.py:82
  321.1 26.2 %input_grad.1 = (f32[256,2048]{1,0:T(8,128)}, bf16[256,2048]{1,0:T(8,128)(2,1)}, f32[256,2048]{1,0:T(8,128)}, bf16[256,2048]{1,0:T(8,128)(2,1)}, f32[8,2048]{1,0:T(8,128)}, /*index=5*/f32[8,128]{1,0:T(8,128)}) custom-call(bf16[1024,1536]{1,0:T(8,128)(2,1)} %get-tuple-element.234.refs_0_.refs_2_.refs_3_, ...), custom_call_target="tpu_custom_call" | custom-call | flops 2000000000 | bytes 1 | tf_op jit(solution)/shard_map/input_grad/pallas_call | solution.py:82
  351.0 11.0 %grad_far.3 = (bf16[256,2048]{1,0:T(8,128)(2,1)}, bf16[256,2048]{1,0:T(8,128)(2,1)}, bf16[256,2048]{1,0:T(8,128)(2,1)}, bf16[256,2048]{1,0:T(8,128)(2,1)}, f32[8,128]{1,0:T(8,128)}) custom-call(bf16[512,2048]{1,0:T(8,128)(2,1)} %get-tuple-element.210.refs_1_.refs_0_, bf16[512,2048]{1,0:T(8,128)(2,1)} %get-tuple-element.211.refs_2_.refs_1_, ...), custom_call_target="tpu_custom_call" | custom-call | bytes 1 | tf_op jit(solution)/shard_map/grad_far/pallas_call | solution.py:82
  372.2 3.8 totals.12
  375.9 10.8 %collective-permute-done.42.refs_1_ = f32[240,128]{1,0:T(8,128)S(1)} collective-permute-done((f32[240,128]{1,0:T(8,128)S(1)}, f32[240,128]{1,0:T(8,128)S(1)}, u32[]{:S(2)}, u32[]{:S(2)}) %collective-permute-start.42) | collective-permute-done | bytes 122912 | tf_op jit(solution)/shard_map/ppermute | solution.py:892
  398.8 12.8 %grad_near.3 = (bf16[256,2048]{1,0:T(8,128)(2,1)}, bf16[256,2048]{1,0:T(8,128)(2,1)}, bf16[256,2048]{1,0:T(8,128)(2,1)}, bf16[256,2048]{1,0:T(8,128)(2,1)}, f32[8,128]{1,0:T(8,128)}) custom-call(bf16[512,2048]{1,0:T(8,128)(2,1)} %get-tuple-element.210.refs_1_.refs_0_, bf16[512,2048]{1,0:T(8,128)(2,1)} %get-tuple-element.211.refs_2_.refs_1_, ...), custom_call_target="tpu_custom_call" | custom-call | bytes 1 | tf_op jit(solution)/shard_map/grad_near/pallas_call | solution.py:82
  411.6 4.3 collective-permute-done.37.refs_2_
  421.5 10.4 %collective-permute-done.32.refs_1_ = bf16[256,2048]{1,0:T(8,128)(2,1)S(1)} collective-permute-done((bf16[256,2048]{1,0:T(8,128)(2,1)}, bf16[256,2048]{1,0:T(8,128)(2,1)S(1)}, u32[]{:S(2)}, u32[]{:S(2)}) %collective-permute-start.32) | collective-permute-done | bytes 1048608 | tf_op jit(solution)/shard_map/ppermute | solution.py:892
  432.8 12.4 %collective-permute-done.36.refs_2_ = bf16[256,2048]{1,0:T(8,128)(2,1)S(1)} collective-permute-done((bf16[256,2048]{1,0:T(8,128)(2,1)}, bf16[256,2048]{1,0:T(8,128)(2,1)S(1)}, u32[]{:S(2)}, u32[]{:S(2)}) %collective-permute-start.36) | collective-permute-done | bytes 1048608 | tf_op jit(solution)/shard_map/ppermute | solution.py:892
  451.5 25.4 %collective-permute-done.31.refs_5_.refs_2_ = bf16[256,2048]{1,0:T(8,128)(2,1)S(1)} collective-permute-done((bf16[256,2048]{1,0:T(8,128)(2,1)}, bf16[256,2048]{1,0:T(8,128)(2,1)S(1)}, u32[]{:S(2)}, u32[]{:S(2)}) %collective-permute-start.31) | collective-permute-done | bytes 1048608 | tf_op jit(solution)/shard_map/ppermute | solution.py:892
  488.9 4.8 collective-permute-done.51.refs_2_
  506.3 6.7 %adam.3 = (f32[128,4096]{1,0:T(8,128)}, f32[2,128,4096]{2,1,0:T(8,128)}, f32[128,4096]{1,0:T(8,128)}, f32[8,128]{1,0:T(8,128)}) custom-call(s32[1]{0:T(128)} %bitcast.27.refs_0_, f32[2]{0:T(128)} %pad_maximum_fusion.5.refs_1_, bf16[128,4096]{1,0:T(8,128)(2,1)} %refs_2_.10, f32[2,128,4096]{2,1,0:T(8,128)} %refs_3_.8, ...), custom_call_target="tpu_custom_call" | custom-call | bytes 1 | tf_op jit(solution)/shard_map/adam/pallas_call | solution.py:82
  512.9 6.7 %adam.4 = (f32[128,4096]{1,0:T(8,128)}, f32[2,128,4096]{2,1,0:T(8,128)}, f32[128,4096]{1,0:T(8,128)}, f32[8,128]{1,0:T(8,128)}) custom-call(s32[1]{0:T(128)} %bitcast.27.refs_0_, f32[2]{0:T(128)} %pad_maximum_fusion.5.refs_1_, bf16[128,4096]{1,0:T(8,128)(2,1)} %refs_2_.11, f32[2,128,4096]{2,1,0:T(8,128)} %refs_3_.9, ...), custom_call_target="tpu_custom_call" | custom-call | flops 2000000000 | bytes 1 | tf_op jit(solution)/shard_map/adam/pallas_call | solution.py:82
  519.7 9.1 %finish.1 = (bf16[512,2048]{1,0:T(8,128)(2,1)}, f32[512,2048]{1,0:T(8,128)}, f32[8,128]{1,0:T(8,128)}) custom-call(s32[33]{0:T(128)} %stack.134.refs_0_, bf16[256,2048]{1,0:T(8,128)(2,1)} %get-tuple-element.249.refs_1_, bf16[256,2048]{1,0:T(8,128)(2,1)} %copy-done.28, bf16[256,2048]{1,0:T(8,128)(2,1)} %get-tuple-element.275.refs_3_, ...), custom_call_target="tpu_custom_call" | custom-call | flops 500000000 | bytes 1 | tf_op jit(solution)/shard_map/finish/pallas_call | solution.py:82
  537.2 7.6 %adam_heads.1 = (f32[128,4,768]{2,1,0:T(4,128)}, f32[2,128,4,768]{3,2,1,0:T(4,128)}, f32[128,4,768]{2,1,0:T(4,128)}, f32[8,128]{1,0:T(8,128)}) custom-call(s32[1]{0:T(128)} %bitcast.27.refs_0_, f32[2]{0:T(128)} %pad_maximum_fusion.5.refs_1_, bf16[128,4,768]{2,1,0:T(4,128)(2,1)} %refs_2_.12, f32[2,128,4,768]{3,2,1,0:T(4,128)} %refs_3_.10, ...), custom_call_target="tpu_custom_call" | custom-call | bytes 1 | tf_op jit(solution)/shard_map/adam_heads/pallas_call | solution.py:82
  (285 shorter events, 169.7 us)
Async XLA Ops:
  7.0 37.6 %collective-permute-start = (bf16[128,6144]{1,0:T(8,128)(2,1)}, bf16[128,6144]{1,0:T(8,128)(2,1)S(1)}, u32[]{:S(2)}, u32[]{:S(2)}) collective-permute-start(bf16[128,6144]{1,0:T(8,128)(2,1)} %get-tuple-element.173.refs_0_), channel_id=1, source_target_pairs={{0,16},{4,20},{8,24},{12,28},{16,0},{20,4},{24,8},{28,12},{1,17},{... | collective-permute-start | bytes 4718600 | tf_op jit(solution)/shard_map/ppermute | solution.py:892
  10.0 36.2 %collective-permute-start.1 = (bf16[128,6144]{1,0:T(8,128)(2,1)}, bf16[128,6144]{1,0:T(8,128)(2,1)}, u32[]{:S(2)}, u32[]{:S(2)}) collective-permute-start(bf16[128,6144]{1,0:T(8,128)(2,1)} %get-tuple-element.173.refs_0_), channel_id=1, source_target_pairs={{0,8},{4,12},{8,0},{12,4},{16,24},{20,28},{24,16},{28,20},{1,9},{5... | collective-permute-start | bytes 4718600 | tf_op jit(solution)/shard_map/ppermute | solution.py:892
  11.4 47.9 %collective-permute-start.4 = (bf16[128,4096]{1,0:T(8,128)(2,1)}, bf16[128,4096]{1,0:T(8,128)(2,1)S(1)}, u32[]{:S(2)}, u32[]{:S(2)}) collective-permute-start(bf16[128,4096]{1,0:T(8,128)(2,1)} %get-tuple-element.178), channel_id=1, source_target_pairs={{0,2},{2,0},{1,3},{3,1},{4,6},{6,4},{5,7},{7,5},{8,10},{10,8},{9,1... | collective-permute-start | bytes 3145736 | tf_op jit(solution)/shard_map/ppermute | solution.py:892
  48.8 43.4 %collective-permute-start.2 = (bf16[64,6144]{1,0:T(8,128)(2,1)}, bf16[64,6144]{1,0:T(8,128)(2,1)S(1)}, u32[]{:S(2)}, u32[]{:S(2)}) collective-permute-start(bf16[64,6144]{1,0:T(8,128)(2,1)} %get-tuple-element.175), channel_id=1, source_target_pairs={{0,8},{4,12},{8,0},{12,4},{16,24},{20,28},{24,16},{28,20},{1,9},{5... | collective-permute-start | bytes 2359304 | tf_op jit(solution)/shard_map/ppermute | solution.py:892
  50.3 42.5 %collective-permute-start.3 = (bf16[64,6144]{1,0:T(8,128)(2,1)}, bf16[64,6144]{1,0:T(8,128)(2,1)S(1)}, u32[]{:S(2)}, u32[]{:S(2)}) collective-permute-start(bf16[64,6144]{1,0:T(8,128)(2,1)} %get-tuple-element.176), channel_id=1, source_target_pairs={{0,16},{4,20},{8,24},{12,28},{16,0},{20,4},{24,8},{28,12},{1,17},{... | collective-permute-start | bytes 2359304 | tf_op jit(solution)/shard_map/ppermute | solution.py:892
  67.0 32.6 %collective-permute-start.6 = (bf16[128,4096]{1,0:T(8,128)(2,1)S(1)}, bf16[128,4096]{1,0:T(8,128)(2,1)S(1)}, u32[]{:S(2)}, u32[]{:S(2)}) collective-permute-start(bf16[128,4096]{1,0:T(8,128)(2,1)S(1)} %copy-done.5), channel_id=1, source_target_pairs={{0,8},{4,12},{8,0},{12,4},{16,24},{20,28},{24,16},{28,20},{1,9},{5... | collective-permute-start | bytes 3145736 | tf_op jit(solution)/shard_map/ppermute | solution.py:892
  67.6 32.1 %collective-permute-start.7 = (bf16[128,4096]{1,0:T(8,128)(2,1)S(1)}, bf16[128,4096]{1,0:T(8,128)(2,1)S(1)}, u32[]{:S(2)}, u32[]{:S(2)}) collective-permute-start(bf16[128,4096]{1,0:T(8,128)(2,1)S(1)} %copy-done.5), channel_id=1, source_target_pairs={{0,16},{4,20},{8,24},{12,28},{16,0},{20,4},{24,8},{28,12},{1,17},{... | collective-permute-start | bytes 3145736 | tf_op jit(solution)/shard_map/ppermute | solution.py:892
  92.2 47.7 %collective-permute-start.14 = (bf16[256,2048]{1,0:T(8,128)(2,1)}, bf16[256,2048]{1,0:T(8,128)(2,1)}, u32[]{:S(2)}, u32[]{:S(2)}) collective-permute-start(bf16[256,2048]{1,0:T(8,128)(2,1)} %get-tuple-element.194), channel_id=1, source_target_pairs={{0,2},{2,0},{1,3},{3,1},{4,6},{6,4},{5,7},{7,5},{8,10},{10,8},{9,1... | collective-permute-start | bytes 3145736 | tf_op jit(solution)/shard_map/ppermute | solution.py:892
  92.2 27.5 %collective-permute-start.12 = (bf16[128,2048]{1,0:T(8,128)(2,1)}, bf16[128,2048]{1,0:T(8,128)(2,1)S(1)}, u32[]{:S(2)}, u32[]{:S(2)}) collective-permute-start(bf16[128,2048]{1,0:T(8,128)(2,1)} %copy-done.31), channel_id=1, source_target_pairs={{0,16},{4,20},{8,24},{12,28},{16,0},{20,4},{24,8},{28,12},{1,17},{... | collective-permute-start | bytes 1572872 | tf_op jit(solution)/shard_map/ppermute | solution.py:892
  92.8 27.3 %collective-permute-start.13 = (bf16[128,2048]{1,0:T(8,128)(2,1)}, bf16[128,2048]{1,0:T(8,128)(2,1)}, u32[]{:S(2)}, u32[]{:S(2)}) collective-permute-start(bf16[128,2048]{1,0:T(8,128)(2,1)} %copy-done.31), channel_id=1, source_target_pairs={{0,8},{4,12},{8,0},{12,4},{16,24},{20,28},{24,16},{28,20},{1,9},{5... | collective-permute-start | bytes 1572872 | tf_op jit(solution)/shard_map/ppermute | solution.py:892
  115.9 34.9 %collective-permute-start.16 = (bf16[512,2048]{1,0:T(8,128)(2,1)}, bf16[512,2048]{1,0:T(8,128)(2,1)}, u32[]{:S(2)}, u32[]{:S(2)}) collective-permute-start(bf16[512,2048]{1,0:T(8,128)(2,1)} %get-tuple-element.197.refs_2_.refs_3_), channel_id=1, source_target_pairs={{0,4},{4,0},{8,12},{12,8},{16,20},{20,16},{24,28},{28,24},{1,5},{5... | collective-permute-start | bytes 6291464 | tf_op jit(solution)/shard_map/ppermute | solution.py:892
  140.0 59.7 %collective-permute-start.20 = (bf16[512,2048]{1,0:T(8,128)(2,1)S(1)}, bf16[512,2048]{1,0:T(8,128)(2,1)S(1)}, u32[]{:S(2)}, u32[]{:S(2)}) collective-permute-start(bf16[512,2048]{1,0:T(8,128)(2,1)S(1)} %copy-done.12), channel_id=1, source_target_pairs={{0,4},{4,0},{8,12},{12,8},{16,20},{20,16},{24,28},{28,24},{1,5},{5... | collective-permute-start | bytes 6291464 | tf_op jit(solution)/shard_map/ppermute | solution.py:892
  140.1 41.1 %collective-permute-start.15 = (bf16[256,2048]{1,0:T(8,128)(2,1)}, bf16[256,2048]{1,0:T(8,128)(2,1)}, u32[]{:S(2)}, u32[]{:S(2)}) collective-permute-start(bf16[256,2048]{1,0:T(8,128)(2,1)} %collective-permute-done.14.refs_3_.refs_0_), channel_id=1, source_target_pairs={{0,1},{1,0},{2,3},{3,2},{4,5},{5,4},{6,7},{7,6},{8,9},{9,8},{10,11... | collective-permute-start | bytes 3145736 | tf_op jit(solution)/shard_map/ppermute | solution.py:892
  150.4 49.2 %collective-permute-start.22 = (bf16[256,2048]{1,0:T(8,128)(2,1)}, bf16[256,2048]{1,0:T(8,128)(2,1)S(1)}, u32[]{:S(2)}, u32[]{:S(2)}) collective-permute-start(bf16[256,2048]{1,0:T(8,128)(2,1)} %get-tuple-element.215), channel_id=1, source_target_pairs={{0,2},{2,0},{1,3},{3,1},{4,6},{6,4},{5,7},{7,5},{8,10},{10,8},{9,1... | collective-permute-start | bytes 3145736 | tf_op jit(solution)/shard_map/ppermute | solution.py:892
  150.8 48.9 %collective-permute-start.21 = (bf16[512,2048]{1,0:T(8,128)(2,1)S(1)}, bf16[512,2048]{1,0:T(8,128)(2,1)}, u32[]{:S(2)}, u32[]{:S(2)}) collective-permute-start(bf16[512,2048]{1,0:T(8,128)(2,1)S(1)} %copy-done.16), channel_id=1, source_target_pairs={{0,4},{4,0},{8,12},{12,8},{16,20},{20,16},{24,28},{28,24},{1,5},{5... | collective-permute-start | bytes 6291464 | tf_op jit(solution)/shard_map/ppermute | solution.py:892
  199.6 40.1 %collective-permute-start.25 = (bf16[256,2048]{1,0:T(8,128)(2,1)S(1)}, bf16[256,2048]{1,0:T(8,128)(2,1)}, u32[]{:S(2)}, u32[]{:S(2)}) collective-permute-start(bf16[256,2048]{1,0:T(8,128)(2,1)S(1)} %collective-permute-done.22.refs_11_.refs_0_), channel_id=1, source_target_pairs={{0,1},{1,0},{2,3},{3,2},{4,5},{5,4},{6,7},{7,6},{8,9},{9,8},{10,11... | collective-permute-start | bytes 3145736 | tf_op jit(solution)/shard_map/ppermute | solution.py:892
  237.9 35.4 %collective-permute-start.24 = (bf16[256,2048]{1,0:T(8,128)(2,1)}, bf16[256,2048]{1,0:T(8,128)(2,1)S(1)}, u32[]{:S(2)}, u32[]{:S(2)}) collective-permute-start(bf16[256,2048]{1,0:T(8,128)(2,1)} %get-tuple-element.221), channel_id=1, source_target_pairs={{0,1},{1,0},{2,3},{3,2},{4,5},{5,4},{6,7},{7,6},{8,9},{9,8},{10,11... | collective-permute-start | bytes 3145736 | tf_op jit(solution)/shard_map/ppermute | solution.py:892
  274.3 45.9 %collective-permute-start.23 = (bf16[256,2048]{1,0:T(8,128)(2,1)}, bf16[256,2048]{1,0:T(8,128)(2,1)S(1)}, u32[]{:S(2)}, u32[]{:S(2)}) collective-permute-start(bf16[256,2048]{1,0:T(8,128)(2,1)} %get-tuple-element.219), channel_id=1, source_target_pairs={{0,1},{1,0},{2,3},{3,2},{4,5},{5,4},{6,7},{7,6},{8,9},{9,8},{10,11... | collective-permute-start | bytes 3145736 | tf_op jit(solution)/shard_map/ppermute | solution.py:892
  292.4 70.0 %collective-permute-start.26 = (bf16[256,2048]{1,0:T(8,128)(2,1)}, bf16[256,2048]{1,0:T(8,128)(2,1)}, u32[]{:S(2)}, u32[]{:S(2)}) collective-permute-start(bf16[256,2048]{1,0:T(8,128)(2,1)} %get-tuple-element.230), channel_id=1, source_target_pairs={{0,2},{2,0},{1,3},{3,1},{4,6},{6,4},{5,7},{7,5},{8,10},{10,8},{9,1... | collective-permute-start | bytes 3145736 | tf_op jit(solution)/shard_map/ppermute | solution.py:892
  318.1 47.4 %collective-permute-start.34 = (bf16[256,4096]{1,0:T(8,128)(2,1)}, bf16[256,4096]{1,0:T(8,128)(2,1)}, u32[]{:S(2)}, u32[]{:S(2)}) collective-permute-start(bf16[256,4096]{1,0:T(8,128)(2,1)} %get-tuple-element.255), channel_id=1, source_target_pairs={{0,16},{4,20},{8,24},{12,28},{16,0},{20,4},{24,8},{28,12},{1,17},{... | collective-permute-start | bytes 6291464 | tf_op jit(solution)/shard_map/ppermute | solution.py:892
  318.7 48.2 %collective-permute-start.35 = (bf16[256,4096]{1,0:T(8,128)(2,1)}, bf16[256,4096]{1,0:T(8,128)(2,1)S(1)}, u32[]{:S(2)}, u32[]{:S(2)}) collective-permute-start(bf16[256,4096]{1,0:T(8,128)(2,1)} %get-tuple-element.257), channel_id=1, source_target_pairs={{0,8},{4,12},{8,0},{12,4},{16,24},{20,28},{24,16},{28,20},{1,9},{5... | collective-permute-start | bytes 6291464 | tf_op jit(solution)/shard_map/ppermute | solution.py:892
  362.3 28.1 %collective-permute-start.38 = (bf16[256,2048]{1,0:T(8,128)(2,1)}, bf16[256,2048]{1,0:T(8,128)(2,1)S(1)}, u32[]{:S(2)}, u32[]{:S(2)}) collective-permute-start(bf16[256,2048]{1,0:T(8,128)(2,1)} %get-tuple-element.262), channel_id=1, source_target_pairs={{0,4},{4,0},{8,12},{12,8},{16,20},{20,16},{24,28},{28,24},{1,5},{5... | collective-permute-start | bytes 3145736 | tf_op jit(solution)/shard_map/ppermute | solution.py:892
  362.3 28.8 %collective-permute-start.39 = (bf16[256,2048]{1,0:T(8,128)(2,1)}, bf16[256,2048]{1,0:T(8,128)(2,1)}, u32[]{:S(2)}, u32[]{:S(2)}) collective-permute-start(bf16[256,2048]{1,0:T(8,128)(2,1)} %get-tuple-element.263), channel_id=1, source_target_pairs={{0,4},{4,0},{8,12},{12,8},{16,20},{20,16},{24,28},{28,24},{1,5},{5... | collective-permute-start | bytes 3145736 | tf_op jit(solution)/shard_map/ppermute | solution.py:892
  367.0 28.3 %collective-permute-start.40 = (bf16[256,2048]{1,0:T(8,128)(2,1)}, bf16[256,2048]{1,0:T(8,128)(2,1)S(1)}, u32[]{:S(2)}, u32[]{:S(2)}) collective-permute-start(bf16[256,2048]{1,0:T(8,128)(2,1)} %get-tuple-element.264), channel_id=1, source_target_pairs={{0,4},{4,0},{8,12},{12,8},{16,20},{20,16},{24,28},{28,24},{1,5},{5... | collective-permute-start | bytes 3145736 | tf_op jit(solution)/shard_map/ppermute | solution.py:892
  389.0 42.9 %collective-permute-start.32 = (bf16[256,2048]{1,0:T(8,128)(2,1)}, bf16[256,2048]{1,0:T(8,128)(2,1)S(1)}, u32[]{:S(2)}, u32[]{:S(2)}) collective-permute-start(bf16[256,2048]{1,0:T(8,128)(2,1)} %get-tuple-element.251), channel_id=1, source_target_pairs={{0,1},{1,0},{2,3},{3,2},{4,5},{5,4},{6,7},{7,6},{8,9},{9,8},{10,11... | collective-permute-start | bytes 3145736 | tf_op jit(solution)/shard_map/ppermute | solution.py:892
  395.3 49.8 %collective-permute-start.36 = (bf16[256,2048]{1,0:T(8,128)(2,1)}, bf16[256,2048]{1,0:T(8,128)(2,1)S(1)}, u32[]{:S(2)}, u32[]{:S(2)}) collective-permute-start(bf16[256,2048]{1,0:T(8,128)(2,1)} %get-tuple-element.260), channel_id=1, source_target_pairs={{0,2},{2,0},{1,3},{3,1},{4,6},{6,4},{5,7},{7,5},{8,10},{10,8},{9,1... | collective-permute-start | bytes 3145736 | tf_op jit(solution)/shard_map/ppermute | solution.py:892
  397.3 79.5 %collective-permute-start.31 = (bf16[256,2048]{1,0:T(8,128)(2,1)}, bf16[256,2048]{1,0:T(8,128)(2,1)S(1)}, u32[]{:S(2)}, u32[]{:S(2)}) collective-permute-start(bf16[256,2048]{1,0:T(8,128)(2,1)} %get-tuple-element.249.refs_1_), channel_id=1, source_target_pairs={{0,1},{1,0},{2,3},{3,2},{4,5},{5,4},{6,7},{7,6},{8,9},{9,8},{10,11... | collective-permute-start | bytes 3145736 | tf_op jit(solution)/shard_map/ppermute | solution.py:892
  415.9 61.0 %collective-permute-start.48 = (bf16[256,2048]{1,0:T(8,128)(2,1)}, bf16[256,2048]{1,0:T(8,128)(2,1)S(1)}, u32[]{:S(2)}, u32[]{:S(2)}) collective-permute-start(bf16[256,2048]{1,0:T(8,128)(2,1)} %get-tuple-element.281), channel_id=1, source_target_pairs={{0,16},{4,20},{8,24},{12,28},{16,0},{20,4},{24,8},{28,12},{1,17},{... | collective-permute-start | bytes 3145736 | tf_op jit(solution)/shard_map/ppermute | solution.py:892
  417.3 59.6 %collective-permute-start.49 = (bf16[256,2048]{1,0:T(8,128)(2,1)}, bf16[256,2048]{1,0:T(8,128)(2,1)S(1)}, u32[]{:S(2)}, u32[]{:S(2)}) collective-permute-start(bf16[256,2048]{1,0:T(8,128)(2,1)} %get-tuple-element.283), channel_id=1, source_target_pairs={{0,8},{4,12},{8,0},{12,4},{16,24},{20,28},{24,16},{28,20},{1,9},{5... | collective-permute-start | bytes 3145736 | tf_op jit(solution)/shard_map/ppermute | solution.py:892
  431.9 73.4 %collective-permute-start.45 = (bf16[128,4096]{1,0:T(8,128)(2,1)}, bf16[128,4096]{1,0:T(8,128)(2,1)S(1)}, u32[]{:S(2)}, u32[]{:S(2)}) collective-permute-start(bf16[128,4096]{1,0:T(8,128)(2,1)} %get-tuple-element.276), channel_id=1, source_target_pairs={{0,2},{2,0},{1,3},{3,1},{4,6},{6,4},{5,7},{7,5},{8,10},{10,8},{9,1... | collective-permute-start | bytes 3145736 | tf_op jit(solution)/shard_map/ppermute | solution.py:892
  449.2 70.4 %collective-permute-start.44 = (bf16[256,2048]{1,0:T(8,128)(2,1)}, bf16[256,2048]{1,0:T(8,128)(2,1)}, u32[]{:S(2)}, u32[]{:S(2)}) collective-permute-start(bf16[256,2048]{1,0:T(8,128)(2,1)} %get-tuple-element.275.refs_3_), channel_id=1, source_target_pairs={{0,1},{1,0},{2,3},{3,2},{4,5},{5,4},{6,7},{7,6},{8,9},{9,8},{10,11... | collective-permute-start | bytes 3145736 | tf_op jit(solution)/shard_map/ppermute | solution.py:892
  502.1 34.3 %collective-permute-start.53 = (bf16[128,2048]{1,0:T(8,128)(2,1)}, bf16[128,2048]{1,0:T(8,128)(2,1)S(1)}, u32[]{:S(2)}, u32[]{:S(2)}) collective-permute-start(bf16[128,2048]{1,0:T(8,128)(2,1)} %get-tuple-element.296), channel_id=1, source_target_pairs={{0,2},{2,0},{1,3},{3,1},{4,6},{6,4},{5,7},{7,5},{8,10},{10,8},{9,1... | collective-permute-start | bytes 1572872 | tf_op jit(solution)/shard_map/ppermute | solution.py:892
  (80 other events, 718.6 us)

commit v6 on v5

--- a/solution.py
+++ b/solution.py
@@ -39,7 +39,7 @@
 
 BLOCK = 128
 MIB = 1024 * 1024
-COSTS = [50, 50, 20, 0.5, 0.5, 0, 0.5, 5, 5, 0, 50, 0, 50, 2, 50, 20, 0, 2, 50, 5, 20, 50, 20, 0.5, 50, 0, 5, 50, 0, 2, 10, 0, 0, 0.5, 10, 0, 0, 0.5, 0, 0, 2, 0, 0, 0, 0, 2, 0.5, 0, 0, 0.5, 10, 0, 0, 0, 20, 0.5, 0, 10, 5, 2, 2, 10, 0, 50, 5, 2]
+COSTS = [0.5, 50, 10, 0.5, 20, 0, 0.5, 5, 5, 0, 50, 50, 50, 10, 50, 20, 0, 0.5, 50, 50, 0.5, 2, 20, 0.5, 50, 2, 0, 50, 0, 2, 10, 0, 0, 0.5, 20, 50, 0, 0.5, 0, 20, 2, 0, 0, 0, 0, 2, 0, 0.5, 0, 0.5, 50, 0, 0, 0, 20, 0.5, 0, 10, 5, 2, 2, 10, 0, 50, 10, 20]
 
 
 def whole(shape):
@@ -642,9 +642,8 @@
     )(d_linear, h0, h1, *xs, *means, *invs, vec, *attn, *up)
 
 
-def grad_kernel(pairs, near, *refs):
-    operands, refs = refs[: 4 * pairs], refs[4 * pairs :]
-    adds, outs = (refs[:4], refs[4:]) if near else (None, refs)
+def grad_kernel(pairs, added, pieces, *refs):
+    operands, adds, outs = refs[: 4 * pairs], refs[4 * pairs : 4 * pairs + added], refs[4 * pairs + added :]
     j = pl.program_id(0)
     col = 0
     for k in range(pairs):
@@ -652,17 +651,19 @@
         part = dot(l0, r0, 0, 0) + dot(l1, r1, 0, 0)
         cols = slice(col, col + part.shape[1])
         col += part.shape[1]
-        for i, out_ref in enumerate(outs):
+        half = part.shape[0] // 2
+        for i, places in enumerate(pieces):
 
             @pl.when(j == i)
-            def _(i=i, out_ref=out_ref, part=part, cols=cols):
-                if near:
-                    out_ref[:, cols] = (part + adds[i][:, cols].astype(F32)).astype(BF)
-                else:
-                    out_ref[:, cols] = part.astype(BF)
-
-
-def grad_of(factors, adds=()):
+            def _(i=i, places=places, part=part, cols=cols):
+                for k in range(added):
+                    if k == i * added // 4:
+                        part = part + adds[k][:, cols].astype(F32)
+                for side, (piece, block) in enumerate(places):
+                    outs[piece][block * half : (block + 1) * half, cols] = part[side * half : (side + 1) * half].astype(BF)
+
+
+def grad_of(factors, pieces, sizes, adds=()):
     width = factors[0][0].shape[1]
     tile = width // 8
     first = 0 if adds else 4
@@ -679,13 +680,17 @@
         n += cols
         flops += 2 * rows * width * cols
         nbytes += 2 * rows * (width + 2 * cols)
-    in_specs += [whole((tile, n)) for _ in adds]
-    return call(
-        functools.partial(grad_kernel, len(factors), bool(adds)),
+    each = 4 // max(len(adds), 1)
+    in_specs += [
+        pl.BlockSpec((tile, n), lambda j, k=k: (jnp.clip(j - k * each, 0, each - 1), 0)) for k in range(len(adds))
+    ]
+    shapes = [(size * tile // 2, n) for size in sizes]
+    return call(
+        functools.partial(grad_kernel, len(factors), len(adds), pieces),
         (4,),
         in_specs,
-        [whole((tile, n))] * 4,
-        [like((tile, n), BF)] * 4,
+        [whole(shape) for shape in shapes],
+        [like(shape, BF) for shape in shapes],
         "grad_near" if adds else "grad_far",
         flops,
         nbytes + width * n,
@@ -979,16 +984,18 @@
     branch_near = to_ten(branch_own[1])
     d_oth = pack(width, d_first, d_second)
 
-    def far_parts(factors):
-        parts = grad_of(factors)
+    def far_parts(factors, count):
+        each = 4 // count
+        steps = [[(k // each, k % each * 2), (k // each, k % each * 2 + 1)] for k in range(4)]
+        parts = grad_of(factors, steps, (2 * each,) * count)
         return [to_core(part) for part in parts] if fast else parts
 
     def near_parts(factors, far):
-        if fast:
-            a_own, a_x, b_own, b_y = grad_of(factors, far)
-            return a_own, b_own, to_y(b_y), to_x(a_x)
-        near = grad_of(factors, [jnp.zeros_like(part) for part in far])
-        return lax.psum_scatter(jnp.concatenate([*near, *far], 0), "shard", scatter_dimension=0, tiled=True)
+        if not fast:
+            (near,) = grad_of(factors, [[(0, 2 * k), (0, 2 * k + 1)] for k in range(4)], (8,), [jnp.zeros_like(part) for part in far])
+            return lax.psum_scatter(jnp.concatenate([near, *far], 0), "shard", scatter_dimension=0, tiled=True)
+        a_own, a_x, b_own, b_y = grad_of(factors, [[(k, 0), (k, 1)] for k in range(4)], (2, 2, 2, 2), far)
+        return a_own, b_own, to_y(b_y), to_x(a_x)
 
     def second(parts):
         if not fast:
@@ -1009,7 +1016,7 @@
 
     low_oth, sum_oth = d_hidden_of(d_oth, w_down, slope_oth)
     unit_factors = [(mlp_own, mlp_oth, (low_own, 0), (low_oth, 0)), (d_own, d_oth, (active_own, 0), (active_oth, 0))]
-    unit_far = far_parts(unit_factors)
+    unit_far = far_parts(unit_factors, 2)
     branch_far = to_ctx(fold(cross, branch_keep, branch_got))
     d_linear, unit_sums = attend_back(z_scalar, packed_qkv, logs, d_own, d_oth, w_attn, cosine, sine)
     unit_pieces = near_parts(unit_factors, unit_far)
@@ -1037,7 +1044,7 @@
         (total,) = totals(total.shape[0], ((total, 0), (moved, 0)), dtype=F32)
         return total, moves[0](total) if moves else None
 
-    attn_far = far_parts(attn_factors)
+    attn_far = far_parts(attn_factors, 2)
     out_bias = (vec[4] + vec[5]).reshape(1, width)
     (out_own,) = totals(quarter, ((branch_own[0], 0), (branch_near, 0), (branch_far, 0), (x_own, 0), (out_bias, 0)), steps=2)
     out_other = to_ten(out_own)

time: 554 us -> 533 us (0.962)
  waiting for transfers between devices: 149 us -> 133 us
  starting transfers between devices: 48.7 us -> 42.9 us
    ppermute x55 -> x51, waiting for transfers between devices: 149 us -> 133 us  [along(): return lambda v: lax.ppermute(v, axis, [(i, i ^ bit) for i in range(size)])]
    ppermute x55 -> x51, starting transfers between devices: 48.7 us -> 42.9 us  [along(): return lambda v: lax.ppermute(v, axis, [(i, i ^ bit) for i in range(size)])]
    unnamed x121 -> x111, local copies, waits for them, and re-layouts: 20.2 us -> 21 us
  transfers between devices with their start and end apart: 55 -> 51, of which waited for: 15 -> 14; matrix products, arithmetic and copies ran while one was open for 3% -> 3% of each run, Pallas kernels for 54% -> 56%
where the time goes in v6:
time: 533 us; the launch traced here: 524 us
  Pallas kernels  309 us (58%)
  waiting for transfers between devices  133 us (25%)
  starting transfers between devices  42.9 us (8%)
  local copies, waits for them, and re-layouts  26.5 us (5%)
  other arithmetic  10.4 us (2%)
    pallas_call x50, Pallas kernels, ordered_call(): *results, token = run(*operands, *waits)  309 us
    ppermute x51, waiting for transfers between devices, along(): return lambda v: lax.ppermute(v, axis, [(i, i ^ bit) for i in range(size)])  133 us
    ppermute x51, starting transfers between devices, along(): return lambda v: lax.ppermute(v, axis, [(i, i ^ bit) for i in range(size)])  42.9 us
    unnamed x111, local copies, waits for them, and re-layouts  21 us
  transfers between devices with their start and end apart: 51, of which 14 were waited for; matrix products, arithmetic and copies ran while one was open for 3% of the time, Pallas kernels for 56%

profile of v6, /device:TPU:0, one launch (start us, length us, event | category | flops | bytes accessed | tf_op | source)
XLA Modules:
  0.0 524.4 jit_solution(6427419426062715797)
XLA Ops:
  3.2 3.8 cut.4
  14.9 6.2 %arrange.1 = (bf16[512,2048]{1,0:T(8,128)(2,1)}, bf16[512,2048]{1,0:T(8,128)(2,1)}, f32[6,2048]{1,0:T(8,128)}, f32[8,128]{1,0:T(8,128)}) custom-call(s32[33]{0:T(128)} %stack.134.refs_0_, bf16[512,2048]{1,0:T(8,128)(2,1)} %bitcast.93, bf16[512,2048]{1,0:T(8,128)(2,1)} %bitcast.95, bf16[6,2048]{1,0:T(8,128)(2,1)} %refs_3_.7, f32[8,128]{1,0:T(8,128)} %get-tuple-element.164.refs_4_), custom_call_target="tpu_custom_call" | custom-call | flops 10000000000 | bytes 1 | tf_op jit(solution)/shard_map/arrange/pallas_call | solution.py:82
  21.1 4.6 norm.2
  28.8 15.7 %collective-permute-done.refs_0_.refs_1_ = bf16[128,6144]{1,0:T(8,128)(2,1)S(1)} collective-permute-done((bf16[128,6144]{1,0:T(8,128)(2,1)}, bf16[128,6144]{1,0:T(8,128)(2,1)S(1)}, u32[]{:S(2)}, u32[]{:S(2)}) %collective-permute-start) | collective-permute-done | bytes 1572896 | tf_op jit(solution)/shard_map/ppermute | solution.py:897
  54.3 5.1 collective-permute-done.4.refs_4_.refs_0_
  66.1 22.1 %collective-permute-done.5.refs_3_.refs_0_ = bf16[128,2048]{1,0:T(8,128)(2,1)S(1)} collective-permute-done((bf16[128,2048]{1,0:T(8,128)(2,1)}, bf16[128,2048]{1,0:T(8,128)(2,1)S(1)}, u32[]{:S(2)}, u32[]{:S(2)}) %collective-permute-start.5) | collective-permute-done | bytes 524320 | tf_op jit(solution)/shard_map/ppermute | solution.py:897
  108.7 6.9 %collective-permute-done.8.refs_3_ = bf16[64,4096]{1,0:T(8,128)(2,1)S(1)} collective-permute-done((bf16[64,4096]{1,0:T(8,128)(2,1)}, bf16[64,4096]{1,0:T(8,128)(2,1)S(1)}, u32[]{:S(2)}, u32[]{:S(2)}) %collective-permute-start.8) | collective-permute-done | bytes 524320 | tf_op jit(solution)/shard_map/ppermute | solution.py:897
  129.0 11.1 %hidden.2 = (bf16[512,2048]{1,0:T(8,128)(2,1)}, f32[512,2048]{1,0:T(8,128)}, f32[8,128]{1,0:T(8,128)}) custom-call(bf16[512,2048]{1,0:T(8,128)(2,1)} %get-tuple-element.168.refs_0_, f32[1,2048]{1,0:T(1,128)} %bitcast.102, bf16[512,2048]{1,0:T(8,128)(2,1)} %get-tuple-element.178.refs_2_.refs_14_, bf16[512,2048]{1,0:T(8,128)(2,1)} %get-tuple-element.185.refs_3_.refs_15_, ...), custom_call_target="tpu_custom_call" | custom-call | flops 49999998976 | bytes 1 | tf_op jit(solution)/shard_map/hidden/pallas_call | solution.py:82
  151.1 9.8 %d_hidden.2 = (bf16[512,2048]{1,0:T(8,128)(2,1)}, f32[8,2048]{1,0:T(8,128)}, f32[8,128]{1,0:T(8,128)}) custom-call(bf16[512,2048]{1,0:T(8,128)(2,1)} %get-tuple-element.191.refs_0_.refs_4_.refs_3_.refs_6_, f32[512,2048]{1,0:T(8,128)} %get-tuple-element.192.refs_1_, bf16[512,2048]{1,0:T(8,128)(2,1)} %get-tuple-element.193.refs_2_.refs_3_, ...), custom_call_target="tpu_custom_call" | custom-call | flops 500000000 | bytes 1 | tf_op jit(solution)/shard_map/d_hidden/pallas_call | solution.py:82
  160.9 20.4 %collective-permute-done.15.refs_1_ = bf16[256,2048]{1,0:T(8,128)(2,1)} collective-permute-done((bf16[256,2048]{1,0:T(8,128)(2,1)}, bf16[256,2048]{1,0:T(8,128)(2,1)}, u32[]{:S(2)}, u32[]{:S(2)}) %collective-permute-start.15) | collective-permute-done | bytes 1048608 | tf_op jit(solution)/shard_map/ppermute | solution.py:897
  184.3 4.6 norm.3
  189.0 10.8 %hidden.3 = (bf16[512,2048]{1,0:T(8,128)(2,1)}, f32[512,2048]{1,0:T(8,128)}, f32[8,128]{1,0:T(8,128)}) custom-call(bf16[512,2048]{1,0:T(8,128)(2,1)} %get-tuple-element.203.refs_0_.refs_1_, f32[1,2048]{1,0:T(1,128)} %bitcast.103, bf16[512,2048]{1,0:T(8,128)(2,1)} %get-tuple-element.178.refs_2_.refs_14_, ...), custom_call_target="tpu_custom_call" | custom-call | flops 500000000 | bytes 1 | tf_op jit(solution)/shard_map/hidden/pallas_call | solution.py:82
  201.5 17.8 %attend.1 = (bf16[1024,512]{1,0:T(8,128)(2,1)}, bf16[1024,1536]{1,0:T(8,128)(2,1)}, f32[1024,256]{1,0:T(8,128)}, f32[8,128]{1,0:T(8,128)}) custom-call(s32[1]{0:T(128)} %bitcast.28.refs_0_, bf16[512,2048]{1,0:T(8,128)(2,1)} %get-tuple-element.206.refs_1_.refs_0_, bf16[512,2048]{1,0:T(8,128)(2,1)} %get-tuple-element.207.refs_2_.refs_1_, f32[1,1536]{1,0:T(1,128)} %bitcast.104, ...), custom_call_target="tpu_custom_call" | custom-call | flops 2000000000 | bytes 1 | tf_op jit(solution)/shard_map/attend/pallas_call | solution.py:82
  219.3 18.8 %branch.1 = (f32[256,2048]{1,0:T(8,128)}, bf16[256,2048]{1,0:T(8,128)(2,1)}, f32[256,2048]{1,0:T(8,128)}, bf16[256,2048]{1,0:T(8,128)(2,1)}, f32[8,128]{1,0:T(8,128)}) custom-call(bf16[512,2048]{1,0:T(8,128)(2,1)} %get-tuple-element.189.refs_0_.refs_6_, bf16[512,2048]{1,0:T(8,128)(2,1)} %get-tuple-element.205.refs_1_.refs_7_, ...), custom_call_target="tpu_custom_call" | custom-call | flops 20000000000 | bytes 1 | tf_op jit(solution)/shard_map/branch/pallas_call | solution.py:82
  242.9 9.8 %d_hidden.3 = (bf16[512,2048]{1,0:T(8,128)(2,1)}, f32[8,2048]{1,0:T(8,128)}, f32[8,128]{1,0:T(8,128)}) custom-call(bf16[512,2048]{1,0:T(8,128)(2,1)} %get-tuple-element.220.refs_0_.refs_5_.refs_4_, f32[512,2048]{1,0:T(8,128)} %get-tuple-element.221.refs_1_, bf16[512,2048]{1,0:T(8,128)(2,1)} %get-tuple-element.193.refs_2_.refs_3_, ...), custom_call_target="tpu_custom_call" | custom-call | flops 49999998976 | bytes 1 | tf_op jit(solution)/shard_map/d_hidden/pallas_call | solution.py:82
  253.6 18.4 %grad_far.2 = (bf16[512,4096]{1,0:T(8,128)(2,1)}, bf16[512,4096]{1,0:T(8,128)(2,1)}, f32[8,128]{1,0:T(8,128)}) custom-call(bf16[512,2048]{1,0:T(8,128)(2,1)} %get-tuple-element.168.refs_0_, bf16[512,2048]{1,0:T(8,128)(2,1)} %get-tuple-element.203.refs_0_.refs_1_, bf16[512,2048]{1,0:T(8,128)(2,1)} %get-tuple-element.218.refs_2_.refs_1_, ...), custom_call_target="tpu_custom_call" | custom-call | flops 2000000000 | bytes 1 | tf_op jit(solution)/shard_map/grad_far/pallas_call | solution.py:82
  276.6 14.2 %attend_back.1 = (bf16[1024,1536]{1,0:T(8,128)(2,1)}, f32[8,1536]{1,0:T(8,128)}, f32[8,128]{1,0:T(8,128)}) custom-call(s32[1]{0:T(128)} %bitcast.28.refs_0_, bf16[1024,1536]{1,0:T(8,128)(2,1)} %get-tuple-element.227.refs_1_, f32[1024,256]{1,0:T(8,128)} %get-tuple-element.228.refs_2_, bf16[512,2048]{1,0:T(8,128)(2,1)} %get-tuple-element.191.refs_0_.refs_4_.refs_3_.refs_6_, ...), custom_call_target="tpu_custom_call" | custom-call | flops 49999998976 | bytes 1 | tf_op jit(solution)/shard_map/attend_back/pallas_call | solution.py:82
  291.6 4.4 collective-permute-start.26
  296.0 20.4 %grad_near.2 = (bf16[256,4096]{1,0:T(8,128)(2,1)}, bf16[256,4096]{1,0:T(8,128)(2,1)}, bf16[256,4096]{1,0:T(8,128)(2,1)}, bf16[256,4096]{1,0:T(8,128)(2,1)}, f32[8,128]{1,0:T(8,128)}) custom-call(bf16[512,2048]{1,0:T(8,128)(2,1)} %get-tuple-element.168.refs_0_, bf16[512,2048]{1,0:T(8,128)(2,1)} %get-tuple-element.203.refs_0_.refs_1_, ...), custom_call_target="tpu_custom_call" | custom-call | bytes 1 | tf_op jit(solution)/shard_map/grad_near/pallas_call | solution.py:82
  319.4 26.0 %input_grad.1 = (f32[256,2048]{1,0:T(8,128)}, bf16[256,2048]{1,0:T(8,128)(2,1)}, f32[256,2048]{1,0:T(8,128)}, bf16[256,2048]{1,0:T(8,128)(2,1)}, f32[8,2048]{1,0:T(8,128)}, /*index=5*/f32[8,128]{1,0:T(8,128)}) custom-call(bf16[1024,1536]{1,0:T(8,128)(2,1)} %get-tuple-element.230.refs_0_.refs_2_.refs_3_, ...), custom_call_target="tpu_custom_call" | custom-call | flops 2000000000 | bytes 1 | tf_op jit(solution)/shard_map/input_grad/pallas_call | solution.py:82
  349.4 11.2 %grad_far.3 = (bf16[512,2048]{1,0:T(8,128)(2,1)}, bf16[512,2048]{1,0:T(8,128)(2,1)}, f32[8,128]{1,0:T(8,128)}) custom-call(bf16[512,2048]{1,0:T(8,128)(2,1)} %get-tuple-element.206.refs_1_.refs_0_, bf16[512,2048]{1,0:T(8,128)(2,1)} %get-tuple-element.207.refs_2_.refs_1_, bf16[1024,1536]{1,0:T(8,128)(2,1)} %get-tuple-element.230.refs_0_.refs_2_.refs_3_, ...), custom_call_target="tpu_custom_call" | custom-call | bytes 1 | tf_op jit(solution)/shard_map/grad_far/pallas_call | solution.py:82
  367.1 3.7 totals.12
  370.8 4.5 collective-permute-done.31.refs_1_
  383.2 12.1 %grad_near.3 = (bf16[256,2048]{1,0:T(8,128)(2,1)}, bf16[256,2048]{1,0:T(8,128)(2,1)}, bf16[256,2048]{1,0:T(8,128)(2,1)}, bf16[256,2048]{1,0:T(8,128)(2,1)}, f32[8,128]{1,0:T(8,128)}) custom-call(bf16[512,2048]{1,0:T(8,128)(2,1)} %get-tuple-element.206.refs_1_.refs_0_, bf16[512,2048]{1,0:T(8,128)(2,1)} %get-tuple-element.207.refs_2_.refs_1_, ...), custom_call_target="tpu_custom_call" | custom-call | bytes 1 | tf_op jit(solution)/shard_map/grad_near/pallas_call | solution.py:82
  397.4 4.4 collective-permute-done.39.refs_4_.refs_6_
  406.8 7.1 %collective-permute-done.30.refs_1_ = bf16[256,2048]{1,0:T(8,128)(2,1)S(1)} collective-permute-done((bf16[256,2048]{1,0:T(8,128)(2,1)S(1)}, bf16[256,2048]{1,0:T(8,128)(2,1)S(1)}, u32[]{:S(2)}, u32[]{:S(2)}) %collective-permute-start.30) | collective-permute-done | bytes 1048608 | tf_op jit(solution)/shard_map/ppermute | solution.py:897
  413.8 13.3 %collective-permute-done.34.refs_2_ = bf16[256,2048]{1,0:T(8,128)(2,1)S(1)} collective-permute-done((bf16[256,2048]{1,0:T(8,128)(2,1)}, bf16[256,2048]{1,0:T(8,128)(2,1)S(1)}, u32[]{:S(2)}, u32[]{:S(2)}) %collective-permute-start.34) | collective-permute-done | bytes 1048608 | tf_op jit(solution)/shard_map/ppermute | solution.py:897
  433.5 25.3 %collective-permute-done.29.refs_5_.refs_2_ = bf16[256,2048]{1,0:T(8,128)(2,1)S(1)} collective-permute-done((bf16[256,2048]{1,0:T(8,128)(2,1)}, bf16[256,2048]{1,0:T(8,128)(2,1)S(1)}, u32[]{:S(2)}, u32[]{:S(2)}) %collective-permute-start.29) | collective-permute-done | bytes 1048608 | tf_op jit(solution)/shard_map/ppermute | solution.py:897
  482.6 6.7 %adam.3 = (f32[128,4096]{1,0:T(8,128)}, f32[2,128,4096]{2,1,0:T(8,128)}, f32[128,4096]{1,0:T(8,128)}, f32[8,128]{1,0:T(8,128)}) custom-call(s32[1]{0:T(128)} %bitcast.27.refs_0_, f32[2]{0:T(128)} %pad_maximum_fusion.5.refs_1_, bf16[128,4096]{1,0:T(8,128)(2,1)} %refs_2_.10, f32[2,128,4096]{2,1,0:T(8,128)} %refs_3_.8, ...), custom_call_target="tpu_custom_call" | custom-call | bytes 1 | tf_op jit(solution)/shard_map/adam/pallas_call | solution.py:82
  489.2 6.7 %adam.4 = (f32[128,4096]{1,0:T(8,128)}, f32[2,128,4096]{2,1,0:T(8,128)}, f32[128,4096]{1,0:T(8,128)}, f32[8,128]{1,0:T(8,128)}) custom-call(s32[1]{0:T(128)} %bitcast.27.refs_0_, f32[2]{0:T(128)} %pad_maximum_fusion.5.refs_1_, bf16[128,4096]{1,0:T(8,128)(2,1)} %refs_2_.11, f32[2,128,4096]{2,1,0:T(8,128)} %refs_3_.9, ...), custom_call_target="tpu_custom_call" | custom-call | flops 2000000000 | bytes 1 | tf_op jit(solution)/shard_map/adam/pallas_call | solution.py:82
  495.9 9.2 %finish.1 = (bf16[512,2048]{1,0:T(8,128)(2,1)}, f32[512,2048]{1,0:T(8,128)}, f32[8,128]{1,0:T(8,128)}) custom-call(s32[33]{0:T(128)} %stack.134.refs_0_, bf16[256,2048]{1,0:T(8,128)(2,1)} %get-tuple-element.243.refs_1_, bf16[256,2048]{1,0:T(8,128)(2,1)} %copy-done.24, bf16[256,2048]{1,0:T(8,128)(2,1)} %get-tuple-element.267.refs_3_, ...), custom_call_target="tpu_custom_call" | custom-call | bytes 1 | tf_op jit(solution)/shard_map/finish/pallas_call | solution.py:82
  513.5 7.6 %adam_heads.1 = (f32[128,4,768]{2,1,0:T(4,128)}, f32[2,128,4,768]{3,2,1,0:T(4,128)}, f32[128,4,768]{2,1,0:T(4,128)}, f32[8,128]{1,0:T(8,128)}) custom-call(s32[1]{0:T(128)} %bitcast.27.refs_0_, f32[2]{0:T(128)} %pad_maximum_fusion.5.refs_1_, bf16[128,4,768]{2,1,0:T(4,128)(2,1)} %refs_2_.12, f32[2,128,4,768]{3,2,1,0:T(4,128)} %refs_3_.10, ...), custom_call_target="tpu_custom_call" | custom-call | bytes 1 | tf_op jit(solution)/shard_map/adam_heads/pallas_call | solution.py:82
  (267 shorter events, 159.3 us)
Async XLA Ops:
  7.0 37.6 %collective-permute-start = (bf16[128,6144]{1,0:T(8,128)(2,1)}, bf16[128,6144]{1,0:T(8,128)(2,1)S(1)}, u32[]{:S(2)}, u32[]{:S(2)}) collective-permute-start(bf16[128,6144]{1,0:T(8,128)(2,1)} %get-tuple-element.169.refs_0_), channel_id=1, source_target_pairs={{0,16},{4,20},{8,24},{12,28},{16,0},{20,4},{24,8},{28,12},{1,17},{... | collective-permute-start | bytes 4718600 | tf_op jit(solution)/shard_map/ppermute | solution.py:897
  10.0 36.2 %collective-permute-start.1 = (bf16[128,6144]{1,0:T(8,128)(2,1)}, bf16[128,6144]{1,0:T(8,128)(2,1)}, u32[]{:S(2)}, u32[]{:S(2)}) collective-permute-start(bf16[128,6144]{1,0:T(8,128)(2,1)} %get-tuple-element.169.refs_0_), channel_id=1, source_target_pairs={{0,8},{4,12},{8,0},{12,4},{16,24},{20,28},{24,16},{28,20},{1,9},{5... | collective-permute-start | bytes 4718600 | tf_op jit(solution)/shard_map/ppermute | solution.py:897
  11.5 47.9 %collective-permute-start.4 = (bf16[128,4096]{1,0:T(8,128)(2,1)}, bf16[128,4096]{1,0:T(8,128)(2,1)S(1)}, u32[]{:S(2)}, u32[]{:S(2)}) collective-permute-start(bf16[128,4096]{1,0:T(8,128)(2,1)} %get-tuple-element.174), channel_id=1, source_target_pairs={{0,2},{2,0},{1,3},{3,1},{4,6},{6,4},{5,7},{7,5},{8,10},{10,8},{9,1... | collective-permute-start | bytes 3145736 | tf_op jit(solution)/shard_map/ppermute | solution.py:897
  48.9 43.2 %collective-permute-start.2 = (bf16[64,6144]{1,0:T(8,128)(2,1)}, bf16[64,6144]{1,0:T(8,128)(2,1)}, u32[]{:S(2)}, u32[]{:S(2)}) collective-permute-start(bf16[64,6144]{1,0:T(8,128)(2,1)} %get-tuple-element.171), channel_id=1, source_target_pairs={{0,8},{4,12},{8,0},{12,4},{16,24},{20,28},{24,16},{28,20},{1,9},{5... | collective-permute-start | bytes 2359304 | tf_op jit(solution)/shard_map/ppermute | solution.py:897
  50.3 42.3 %collective-permute-start.3 = (bf16[64,6144]{1,0:T(8,128)(2,1)}, bf16[64,6144]{1,0:T(8,128)(2,1)}, u32[]{:S(2)}, u32[]{:S(2)}) collective-permute-start(bf16[64,6144]{1,0:T(8,128)(2,1)} %get-tuple-element.172), channel_id=1, source_target_pairs={{0,16},{4,20},{8,24},{12,28},{16,0},{20,4},{24,8},{28,12},{1,17},{... | collective-permute-start | bytes 2359304 | tf_op jit(solution)/shard_map/ppermute | solution.py:897
  63.0 25.1 %collective-permute-start.5 = (bf16[128,2048]{1,0:T(8,128)(2,1)}, bf16[128,2048]{1,0:T(8,128)(2,1)S(1)}, u32[]{:S(2)}, u32[]{:S(2)}) collective-permute-start(bf16[128,2048]{1,0:T(8,128)(2,1)} %get-tuple-element.176), channel_id=1, source_target_pairs={{0,2},{2,0},{1,3},{3,1},{4,6},{6,4},{5,7},{7,5},{8,10},{10,8},{9,1... | collective-permute-start | bytes 1572872 | tf_op jit(solution)/shard_map/ppermute | solution.py:897
  64.6 34.4 %collective-permute-start.6 = (bf16[128,4096]{1,0:T(8,128)(2,1)}, bf16[128,4096]{1,0:T(8,128)(2,1)S(1)}, u32[]{:S(2)}, u32[]{:S(2)}) collective-permute-start(bf16[128,4096]{1,0:T(8,128)(2,1)} %copy-done.18), channel_id=1, source_target_pairs={{0,8},{4,12},{8,0},{12,4},{16,24},{20,28},{24,16},{28,20},{1,9},{5... | collective-permute-start | bytes 3145736 | tf_op jit(solution)/shard_map/ppermute | solution.py:897
  65.1 33.8 %collective-permute-start.7 = (bf16[128,4096]{1,0:T(8,128)(2,1)}, bf16[128,4096]{1,0:T(8,128)(2,1)S(1)}, u32[]{:S(2)}, u32[]{:S(2)}) collective-permute-start(bf16[128,4096]{1,0:T(8,128)(2,1)} %copy-done.18), channel_id=1, source_target_pairs={{0,16},{4,20},{8,24},{12,28},{16,0},{20,4},{24,8},{28,12},{1,17},{... | collective-permute-start | bytes 3145736 | tf_op jit(solution)/shard_map/ppermute | solution.py:897
  92.1 48.0 %collective-permute-start.14 = (bf16[256,2048]{1,0:T(8,128)(2,1)}, bf16[256,2048]{1,0:T(8,128)(2,1)}, u32[]{:S(2)}, u32[]{:S(2)}) collective-permute-start(bf16[256,2048]{1,0:T(8,128)(2,1)} %get-tuple-element.190), channel_id=1, source_target_pairs={{0,2},{2,0},{1,3},{3,1},{4,6},{6,4},{5,7},{7,5},{8,10},{10,8},{9,1... | collective-permute-start | bytes 3145736 | tf_op jit(solution)/shard_map/ppermute | solution.py:897
  92.1 27.5 %collective-permute-start.12 = (bf16[128,2048]{1,0:T(8,128)(2,1)}, bf16[128,2048]{1,0:T(8,128)(2,1)S(1)}, u32[]{:S(2)}, u32[]{:S(2)}) collective-permute-start(bf16[128,2048]{1,0:T(8,128)(2,1)} %copy-done.25), channel_id=1, source_target_pairs={{0,16},{4,20},{8,24},{12,28},{16,0},{20,4},{24,8},{28,12},{1,17},{... | collective-permute-start | bytes 1572872 | tf_op jit(solution)/shard_map/ppermute | solution.py:897
  92.6 27.3 %collective-permute-start.13 = (bf16[128,2048]{1,0:T(8,128)(2,1)}, bf16[128,2048]{1,0:T(8,128)(2,1)S(1)}, u32[]{:S(2)}, u32[]{:S(2)}) collective-permute-start(bf16[128,2048]{1,0:T(8,128)(2,1)} %copy-done.25), channel_id=1, source_target_pairs={{0,8},{4,12},{8,0},{12,4},{16,24},{20,28},{24,16},{28,20},{1,9},{5... | collective-permute-start | bytes 1572872 | tf_op jit(solution)/shard_map/ppermute | solution.py:897
  115.7 35.4 %collective-permute-start.16 = (bf16[512,2048]{1,0:T(8,128)(2,1)}, bf16[512,2048]{1,0:T(8,128)(2,1)}, u32[]{:S(2)}, u32[]{:S(2)}) collective-permute-start(bf16[512,2048]{1,0:T(8,128)(2,1)} %get-tuple-element.193.refs_2_.refs_3_), channel_id=1, source_target_pairs={{0,4},{4,0},{8,12},{12,8},{16,20},{20,16},{24,28},{28,24},{1,5},{5... | collective-permute-start | bytes 6291464 | tf_op jit(solution)/shard_map/ppermute | solution.py:897
  140.1 59.7 %collective-permute-start.20 = (bf16[512,2048]{1,0:T(8,128)(2,1)S(1)}, bf16[512,2048]{1,0:T(8,128)(2,1)S(1)}, u32[]{:S(2)}, u32[]{:S(2)}) collective-permute-start(bf16[512,2048]{1,0:T(8,128)(2,1)S(1)} %copy-done.4), channel_id=1, source_target_pairs={{0,4},{4,0},{8,12},{12,8},{16,20},{20,16},{24,28},{28,24},{1,5},{5... | collective-permute-start | bytes 6291464 | tf_op jit(solution)/shard_map/ppermute | solution.py:897
  140.2 41.1 %collective-permute-start.15 = (bf16[256,2048]{1,0:T(8,128)(2,1)}, bf16[256,2048]{1,0:T(8,128)(2,1)}, u32[]{:S(2)}, u32[]{:S(2)}) collective-permute-start(bf16[256,2048]{1,0:T(8,128)(2,1)} %collective-permute-done.14.refs_3_.refs_0_), channel_id=1, source_target_pairs={{0,1},{1,0},{2,3},{3,2},{4,5},{5,4},{6,7},{7,6},{8,9},{9,8},{10,11... | collective-permute-start | bytes 3145736 | tf_op jit(solution)/shard_map/ppermute | solution.py:897
  150.8 49.0 %collective-permute-start.22 = (bf16[256,2048]{1,0:T(8,128)(2,1)}, bf16[256,2048]{1,0:T(8,128)(2,1)S(1)}, u32[]{:S(2)}, u32[]{:S(2)}) collective-permute-start(bf16[256,2048]{1,0:T(8,128)(2,1)} %get-tuple-element.211), channel_id=1, source_target_pairs={{0,2},{2,0},{1,3},{3,1},{4,6},{6,4},{5,7},{7,5},{8,10},{10,8},{9,1... | collective-permute-start | bytes 3145736 | tf_op jit(solution)/shard_map/ppermute | solution.py:897
  151.1 48.8 %collective-permute-start.21 = (bf16[512,2048]{1,0:T(8,128)(2,1)S(1)}, bf16[512,2048]{1,0:T(8,128)(2,1)}, u32[]{:S(2)}, u32[]{:S(2)}) collective-permute-start(bf16[512,2048]{1,0:T(8,128)(2,1)S(1)} %copy-done.8), channel_id=1, source_target_pairs={{0,4},{4,0},{8,12},{12,8},{16,20},{20,16},{24,28},{28,24},{1,5},{5... | collective-permute-start | bytes 6291464 | tf_op jit(solution)/shard_map/ppermute | solution.py:897
  199.7 40.2 %collective-permute-start.25 = (bf16[256,2048]{1,0:T(8,128)(2,1)S(1)}, bf16[256,2048]{1,0:T(8,128)(2,1)}, u32[]{:S(2)}, u32[]{:S(2)}) collective-permute-start(bf16[256,2048]{1,0:T(8,128)(2,1)S(1)} %collective-permute-done.22.refs_11_.refs_0_), channel_id=1, source_target_pairs={{0,1},{1,0},{2,3},{3,2},{4,5},{5,4},{6,7},{7,6},{8,9},{9,8},{10,11... | collective-permute-start | bytes 3145736 | tf_op jit(solution)/shard_map/ppermute | solution.py:897
  238.1 34.7 %collective-permute-start.24 = (bf16[256,2048]{1,0:T(8,128)(2,1)}, bf16[256,2048]{1,0:T(8,128)(2,1)S(1)}, u32[]{:S(2)}, u32[]{:S(2)}) collective-permute-start(bf16[256,2048]{1,0:T(8,128)(2,1)} %get-tuple-element.217), channel_id=1, source_target_pairs={{0,1},{1,0},{2,3},{3,2},{4,5},{5,4},{6,7},{7,6},{8,9},{9,8},{10,11... | collective-permute-start | bytes 3145736 | tf_op jit(solution)/shard_map/ppermute | solution.py:897
  272.5 45.9 %collective-permute-start.23 = (bf16[256,2048]{1,0:T(8,128)(2,1)}, bf16[256,2048]{1,0:T(8,128)(2,1)S(1)}, u32[]{:S(2)}, u32[]{:S(2)}) collective-permute-start(bf16[256,2048]{1,0:T(8,128)(2,1)} %get-tuple-element.215), channel_id=1, source_target_pairs={{0,1},{1,0},{2,3},{3,2},{4,5},{5,4},{6,7},{7,6},{8,9},{9,8},{10,11... | collective-permute-start | bytes 3145736 | tf_op jit(solution)/shard_map/ppermute | solution.py:897
  291.6 69.4 %collective-permute-start.26 = (bf16[256,2048]{1,0:T(8,128)(2,1)}, bf16[256,2048]{1,0:T(8,128)(2,1)}, u32[]{:S(2)}, u32[]{:S(2)}) collective-permute-start(bf16[256,2048]{1,0:T(8,128)(2,1)} %get-tuple-element.226), channel_id=1, source_target_pairs={{0,2},{2,0},{1,3},{3,1},{4,6},{6,4},{5,7},{7,5},{8,10},{10,8},{9,1... | collective-permute-start | bytes 3145736 | tf_op jit(solution)/shard_map/ppermute | solution.py:897
  316.4 48.4 %collective-permute-start.32 = (bf16[256,4096]{1,0:T(8,128)(2,1)}, bf16[256,4096]{1,0:T(8,128)(2,1)}, u32[]{:S(2)}, u32[]{:S(2)}) collective-permute-start(bf16[256,4096]{1,0:T(8,128)(2,1)} %get-tuple-element.249), channel_id=1, source_target_pairs={{0,16},{4,20},{8,24},{12,28},{16,0},{20,4},{24,8},{28,12},{1,17},{... | collective-permute-start | bytes 6291464 | tf_op jit(solution)/shard_map/ppermute | solution.py:897
  316.9 48.3 %collective-permute-start.33 = (bf16[256,4096]{1,0:T(8,128)(2,1)}, bf16[256,4096]{1,0:T(8,128)(2,1)S(1)}, u32[]{:S(2)}, u32[]{:S(2)}) collective-permute-start(bf16[256,4096]{1,0:T(8,128)(2,1)} %get-tuple-element.251), channel_id=1, source_target_pairs={{0,8},{4,12},{8,0},{12,4},{16,24},{20,28},{24,16},{28,20},{1,9},{5... | collective-permute-start | bytes 6291464 | tf_op jit(solution)/shard_map/ppermute | solution.py:897
  346.3 29.0 %collective-permute-start.31 = (bf16[256,2048]{1,0:T(8,128)(2,1)}, bf16[256,2048]{1,0:T(8,128)(2,1)}, u32[]{:S(2)}, u32[]{:S(2)}) collective-permute-start(bf16[256,2048]{1,0:T(8,128)(2,1)} %get-tuple-element.247), channel_id=1, source_target_pairs={{0,1},{1,0},{2,3},{3,2},{4,5},{5,4},{6,7},{7,6},{8,9},{9,8},{10,11... | collective-permute-start | bytes 3145736 | tf_op jit(solution)/shard_map/ppermute | solution.py:897
  365.2 48.6 %collective-permute-start.30 = (bf16[256,2048]{1,0:T(8,128)(2,1)S(1)}, bf16[256,2048]{1,0:T(8,128)(2,1)S(1)}, u32[]{:S(2)}, u32[]{:S(2)}) collective-permute-start(bf16[256,2048]{1,0:T(8,128)(2,1)S(1)} %copy-done.41), channel_id=1, source_target_pairs={{0,1},{1,0},{2,3},{3,2},{4,5},{5,4},{6,7},{7,6},{8,9},{9,8},{10,11... | collective-permute-start | bytes 3145736 | tf_op jit(solution)/shard_map/ppermute | solution.py:897
  380.2 46.9 %collective-permute-start.34 = (bf16[256,2048]{1,0:T(8,128)(2,1)}, bf16[256,2048]{1,0:T(8,128)(2,1)S(1)}, u32[]{:S(2)}, u32[]{:S(2)}) collective-permute-start(bf16[256,2048]{1,0:T(8,128)(2,1)} %get-tuple-element.254), channel_id=1, source_target_pairs={{0,2},{2,0},{1,3},{3,1},{4,6},{6,4},{5,7},{7,5},{8,10},{10,8},{9,1... | collective-permute-start | bytes 3145736 | tf_op jit(solution)/shard_map/ppermute | solution.py:897
  381.9 49.4 %collective-permute-start.42 = (f32[240,128]{1,0:T(8,128)}, f32[240,128]{1,0:T(8,128)S(1)}, u32[]{:S(2)}, u32[]{:S(2)}) collective-permute-start(f32[240,128]{1,0:T(8,128)} %get-tuple-element.269.refs_0_), channel_id=1, source_target_pairs={{0,4},{4,0},{8,12},{12,8},{16,20},{20,16},{24,28},{28,24},{1,5},{5... | collective-permute-start | bytes 368648 | tf_op jit(solution)/shard_map/ppermute | solution.py:897
  396.6 62.2 %collective-permute-start.29 = (bf16[256,2048]{1,0:T(8,128)(2,1)}, bf16[256,2048]{1,0:T(8,128)(2,1)S(1)}, u32[]{:S(2)}, u32[]{:S(2)}) collective-permute-start(bf16[256,2048]{1,0:T(8,128)(2,1)} %get-tuple-element.243.refs_1_), channel_id=1, source_target_pairs={{0,1},{1,0},{2,3},{3,2},{4,5},{5,4},{6,7},{7,6},{8,9},{9,8},{10,11... | collective-permute-start | bytes 3145736 | tf_op jit(solution)/shard_map/ppermute | solution.py:897
  401.8 57.0 %collective-permute-start.44 = (bf16[256,2048]{1,0:T(8,128)(2,1)}, bf16[256,2048]{1,0:T(8,128)(2,1)S(1)}, u32[]{:S(2)}, u32[]{:S(2)}) collective-permute-start(bf16[256,2048]{1,0:T(8,128)(2,1)} %get-tuple-element.273), channel_id=1, source_target_pairs={{0,16},{4,20},{8,24},{12,28},{16,0},{20,4},{24,8},{28,12},{1,17},{... | collective-permute-start | bytes 3145736 | tf_op jit(solution)/shard_map/ppermute | solution.py:897
  413.8 45.0 %collective-permute-start.45 = (bf16[256,2048]{1,0:T(8,128)(2,1)}, bf16[256,2048]{1,0:T(8,128)(2,1)S(1)}, u32[]{:S(2)}, u32[]{:S(2)}) collective-permute-start(bf16[256,2048]{1,0:T(8,128)(2,1)} %get-tuple-element.275), channel_id=1, source_target_pairs={{0,8},{4,12},{8,0},{12,4},{16,24},{20,28},{24,16},{28,20},{1,9},{5... | collective-permute-start | bytes 3145736 | tf_op jit(solution)/shard_map/ppermute | solution.py:897
  427.1 54.4 %collective-permute-start.41 = (bf16[128,4096]{1,0:T(8,128)(2,1)}, bf16[128,4096]{1,0:T(8,128)(2,1)S(1)}, u32[]{:S(2)}, u32[]{:S(2)}) collective-permute-start(bf16[128,4096]{1,0:T(8,128)(2,1)} %get-tuple-element.268), channel_id=1, source_target_pairs={{0,2},{2,0},{1,3},{3,1},{4,6},{6,4},{5,7},{7,5},{8,10},{10,8},{9,1... | collective-permute-start | bytes 3145736 | tf_op jit(solution)/shard_map/ppermute | solution.py:897
  431.2 64.7 %collective-permute-start.40 = (bf16[256,2048]{1,0:T(8,128)(2,1)}, bf16[256,2048]{1,0:T(8,128)(2,1)}, u32[]{:S(2)}, u32[]{:S(2)}) collective-permute-start(bf16[256,2048]{1,0:T(8,128)(2,1)} %get-tuple-element.267.refs_3_), channel_id=1, source_target_pairs={{0,1},{1,0},{2,3},{3,2},{4,5},{5,4},{6,7},{7,6},{8,9},{9,8},{10,11... | collective-permute-start | bytes 3145736 | tf_op jit(solution)/shard_map/ppermute | solution.py:897
  481.6 31.1 %collective-permute-start.49 = (bf16[128,2048]{1,0:T(8,128)(2,1)}, bf16[128,2048]{1,0:T(8,128)(2,1)S(1)}, u32[]{:S(2)}, u32[]{:S(2)}) collective-permute-start(bf16[128,2048]{1,0:T(8,128)(2,1)} %get-tuple-element.288), channel_id=1, source_target_pairs={{0,2},{2,0},{1,3},{3,1},{4,6},{6,4},{5,7},{7,5},{8,10},{10,8},{9,1... | collective-permute-start | bytes 1572872 | tf_op jit(solution)/shard_map/ppermute | solution.py:897
  (71 other events, 541.1 us)

commit v7 on v6

--- a/solution.py
+++ b/solution.py
@@ -39,7 +39,7 @@
 
 BLOCK = 128
 MIB = 1024 * 1024
-COSTS = [0.5, 50, 10, 0.5, 20, 0, 0.5, 5, 5, 0, 50, 50, 50, 10, 50, 20, 0, 0.5, 50, 50, 0.5, 2, 20, 0.5, 50, 2, 0, 50, 0, 2, 10, 0, 0, 0.5, 20, 50, 0, 0.5, 0, 20, 2, 0, 0, 0, 0, 2, 0, 0.5, 0, 0.5, 50, 0, 0, 0, 20, 0.5, 0, 10, 5, 2, 2, 10, 0, 50, 10, 20]
+COSTS = [50, 10, 20, 0.5, 0, 0, 2, 50, 5, 2, 50, 0.5, 50, 10, 50, 20, 0, 20, 50, 50, 10, 2, 20, 0.5, 50, 10, 50, 50, 50, 2, 10, 0, 5, 0.5, 20, 50, 0, 0.5, 0, 10, 5, 0, 0, 0, 2, 2, 5, 0, 2, 0.5, 20, 0.5, 0, 2, 20, 0.5, 0, 0.5, 5, 0, 2, 0, 5, 0, 0, 20]
 
 
 def whole(shape):
@@ -1016,7 +1016,7 @@
 
     low_oth, sum_oth = d_hidden_of(d_oth, w_down, slope_oth)
     unit_factors = [(mlp_own, mlp_oth, (low_own, 0), (low_oth, 0)), (d_own, d_oth, (active_own, 0), (active_oth, 0))]
-    unit_far = far_parts(unit_factors, 2)
+    unit_far = far_parts(unit_factors, 1)
     branch_far = to_ctx(fold(cross, branch_keep, branch_got))
     d_linear, unit_sums = attend_back(z_scalar, packed_qkv, logs, d_own, d_oth, w_attn, cosine, sine)
     unit_pieces = near_parts(unit_factors, unit_far)
@@ -1044,7 +1044,7 @@
         (total,) = totals(total.shape[0], ((total, 0), (moved, 0)), dtype=F32)
         return total, moves[0](total) if moves else None
 
-    attn_far = far_parts(attn_factors, 2)
+    attn_far = far_parts(attn_factors, 1)
     out_bias = (vec[4] + vec[5]).reshape(1, width)
     (out_own,) = totals(quarter, ((branch_own[0], 0), (branch_near, 0), (branch_far, 0), (x_own, 0), (out_bias, 0)), steps=2)
     out_other = to_ten(out_own)

time: 533 us -> 534 us (level)
    ppermute x51 -> x49, waiting for transfers between devices: 133 us -> 131 us  [along(): return lambda v: lax.ppermute(v, axis, [(i, i ^ bit) for i in range(size)])]
    ppermute x51 -> x49, starting transfers between devices: 42.9 us -> 43.3 us  [along(): return lambda v: lax.ppermute(v, axis, [(i, i ^ bit) for i in range(size)])]
  transfers between devices with their start and end apart: 51 -> 49, of which waited for: 14 -> 13; matrix products, arithmetic and copies ran while one was open for 3% -> 4% of each run, Pallas kernels for 56% -> 56%
where the time goes in v7:
time: 534 us; the launch traced here: 526 us
  Pallas kernels  309 us (58%)
  waiting for transfers between devices  131 us (25%)
  starting transfers between devices  43.3 us (8%)
  local copies, waits for them, and re-layouts  30 us (6%)
  other arithmetic  10.5 us (2%)
    pallas_call x50, Pallas kernels, ordered_call(): *results, token = run(*operands, *waits)  309 us
    ppermute x49, waiting for transfers between devices, along(): return lambda v: lax.ppermute(v, axis, [(i, i ^ bit) for i in range(size)])  131 us
    ppermute x49, starting transfers between devices, along(): return lambda v: lax.ppermute(v, axis, [(i, i ^ bit) for i in range(size)])  43.3 us
    unnamed x111, local copies, waits for them, and re-layouts  24.6 us
  transfers between devices with their start and end apart: 49, of which 13 were waited for; matrix products, arithmetic and copies ran while one was open for 4% of the time, Pallas kernels for 56%

profile of v7, /device:TPU:0, one launch (start us, length us, event | category | flops | bytes accessed | tf_op | source)
XLA Modules:
  0.0 525.6 jit_solution(11644800192534677693)
XLA Ops:
  3.2 3.7 cut.4
  14.7 6.3 %arrange.1 = (bf16[512,2048]{1,0:T(8,128)(2,1)}, bf16[512,2048]{1,0:T(8,128)(2,1)}, f32[6,2048]{1,0:T(8,128)}, f32[8,128]{1,0:T(8,128)}) custom-call(s32[33]{0:T(128)} %stack.134.refs_0_, bf16[512,2048]{1,0:T(8,128)(2,1)} %bitcast.104, bf16[512,2048]{1,0:T(8,128)(2,1)} %bitcast.93, bf16[6,2048]{1,0:T(8,128)(2,1)} %refs_3_.7, f32[8,128]{1,0:T(8,128)} %get-tuple-element.162.refs_4_), custom_call_target="tpu_custom_call" | custom-call | flops 20000000000 | bytes 1 | tf_op jit(solution)/shard_map/arrange/pallas_call | solution.py:82
  21.1 4.7 norm.2
  29.9 14.8 %collective-permute-done.refs_0_.refs_1_ = bf16[128,6144]{1,0:T(8,128)(2,1)} collective-permute-done((bf16[128,6144]{1,0:T(8,128)(2,1)}, bf16[128,6144]{1,0:T(8,128)(2,1)}, u32[]{:S(2)}, u32[]{:S(2)}) %collective-permute-start) | collective-permute-done | bytes 1572896 | tf_op jit(solution)/shard_map/ppermute | solution.py:897
  52.5 6.9 %collective-permute-done.4.refs_4_.refs_0_ = bf16[128,4096]{1,0:T(8,128)(2,1)S(1)} collective-permute-done((bf16[128,4096]{1,0:T(8,128)(2,1)}, bf16[128,4096]{1,0:T(8,128)(2,1)S(1)}, u32[]{:S(2)}, u32[]{:S(2)}) %collective-permute-start.4) | collective-permute-done | bytes 1048608 | tf_op jit(solution)/shard_map/ppermute | solution.py:897
  66.1 22.1 %collective-permute-done.5.refs_3_.refs_0_ = bf16[128,2048]{1,0:T(8,128)(2,1)S(1)} collective-permute-done((bf16[128,2048]{1,0:T(8,128)(2,1)}, bf16[128,2048]{1,0:T(8,128)(2,1)S(1)}, u32[]{:S(2)}, u32[]{:S(2)}) %collective-permute-start.5) | collective-permute-done | bytes 524320 | tf_op jit(solution)/shard_map/ppermute | solution.py:897
  108.8 6.9 %collective-permute-done.8.refs_3_ = bf16[64,4096]{1,0:T(8,128)(2,1)S(1)} collective-permute-done((bf16[64,4096]{1,0:T(8,128)(2,1)}, bf16[64,4096]{1,0:T(8,128)(2,1)S(1)}, u32[]{:S(2)}, u32[]{:S(2)}) %collective-permute-start.8) | collective-permute-done | bytes 524320 | tf_op jit(solution)/shard_map/ppermute | solution.py:897
  128.9 11.3 %hidden.2 = (bf16[512,2048]{1,0:T(8,128)(2,1)}, f32[512,2048]{1,0:T(8,128)}, f32[8,128]{1,0:T(8,128)}) custom-call(bf16[512,2048]{1,0:T(8,128)(2,1)} %get-tuple-element.166.refs_0_, f32[1,2048]{1,0:T(1,128)} %bitcast.102, bf16[512,2048]{1,0:T(8,128)(2,1)} %get-tuple-element.176.refs_2_.refs_14_, bf16[512,2048]{1,0:T(8,128)(2,1)} %get-tuple-element.183.refs_3_.refs_15_, ...), custom_call_target="tpu_custom_call" | custom-call | flops 49999998976 | bytes 1 | tf_op jit(solution)/shard_map/hidden/pallas_call | solution.py:82
  151.1 9.8 %d_hidden.2 = (bf16[512,2048]{1,0:T(8,128)(2,1)}, f32[8,2048]{1,0:T(8,128)}, f32[8,128]{1,0:T(8,128)}) custom-call(bf16[512,2048]{1,0:T(8,128)(2,1)} %get-tuple-element.189.refs_0_.refs_4_.refs_3_.refs_6_, f32[512,2048]{1,0:T(8,128)} %get-tuple-element.190.refs_1_, bf16[512,2048]{1,0:T(8,128)(2,1)} %get-tuple-element.191.refs_2_.refs_3_, ...), custom_call_target="tpu_custom_call" | custom-call | flops 20000000000 | bytes 1 | tf_op jit(solution)/shard_map/d_hidden/pallas_call | solution.py:82
  160.9 20.4 %collective-permute-done.15.refs_1_ = bf16[256,2048]{1,0:T(8,128)(2,1)S(1)} collective-permute-done((bf16[256,2048]{1,0:T(8,128)(2,1)}, bf16[256,2048]{1,0:T(8,128)(2,1)S(1)}, u32[]{:S(2)}, u32[]{:S(2)}) %collective-permute-start.15) | collective-permute-done | bytes 1048608 | tf_op jit(solution)/shard_map/ppermute | solution.py:897
  185.3 4.6 norm.3
  189.9 10.8 %hidden.3 = (bf16[512,2048]{1,0:T(8,128)(2,1)}, f32[512,2048]{1,0:T(8,128)}, f32[8,128]{1,0:T(8,128)}) custom-call(bf16[512,2048]{1,0:T(8,128)(2,1)} %get-tuple-element.201.refs_0_.refs_1_, f32[1,2048]{1,0:T(1,128)} %bitcast.103, bf16[512,2048]{1,0:T(8,128)(2,1)} %get-tuple-element.176.refs_2_.refs_14_, ...), custom_call_target="tpu_custom_call" | custom-call | flops 10000000000 | bytes 1 | tf_op jit(solution)/shard_map/hidden/pallas_call | solution.py:82
  202.4 17.8 %attend.1 = (bf16[1024,512]{1,0:T(8,128)(2,1)}, bf16[1024,1536]{1,0:T(8,128)(2,1)}, f32[1024,256]{1,0:T(8,128)}, f32[8,128]{1,0:T(8,128)}) custom-call(s32[1]{0:T(128)} %bitcast.28.refs_0_, bf16[512,2048]{1,0:T(8,128)(2,1)} %get-tuple-element.204.refs_1_.refs_0_, bf16[512,2048]{1,0:T(8,128)(2,1)} %get-tuple-element.205.refs_2_.refs_1_, f32[1,1536]{1,0:T(1,128)} %bitcast.100, ...), custom_call_target="tpu_custom_call" | custom-call | flops 2000000000 | bytes 1 | tf_op jit(solution)/shard_map/attend/pallas_call | solution.py:82
  220.2 18.6 %branch.1 = (f32[256,2048]{1,0:T(8,128)}, bf16[256,2048]{1,0:T(8,128)(2,1)}, f32[256,2048]{1,0:T(8,128)}, bf16[256,2048]{1,0:T(8,128)(2,1)}, f32[8,128]{1,0:T(8,128)}) custom-call(bf16[512,2048]{1,0:T(8,128)(2,1)} %get-tuple-element.187.refs_0_.refs_6_, bf16[512,2048]{1,0:T(8,128)(2,1)} %get-tuple-element.203.refs_1_.refs_7_, ...), custom_call_target="tpu_custom_call" | custom-call | flops 20000000000 | bytes 1 | tf_op jit(solution)/shard_map/branch/pallas_call | solution.py:82
  244.6 9.8 %d_hidden.3 = (bf16[512,2048]{1,0:T(8,128)(2,1)}, f32[8,2048]{1,0:T(8,128)}, f32[8,128]{1,0:T(8,128)}) custom-call(bf16[512,2048]{1,0:T(8,128)(2,1)} %get-tuple-element.218.refs_0_.refs_5_.refs_4_, f32[512,2048]{1,0:T(8,128)} %get-tuple-element.219.refs_1_, bf16[512,2048]{1,0:T(8,128)(2,1)} %get-tuple-element.191.refs_2_.refs_3_, ...), custom_call_target="tpu_custom_call" | custom-call | flops 49999998976 | bytes 1 | tf_op jit(solution)/shard_map/d_hidden/pallas_call | solution.py:82
  255.3 18.3 %grad_far.2 = (bf16[1024,4096]{1,0:T(8,128)(2,1)}, f32[8,128]{1,0:T(8,128)}) custom-call(bf16[512,2048]{1,0:T(8,128)(2,1)} %get-tuple-element.166.refs_0_, bf16[512,2048]{1,0:T(8,128)(2,1)} %get-tuple-element.201.refs_0_.refs_1_, bf16[512,2048]{1,0:T(8,128)(2,1)} %get-tuple-element.216.refs_2_.refs_1_, bf16[512,2048]{1,0:T(8,128)(2,1)} %get-tuple-element.221.refs_3_.refs_2_, ...), custom_call_target="tpu_custom_call" | custom-call | flops 10000000000 | bytes 1 | tf_op jit(solution)/shard_map/grad_far/pallas_call | solution.py:82
  277.7 14.3 %attend_back.1 = (bf16[1024,1536]{1,0:T(8,128)(2,1)}, f32[8,1536]{1,0:T(8,128)}, f32[8,128]{1,0:T(8,128)}) custom-call(s32[1]{0:T(128)} %bitcast.28.refs_0_, bf16[1024,1536]{1,0:T(8,128)(2,1)} %get-tuple-element.225.refs_1_, f32[1024,256]{1,0:T(8,128)} %get-tuple-element.226.refs_2_, bf16[512,2048]{1,0:T(8,128)(2,1)} %get-tuple-element.189.refs_0_.refs_4_.refs_3_.refs_6_, ...), custom_call_target="tpu_custom_call" | custom-call | flops 49999998976 | bytes 1 | tf_op jit(solution)/shard_map/attend_back/pallas_call | solution.py:82
  293.1 4.4 collective-permute-start.26
  297.5 19.7 %grad_near.2 = (bf16[256,4096]{1,0:T(8,128)(2,1)}, bf16[256,4096]{1,0:T(8,128)(2,1)}, bf16[256,4096]{1,0:T(8,128)(2,1)}, bf16[256,4096]{1,0:T(8,128)(2,1)}, f32[8,128]{1,0:T(8,128)}) custom-call(bf16[512,2048]{1,0:T(8,128)(2,1)} %get-tuple-element.166.refs_0_, bf16[512,2048]{1,0:T(8,128)(2,1)} %get-tuple-element.201.refs_0_.refs_1_, ...), custom_call_target="tpu_custom_call" | custom-call | flops 49999998976 | bytes 1 | tf_op jit(solution)/shard_map/grad_near/pallas_call | solution.py:82
  319.2 26.2 %input_grad.1 = (f32[256,2048]{1,0:T(8,128)}, bf16[256,2048]{1,0:T(8,128)(2,1)}, f32[256,2048]{1,0:T(8,128)}, bf16[256,2048]{1,0:T(8,128)(2,1)}, f32[8,2048]{1,0:T(8,128)}, /*index=5*/f32[8,128]{1,0:T(8,128)}) custom-call(bf16[1024,1536]{1,0:T(8,128)(2,1)} %get-tuple-element.228.refs_0_.refs_2_.refs_3_, ...), custom_call_target="tpu_custom_call" | custom-call | flops 2000000000 | bytes 1 | tf_op jit(solution)/shard_map/input_grad/pallas_call | solution.py:82
  350.3 11.4 %grad_far.3 = (bf16[1024,2048]{1,0:T(8,128)(2,1)}, f32[8,128]{1,0:T(8,128)}) custom-call(bf16[512,2048]{1,0:T(8,128)(2,1)} %get-tuple-element.204.refs_1_.refs_0_, bf16[512,2048]{1,0:T(8,128)(2,1)} %get-tuple-element.205.refs_2_.refs_1_, bf16[1024,1536]{1,0:T(8,128)(2,1)} %get-tuple-element.228.refs_0_.refs_2_.refs_3_, ...), custom_call_target="tpu_custom_call" | custom-call | bytes 1 | tf_op jit(solution)/shard_map/grad_far/pallas_call | solution.py:82
  362.7 3.6 totals.11
  369.5 3.7 totals.12
  382.8 11.9 %grad_near.3 = (bf16[256,2048]{1,0:T(8,128)(2,1)}, bf16[256,2048]{1,0:T(8,128)(2,1)}, bf16[256,2048]{1,0:T(8,128)(2,1)}, bf16[256,2048]{1,0:T(8,128)(2,1)}, f32[8,128]{1,0:T(8,128)}) custom-call(bf16[512,2048]{1,0:T(8,128)(2,1)} %get-tuple-element.204.refs_1_.refs_0_, bf16[512,2048]{1,0:T(8,128)(2,1)} %get-tuple-element.205.refs_2_.refs_1_, ...), custom_call_target="tpu_custom_call" | custom-call | bytes 1 | tf_op jit(solution)/shard_map/grad_near/pallas_call | solution.py:82
  394.6 16.0 %collective-permute-done.29.refs_1_ = bf16[256,2048]{1,0:T(8,128)(2,1)S(1)} collective-permute-done((bf16[256,2048]{1,0:T(8,128)(2,1)S(1)}, bf16[256,2048]{1,0:T(8,128)(2,1)S(1)}, u32[]{:S(2)}, u32[]{:S(2)}) %collective-permute-start.29) | collective-permute-done | bytes 1048608 | tf_op jit(solution)/shard_map/ppermute | solution.py:897
  417.3 8.8 %collective-permute-done.33.refs_2_ = bf16[256,2048]{1,0:T(8,128)(2,1)S(1)} collective-permute-done((bf16[256,2048]{1,0:T(8,128)(2,1)}, bf16[256,2048]{1,0:T(8,128)(2,1)S(1)}, u32[]{:S(2)}, u32[]{:S(2)}) %collective-permute-start.33) | collective-permute-done | bytes 1048608 | tf_op jit(solution)/shard_map/ppermute | solution.py:897
  433.8 22.6 %collective-permute-done.28.refs_5_.refs_2_ = bf16[256,2048]{1,0:T(8,128)(2,1)} collective-permute-done((bf16[256,2048]{1,0:T(8,128)(2,1)}, bf16[256,2048]{1,0:T(8,128)(2,1)}, u32[]{:S(2)}, u32[]{:S(2)}) %collective-permute-start.28) | collective-permute-done | bytes 1048608 | tf_op jit(solution)/shard_map/ppermute | solution.py:897
  466.4 5.5 %collective-permute-done.45.refs_2_ = bf16[128,2048]{1,0:T(8,128)(2,1)S(1)} collective-permute-done((bf16[128,2048]{1,0:T(8,128)(2,1)}, bf16[128,2048]{1,0:T(8,128)(2,1)S(1)}, u32[]{:S(2)}, u32[]{:S(2)}) %collective-permute-start.45) | collective-permute-done | bytes 524320 | tf_op jit(solution)/shard_map/ppermute | solution.py:897
  481.9 6.7 %adam.3 = (f32[128,4096]{1,0:T(8,128)}, f32[2,128,4096]{2,1,0:T(8,128)}, f32[128,4096]{1,0:T(8,128)}, f32[8,128]{1,0:T(8,128)}) custom-call(s32[1]{0:T(128)} %bitcast.27.refs_0_, f32[2]{0:T(128)} %pad_maximum_fusion.5.refs_1_, bf16[128,4096]{1,0:T(8,128)(2,1)} %refs_2_.10, f32[2,128,4096]{2,1,0:T(8,128)} %refs_3_.8, ...), custom_call_target="tpu_custom_call" | custom-call | flops 2000000000 | bytes 1 | tf_op jit(solution)/shard_map/adam/pallas_call | solution.py:82
  488.5 6.7 %adam.4 = (f32[128,4096]{1,0:T(8,128)}, f32[2,128,4096]{2,1,0:T(8,128)}, f32[128,4096]{1,0:T(8,128)}, f32[8,128]{1,0:T(8,128)}) custom-call(s32[1]{0:T(128)} %bitcast.27.refs_0_, f32[2]{0:T(128)} %pad_maximum_fusion.5.refs_1_, bf16[128,4096]{1,0:T(8,128)(2,1)} %refs_2_.11, f32[2,128,4096]{2,1,0:T(8,128)} %refs_3_.9, ...), custom_call_target="tpu_custom_call" | custom-call | flops 2000000000 | bytes 1 | tf_op jit(solution)/shard_map/adam/pallas_call | solution.py:82
  497.4 9.3 %finish.1 = (bf16[512,2048]{1,0:T(8,128)(2,1)}, f32[512,2048]{1,0:T(8,128)}, f32[8,128]{1,0:T(8,128)}) custom-call(s32[33]{0:T(128)} %stack.134.refs_0_, bf16[256,2048]{1,0:T(8,128)(2,1)} %get-tuple-element.240.refs_1_, bf16[256,2048]{1,0:T(8,128)(2,1)} %collective-permute-done.28.refs_5_.refs_2_, bf16[256,2048]{1,0:T(8,128)(2,1)} %get-tuple-element.263.refs_3_, ...), custom_call_target="tpu_custom_call" | custom-call | flops 5000000000 | bytes 1 | tf_op jit(solution)/shard_map/finish/pallas_call | solution.py:82
  515.0 7.6 %adam_heads.1 = (f32[128,4,768]{2,1,0:T(4,128)}, f32[2,128,4,768]{3,2,1,0:T(4,128)}, f32[128,4,768]{2,1,0:T(4,128)}, f32[8,128]{1,0:T(8,128)}) custom-call(s32[1]{0:T(128)} %bitcast.27.refs_0_, f32[2]{0:T(128)} %pad_maximum_fusion.5.refs_1_, bf16[128,4,768]{2,1,0:T(4,128)(2,1)} %refs_2_.12, f32[2,128,4,768]{3,2,1,0:T(4,128)} %refs_3_.10, ...), custom_call_target="tpu_custom_call" | custom-call | flops 2000000000 | bytes 1 | tf_op jit(solution)/shard_map/adam_heads/pallas_call | solution.py:82
  (263 shorter events, 158.3 us)
Async XLA Ops:
  7.0 37.7 %collective-permute-start = (bf16[128,6144]{1,0:T(8,128)(2,1)}, bf16[128,6144]{1,0:T(8,128)(2,1)}, u32[]{:S(2)}, u32[]{:S(2)}) collective-permute-start(bf16[128,6144]{1,0:T(8,128)(2,1)} %get-tuple-element.167.refs_0_), channel_id=1, source_target_pairs={{0,16},{4,20},{8,24},{12,28},{16,0},{20,4},{24,8},{28,12},{1,17},{... | collective-permute-start | bytes 4718600 | tf_op jit(solution)/shard_map/ppermute | solution.py:897
  10.0 36.2 %collective-permute-start.1 = (bf16[128,6144]{1,0:T(8,128)(2,1)}, bf16[128,6144]{1,0:T(8,128)(2,1)}, u32[]{:S(2)}, u32[]{:S(2)}) collective-permute-start(bf16[128,6144]{1,0:T(8,128)(2,1)} %get-tuple-element.167.refs_0_), channel_id=1, source_target_pairs={{0,8},{4,12},{8,0},{12,4},{16,24},{20,28},{24,16},{28,20},{1,9},{5... | collective-permute-start | bytes 4718600 | tf_op jit(solution)/shard_map/ppermute | solution.py:897
  11.4 47.9 %collective-permute-start.4 = (bf16[128,4096]{1,0:T(8,128)(2,1)}, bf16[128,4096]{1,0:T(8,128)(2,1)S(1)}, u32[]{:S(2)}, u32[]{:S(2)}) collective-permute-start(bf16[128,4096]{1,0:T(8,128)(2,1)} %get-tuple-element.172), channel_id=1, source_target_pairs={{0,2},{2,0},{1,3},{3,1},{4,6},{6,4},{5,7},{7,5},{8,10},{10,8},{9,1... | collective-permute-start | bytes 3145736 | tf_op jit(solution)/shard_map/ppermute | solution.py:897
  48.7 43.4 %collective-permute-start.2 = (bf16[64,6144]{1,0:T(8,128)(2,1)}, bf16[64,6144]{1,0:T(8,128)(2,1)S(1)}, u32[]{:S(2)}, u32[]{:S(2)}) collective-permute-start(bf16[64,6144]{1,0:T(8,128)(2,1)} %get-tuple-element.169), channel_id=1, source_target_pairs={{0,8},{4,12},{8,0},{12,4},{16,24},{20,28},{24,16},{28,20},{1,9},{5... | collective-permute-start | bytes 2359304 | tf_op jit(solution)/shard_map/ppermute | solution.py:897
  50.2 42.5 %collective-permute-start.3 = (bf16[64,6144]{1,0:T(8,128)(2,1)}, bf16[64,6144]{1,0:T(8,128)(2,1)S(1)}, u32[]{:S(2)}, u32[]{:S(2)}) collective-permute-start(bf16[64,6144]{1,0:T(8,128)(2,1)} %get-tuple-element.170), channel_id=1, source_target_pairs={{0,16},{4,20},{8,24},{12,28},{16,0},{20,4},{24,8},{28,12},{1,17},{... | collective-permute-start | bytes 2359304 | tf_op jit(solution)/shard_map/ppermute | solution.py:897
  65.1 34.4 %collective-permute-start.6 = (bf16[128,4096]{1,0:T(8,128)(2,1)}, bf16[128,4096]{1,0:T(8,128)(2,1)S(1)}, u32[]{:S(2)}, u32[]{:S(2)}) collective-permute-start(bf16[128,4096]{1,0:T(8,128)(2,1)} %copy-done.6), channel_id=1, source_target_pairs={{0,8},{4,12},{8,0},{12,4},{16,24},{20,28},{24,16},{28,20},{1,9},{5... | collective-permute-start | bytes 3145736 | tf_op jit(solution)/shard_map/ppermute | solution.py:897
  65.6 33.8 %collective-permute-start.7 = (bf16[128,4096]{1,0:T(8,128)(2,1)}, bf16[128,4096]{1,0:T(8,128)(2,1)S(1)}, u32[]{:S(2)}, u32[]{:S(2)}) collective-permute-start(bf16[128,4096]{1,0:T(8,128)(2,1)} %copy-done.6), channel_id=1, source_target_pairs={{0,16},{4,20},{8,24},{12,28},{16,0},{20,4},{24,8},{28,12},{1,17},{... | collective-permute-start | bytes 3145736 | tf_op jit(solution)/shard_map/ppermute | solution.py:897
  92.1 48.1 %collective-permute-start.14 = (bf16[256,2048]{1,0:T(8,128)(2,1)}, bf16[256,2048]{1,0:T(8,128)(2,1)}, u32[]{:S(2)}, u32[]{:S(2)}) collective-permute-start(bf16[256,2048]{1,0:T(8,128)(2,1)} %get-tuple-element.188), channel_id=1, source_target_pairs={{0,2},{2,0},{1,3},{3,1},{4,6},{6,4},{5,7},{7,5},{8,10},{10,8},{9,1... | collective-permute-start | bytes 3145736 | tf_op jit(solution)/shard_map/ppermute | solution.py:897
  115.7 35.3 %collective-permute-start.16 = (bf16[512,2048]{1,0:T(8,128)(2,1)}, bf16[512,2048]{1,0:T(8,128)(2,1)}, u32[]{:S(2)}, u32[]{:S(2)}) collective-permute-start(bf16[512,2048]{1,0:T(8,128)(2,1)} %get-tuple-element.191.refs_2_.refs_3_), channel_id=1, source_target_pairs={{0,4},{4,0},{8,12},{12,8},{16,20},{20,16},{24,28},{28,24},{1,5},{5... | collective-permute-start | bytes 6291464 | tf_op jit(solution)/shard_map/ppermute | solution.py:897
  140.2 60.6 %collective-permute-start.20 = (bf16[512,2048]{1,0:T(8,128)(2,1)}, bf16[512,2048]{1,0:T(8,128)(2,1)}, u32[]{:S(2)}, u32[]{:S(2)}) collective-permute-start(bf16[512,2048]{1,0:T(8,128)(2,1)} %get-tuple-element.206.refs_6_.refs_7_.refs_10_), channel_id=1, source_target_pairs={{0,4},{4,0},{8,12},{12,8},{16,20},{20,16},{24,28},{28,24},{1,5},{5... | collective-permute-start | bytes 6291464 | tf_op jit(solution)/shard_map/ppermute | solution.py:897
  140.3 41.0 %collective-permute-start.15 = (bf16[256,2048]{1,0:T(8,128)(2,1)}, bf16[256,2048]{1,0:T(8,128)(2,1)S(1)}, u32[]{:S(2)}, u32[]{:S(2)}) collective-permute-start(bf16[256,2048]{1,0:T(8,128)(2,1)} %collective-permute-done.14.refs_3_.refs_0_), channel_id=1, source_target_pairs={{0,1},{1,0},{2,3},{3,2},{4,5},{5,4},{6,7},{7,6},{8,9},{9,8},{10,11... | collective-permute-start | bytes 3145736 | tf_op jit(solution)/shard_map/ppermute | solution.py:897
  150.7 50.0 %collective-permute-start.22 = (bf16[256,2048]{1,0:T(8,128)(2,1)}, bf16[256,2048]{1,0:T(8,128)(2,1)S(1)}, u32[]{:S(2)}, u32[]{:S(2)}) collective-permute-start(bf16[256,2048]{1,0:T(8,128)(2,1)} %get-tuple-element.209), channel_id=1, source_target_pairs={{0,2},{2,0},{1,3},{3,1},{4,6},{6,4},{5,7},{7,5},{8,10},{10,8},{9,1... | collective-permute-start | bytes 3145736 | tf_op jit(solution)/shard_map/ppermute | solution.py:897
  151.1 49.7 %collective-permute-start.21 = (bf16[512,2048]{1,0:T(8,128)(2,1)S(1)}, bf16[512,2048]{1,0:T(8,128)(2,1)S(1)}, u32[]{:S(2)}, u32[]{:S(2)}) collective-permute-start(bf16[512,2048]{1,0:T(8,128)(2,1)S(1)} %copy-done.3), channel_id=1, source_target_pairs={{0,4},{4,0},{8,12},{12,8},{16,20},{20,16},{24,28},{28,24},{1,5},{5... | collective-permute-start | bytes 6291464 | tf_op jit(solution)/shard_map/ppermute | solution.py:897
  200.7 40.0 %collective-permute-start.25 = (bf16[256,2048]{1,0:T(8,128)(2,1)S(1)}, bf16[256,2048]{1,0:T(8,128)(2,1)S(1)}, u32[]{:S(2)}, u32[]{:S(2)}) collective-permute-start(bf16[256,2048]{1,0:T(8,128)(2,1)S(1)} %collective-permute-done.22.refs_11_.refs_0_), channel_id=1, source_target_pairs={{0,1},{1,0},{2,3},{3,2},{4,5},{5,4},{6,7},{7,6},{8,9},{9,8},{10,11... | collective-permute-start | bytes 3145736 | tf_op jit(solution)/shard_map/ppermute | solution.py:897
  238.8 35.2 %collective-permute-start.24 = (bf16[256,2048]{1,0:T(8,128)(2,1)}, bf16[256,2048]{1,0:T(8,128)(2,1)S(1)}, u32[]{:S(2)}, u32[]{:S(2)}) collective-permute-start(bf16[256,2048]{1,0:T(8,128)(2,1)} %get-tuple-element.215), channel_id=1, source_target_pairs={{0,1},{1,0},{2,3},{3,2},{4,5},{5,4},{6,7},{7,6},{8,9},{9,8},{10,11... | collective-permute-start | bytes 3145736 | tf_op jit(solution)/shard_map/ppermute | solution.py:897
  273.7 45.5 %collective-permute-start.23 = (bf16[256,2048]{1,0:T(8,128)(2,1)}, bf16[256,2048]{1,0:T(8,128)(2,1)}, u32[]{:S(2)}, u32[]{:S(2)}) collective-permute-start(bf16[256,2048]{1,0:T(8,128)(2,1)} %get-tuple-element.213), channel_id=1, source_target_pairs={{0,1},{1,0},{2,3},{3,2},{4,5},{5,4},{6,7},{7,6},{8,9},{9,8},{10,11... | collective-permute-start | bytes 3145736 | tf_op jit(solution)/shard_map/ppermute | solution.py:897
  293.1 68.6 %collective-permute-start.26 = (bf16[256,2048]{1,0:T(8,128)(2,1)S(1)}, bf16[256,2048]{1,0:T(8,128)(2,1)S(1)}, u32[]{:S(2)}, u32[]{:S(2)}) collective-permute-start(bf16[256,2048]{1,0:T(8,128)(2,1)S(1)} %copy-done.39), channel_id=1, source_target_pairs={{0,2},{2,0},{1,3},{3,1},{4,6},{6,4},{5,7},{7,5},{8,10},{10,8},{9,1... | collective-permute-start | bytes 3145736 | tf_op jit(solution)/shard_map/ppermute | solution.py:897
  317.2 49.0 %collective-permute-start.31 = (bf16[256,4096]{1,0:T(8,128)(2,1)}, bf16[256,4096]{1,0:T(8,128)(2,1)S(1)}, u32[]{:S(2)}, u32[]{:S(2)}) collective-permute-start(bf16[256,4096]{1,0:T(8,128)(2,1)} %get-tuple-element.246), channel_id=1, source_target_pairs={{0,16},{4,20},{8,24},{12,28},{16,0},{20,4},{24,8},{28,12},{1,17},{... | collective-permute-start | bytes 6291464 | tf_op jit(solution)/shard_map/ppermute | solution.py:897
  317.8 50.4 %collective-permute-start.32 = (bf16[256,4096]{1,0:T(8,128)(2,1)}, bf16[256,4096]{1,0:T(8,128)(2,1)S(1)}, u32[]{:S(2)}, u32[]{:S(2)}) collective-permute-start(bf16[256,4096]{1,0:T(8,128)(2,1)} %get-tuple-element.248), channel_id=1, source_target_pairs={{0,8},{4,12},{8,0},{12,4},{16,24},{20,28},{24,16},{28,20},{1,9},{5... | collective-permute-start | bytes 6291464 | tf_op jit(solution)/shard_map/ppermute | solution.py:897
  350.2 29.3 %collective-permute-start.36 = (f32[240,128]{1,0:T(8,128)S(1)}, f32[240,128]{1,0:T(8,128)S(1)}, u32[]{:S(2)}, u32[]{:S(2)}) collective-permute-start(f32[240,128]{1,0:T(8,128)S(1)} %maximum_bitcast_fusion.refs_0_), channel_id=1, source_target_pairs={{0,2},{2,0},{1,3},{3,1},{4,6},{6,4},{5,7},{7,5},{8,10},{10,8},{9,1... | collective-permute-start | bytes 368648 | tf_op jit(solution)/shard_map/ppermute | solution.py:897
  366.3 44.4 %collective-permute-start.29 = (bf16[256,2048]{1,0:T(8,128)(2,1)S(1)}, bf16[256,2048]{1,0:T(8,128)(2,1)S(1)}, u32[]{:S(2)}, u32[]{:S(2)}) collective-permute-start(bf16[256,2048]{1,0:T(8,128)(2,1)S(1)} %copy-done.38), channel_id=1, source_target_pairs={{0,1},{1,0},{2,3},{3,2},{4,5},{5,4},{6,7},{7,6},{8,9},{9,8},{10,11... | collective-permute-start | bytes 3145736 | tf_op jit(solution)/shard_map/ppermute | solution.py:897
  373.3 37.4 %collective-permute-start.34 = (bf16[128,4096]{1,0:T(8,128)(2,1)}, bf16[128,4096]{1,0:T(8,128)(2,1)S(1)}, u32[]{:S(2)}, u32[]{:S(2)}) collective-permute-start(bf16[128,4096]{1,0:T(8,128)(2,1)} %get-tuple-element.252), channel_id=1, source_target_pairs={{0,8},{4,12},{8,0},{12,4},{16,24},{20,28},{24,16},{28,20},{1,9},{5... | collective-permute-start | bytes 3145736 | tf_op jit(solution)/shard_map/ppermute | solution.py:897
  375.2 37.9 %collective-permute-start.37 = (bf16[128,4096]{1,0:T(8,128)(2,1)}, bf16[128,4096]{1,0:T(8,128)(2,1)S(1)}, u32[]{:S(2)}, u32[]{:S(2)}) collective-permute-start(bf16[128,4096]{1,0:T(8,128)(2,1)} %get-tuple-element.261), channel_id=1, source_target_pairs={{0,16},{4,20},{8,24},{12,28},{16,0},{20,4},{24,8},{28,12},{1,17},{... | collective-permute-start | bytes 3145736 | tf_op jit(solution)/shard_map/ppermute | solution.py:897
  379.5 46.6 %collective-permute-start.33 = (bf16[256,2048]{1,0:T(8,128)(2,1)}, bf16[256,2048]{1,0:T(8,128)(2,1)S(1)}, u32[]{:S(2)}, u32[]{:S(2)}) collective-permute-start(bf16[256,2048]{1,0:T(8,128)(2,1)} %get-tuple-element.251), channel_id=1, source_target_pairs={{0,2},{2,0},{1,3},{3,1},{4,6},{6,4},{5,7},{7,5},{8,10},{10,8},{9,1... | collective-permute-start | bytes 3145736 | tf_op jit(solution)/shard_map/ppermute | solution.py:897
  382.8 47.4 %collective-permute-start.40 = (f32[240,128]{1,0:T(8,128)}, f32[240,128]{1,0:T(8,128)S(1)}, u32[]{:S(2)}, u32[]{:S(2)}) collective-permute-start(f32[240,128]{1,0:T(8,128)} %get-tuple-element.265.refs_0_), channel_id=1, source_target_pairs={{0,4},{4,0},{8,12},{12,8},{16,20},{20,16},{24,28},{28,24},{1,5},{5... | collective-permute-start | bytes 368648 | tf_op jit(solution)/shard_map/ppermute | solution.py:897
  410.7 45.7 %collective-permute-start.28 = (bf16[256,2048]{1,0:T(8,128)(2,1)}, bf16[256,2048]{1,0:T(8,128)(2,1)}, u32[]{:S(2)}, u32[]{:S(2)}) collective-permute-start(bf16[256,2048]{1,0:T(8,128)(2,1)} %get-tuple-element.240.refs_1_), channel_id=1, source_target_pairs={{0,1},{1,0},{2,3},{3,2},{4,5},{5,4},{6,7},{7,6},{8,9},{9,8},{10,11... | collective-permute-start | bytes 3145736 | tf_op jit(solution)/shard_map/ppermute | solution.py:897
  410.7 45.6 %collective-permute-start.42 = (bf16[256,2048]{1,0:T(8,128)(2,1)}, bf16[256,2048]{1,0:T(8,128)(2,1)S(1)}, u32[]{:S(2)}, u32[]{:S(2)}) collective-permute-start(bf16[256,2048]{1,0:T(8,128)(2,1)} %get-tuple-element.269), channel_id=1, source_target_pairs={{0,16},{4,20},{8,24},{12,28},{16,0},{20,4},{24,8},{28,12},{1,17},{... | collective-permute-start | bytes 3145736 | tf_op jit(solution)/shard_map/ppermute | solution.py:897
  413.1 43.2 %collective-permute-start.43 = (bf16[256,2048]{1,0:T(8,128)(2,1)}, bf16[256,2048]{1,0:T(8,128)(2,1)S(1)}, u32[]{:S(2)}, u32[]{:S(2)}) collective-permute-start(bf16[256,2048]{1,0:T(8,128)(2,1)} %get-tuple-element.271), channel_id=1, source_target_pairs={{0,8},{4,12},{8,0},{12,4},{16,24},{20,28},{24,16},{28,20},{1,9},{5... | collective-permute-start | bytes 3145736 | tf_op jit(solution)/shard_map/ppermute | solution.py:897
  426.1 54.8 %collective-permute-start.39 = (bf16[128,4096]{1,0:T(8,128)(2,1)}, bf16[128,4096]{1,0:T(8,128)(2,1)S(1)}, u32[]{:S(2)}, u32[]{:S(2)}) collective-permute-start(bf16[128,4096]{1,0:T(8,128)(2,1)} %get-tuple-element.264), channel_id=1, source_target_pairs={{0,2},{2,0},{1,3},{3,1},{4,6},{6,4},{5,7},{7,5},{8,10},{10,8},{9,1... | collective-permute-start | bytes 3145736 | tf_op jit(solution)/shard_map/ppermute | solution.py:897
  432.4 30.2 %collective-permute-start.41 = (f32[240,128]{1,0:T(8,128)}, f32[240,128]{1,0:T(8,128)S(1)}, u32[]{:S(2)}, u32[]{:S(2)}) collective-permute-start(f32[240,128]{1,0:T(8,128)} %get-tuple-element.267.refs_0_), channel_id=1, source_target_pairs={{0,8},{4,12},{8,0},{12,4},{16,24},{20,28},{24,16},{28,20},{1,9},{5... | collective-permute-start | bytes 368648 | tf_op jit(solution)/shard_map/ppermute | solution.py:897
  456.3 41.0 %collective-permute-start.38 = (bf16[256,2048]{1,0:T(8,128)(2,1)}, bf16[256,2048]{1,0:T(8,128)(2,1)}, u32[]{:S(2)}, u32[]{:S(2)}) collective-permute-start(bf16[256,2048]{1,0:T(8,128)(2,1)} %get-tuple-element.263.refs_3_), channel_id=1, source_target_pairs={{0,1},{1,0},{2,3},{3,2},{4,5},{5,4},{6,7},{7,6},{8,9},{9,8},{10,11... | collective-permute-start | bytes 3145736 | tf_op jit(solution)/shard_map/ppermute | solution.py:897
  480.9 33.3 %collective-permute-start.47 = (bf16[128,2048]{1,0:T(8,128)(2,1)}, bf16[128,2048]{1,0:T(8,128)(2,1)S(1)}, u32[]{:S(2)}, u32[]{:S(2)}) collective-permute-start(bf16[128,2048]{1,0:T(8,128)(2,1)} %get-tuple-element.284), channel_id=1, source_target_pairs={{0,2},{2,0},{1,3},{3,1},{4,6},{6,4},{5,7},{7,5},{8,10},{10,8},{9,1... | collective-permute-start | bytes 1572872 | tf_op jit(solution)/shard_map/ppermute | solution.py:897
  (69 other events, 566.2 us)
